TPU v7x, 256 devices: a whole 4x4x8 slice. The times are simulated.
256 devices in a mesh: dp: 2 (over core), tensor: 8 (over z), expert: 16 (over y, x).
Axes of the slice: x: 4, y: 4, z: 8, core: 2. Of those that a mesh axis runs over, the one named last changes fastest.
Arguments:
- attn_heads: bfloat16 [32, 64, 4096], P(('dp', 'expert'), None, 'tensor'), may hold values from -6 to 6
- out_proj: bfloat16 [4096, 4096], P('tensor'), may hold values from -0.09375 to 0.09375
- residual: bfloat16 [32, 64, 4096], P(('dp', 'expert'), 'tensor'), may hold values from -6 to 6
- norm_gain: float32 [4096], replicated, may hold values from 0.25 to 1.75
- expert_ids: int32 [32, 64, 8], P(('dp', 'expert'), 'tensor'), may hold values from 0 to 15, all different within a row; in each aligned block of 8 rows (0 to 7, 8 to 15, ..., all dimensions but the last counted through in order) at most 6 rows name the same one
- weight_codes: int32 [32, 64, 8], P(('dp', 'expert'), 'tensor'), may hold values from 1 to 16
- w_gate: bfloat16 [16, 1536, 4096], P('expert', 'tensor'), may hold values from -0.09375 to 0.09375
- w_up: bfloat16 [16, 1536, 4096], P('expert', 'tensor'), may hold values from -0.09375 to 0.09375
- w_down: bfloat16 [16, 1536, 4096], P('expert', 'tensor'), may hold values from -0.625 to 0.625
Outputs:
- layer_out: bfloat16 [32, 64, 4096], P(('dp', 'expert'), 'tensor')
Inputs may be any that keep to these rules, and one draw needn't show every extreme that they name: `expert_ids`: each token names 8 different experts. Among the 8 consecutive tokens of one device (aligned blocks of the flattened first two dimensions) no expert is named by more than 6 rows, and every draw has an expert named exactly 6 times in some device's rows.
All inputs are finite; a program needn't handle non-finite values.
Results may differ from a plain program's by a relative error of at most 0.022.
Values may be sent and summed in bfloat16 or wider, within the bound.
No kernel may reach another device: no remote copies, remote signals or barrier semaphores. Data moves between devices by JAX's collectives and lax.ppermute only.
A program may use at most 128 MiB of HBM per device.

v0:
```python
import jax
import jax.numpy as jnp
from jax import lax
from jax.sharding import PartitionSpec as P

EXPERTS = 16
TOP = 8
CAP = 6


def normalize(hidden, norm_gain):
    mean_square = jnp.mean(hidden * hidden, axis=-1, keepdims=True)
    return (hidden * lax.rsqrt(mean_square + 1e-06) * norm_gain).astype(jnp.bfloat16)


def place_rows(route_ids, per_device):
    flat_rows = route_ids.reshape(-1)
    one_hot = (flat_rows[:, None] == jnp.arange(EXPERTS, dtype=jnp.int32)[None, :]).astype(
        jnp.int32
    )
    position = jnp.sum((jnp.cumsum(one_hot, axis=0) - one_hot) * one_hot, axis=1)
    owner_dev = flat_rows // per_device
    local_expert = flat_rows % per_device
    slot_index = owner_dev * (CAP * per_device) + position * per_device + local_expert
    return slot_index.reshape(route_ids.shape)


def build_outgoing(normed, slot_index, slot_count):
    placement = jnp.any(
        slot_index[None, :, :] == jnp.arange(slot_count, dtype=jnp.int32)[:, None, None], axis=2
    )
    return jnp.dot(
        placement.astype(jnp.bfloat16), normed, preferred_element_type=jnp.float32
    ).astype(jnp.bfloat16)


def on_device(
    attn_heads, out_proj, residual, norm_gain, expert_ids, weight_codes, w_gate, w_up, w_down
):
    tensor_count = lax.axis_size("tensor")
    expert_count = lax.axis_size("expert")
    per_device = w_gate.shape[0]
    head_rows = attn_heads[0]
    own_residual = residual[0]
    own_ids = expert_ids[0]
    own_codes = weight_codes[0]
    tok_own = own_residual.shape[0]
    model_width = own_residual.shape[1]
    slot_count = expert_count * CAP * per_device
    attn_sum = lax.psum_scatter(
        jnp.dot(head_rows, out_proj, preferred_element_type=jnp.float32).astype(jnp.bfloat16),
        "tensor",
        scatter_dimension=0,
        tiled=True,
    ).astype(jnp.float32)
    hidden = own_residual.astype(jnp.float32) + attn_sum
    normed = normalize(hidden, norm_gain)
    slot_index = place_rows(own_ids, per_device)
    outgoing = build_outgoing(normed, slot_index, slot_count).reshape(
        expert_count, CAP * per_device, model_width
    )
    arrived = lax.all_to_all(outgoing, "expert", split_axis=0, concat_axis=0, tiled=True)
    arrived = arrived.reshape(expert_count * CAP, per_device, model_width)
    portion = lax.all_gather(arrived, "tensor", axis=0, tiled=True)
    gate_value = jnp.einsum("red,efd->ref", portion, w_gate, preferred_element_type=jnp.float32)
    up_value = jnp.einsum("red,efd->ref", portion, w_up, preferred_element_type=jnp.float32)
    activated = (jax.nn.silu(gate_value) * up_value).astype(jnp.bfloat16)
    partial_out = jnp.einsum("ref,efd->red", activated, w_down, preferred_element_type=jnp.float32)
    partial_out = partial_out.astype(jnp.bfloat16).reshape(
        tensor_count * expert_count, CAP * per_device, model_width
    )
    received = lax.all_to_all(
        partial_out, ("tensor", "expert"), split_axis=0, concat_axis=0, tiled=True
    )
    received = received.reshape(tensor_count, slot_count, model_width)
    returned_flat = jnp.sum(received, axis=0, dtype=jnp.float32).astype(jnp.bfloat16)
    picked = jnp.take(returned_flat, slot_index.reshape(-1), axis=0).reshape(
        tok_own, TOP, model_width
    )
    code_values = own_codes.astype(jnp.float32)
    mixing = code_values / jnp.sum(code_values, axis=-1, keepdims=True)
    expert_mix = jnp.sum(mixing[:, :, None] * picked.astype(jnp.float32), axis=1)
    layer_out = (hidden + expert_mix).astype(jnp.bfloat16)
    return layer_out[None]


def solution(mesh):
    return jax.shard_map(
        on_device,
        mesh=mesh,
        in_specs=(
            P(("dp", "expert"), None, "tensor"),
            P("tensor", None),
            P(("dp", "expert"), "tensor", None),
            P(),
            P(("dp", "expert"), "tensor", None),
            P(("dp", "expert"), "tensor", None),
            P("expert", "tensor", None),
            P("expert", "tensor", None),
            P("expert", "tensor", None),
        ),
        out_specs=P(("dp", "expert"), "tensor", None),
        check_vma=False,
    )
```

profile of v0, /device:TPU:24, one launch (start us, length us, event | category | flops | bytes accessed | tf_op | source)
XLA Modules:
  0.0 394.1 jit_solution(4905630625477676545)
XLA Ops:
  6.5 0.0 copy-start
  6.5 0.0 copy-start.4
  6.5 0.0 copy-start.2
  6.5 0.0 copy-start.5
  6.5 0.0 reduce-scatter.2.cloned.1.call-start
  6.6 4.0 %convolution_convert_fusion.2 = bf16[64,4096]{1,0:T(8,128)(2,1)} fusion(bf16[512,4096]{1,0:T(8,128)(2,1)} %param.10, bf16[1,64,512]{2,1,0:T(8,128)(2,1)} %param.9), kind=kOutput, calls=%fused_computation.8 | convolution fusion | flops 268697600 | bytes 4784128 | tf_op jit(solution)/shard_map/dot_general | solution.py:51
  10.6 0.0 reduce-scatter.2.cloned.1.call-update
  10.6 0.0 all-gather.2.cloned.1.call-start
  10.6 0.0 copy-done.4
  10.6 0.1 reshape_squeeze.3
  10.7 0.1 fusion.48
  10.8 0.1 reduce_window_sum.11
  10.9 0.2 select_reduce_fusion
  11.1 0.1 reduce_sum.57
  11.2 0.1 fusion.49
  11.3 39.4 %reduce-scatter.2.cloned.1.call-done = bf16[8,4096]{1,0:T(8,128)(2,1)} async-done(((bf16[64,4096]{1,0:T(8,128)(2,1)}), bf16[8,4096]{1,0:T(8,128)(2,1)}) %reduce-scatter.2.cloned.1.call-update) | async-done | bytes 65552 | tf_op jit(solution)/shard_map/reduce_scatter | solution.py:50
  50.7 0.0 copy-done.2
  50.7 1.0 multiply_reduce_fusion.1
  51.7 0.0 copy-done.5
  51.7 1.3 convolution_convert_fusion.1
  52.9 0.3 reshape.115
  53.2 17.8 %all_to_all.10 = bf16[16,6,4096]{2,1,0:T(8,128)(2,1)} all-to-all(bf16[16,6,4096]{2,1,0:T(8,128)(2,1)S(1)} %reshape.115), channel_id=1, replica_groups=mesh['dp'=2,'tensor'=8,'expert'=16] {'expert'}, dimensions={0} | all-to-all | bytes 1572864 | tf_op jit(solution)/shard_map/all_to_all | solution.py:62
  71.0 2.2 reshape.116
  73.2 0.0 all-gather.2.cloned.1.call-update
  73.3 0.0 copy-start.1
  73.3 71.5 %all-gather.2.cloned.1.call-done = bf16[768,1,4096]{2,0,1:T(8,128)(2,1)} async-done(((bf16[96,1,4096]{2,0,1:T(8,128)(2,1)}), bf16[768,1,4096]{2,0,1:T(8,128)(2,1)}) %all-gather.2.cloned.1.call-update) | async-done | bytes 6291472 | tf_op jit(solution)/shard_map/all_gather | solution.py:64
  144.8 6.3 %fusion.8 = f32[768,1,192]{0,2,1:T(8,128)} fusion(bf16[1,192,4096]{2,1,0:T(8,128)(2,1)} %param.15, bf16[768,1,4096]{2,0,1:T(8,128)(2,1)} %all-gather.2.cloned.1.call-done), kind=kOutput, calls=%fused_computation.12 | convolution fusion | flops 1207959552 | bytes 8454144 | tf_op jit(solution)/shard_map/red,efd->ref/dot_general | solution.py:65
  151.1 0.0 copy-done
  151.1 0.0 copy-done.1
  151.1 13.0 %fusion.4 = bf16[768,1,4096]{2,0,1:T(8,128)(2,1)} fusion(bf16[1,192,4096]{2,1,0:T(8,128)(2,1)S(1)} %copy-done, bf16[1,192,4096]{2,1,0:T(8,128)(2,1)S(1)} %copy-done.1, bf16[768,1,4096]{2,0,1:T(8,128)(2,1)} %all-gather.2.cloned.1.call-done, f32[768,1,192]{0,2,1:T(8,128)} %fusion.8), kind=kOutput, calls=%fused_computation.6 | convolution fusion | flops 2419949568 | bytes 16318464 | tf_op jit(solution)/shard_map/ref,efd->red/dot_general | solution.py:68
  164.1 10.1 %reshape.122 = bf16[128,6,4096]{2,1,0:T(8,128)(2,1)} reshape(bf16[768,1,4096]{2,0,1:T(8,128)(2,1)} %fusion.4) | data formatting | bytes 12582912 | tf_op jit(solution)/shard_map/reshape | solution.py:69
  174.2 0.0 copy-start.6
  174.2 11.6 %all-to-all-start.1 = ((bf16[128,6,4096]{2,1,0:T(8,128)(2,1)}), bf16[128,6,4096]{2,1,0:T(8,128)(2,1)}, u32[]{:S(2)}, u32[]{:S(2)}) async-start(bf16[128,6,4096]{2,1,0:T(8,128)(2,1)} %reshape.122), calls=%async_computation.2 | async-start | bytes 16777216 | tf_op jit(solution)/shard_map/all_to_all | solution.py:72
  185.9 0.1 reduce_sum.56
  186.0 0.1 mul.72
  186.1 0.0 copy-done.6
  186.1 0.1 convert_reduce_fusion
  186.2 0.1 bitcast_divide_fusion
  186.3 184.9 %all-to-all-done.1 = bf16[128,6,4096]{2,1,0:T(8,128)(2,1)} async-done(((bf16[128,6,4096]{2,1,0:T(8,128)(2,1)}), bf16[128,6,4096]{2,1,0:T(8,128)(2,1)}, u32[]{:S(2)}, u32[]{:S(2)}) %all-to-all-start.1) | async-done | bytes 6291488 | tf_op jit(solution)/shard_map/all_to_all | solution.py:72
  371.2 10.2 %reshape.123 = bf16[8,96,4096]{2,1,0:T(8,128)(2,1)} reshape(bf16[128,6,4096]{2,1,0:T(8,128)(2,1)} %all-to-all-done.1) | data formatting | bytes 12582912 | tf_op jit(solution)/shard_map/reshape | solution.py:75
  381.4 4.0 %reduce_sum.59 = bf16[96,4096]{1,0:T(8,128)(2,1)S(1)} reduce(bf16[8,96,4096]{2,1,0:T(8,128)(2,1)} %reshape.123, bf16[]{:T(256)} %constant.65.clone.1), dimensions={0}, to_apply=%region_6.7 | reduce | flops 2752512 | bytes 7077890 | tf_op jit(solution)/shard_map/reduce_sum | solution.py:76
  385.3 0.0 copy-start.3
  385.3 0.9 gather_fusion
  386.2 0.4 multiply_reduce_fusion
  386.6 0.0 copy-done.3
  386.6 0.7 fusion.43
  (5 shorter events, 0.0 us)
Async XLA Ops:
  6.5 144.6 %copy-start = (bf16[1,192,4096]{2,1,0:T(8,128)(2,1)S(1)}, bf16[1,192,4096]{2,1,0:T(8,128)(2,1)}, u32[]{:S(2)}) copy-start(bf16[1,192,4096]{2,1,0:T(8,128)(2,1)} %param.17) | copy-start | bytes 4718596
  6.5 4.1 %copy-start.4 = (s32[1,8,8]{2,1,0:T(8,128)S(1)}, s32[1,8,8]{2,1,0:T(8,128)}, u32[]{:S(2)}) copy-start(s32[1,8,8]{2,1,0:T(8,128)} %param.13) | copy-start | bytes 772
  6.5 44.1 %copy-start.2 = (bf16[1,8,4096]{2,1,0:T(8,128)(2,1)S(1)}, bf16[1,8,4096]{2,1,0:T(8,128)(2,1)}, u32[]{:S(2)}) copy-start(bf16[1,8,4096]{2,1,0:T(8,128)(2,1)} %param.11) | copy-start | bytes 196612
  6.5 45.1 %copy-start.5 = (f32[4096]{0:T(1024)S(1)}, f32[4096]{0:T(1024)}, u32[]{:S(2)}) copy-start(f32[4096]{0:T(1024)} %param.12) | copy-start | bytes 49156
  6.5 44.1 %reduce-scatter.2.cloned.1.call-start = ((), (), s32[]{:S(2)}) async-start(), calls=%async_computation.3 | async-start | bytes 589824 | tf_op jit(solution)/shard_map/reduce_scatter | solution.py:50
  10.6 134.2 %all-gather.2.cloned.1.call-start = ((), (), s32[]{:S(2)}) async-start(), calls=%async_computation.4 | async-start | bytes 7077888 | tf_op jit(solution)/shard_map/all_gather | solution.py:64
  73.3 77.8 %copy-start.1 = (bf16[1,192,4096]{2,1,0:T(8,128)(2,1)S(1)}, bf16[1,192,4096]{2,1,0:T(8,128)(2,1)}, u32[]{:S(2)}) copy-start(bf16[1,192,4096]{2,1,0:T(8,128)(2,1)} %param.16) | copy-start | bytes 4718596
  174.2 11.8 %copy-start.6 = (s32[1,8,8]{2,1,0:T(8,128)S(1)}, s32[1,8,8]{2,1,0:T(8,128)}, u32[]{:S(2)}) copy-start(s32[1,8,8]{2,1,0:T(8,128)} %param.14) | copy-start | bytes 772
  174.2 196.9 %all-to-all-start.1 = ((bf16[128,6,4096]{2,1,0:T(8,128)(2,1)}), bf16[128,6,4096]{2,1,0:T(8,128)(2,1)}, u32[]{:S(2)}, u32[]{:S(2)}) async-start(bf16[128,6,4096]{2,1,0:T(8,128)(2,1)} %reshape.122), calls=%async_computation.2 | async-start | bytes 16777216 | tf_op jit(solution)/shard_map/all_to_all | solution.py:72
  385.3 1.3 copy-start.3
Sparse Core Ops, SparseCore 0:
  10.7 39.9 reduce-scatter.1
  73.4 71.3 all-gather.1
where the time goes:
time: 397 us; the launch traced here: 394 us
  waiting for transfers between devices  296 us (75%)
  matrix products  24.6 us (6%)
  local copies, waits for them, and re-layouts  24 us (6%)
  blocking collectives  17.8 us (4%)
  between operations  13.5 us (3%)
  starting transfers between devices  11.7 us (3%)
  other arithmetic  6.73 us (2%)
    all_to_all x1, waiting for transfers between devices, on_device(): lax.all_to_all(partial_out, ('tensor', 'expert'), split_axis=0, concat_ax...  185 us
    all_gather x1, waiting for transfers between devices, on_device(): portion = lax.all_gather(arrived, 'tensor', axis=0, tiled=True)  71.5 us
    reduce_scatter x1, waiting for transfers between devices, on_device(): lax.psum_scatter(jnp.dot(head_rows, out_proj, preferred_element_type=jnp....  39.4 us
    all_to_all x1, blocking collectives, on_device(): lax.all_to_all(outgoing, 'expert', split_axis=0, concat_axis=0, tiled=True)  17.8 us
    dot_general x1, matrix products, on_device(): jnp.einsum('ref,efd->red', activated, w_down, preferred_element_type=jnp....  13 us
    all_to_all x1, starting transfers between devices, on_device(): lax.all_to_all(partial_out, ('tensor', 'expert'), split_axis=0, concat_ax...  11.6 us
    reshape x1, local copies, waits for them, and re-layouts, on_device(): received = received.reshape(tensor_count, slot_count, model_width)  10.2 us
    reshape x1, local copies, waits for them, and re-layouts, on_device(): partial_out.astype(jnp.bfloat16)  10.1 us
  transfers between devices with their start and end apart: 3, of which 3 were waited for; matrix products, arithmetic and copies ran while one was open for 0% of the time, Pallas kernels for 0%

commit v1 on v0

v1 whole, which is shorter than its diff:
```python
import jax
import jax.numpy as jnp
from jax import lax
from jax.sharding import PartitionSpec as P

EXPERTS = 16
TOP = 8
CAP = 6
EXTRA = 128


def normalize(hidden, norm_gain):
    mean_square = jnp.mean(hidden * hidden, axis=-1, keepdims=True)
    return (hidden * lax.rsqrt(mean_square + 1e-06) * norm_gain).astype(jnp.bfloat16)


def reduce_over_tensor(partial):
    count = lax.axis_size("tensor")
    parts = lax.all_to_all(
        partial.astype(jnp.bfloat16), "tensor", split_axis=0, concat_axis=0, tiled=True
    )
    parts = parts.reshape(count, partial.shape[0] // count, partial.shape[1])
    return jnp.sum(parts.astype(jnp.float32), axis=0)


def on_device(
    attn_heads, out_proj, residual, norm_gain, expert_ids, weight_codes, w_gate, w_up, w_down
):
    tensor_count = lax.axis_size("tensor")
    expert_count = lax.axis_size("expert")
    own_residual = residual[0]
    tok_own, model_width = own_residual.shape
    tokens = tok_own * tensor_count
    slots = CAP * tensor_count

    partial = jnp.dot(attn_heads[0], out_proj, preferred_element_type=jnp.float32)
    hidden = own_residual.astype(jnp.float32) + reduce_over_tensor(partial)
    normed = normalize(hidden, norm_gain)

    routes = jnp.concatenate([expert_ids[0], weight_codes[0]], axis=1).astype(jnp.bfloat16)
    routes = jnp.pad(routes, ((0, 0), (0, EXTRA - 2 * TOP)))
    group = lax.all_gather(
        jnp.concatenate([normed, routes], axis=1), "tensor", axis=0, tiled=True
    )
    group_normed = group[:, :model_width]
    ids = group[:, model_width : model_width + TOP].astype(jnp.int32)
    codes = group[:, model_width + TOP : model_width + 2 * TOP].astype(jnp.float32)

    names = ids[:, :, None] == jnp.arange(EXPERTS, dtype=jnp.int32)[None, None, :]
    table = jnp.sum(jnp.where(names, codes[:, :, None], 0.0), axis=1)
    routed = jnp.any(names, axis=1)
    earlier = jnp.tril(jnp.ones((tokens, tokens), jnp.float32), -1)
    place = jnp.dot(earlier, routed.astype(jnp.float32)).astype(jnp.int32)
    place = jnp.where(routed, place, -1)
    at_slot = place.T[:, None, :] == jnp.arange(slots, dtype=jnp.int32)[None, :, None]
    spread = at_slot.astype(jnp.bfloat16).reshape(EXPERTS * slots, tokens)
    outgoing = jnp.dot(spread, group_normed, preferred_element_type=jnp.float32)
    arrived = lax.all_to_all(
        outgoing.astype(jnp.bfloat16), "expert", split_axis=0, concat_axis=0, tiled=True
    )

    gate_value = jnp.einsum("rd,fd->rf", arrived, w_gate[0], preferred_element_type=jnp.float32)
    up_value = jnp.einsum("rd,fd->rf", arrived, w_up[0], preferred_element_type=jnp.float32)
    activated = (jax.nn.silu(gate_value) * up_value).astype(jnp.bfloat16)
    expert_part = jnp.dot(activated, w_down[0], preferred_element_type=jnp.float32)

    returned = lax.all_to_all(
        expert_part.astype(jnp.bfloat16), "expert", split_axis=0, concat_axis=0, tiled=True
    )
    weighted = jnp.where(at_slot, table.T[:, None, :], 0.0).astype(jnp.bfloat16)
    weighted = weighted.reshape(EXPERTS * slots, tokens)
    mixed = jnp.einsum("st,sd->td", weighted, returned, preferred_element_type=jnp.float32)
    mixed = mixed / jnp.sum(codes, axis=-1, keepdims=True)
    layer_out = (hidden + reduce_over_tensor(mixed)).astype(jnp.bfloat16)
    return layer_out[None]


def solution(mesh):
    return jax.shard_map(
        on_device,
        mesh=mesh,
        in_specs=(
            P(("dp", "expert"), None, "tensor"),
            P("tensor", None),
            P(("dp", "expert"), "tensor", None),
            P(),
            P(("dp", "expert"), "tensor", None),
            P(("dp", "expert"), "tensor", None),
            P("expert", "tensor", None),
            P("expert", "tensor", None),
            P("expert", "tensor", None),
        ),
        out_specs=P(("dp", "expert"), "tensor", None),
        check_vma=False,
    )
```

time: 397 us -> 253 us (0.64)
  waiting for transfers between devices: 296 us -> 90.5 us
  blocking collectives: 17.8 us -> 114 us
  local copies, waits for them, and re-layouts: 24 us -> 2.88 us
  between operations: 13.5 us -> 0.11 us
  other arithmetic: 6.73 us -> 2.33 us
    all_to_all x1 -> x2, waiting for transfers between devices: 185 us -> 90.5 us  [the longest x1 73.9 us: on_device(): lax.all_to_all(expert_part.astype(jnp.bfloat16), 'expert', split_axis=0,...]
    all_gather x1 -> x0, waiting for transfers between devices: 71.5 us -> none  [on_device(): portion = lax.all_gather(arrived, 'tensor', axis=0, tiled=True)]
    all_to_all x1 -> x2, blocking collectives: 17.8 us -> 88.7 us  [the longest x1 72.4 us: on_device(): lax.all_to_all(outgoing.astype(jnp.bfloat16), 'expert', split_axis=0, con...]
    reduce_scatter x1 -> x0, waiting for transfers between devices: 39.4 us -> none  [on_device(): lax.psum_scatter(jnp.dot(head_rows, out_proj, preferred_element_type=jnp....]
    all_gather x0 -> x1, blocking collectives: none -> 25.5 us  [on_device(): lax.all_gather(jnp.concatenate([normed, routes], axis=1), 'tensor', axis=...]
    reshape x4 -> x0, local copies, waits for them, and re-layouts: 22.8 us -> none  [the longest x1 10.2 us: on_device(): received = received.reshape(tensor_count, slot_count, model_width)]
    reduce_sum x4, other arithmetic: 4.69 us -> 0.34 us  [the longest x1 0.18 us: on_device(): mixed = mixed / jnp.sum(codes, axis=-1, keepdims=True)]
    all_to_all x1 -> x2, starting transfers between devices: 11.6 us -> 15.3 us  [the longest x1 8.46 us: reduce_over_tensor(): lax.all_to_all(partial.astype(jnp.bfloat16), 'tensor', split_axis=0, conc...]
  transfers between devices with their start and end apart: 3 -> 2, of which waited for: 3 -> 2; matrix products, arithmetic and copies ran while one was open for 0% -> 0% of each run, Pallas kernels for 0% -> 0%
where the time goes in v1:
time: 253 us; the launch traced here: 251 us
  blocking collectives  114 us (45%)
  waiting for transfers between devices  90.5 us (36%)
  matrix products  25.4 us (10%)
  starting transfers between devices  15.3 us (6%)
  local copies, waits for them, and re-layouts  2.88 us (1%)
    all_to_all x1, waiting for transfers between devices, on_device(): lax.all_to_all(expert_part.astype(jnp.bfloat16), 'expert', split_axis=0,...  73.9 us
    all_to_all x1, blocking collectives, on_device(): lax.all_to_all(outgoing.astype(jnp.bfloat16), 'expert', split_axis=0, con...  72.4 us
    all_gather x1, blocking collectives, on_device(): lax.all_gather(jnp.concatenate([normed, routes], axis=1), 'tensor', axis=...  25.5 us
    all_to_all x1, waiting for transfers between devices, reduce_over_tensor(): lax.all_to_all(partial.astype(jnp.bfloat16), 'tensor', split_axis=0, conc...  16.6 us
    all_to_all x1, blocking collectives, reduce_over_tensor(): lax.all_to_all(partial.astype(jnp.bfloat16), 'tensor', split_axis=0, conc...  16.4 us
    dot_general x1, matrix products, on_device(): jnp.dot(activated, w_down[0], preferred_element_type=jnp.float32)  13.3 us
    all_to_all x1, starting transfers between devices, reduce_over_tensor(): lax.all_to_all(partial.astype(jnp.bfloat16), 'tensor', split_axis=0, conc...  8.46 us
    all_to_all x1, starting transfers between devices, on_device(): lax.all_to_all(expert_part.astype(jnp.bfloat16), 'expert', split_axis=0,...  6.84 us
  transfers between devices with their start and end apart: 2, of which 2 were waited for; matrix products, arithmetic and copies ran while one was open for 0% of the time, Pallas kernels for 0%

profile of v1, /device:TPU:24, one launch (start us, length us, event | category | flops | bytes accessed | tf_op | source)
XLA Modules:
  0.0 250.9 jit_solution(5429467721831321071)
XLA Ops:
  0.0 0.0 copy-start
  0.0 0.0 copy-start.2
  0.0 0.0 copy-start.3
  0.0 4.0 %fusion.3 = bf16[8,8,4096]{2,1,0:T(8,128)(2,1)} fusion(bf16[512,4096]{1,0:T(8,128)(2,1)} %param.10, bf16[1,64,512]{2,1,0:T(8,128)(2,1)} %param.9), kind=kOutput, calls=%fused_computation.7 | convolution fusion | flops 268697600 | bytes 4784128 | tf_op jit(solution)/shard_map/dot_general | solution.py:36
  4.0 8.5 %all-to-all-start = ((bf16[8,8,4096]{2,1,0:T(8,128)(2,1)}), bf16[8,8,4096]{2,1,0:T(8,128)(2,1)S(1)}, u32[]{:S(2)}, u32[]{:S(2)}) async-start(bf16[8,8,4096]{2,1,0:T(8,128)(2,1)} %fusion.3), calls=%async_computation | async-start | bytes 1048576 | tf_op jit(solution)/shard_map/all_to_all | solution.py:19
  12.5 0.1 eq.45
  12.5 0.7 convert_bitcast_fusion.1
  13.2 0.1 fusion.40
  13.3 16.6 %all-to-all-done = bf16[8,8,4096]{2,1,0:T(8,128)(2,1)S(1)} async-done(((bf16[8,8,4096]{2,1,0:T(8,128)(2,1)}), bf16[8,8,4096]{2,1,0:T(8,128)(2,1)S(1)}, u32[]{:S(2)}, u32[]{:S(2)}) %all-to-all-start) | async-done | bytes 524320 | tf_op jit(solution)/shard_map/all_to_all | solution.py:19
  29.9 0.1 convert_reduce_fusion.1
  30.0 0.0 copy-done.2
  30.0 0.1 multiply_reduce_fusion
  30.2 0.0 copy-done.3
  30.2 0.1 multiply_convert_fusion
  30.3 25.5 %all_gather.3 = bf16[64,4224]{1,0:T(8,128)(2,1)S(1)} all-gather(bf16[8,4224]{1,0:T(8,128)(2,1)S(1)} %pad_maximum_fusion), channel_id=1, replica_groups=mesh['dp'=2,'tensor'=8,'expert'=16] {'tensor'}, dimensions={0}, use_global_device_ids=true | all-gather | bytes 608256 | tf_op jit(solution)/shard_map/all_gather | solution.py:42
  55.8 0.1 slice_convert_fusion
  55.9 0.1 copy.18
  56.0 0.2 fusion.17
  56.2 0.2 bitcast_compare_fusion
  56.4 1.8 convolution_convert_fusion
  58.2 0.0 copy-start.4
  58.2 72.4 %all_to_all.39 = bf16[16,48,4096]{2,1,0:T(8,128)(2,1)S(1)} all-to-all(bf16[16,48,4096]{2,1,0:T(8,128)(2,1)S(1)} %bitcast.60), channel_id=1, replica_groups=mesh['dp'=2,'tensor'=8,'expert'=16] {'expert'}, dimensions={0} | all-to-all | bytes 12582912 | tf_op jit(solution)/shard_map/all_to_all | solution.py:58
  130.6 0.0 copy-start.1
  130.6 2.7 %copy-done.1 = bf16[16,48,4096]{2,1,0:T(8,128)(2,1)} copy-done((bf16[16,48,4096]{2,1,0:T(8,128)(2,1)}, bf16[16,48,4096]{2,1,0:T(8,128)(2,1)S(1)}, u32[]{:S(2)}) %copy-start.1) | copy-done | bytes 6291480
  133.3 0.0 copy-done.4
  133.3 2.2 fusion.7
  135.5 0.0 copy-done
  135.5 13.3 %convolution_convert_fusion.1 = bf16[768,4096]{1,0:T(8,128)(2,1)} fusion(bf16[1,192,4096]{2,1,0:T(8,128)(2,1)S(1)} %copy-done, bf16[768,4096]{1,0:T(8,128)(2,1)} %bitcast.63, bf16[1,192,4096]{2,1,0:T(8,128)(2,1)} %param.16, f32[768,192]{0,1:T(8,128)S(1)} %fusion.7), kind=kOutput, calls=%fused_computation.1 | convolution fusion | flops 2419949568 | bytes 16318464 | tf_op jit(solution)/shard_map/dot_general | solution.py:65
  148.8 6.8 %all-to-all-start.2 = ((bf16[16,48,4096]{2,1,0:T(8,128)(2,1)}), bf16[16,48,4096]{2,1,0:T(8,128)(2,1)}, u32[]{:S(2)}, u32[]{:S(2)}) async-start(bf16[16,48,4096]{2,1,0:T(8,128)(2,1)} %bitcast.61), calls=%async_computation.2 | async-start | bytes 12582912 | tf_op jit(solution)/shard_map/all_to_all | solution.py:67
  155.6 0.1 copy.17
  155.7 0.2 fusion.37
  155.9 73.9 %all-to-all-done.2 = bf16[16,48,4096]{2,1,0:T(8,128)(2,1)} async-done(((bf16[16,48,4096]{2,1,0:T(8,128)(2,1)}), bf16[16,48,4096]{2,1,0:T(8,128)(2,1)}, u32[]{:S(2)}, u32[]{:S(2)}) %all-to-all-start.2) | async-done | bytes 6291488 | tf_op jit(solution)/shard_map/all_to_all | solution.py:67
  229.8 4.0 %fusion.2 = bf16[8,8,4096]{2,1,0:T(8,128)(2,1)S(1)} fusion(bf16[16,48,4096]{2,1,0:T(8,128)(2,1)} %all-to-all-done.2, f32[64]{0:T(128)S(1)} %fusion.37, bf16[16,64]{1,0:T(8,128)(2,1)S(1)} %bitcast.64, s32[16,64]{1,0:T(8,128)S(1)} %fusion.17), kind=kOutput, calls=%fused_computation.6 | convolution fusion | flops 403275776 | bytes 6822144 | tf_op jit(solution)/shard_map/st,sd->td/dot_general | solution.py:72
  233.8 16.4 %all_to_all.40 = bf16[8,8,4096]{2,1,0:T(8,128)(2,1)S(1)} all-to-all(bf16[8,8,4096]{2,1,0:T(8,128)(2,1)S(1)} %fusion.2), channel_id=1, replica_groups=mesh['dp'=2,'tensor'=8,'expert'=16] {'tensor'}, dimensions={0} | all-to-all | bytes 1048576 | tf_op jit(solution)/shard_map/all_to_all | solution.py:19
  250.2 0.1 convert_reduce_fusion
  250.3 0.7 fusion.29
  (7 shorter events, 0.1 us)
Async XLA Ops:
  0.0 135.5 %copy-start = (bf16[1,192,4096]{2,1,0:T(8,128)(2,1)S(1)}, bf16[1,192,4096]{2,1,0:T(8,128)(2,1)}, u32[]{:S(2)}) copy-start(bf16[1,192,4096]{2,1,0:T(8,128)(2,1)} %param.17) | copy-start | bytes 4718596
  0.0 30.0 %copy-start.2 = (bf16[1,8,4096]{2,1,0:T(8,128)(2,1)S(1)}, bf16[1,8,4096]{2,1,0:T(8,128)(2,1)}, u32[]{:S(2)}) copy-start(bf16[1,8,4096]{2,1,0:T(8,128)(2,1)} %param.11) | copy-start | bytes 196612
  0.0 30.2 %copy-start.3 = (f32[4096]{0:T(1024)S(1)}, f32[4096]{0:T(1024)}, u32[]{:S(2)}) copy-start(f32[4096]{0:T(1024)} %param.12) | copy-start | bytes 49156
  4.0 26.0 %all-to-all-start = ((bf16[8,8,4096]{2,1,0:T(8,128)(2,1)}), bf16[8,8,4096]{2,1,0:T(8,128)(2,1)S(1)}, u32[]{:S(2)}, u32[]{:S(2)}) async-start(bf16[8,8,4096]{2,1,0:T(8,128)(2,1)} %fusion.3), calls=%async_computation | async-start | bytes 1048576 | tf_op jit(solution)/shard_map/all_to_all | solution.py:19
  58.2 75.1 %copy-start.4 = (bf16[1,192,4096]{2,1,0:T(8,128)(2,1)S(1)}, bf16[1,192,4096]{2,1,0:T(8,128)(2,1)}, u32[]{:S(2)}) copy-start(bf16[1,192,4096]{2,1,0:T(8,128)(2,1)} %param.15) | copy-start | bytes 4718596
  130.6 2.7 %copy-start.1 = (bf16[16,48,4096]{2,1,0:T(8,128)(2,1)}, bf16[16,48,4096]{2,1,0:T(8,128)(2,1)S(1)}, u32[]{:S(2)}) copy-start(bf16[16,48,4096]{2,1,0:T(8,128)(2,1)S(1)} %all_to_all.39) | copy-start | bytes 18874372
  148.8 81.0 %all-to-all-start.2 = ((bf16[16,48,4096]{2,1,0:T(8,128)(2,1)}), bf16[16,48,4096]{2,1,0:T(8,128)(2,1)}, u32[]{:S(2)}, u32[]{:S(2)}) async-start(bf16[16,48,4096]{2,1,0:T(8,128)(2,1)} %bitcast.61), calls=%async_computation.2 | async-start | bytes 12582912 | tf_op jit(solution)/shard_map/all_to_all | solution.py:67

commit v2 on v1

v2 whole, which is shorter than its diff:
```python
import jax
import jax.numpy as jnp
from jax import lax
from jax.sharding import PartitionSpec as P

EXPERTS = 16
SIDE = 4
LANES = 128


def normalize(hidden, norm_gain):
    mean_square = jnp.mean(hidden * hidden, axis=-1, keepdims=True)
    return (hidden * lax.rsqrt(mean_square + 1e-06) * norm_gain).astype(jnp.bfloat16)


def together(*values):
    return lax.optimization_barrier(values)


def reduce_over_tensor(partial):
    count = lax.axis_size("tensor")
    parts = lax.all_to_all(
        partial.astype(jnp.bfloat16), "tensor", split_axis=0, concat_axis=0, tiled=True
    )
    parts = parts.reshape(count, partial.shape[0] // count, partial.shape[1])
    return jnp.sum(parts.astype(jnp.float32), axis=0)


def shift(value, axis, step):
    pairs = []
    for row in range(SIDE):
        for col in range(SIDE):
            if axis == "y":
                target = ((row + step) % SIDE) * SIDE + col
            else:
                target = row * SIDE + (col + step) % SIDE
            pairs.append((row * SIDE + col, target))
    return lax.ppermute(value, "expert", pairs)


def spread(first, first_axis, second, second_axis):
    half = first.shape[0] // 2
    near = together(
        shift(first, first_axis, 1),
        shift(first, first_axis, -1),
        shift(second, second_axis, 1),
        shift(second, second_axis, -1),
    )
    far = together(
        shift(near[0][:half], first_axis, 1),
        shift(near[1][half:], first_axis, -1),
        shift(near[2][:half], second_axis, 1),
        shift(near[3][half:], second_axis, -1),
    )
    return near, far


def add(*values):
    total = values[0].astype(jnp.float32)
    for value in values[1:]:
        total = total + value.astype(jnp.float32)
    return total


def collect(first, first_axis, second, second_axis):
    half = first[0].shape[0] // 2
    rp, rm, sp, sm = together(
        shift(first[2][:half], first_axis, 1),
        shift(first[2][half:], first_axis, -1),
        shift(second[2][:half], second_axis, 1),
        shift(second[2][half:], second_axis, -1),
    )

    def ahead(block, arrived):
        return jnp.concatenate([add(block[:half], arrived).astype(jnp.bfloat16), block[half:]])

    def behind(block, arrived):
        return jnp.concatenate([block[:half], add(block[half:], arrived).astype(jnp.bfloat16)])

    qp, qm, tp, tm = together(
        shift(ahead(first[3], rp), first_axis, 1),
        shift(behind(first[1], rm), first_axis, -1),
        shift(ahead(second[3], sp), second_axis, 1),
        shift(behind(second[1], sm), second_axis, -1),
    )
    return add(first[0], qp, qm), add(second[0], tp, tm)


def on_device(
    attn_heads, out_proj, residual, norm_gain, expert_ids, weight_codes, w_gate, w_up, w_down
):
    tensor_count = lax.axis_size("tensor")
    own_residual = residual[0]
    tok_own, model_width = own_residual.shape
    tokens = tok_own * tensor_count
    half = tokens // 2
    me = lax.axis_index("expert")
    my_row, my_col = me // SIDE, me % SIDE

    codes = weight_codes[0].astype(jnp.float32)
    mixing = codes / jnp.sum(codes, axis=-1, keepdims=True)
    names = expert_ids[0][:, :, None] == jnp.arange(LANES, dtype=jnp.int32)[None, None, :]
    table = jnp.sum(jnp.where(names, mixing[:, :, None], 0.0), axis=1)
    tables = lax.all_gather(table, ("expert", "tensor"), axis=0, tiled=True)
    mine = jnp.arange(LANES, dtype=jnp.int32)[None, :] == me
    weight = jnp.sum(jnp.where(mine, tables, 0.0), axis=1).reshape(EXPERTS, tokens)
    offsets = jnp.array([0, -1, 2, 1], dtype=jnp.int32)
    rows = (my_row + offsets) % SIDE
    cols = (my_col + offsets) % SIDE
    from_first = (rows[:, None] * SIDE + cols[None, :]).reshape(-1)
    from_second = (rows[None, :] * SIDE + cols[:, None]).reshape(-1)
    weight_first = jnp.take(weight[:, :half], from_first, axis=0).reshape(SIDE, SIDE * half)
    weight_second = jnp.take(weight[:, half:], from_second, axis=0).reshape(SIDE, SIDE * half)

    partial = jnp.dot(attn_heads[0], out_proj, preferred_element_type=jnp.float32)
    hidden = own_residual.astype(jnp.float32) + reduce_over_tensor(partial)
    normed = normalize(hidden, norm_gain)
    group = lax.all_to_all(
        jnp.tile(normed, (tensor_count, 1)), "tensor", split_axis=0, concat_axis=0, tiled=True
    )

    def expert(parts, weights):
        x = jnp.concatenate(parts)
        scale = jnp.concatenate(weights)[:, None]
        gate_value = jnp.einsum("rd,fd->rf", x, w_gate[0], preferred_element_type=jnp.float32)
        up_value = jnp.einsum("rd,fd->rf", x, w_up[0], preferred_element_type=jnp.float32)
        activated = (jax.nn.silu(gate_value) * up_value).astype(jnp.bfloat16)
        activated = lax.optimization_barrier(activated)
        down = jnp.dot(activated, w_down[0], preferred_element_type=jnp.float32)
        return (down * scale).astype(jnp.bfloat16)

    near, far = spread(group[:half], "x", group[half:], "y")
    first = jnp.concatenate([group[:half], near[0], far[0], far[1], near[1]])
    second = jnp.concatenate([group[half:], near[2], far[2], far[3], near[3]])
    first, second = together(first, second)
    near, far = spread(first, "y", second, "x")

    out_own = expert([first, second], [weight_first[0], weight_second[0]])
    out_near = expert(
        [near[0], near[1], near[2], near[3]],
        [weight_first[1], weight_first[3], weight_second[1], weight_second[3]],
    )
    out_far = expert(
        [far[0], far[1], far[2], far[3]],
        [weight_first[2], weight_second[2]],
    )
    size = SIDE * half
    first_sum, second_sum = collect(
        (out_own[:size], out_near[:size], out_far[:size], out_near[size : 2 * size]),
        "y",
        (out_own[size:], out_near[2 * size : 3 * size], out_far[size:], out_near[3 * size :]),
        "x",
    )
    first_sum = first_sum.astype(jnp.bfloat16).reshape(SIDE, half, model_width)
    second_sum = second_sum.astype(jnp.bfloat16).reshape(SIDE, half, model_width)
    first_mix, second_mix = collect(
        tuple(first_sum[i] for i in range(SIDE)),
        "x",
        tuple(second_sum[i] for i in range(SIDE)),
        "y",
    )
    mixed = jnp.concatenate([first_mix, second_mix])
    layer_out = (hidden + reduce_over_tensor(mixed)).astype(jnp.bfloat16)
    return layer_out[None]


def solution(mesh):
    return jax.shard_map(
        on_device,
        mesh=mesh,
        in_specs=(
            P(("dp", "expert"), None, "tensor"),
            P("tensor", None),
            P(("dp", "expert"), "tensor", None),
            P(),
            P(("dp", "expert"), "tensor", None),
            P(("dp", "expert"), "tensor", None),
            P("expert", "tensor", None),
            P("expert", "tensor", None),
            P("expert", "tensor", None),
        ),
        out_specs=P(("dp", "expert"), "tensor", None),
        check_vma=False,
    )
```

time: 253 us -> 547 us (2.16)
  blocking collectives: 114 us -> 326 us
  starting transfers between devices: 15.3 us -> 106 us
  local copies, waits for them, and re-layouts: 2.88 us -> 19.4 us
  waiting for transfers between devices: 90.5 us -> 76.3 us
  matrix products: 25.4 us -> 13.4 us
    all_gather x1, blocking collectives: 25.5 us -> 310 us  [on_device(): tables = lax.all_gather(table, ('expert', 'tensor'), axis=0, tiled=True)]
    ppermute x0 -> x32, starting transfers between devices: none -> 93.6 us  [shift(): return lax.ppermute(value, 'expert', pairs)]
    all_to_all x1 -> x0, blocking collectives: 72.4 us -> none  [on_device(): lax.all_to_all(outgoing.astype(jnp.bfloat16), 'expert', split_axis=0, con...]
    ppermute x0 -> x32, waiting for transfers between devices: none -> 64.5 us  [shift(): return lax.ppermute(value, 'expert', pairs)]
    all_to_all x1, waiting for transfers between devices: 73.9 us -> 11.9 us  [on_device(): lax.all_to_all(jnp.tile(normed, (tensor_count, 1)), 'tensor', split_axis=...]
    all_to_all x1, waiting for transfers between devices: 16.6 us -> 0.01 us  [reduce_over_tensor(): lax.all_to_all(partial.astype(jnp.bfloat16), 'tensor', split_axis=0, conc...]
    dot_general x5 -> x9, matrix products: 21.5 us -> 9.43 us  [the longest x3 3.39 us: expert(): jnp.einsum('rd,fd->rf', x, w_up[0], preferred_element_type=jnp.float32)]
    unnamed x11 -> x29, local copies, waits for them, and re-layouts: 2.74 us -> 8.55 us
  transfers between devices with their start and end apart: 2 -> 34, of which waited for: 2 -> 22; matrix products, arithmetic and copies ran while one was open for 0% -> 3% of each run, Pallas kernels for 0% -> 0%
where the time goes in v2:
time: 547 us; the launch traced here: 546 us
  blocking collectives  326 us (60%)
  starting transfers between devices  106 us (19%)
  waiting for transfers between devices  76.3 us (14%)
  local copies, waits for them, and re-layouts  19.4 us (4%)
  matrix products  13.4 us (2%)
    all_gather x1, blocking collectives, on_device(): tables = lax.all_gather(table, ('expert', 'tensor'), axis=0, tiled=True)  310 us
    ppermute x32, starting transfers between devices, shift(): return lax.ppermute(value, 'expert', pairs)  93.6 us
    ppermute x32, waiting for transfers between devices, shift(): return lax.ppermute(value, 'expert', pairs)  64.5 us
    all_to_all x1, blocking collectives, reduce_over_tensor(): lax.all_to_all(partial.astype(jnp.bfloat16), 'tensor', split_axis=0, conc...  15.7 us
    all_to_all x1, waiting for transfers between devices, on_device(): lax.all_to_all(jnp.tile(normed, (tensor_count, 1)), 'tensor', split_axis=...  11.9 us
  transfers between devices with their start and end apart: 34, of which 22 were waited for; matrix products, arithmetic and copies ran while one was open for 3% of the time, Pallas kernels for 0%

profile of v2, /device:TPU:24, one launch (start us, length us, event | category | flops | bytes accessed | tf_op | source)
XLA Modules:
  0.0 545.9 jit_solution(3115669993532460682)
XLA Ops:
  0.0 4.0 fusion.2
  4.0 8.6 %all-to-all-start = ((bf16[8,8,4096]{2,1,0:T(8,128)(2,1)}), bf16[8,8,4096]{2,1,0:T(8,128)(2,1)S(1)}, u32[]{:S(2)}, u32[]{:S(2)}) async-start(bf16[8,8,4096]{2,1,0:T(8,128)(2,1)} %fusion.2), calls=%async_computation | async-start | bytes 1048576 | tf_op jit(solution)/shard_map/all_to_all | solution.py:22
  12.9 310.4 %all_gather.3 = f32[1024,128]{1,0:T(8,128)S(1)} all-gather(f32[8,128]{1,0:T(8,128)S(1)} %select_reduce_fusion.1), channel_id=1, replica_groups=mesh['dp'=2,'tensor'=8,'expert'=16] {'expert','tensor'}, dimensions={0}, use_global_device_ids=true | all-gather | bytes 528384 | tf_op jit(solution)/shard_map/all_gather | solution.py:104
  325.1 3.5 all-to-all-start.1
  329.9 11.9 %all-to-all-done.1 = bf16[8,8,4096]{2,1,0:T(8,128)(2,1)S(1)} async-done(((bf16[8,8,4096]{2,1,0:T(8,128)(2,1)}), bf16[8,8,4096]{2,1,0:T(8,128)(2,1)S(1)}, u32[]{:S(2)}, u32[]{:S(2)}) %all-to-all-start.1) | async-done | bytes 524320 | tf_op jit(solution)/shard_map/all_to_all | solution.py:118
  342.0 36.2 %collective-permute-start.1 = (bf16[32,4096]{1,0:T(8,128)(2,1)S(1)}, bf16[32,4096]{1,0:T(8,128)(2,1)S(1)}, u32[]{:S(2)}, u32[]{:S(2)}) collective-permute-start(bf16[32,4096]{1,0:T(8,128)(2,1)S(1)} %get-tuple-element.103), channel_id=1, source_target_pairs={{0,3},{1,0},{2,1},{3,2},{4,7},{5,4},{6,5},{7,6},{8,11},{9,8},{10,9... | collective-permute-start | bytes 786440 | tf_op jit(solution)/shard_map/ppermute | solution.py:38
  378.2 7.4 %collective-permute-start.2 = (bf16[32,4096]{1,0:T(8,128)(2,1)S(1)}, bf16[32,4096]{1,0:T(8,128)(2,1)S(1)}, u32[]{:S(2)}, u32[]{:S(2)}) collective-permute-start(bf16[32,4096]{1,0:T(8,128)(2,1)S(1)} %get-tuple-element.102), channel_id=1, source_target_pairs={{0,4},{1,5},{2,6},{3,7},{4,8},{5,9},{6,10},{7,11},{8,12},{9,13},{1... | collective-permute-start | bytes 786440 | tf_op jit(solution)/shard_map/ppermute | solution.py:38
  386.5 3.2 collective-permute-done.2
  389.7 3.9 collective-permute-done.3
  393.7 3.3 collective-permute-start.5
  397.2 2.0 collective-permute-start.7
  400.0 1.2 collective-permute-done.4
  402.1 1.4 collective-permute-done.7
  407.5 2.0 collective-permute-start.9
  409.5 3.5 collective-permute-start.11
  413.7 1.3 constant_dynamic-update-slice_fusion.11
  415.0 17.6 %collective-permute-done.8 = bf16[128,4096]{1,0:T(8,128)(2,1)S(1)} collective-permute-done((bf16[128,4096]{1,0:T(8,128)(2,1)}, bf16[128,4096]{1,0:T(8,128)(2,1)S(1)}, u32[]{:S(2)}, u32[]{:S(2)}) %collective-permute-start.8) | collective-permute-done | bytes 1048608 | tf_op jit(solution)/shard_map/ppermute | solution.py:38
  432.6 3.0 collective-permute-done.10
  436.9 1.3 constant_dynamic-update-slice_fusion.14
  439.3 1.4 constant_dynamic-update-slice_fusion.13
  441.8 1.3 constant_dynamic-update-slice_fusion.12
  443.3 2.0 collective-permute-start.13
  445.3 3.7 collective-permute-start.15
  449.0 1.5 fusion.14
  450.5 1.6 fusion.21
  452.2 1.3 multiply_convert_fusion
  453.7 5.2 collective-permute-done.14
  461.8 1.1 collective-permute-start.16
  463.9 1.4 collective-permute-start.18
  465.4 11.5 %collective-permute-start.19 = (bf16[64,4096]{1,0:T(8,128)(2,1)S(1)}, bf16[64,4096]{1,0:T(8,128)(2,1)S(1)}, u32[]{:S(2)}, u32[]{:S(2)}) collective-permute-start(bf16[64,4096]{1,0:T(8,128)(2,1)S(1)} %get-tuple-element.84), channel_id=1, source_target_pairs={{0,3},{1,0},{2,1},{3,2},{4,7},{5,4},{6,5},{7,6},{8,11},{9,8},{10,9... | collective-permute-start | bytes 1572872 | tf_op jit(solution)/shard_map/ppermute | solution.py:38
  477.1 7.1 %collective-permute-done.19 = bf16[64,4096]{1,0:T(8,128)(2,1)S(1)} collective-permute-done((bf16[64,4096]{1,0:T(8,128)(2,1)S(1)}, bf16[64,4096]{1,0:T(8,128)(2,1)S(1)}, u32[]{:S(2)}, u32[]{:S(2)}) %collective-permute-start.19) | collective-permute-done | bytes 524320 | tf_op jit(solution)/shard_map/ppermute | solution.py:38
  485.0 2.2 collective-permute-start.20
  487.4 1.3 collective-permute-start.22
  488.8 2.1 collective-permute-start.23
  490.9 1.3 constant_dynamic-update-slice_fusion.10
  494.7 5.1 collective-permute-done.20
  499.9 3.5 collective-permute-done.21
  504.8 2.1 collective-permute-start.24
  506.9 1.3 collective-permute-start.25
  508.2 3.3 collective-permute-start.26
  511.8 2.2 collective-permute-done.26
  514.1 3.7 collective-permute-done.27
  518.6 2.6 collective-permute-start.29
  521.4 2.1 collective-permute-start.31
  523.5 2.0 collective-permute-done.28
  525.5 2.3 collective-permute-done.30
  527.8 1.3 collective-permute-done.31
  529.3 15.7 %all_to_all.21 = bf16[8,8,4096]{2,1,0:T(8,128)(2,1)S(1)} all-to-all(bf16[8,8,4096]{2,1,0:T(8,128)(2,1)S(1)} %maximum_bitcast_fusion), channel_id=1, replica_groups=mesh['dp'=2,'tensor'=8,'expert'=16] {'tensor'}, dimensions={0} | all-to-all | bytes 1048576 | tf_op jit(solution)/shard_map/all_to_all | solution.py:22
  (134 shorter events, 26.2 us)
Async XLA Ops:
  0.0 452.2 %copy-start = (bf16[1,192,4096]{2,1,0:T(8,128)(2,1)S(1)}, bf16[1,192,4096]{2,1,0:T(8,128)(2,1)}, u32[]{:S(2)}) copy-start(bf16[1,192,4096]{2,1,0:T(8,128)(2,1)} %param.20) | copy-start | bytes 4718596
  0.0 323.3 %copy-start.6 = (s32[4]{0:T(128)S(1)}, s32[4]{0:T(128)}, u32[]{:S(2)}) copy-start(s32[4]{0:T(128)} %constant.70.clone) | copy-start | bytes 52
  0.0 12.6 %copy-start.4 = (s32[1,8,8]{2,1,0:T(8,128)S(1)}, s32[1,8,8]{2,1,0:T(8,128)}, u32[]{:S(2)}) copy-start(s32[1,8,8]{2,1,0:T(8,128)} %param.17) | copy-start | bytes 772
  0.0 12.8 %copy-start.5 = (s32[1,8,8]{2,1,0:T(8,128)S(1)}, s32[1,8,8]{2,1,0:T(8,128)}, u32[]{:S(2)}) copy-start(s32[1,8,8]{2,1,0:T(8,128)} %param.16) | copy-start | bytes 772
  4.0 320.1 %copy-start.2 = (bf16[1,8,4096]{2,1,0:T(8,128)(2,1)S(1)}, bf16[1,8,4096]{2,1,0:T(8,128)(2,1)}, u32[]{:S(2)}) copy-start(bf16[1,8,4096]{2,1,0:T(8,128)(2,1)} %param.14) | copy-start | bytes 196612
  4.0 320.2 %copy-start.3 = (f32[4096]{0:T(1024)S(1)}, f32[4096]{0:T(1024)}, u32[]{:S(2)}) copy-start(f32[4096]{0:T(1024)} %param.15) | copy-start | bytes 49156
  4.0 320.0 %all-to-all-start = ((bf16[8,8,4096]{2,1,0:T(8,128)(2,1)}), bf16[8,8,4096]{2,1,0:T(8,128)(2,1)S(1)}, u32[]{:S(2)}, u32[]{:S(2)}) async-start(bf16[8,8,4096]{2,1,0:T(8,128)(2,1)} %fusion.2), calls=%async_computation | async-start | bytes 1048576 | tf_op jit(solution)/shard_map/all_to_all | solution.py:22
  325.1 16.7 %all-to-all-start.1 = ((bf16[8,8,4096]{2,1,0:T(8,128)(2,1)}), bf16[8,8,4096]{2,1,0:T(8,128)(2,1)S(1)}, u32[]{:S(2)}, u32[]{:S(2)}) async-start(bf16[8,8,4096]{2,1,0:T(8,128)(2,1)} %tile.2), calls=%async_computation.1 | async-start | bytes 1048576 | tf_op jit(solution)/shard_map/all_to_all | solution.py:118
  341.9 44.6 %collective-permute-start = (bf16[32,4096]{1,0:T(8,128)(2,1)S(1)}, bf16[32,4096]{1,0:T(8,128)(2,1)S(1)}, u32[]{:S(2)}, u32[]{:S(2)}) collective-permute-start(bf16[32,4096]{1,0:T(8,128)(2,1)S(1)} %get-tuple-element.103), channel_id=1, source_target_pairs={{0,1},{1,2},{2,3},{3,0},{4,5},{5,6},{6,7},{7,4},{8,9},{9,10},{10,1... | collective-permute-start | bytes 786440 | tf_op jit(solution)/shard_map/ppermute | solution.py:38
  342.0 44.5 %collective-permute-start.1 = (bf16[32,4096]{1,0:T(8,128)(2,1)S(1)}, bf16[32,4096]{1,0:T(8,128)(2,1)S(1)}, u32[]{:S(2)}, u32[]{:S(2)}) collective-permute-start(bf16[32,4096]{1,0:T(8,128)(2,1)S(1)} %get-tuple-element.103), channel_id=1, source_target_pairs={{0,3},{1,0},{2,1},{3,2},{4,7},{5,4},{6,5},{7,6},{8,11},{9,8},{10,9... | collective-permute-start | bytes 786440 | tf_op jit(solution)/shard_map/ppermute | solution.py:38
  378.2 11.5 %collective-permute-start.2 = (bf16[32,4096]{1,0:T(8,128)(2,1)S(1)}, bf16[32,4096]{1,0:T(8,128)(2,1)S(1)}, u32[]{:S(2)}, u32[]{:S(2)}) collective-permute-start(bf16[32,4096]{1,0:T(8,128)(2,1)S(1)} %get-tuple-element.102), channel_id=1, source_target_pairs={{0,4},{1,5},{2,6},{3,7},{4,8},{5,9},{6,10},{7,11},{8,12},{9,13},{1... | collective-permute-start | bytes 786440 | tf_op jit(solution)/shard_map/ppermute | solution.py:38
  385.6 7.9 %collective-permute-start.3 = (bf16[32,4096]{1,0:T(8,128)(2,1)S(1)}, bf16[32,4096]{1,0:T(8,128)(2,1)S(1)}, u32[]{:S(2)}, u32[]{:S(2)}) collective-permute-start(bf16[32,4096]{1,0:T(8,128)(2,1)S(1)} %get-tuple-element.102), channel_id=1, source_target_pairs={{0,12},{1,13},{2,14},{3,15},{4,0},{5,1},{6,2},{7,3},{8,4},{9,5},{1... | collective-permute-start | bytes 786440 | tf_op jit(solution)/shard_map/ppermute | solution.py:38
  393.6 7.6 %collective-permute-start.4 = (bf16[16,4096]{1,0:T(8,128)(2,1)S(1)}, bf16[16,4096]{1,0:T(8,128)(2,1)S(1)}, u32[]{:S(2)}, u32[]{:S(2)}) collective-permute-start(bf16[16,4096]{1,0:T(8,128)(2,1)S(1)} %slice.214), channel_id=1, source_target_pairs={{0,1},{1,2},{2,3},{3,0},{4,5},{5,6},{6,7},{7,4},{8,9},{9,10},{10,1... | collective-permute-start | bytes 393224 | tf_op jit(solution)/shard_map/ppermute | solution.py:38
  393.7 7.5 %collective-permute-start.5 = (bf16[16,4096]{1,0:T(8,128)(2,1)S(1)}, bf16[16,4096]{1,0:T(8,128)(2,1)S(1)}, u32[]{:S(2)}, u32[]{:S(2)}) collective-permute-start(bf16[16,4096]{1,0:T(8,128)(2,1)S(1)} %slice.215), channel_id=1, source_target_pairs={{0,3},{1,0},{2,1},{3,2},{4,7},{5,4},{6,5},{7,6},{8,11},{9,8},{10,9... | collective-permute-start | bytes 393224 | tf_op jit(solution)/shard_map/ppermute | solution.py:38
  397.0 5.0 collective-permute-start.6
  397.2 6.3 %collective-permute-start.7 = (bf16[16,4096]{1,0:T(8,128)(2,1)S(1)}, bf16[16,4096]{1,0:T(8,128)(2,1)S(1)}, u32[]{:S(2)}, u32[]{:S(2)}) collective-permute-start(bf16[16,4096]{1,0:T(8,128)(2,1)S(1)} %slice.217), channel_id=1, source_target_pairs={{0,12},{1,13},{2,14},{3,15},{4,0},{5,1},{6,2},{7,3},{8,4},{9,5},{1... | collective-permute-start | bytes 393224 | tf_op jit(solution)/shard_map/ppermute | solution.py:38
  407.5 25.1 %collective-permute-start.8 = (bf16[128,4096]{1,0:T(8,128)(2,1)}, bf16[128,4096]{1,0:T(8,128)(2,1)S(1)}, u32[]{:S(2)}, u32[]{:S(2)}) collective-permute-start(bf16[128,4096]{1,0:T(8,128)(2,1)} %constant_dynamic-update-slice_fusion), channel_id=1, source_target_pairs={{0,4},{1,5},{2,6},{3,7},{4,8},{5,9},{6,10},{7,11},{8,12},{9,13},{1... | collective-permute-start | bytes 3145736 | tf_op jit(solution)/shard_map/ppermute | solution.py:38
  407.5 25.1 %collective-permute-start.9 = (bf16[128,4096]{1,0:T(8,128)(2,1)}, bf16[128,4096]{1,0:T(8,128)(2,1)}, u32[]{:S(2)}, u32[]{:S(2)}) collective-permute-start(bf16[128,4096]{1,0:T(8,128)(2,1)} %constant_dynamic-update-slice_fusion), channel_id=1, source_target_pairs={{0,12},{1,13},{2,14},{3,15},{4,0},{5,1},{6,2},{7,3},{8,4},{9,5},{1... | collective-permute-start | bytes 3145736 | tf_op jit(solution)/shard_map/ppermute | solution.py:38
  409.5 26.1 %collective-permute-start.10 = (bf16[128,4096]{1,0:T(8,128)(2,1)}, bf16[128,4096]{1,0:T(8,128)(2,1)}, u32[]{:S(2)}, u32[]{:S(2)}) collective-permute-start(bf16[128,4096]{1,0:T(8,128)(2,1)} %constant_dynamic-update-slice_fusion.5), channel_id=1, source_target_pairs={{0,1},{1,2},{2,3},{3,0},{4,5},{5,6},{6,7},{7,4},{8,9},{9,10},{10,1... | collective-permute-start | bytes 3145736 | tf_op jit(solution)/shard_map/ppermute | solution.py:38
  409.5 26.2 %collective-permute-start.11 = (bf16[128,4096]{1,0:T(8,128)(2,1)}, bf16[128,4096]{1,0:T(8,128)(2,1)}, u32[]{:S(2)}, u32[]{:S(2)}) collective-permute-start(bf16[128,4096]{1,0:T(8,128)(2,1)} %constant_dynamic-update-slice_fusion.5), channel_id=1, source_target_pairs={{0,3},{1,0},{2,1},{3,2},{4,7},{5,4},{6,5},{7,6},{8,11},{9,8},{10,9... | collective-permute-start | bytes 3145736 | tf_op jit(solution)/shard_map/ppermute | solution.py:38
  439.3 9.7 %copy-start.1 = (bf16[1,192,4096]{2,1,0:T(8,128)(2,1)S(1)}, bf16[1,192,4096]{2,1,0:T(8,128)(2,1)}, u32[]{:S(2)}) copy-start(bf16[1,192,4096]{2,1,0:T(8,128)(2,1)} %param.18) | copy-start | bytes 4718596
  443.2 7.4 %copy-start.7 = (bf16[1,192,4096]{2,1,0:T(8,128)(2,1)S(1)}, bf16[1,192,4096]{2,1,0:T(8,128)(2,1)}, u32[]{:S(2)}) copy-start(bf16[1,192,4096]{2,1,0:T(8,128)(2,1)} %param.19) | copy-start | bytes 4718596
  443.2 10.3 %collective-permute-start.12 = (bf16[64,4096]{1,0:T(8,128)(2,1)S(1)}, bf16[64,4096]{1,0:T(8,128)(2,1)S(1)}, u32[]{:S(2)}, u32[]{:S(2)}) collective-permute-start(bf16[64,4096]{1,0:T(8,128)(2,1)S(1)} %slice.228), channel_id=1, source_target_pairs={{0,4},{1,5},{2,6},{3,7},{4,8},{5,9},{6,10},{7,11},{8,12},{9,13},{1... | collective-permute-start | bytes 1572872 | tf_op jit(solution)/shard_map/ppermute | solution.py:38
  443.3 10.5 %collective-permute-start.13 = (bf16[64,4096]{1,0:T(8,128)(2,1)S(1)}, bf16[64,4096]{1,0:T(8,128)(2,1)S(1)}, u32[]{:S(2)}, u32[]{:S(2)}) collective-permute-start(bf16[64,4096]{1,0:T(8,128)(2,1)S(1)} %slice.229), channel_id=1, source_target_pairs={{0,12},{1,13},{2,14},{3,15},{4,0},{5,1},{6,2},{7,3},{8,4},{9,5},{1... | collective-permute-start | bytes 1572872 | tf_op jit(solution)/shard_map/ppermute | solution.py:38
  445.3 13.7 %collective-permute-start.14 = (bf16[64,4096]{1,0:T(8,128)(2,1)S(1)}, bf16[64,4096]{1,0:T(8,128)(2,1)S(1)}, u32[]{:S(2)}, u32[]{:S(2)}) collective-permute-start(bf16[64,4096]{1,0:T(8,128)(2,1)S(1)} %slice.230), channel_id=1, source_target_pairs={{0,1},{1,2},{2,3},{3,0},{4,5},{5,6},{6,7},{7,4},{8,9},{9,10},{10,1... | collective-permute-start | bytes 1572872 | tf_op jit(solution)/shard_map/ppermute | solution.py:38
  445.3 13.7 %collective-permute-start.15 = (bf16[64,4096]{1,0:T(8,128)(2,1)S(1)}, bf16[64,4096]{1,0:T(8,128)(2,1)S(1)}, u32[]{:S(2)}, u32[]{:S(2)}) collective-permute-start(bf16[64,4096]{1,0:T(8,128)(2,1)S(1)} %slice.231), channel_id=1, source_target_pairs={{0,3},{1,0},{2,1},{3,2},{4,7},{5,4},{6,5},{7,6},{8,11},{9,8},{10,9... | collective-permute-start | bytes 1572872 | tf_op jit(solution)/shard_map/ppermute | solution.py:38
  461.8 15.2 %collective-permute-start.16 = (bf16[64,4096]{1,0:T(8,128)(2,1)S(1)}, bf16[64,4096]{1,0:T(8,128)(2,1)S(1)}, u32[]{:S(2)}, u32[]{:S(2)}) collective-permute-start(bf16[64,4096]{1,0:T(8,128)(2,1)S(1)} %get-tuple-element.87), channel_id=1, source_target_pairs={{0,4},{1,5},{2,6},{3,7},{4,8},{5,9},{6,10},{7,11},{8,12},{9,13},{1... | collective-permute-start | bytes 1572872 | tf_op jit(solution)/shard_map/ppermute | solution.py:38
  463.0 14.1 %collective-permute-start.17 = (bf16[64,4096]{1,0:T(8,128)(2,1)S(1)}, bf16[64,4096]{1,0:T(8,128)(2,1)S(1)}, u32[]{:S(2)}, u32[]{:S(2)}) collective-permute-start(bf16[64,4096]{1,0:T(8,128)(2,1)S(1)} %get-tuple-element.86), channel_id=1, source_target_pairs={{0,12},{1,13},{2,14},{3,15},{4,0},{5,1},{6,2},{7,3},{8,4},{9,5},{1... | collective-permute-start | bytes 1572872 | tf_op jit(solution)/shard_map/ppermute | solution.py:38
  463.9 13.1 %collective-permute-start.18 = (bf16[64,4096]{1,0:T(8,128)(2,1)S(1)}, bf16[64,4096]{1,0:T(8,128)(2,1)S(1)}, u32[]{:S(2)}, u32[]{:S(2)}) collective-permute-start(bf16[64,4096]{1,0:T(8,128)(2,1)S(1)} %get-tuple-element.85), channel_id=1, source_target_pairs={{0,1},{1,2},{2,3},{3,0},{4,5},{5,6},{6,7},{7,4},{8,9},{9,10},{10,1... | collective-permute-start | bytes 1572872 | tf_op jit(solution)/shard_map/ppermute | solution.py:38
  465.4 18.8 %collective-permute-start.19 = (bf16[64,4096]{1,0:T(8,128)(2,1)S(1)}, bf16[64,4096]{1,0:T(8,128)(2,1)S(1)}, u32[]{:S(2)}, u32[]{:S(2)}) collective-permute-start(bf16[64,4096]{1,0:T(8,128)(2,1)S(1)} %get-tuple-element.84), channel_id=1, source_target_pairs={{0,3},{1,0},{2,1},{3,2},{4,7},{5,4},{6,5},{7,6},{8,11},{9,8},{10,9... | collective-permute-start | bytes 1572872 | tf_op jit(solution)/shard_map/ppermute | solution.py:38
  485.0 14.9 %collective-permute-start.20 = (bf16[128,4096]{1,0:T(8,128)(2,1)S(1)}, bf16[128,4096]{1,0:T(8,128)(2,1)S(1)}, u32[]{:S(2)}, u32[]{:S(2)}) collective-permute-start(bf16[128,4096]{1,0:T(8,128)(2,1)S(1)} %pad_maximum_fusion), channel_id=1, source_target_pairs={{0,4},{1,5},{2,6},{3,7},{4,8},{5,9},{6,10},{7,11},{8,12},{9,13},{1... | collective-permute-start | bytes 3145736 | tf_op jit(solution)/shard_map/ppermute | solution.py:38
  487.3 16.1 %collective-permute-start.21 = (bf16[128,4096]{1,0:T(8,128)(2,1)S(1)}, bf16[128,4096]{1,0:T(8,128)(2,1)S(1)}, u32[]{:S(2)}, u32[]{:S(2)}) collective-permute-start(bf16[128,4096]{1,0:T(8,128)(2,1)S(1)} %pad_maximum_fusion.1), channel_id=1, source_target_pairs={{0,12},{1,13},{2,14},{3,15},{4,0},{5,1},{6,2},{7,3},{8,4},{9,5},{1... | collective-permute-start | bytes 3145736 | tf_op jit(solution)/shard_map/ppermute | solution.py:38
  487.4 16.1 %collective-permute-start.22 = (bf16[128,4096]{1,0:T(8,128)(2,1)S(1)}, bf16[128,4096]{1,0:T(8,128)(2,1)S(1)}, u32[]{:S(2)}, u32[]{:S(2)}) collective-permute-start(bf16[128,4096]{1,0:T(8,128)(2,1)S(1)} %pad_maximum_fusion.2), channel_id=1, source_target_pairs={{0,1},{1,2},{2,3},{3,0},{4,5},{5,6},{6,7},{7,4},{8,9},{9,10},{10,1... | collective-permute-start | bytes 3145736 | tf_op jit(solution)/shard_map/ppermute | solution.py:38
  488.8 14.9 %collective-permute-start.23 = (bf16[128,4096]{1,0:T(8,128)(2,1)S(1)}, bf16[128,4096]{1,0:T(8,128)(2,1)S(1)}, u32[]{:S(2)}, u32[]{:S(2)}) collective-permute-start(bf16[128,4096]{1,0:T(8,128)(2,1)S(1)} %pad_maximum_fusion.3), channel_id=1, source_target_pairs={{0,3},{1,0},{2,1},{3,2},{4,7},{5,4},{6,5},{7,6},{8,11},{9,8},{10,9... | collective-permute-start | bytes 3145736 | tf_op jit(solution)/shard_map/ppermute | solution.py:38
  504.8 6.8 %collective-permute-start.24 = (bf16[16,4096]{1,0:T(8,128)(2,1)S(1)}, bf16[16,4096]{1,0:T(8,128)(2,1)S(1)}, u32[]{:S(2)}, u32[]{:S(2)}) collective-permute-start(bf16[16,4096]{1,0:T(8,128)(2,1)S(1)} %get-tuple-element.97), channel_id=1, source_target_pairs={{0,1},{1,2},{2,3},{3,0},{4,5},{5,6},{6,7},{7,4},{8,9},{9,10},{10,1... | collective-permute-start | bytes 393224 | tf_op jit(solution)/shard_map/ppermute | solution.py:38
  506.9 5.0 collective-permute-start.25
  508.2 5.8 %collective-permute-start.26 = (bf16[16,4096]{1,0:T(8,128)(2,1)S(1)}, bf16[16,4096]{1,0:T(8,128)(2,1)S(1)}, u32[]{:S(2)}, u32[]{:S(2)}) collective-permute-start(bf16[16,4096]{1,0:T(8,128)(2,1)S(1)} %get-tuple-element.91), channel_id=1, source_target_pairs={{0,4},{1,5},{2,6},{3,7},{4,8},{5,9},{6,10},{7,11},{8,12},{9,13},{1... | collective-permute-start | bytes 393224 | tf_op jit(solution)/shard_map/ppermute | solution.py:38
  511.5 6.2 %collective-permute-start.27 = (bf16[16,4096]{1,0:T(8,128)(2,1)S(1)}, bf16[16,4096]{1,0:T(8,128)(2,1)S(1)}, u32[]{:S(2)}, u32[]{:S(2)}) collective-permute-start(bf16[16,4096]{1,0:T(8,128)(2,1)S(1)} %get-tuple-element.90), channel_id=1, source_target_pairs={{0,12},{1,13},{2,14},{3,15},{4,0},{5,1},{6,2},{7,3},{8,4},{9,5},{1... | collective-permute-start | bytes 393224 | tf_op jit(solution)/shard_map/ppermute | solution.py:38
  517.8 7.7 %collective-permute-start.28 = (bf16[32,4096]{1,0:T(8,128)(2,1)S(1)}, bf16[32,4096]{1,0:T(8,128)(2,1)S(1)}, u32[]{:S(2)}, u32[]{:S(2)}) collective-permute-start(bf16[32,4096]{1,0:T(8,128)(2,1)S(1)} %pad_maximum_fusion.4), channel_id=1, source_target_pairs={{0,1},{1,2},{2,3},{3,0},{4,5},{5,6},{6,7},{7,4},{8,9},{9,10},{10,1... | collective-permute-start | bytes 786440 | tf_op jit(solution)/shard_map/ppermute | solution.py:38
  518.6 6.9 %collective-permute-start.29 = (bf16[32,4096]{1,0:T(8,128)(2,1)S(1)}, bf16[32,4096]{1,0:T(8,128)(2,1)S(1)}, u32[]{:S(2)}, u32[]{:S(2)}) collective-permute-start(bf16[32,4096]{1,0:T(8,128)(2,1)S(1)} %pad_maximum_fusion.5), channel_id=1, source_target_pairs={{0,3},{1,0},{2,1},{3,2},{4,7},{5,4},{6,5},{7,6},{8,11},{9,8},{10,9... | collective-permute-start | bytes 786440 | tf_op jit(solution)/shard_map/ppermute | solution.py:38
  521.3 6.4 %collective-permute-start.30 = (bf16[32,4096]{1,0:T(8,128)(2,1)S(1)}, bf16[32,4096]{1,0:T(8,128)(2,1)S(1)}, u32[]{:S(2)}, u32[]{:S(2)}) collective-permute-start(bf16[32,4096]{1,0:T(8,128)(2,1)S(1)} %pad_maximum_fusion.6), channel_id=1, source_target_pairs={{0,4},{1,5},{2,6},{3,7},{4,8},{5,9},{6,10},{7,11},{8,12},{9,13},{1... | collective-permute-start | bytes 786440 | tf_op jit(solution)/shard_map/ppermute | solution.py:38
  521.4 7.7 %collective-permute-start.31 = (bf16[32,4096]{1,0:T(8,128)(2,1)S(1)}, bf16[32,4096]{1,0:T(8,128)(2,1)S(1)}, u32[]{:S(2)}, u32[]{:S(2)}) collective-permute-start(bf16[32,4096]{1,0:T(8,128)(2,1)S(1)} %pad_maximum_fusion.7), channel_id=1, source_target_pairs={{0,12},{1,13},{2,14},{3,15},{4,0},{5,1},{6,2},{7,3},{8,4},{9,5},{1... | collective-permute-start | bytes 786440 | tf_op jit(solution)/shard_map/ppermute | solution.py:38

commit v3 on v1

v3 whole, which is shorter than its diff:
```python
import jax
import jax.numpy as jnp
from jax import lax
from jax.sharding import PartitionSpec as P

EXPERTS = 16
SIDE = 4
LANES = 128


def normalize(hidden, norm_gain):
    mean_square = jnp.mean(hidden * hidden, axis=-1, keepdims=True)
    return (hidden * lax.rsqrt(mean_square + 1e-06) * norm_gain).astype(jnp.bfloat16)


def together(*values):
    return lax.optimization_barrier(values)


def reduce_over_tensor(partial):
    count = lax.axis_size("tensor")
    parts = lax.all_to_all(
        partial.astype(jnp.bfloat16), "tensor", split_axis=0, concat_axis=0, tiled=True
    )
    parts = parts.reshape(count, partial.shape[0] // count, partial.shape[1])
    return jnp.sum(parts.astype(jnp.float32), axis=0)


def shift(value, turn, step):
    pairs = []
    for half in range(lax.axis_size("dp")):
        for row in range(SIDE):
            for col in range(SIDE):
                if (half + turn) % 2:
                    to_row, to_col = (row + step) % SIDE, col
                else:
                    to_row, to_col = row, (col + step) % SIDE
                base = half * SIDE * SIDE
                pairs.append((base + row * SIDE + col, base + to_row * SIDE + to_col))
    return lax.ppermute(value, ("dp", "expert"), pairs)


def spread(block, turn):
    half = block.shape[0] // 2
    back, front = together(shift(block, turn, 1), shift(block, turn, -1))
    far = together(shift(back[:half], turn, 1), shift(front[half:], turn, -1))
    return back, front, far[0], far[1]


def add(*values):
    total = values[0].astype(jnp.float32)
    for value in values[1:]:
        total = total + value.astype(jnp.float32)
    return total


def collect(own, back, front, far_low, far_high, turn):
    half = far_low.shape[0]
    up, down = together(shift(far_low, turn, 1), shift(far_high, turn, -1))
    front = jnp.concatenate([add(front[:half], up).astype(jnp.bfloat16), front[half:]])
    back = jnp.concatenate([back[:half], add(back[half:], down).astype(jnp.bfloat16)])
    from_back, from_front = together(shift(front, turn, 1), shift(back, turn, -1))
    return add(own, from_back, from_front)


def on_device(
    attn_heads, out_proj, residual, norm_gain, expert_ids, weight_codes, w_gate, w_up, w_down
):
    tensor_count = lax.axis_size("tensor")
    own_residual = residual[0]
    tok_own, model_width = own_residual.shape
    tokens = tok_own * tensor_count
    me = lax.axis_index("expert")

    lane = jnp.arange(LANES, dtype=jnp.int32)
    codes = weight_codes[0]
    names = expert_ids[0][:, :, None] == lane[None, None, :]
    table = jnp.sum(jnp.where(names, codes[:, :, None], 0), axis=1)
    table = table + jnp.where(lane == EXPERTS, jnp.sum(codes, axis=1, keepdims=True), 0)

    partial = jnp.dot(attn_heads[0], out_proj, preferred_element_type=jnp.float32)
    hidden = own_residual.astype(jnp.float32) + reduce_over_tensor(partial)
    normed = normalize(hidden, norm_gain)
    rows = jnp.concatenate([normed, table.astype(jnp.bfloat16)], axis=1)
    group = lax.all_to_all(
        jnp.tile(rows, (tensor_count, 1)), "tensor", split_axis=0, concat_axis=0, tiled=True
    )

    def expert(rows):
        x = rows[:, :model_width]
        tail = rows[:, model_width:].astype(jnp.float32)
        code = jnp.sum(jnp.where(lane == me, tail, 0.0), axis=1, keepdims=True)
        total = jnp.sum(jnp.where(lane == EXPERTS, tail, 0.0), axis=1, keepdims=True)
        gate_value = jnp.einsum("rd,fd->rf", x, w_gate[0], preferred_element_type=jnp.float32)
        up_value = jnp.einsum("rd,fd->rf", x, w_up[0], preferred_element_type=jnp.float32)
        activated = (jax.nn.silu(gate_value) * up_value).astype(jnp.bfloat16)
        activated = lax.optimization_barrier(activated)
        down = jnp.dot(activated, w_down[0], preferred_element_type=jnp.float32)
        return (down * (code / total)).astype(jnp.bfloat16)

    back, front, far_low, far_high = spread(group, 0)
    line = lax.optimization_barrier(jnp.concatenate([group, back, front, far_low, far_high]))
    blocks = (line, *spread(line, 1))
    line_sum = collect(*(expert(block) for block in blocks), 1).astype(jnp.bfloat16)
    edges = [0, tokens, 2 * tokens, 3 * tokens, 3 * tokens + tokens // 2, 4 * tokens]
    mixed = collect(*(line_sum[i:j] for i, j in zip(edges[:-1], edges[1:])), 0)
    layer_out = (hidden + reduce_over_tensor(mixed)).astype(jnp.bfloat16)
    return layer_out[None]


def solution(mesh):
    return jax.shard_map(
        on_device,
        mesh=mesh,
        in_specs=(
            P(("dp", "expert"), None, "tensor"),
            P("tensor", None),
            P(("dp", "expert"), "tensor", None),
            P(),
            P(("dp", "expert"), "tensor", None),
            P(("dp", "expert"), "tensor", None),
            P("expert", "tensor", None),
            P("expert", "tensor", None),
            P("expert", "tensor", None),
        ),
        out_specs=P(("dp", "expert"), "tensor", None),
        check_vma=False,
    )
```

time: 253 us -> 213 us (0.84)
  blocking collectives: 114 us -> 36.4 us
  waiting for transfers between devices: 90.5 us -> 109 us
  starting transfers between devices: 15.3 us -> 28.9 us
  local copies, waits for them, and re-layouts: 2.88 us -> 7.83 us
    ppermute x0 -> x16, waiting for transfers between devices: none -> 92.3 us  [shift(): return lax.ppermute(value, ('dp', 'expert'), pairs)]
    all_to_all x1 -> x0, waiting for transfers between devices: 73.9 us -> none  [on_device(): lax.all_to_all(expert_part.astype(jnp.bfloat16), 'expert', split_axis=0,...]
    all_to_all x1, blocking collectives: 72.4 us -> 20.7 us  [on_device(): lax.all_to_all(jnp.tile(rows, (tensor_count, 1)), 'tensor', split_axis=0,...]
    all_gather x1 -> x0, blocking collectives: 25.5 us -> none  [on_device(): lax.all_gather(jnp.concatenate([normed, routes], axis=1), 'tensor', axis=...]
    ppermute x0 -> x16, starting transfers between devices: none -> 20.4 us  [shift(): return lax.ppermute(value, ('dp', 'expert'), pairs)]
    all_to_all x1 -> x0, starting transfers between devices: 6.84 us -> none  [on_device(): lax.all_to_all(expert_part.astype(jnp.bfloat16), 'expert', split_axis=0,...]
    slice x0 -> x8, local copies, waits for them, and re-layouts: none -> 3.8 us  [the longest x4 2.66 us: spread(): far = together(shift(back[:half], turn, 1), shift(front[half:], turn, -1))]
    dot_general x5 -> x15, matrix products: 21.5 us -> 20.5 us  [the longest x5 8.74 us: expert(): jnp.einsum('rd,fd->rf', x, w_gate[0], preferred_element_type=jnp.float32)]
  transfers between devices with their start and end apart: 2 -> 17, of which waited for: 2 -> 15; matrix products, arithmetic and copies ran while one was open for 0% -> 10% of each run, Pallas kernels for 0% -> 0%
where the time goes in v3:
time: 213 us; the launch traced here: 212 us
  waiting for transfers between devices  109 us (51%)
  blocking collectives  36.4 us (17%)
  starting transfers between devices  28.9 us (14%)
  matrix products  24.5 us (12%)
  local copies, waits for them, and re-layouts  7.83 us (4%)
  other arithmetic  4.8 us (2%)
    ppermute x16, waiting for transfers between devices, shift(): return lax.ppermute(value, ('dp', 'expert'), pairs)  92.3 us
    all_to_all x1, blocking collectives, on_device(): lax.all_to_all(jnp.tile(rows, (tensor_count, 1)), 'tensor', split_axis=0,...  20.7 us
    ppermute x16, starting transfers between devices, shift(): return lax.ppermute(value, ('dp', 'expert'), pairs)  20.4 us
    all_to_all x1, waiting for transfers between devices, reduce_over_tensor(): lax.all_to_all(partial.astype(jnp.bfloat16), 'tensor', split_axis=0, conc...  17.2 us
    all_to_all x1, blocking collectives, reduce_over_tensor(): lax.all_to_all(partial.astype(jnp.bfloat16), 'tensor', split_axis=0, conc...  15.7 us
    dot_general x5, matrix products, expert(): jnp.einsum('rd,fd->rf', x, w_gate[0], preferred_element_type=jnp.float32)  8.74 us
    dot_general x5, matrix products, expert(): jnp.einsum('rd,fd->rf', x, w_up[0], preferred_element_type=jnp.float32)  8.66 us
    all_to_all x1, starting transfers between devices, reduce_over_tensor(): lax.all_to_all(partial.astype(jnp.bfloat16), 'tensor', split_axis=0, conc...  8.46 us
  transfers between devices with their start and end apart: 17, of which 15 were waited for; matrix products, arithmetic and copies ran while one was open for 10% of the time, Pallas kernels for 0%

profile of v3, /device:TPU:24, one launch (start us, length us, event | category | flops | bytes accessed | tf_op | source)
XLA Modules:
  0.0 212.3 jit_solution(15169667403758891817)
XLA Ops:
  0.0 4.0 %fusion.6 = bf16[8,8,4096]{2,1,0:T(8,128)(2,1)} fusion(bf16[512,4096]{1,0:T(8,128)(2,1)} %param.10, bf16[1,64,512]{2,1,0:T(8,128)(2,1)} %param.9), kind=kOutput, calls=%fused_computation.12 | convolution fusion | flops 268697600 | bytes 4784128 | tf_op jit(solution)/shard_map/dot_general | solution.py:81
  4.0 8.5 %all-to-all-start = ((bf16[8,8,4096]{2,1,0:T(8,128)(2,1)}), bf16[8,8,4096]{2,1,0:T(8,128)(2,1)S(1)}, u32[]{:S(2)}, u32[]{:S(2)}) async-start(bf16[8,8,4096]{2,1,0:T(8,128)(2,1)} %fusion.6), calls=%async_computation | async-start | bytes 1048576 | tf_op jit(solution)/shard_map/all_to_all | solution.py:22
  12.8 17.2 %all-to-all-done = bf16[8,8,4096]{2,1,0:T(8,128)(2,1)S(1)} async-done(((bf16[8,8,4096]{2,1,0:T(8,128)(2,1)}), bf16[8,8,4096]{2,1,0:T(8,128)(2,1)S(1)}, u32[]{:S(2)}, u32[]{:S(2)}) %all-to-all-start) | async-done | bytes 524320 | tf_op jit(solution)/shard_map/all_to_all | solution.py:22
  30.4 20.7 %all_to_all.27 = bf16[8,8,4224]{2,1,0:T(8,128)(2,1)S(1)} all-to-all(bf16[8,8,4224]{2,1,0:T(8,128)(2,1)S(1)} %tile.2), channel_id=1, replica_groups=mesh['dp'=2,'tensor'=8,'expert'=16] {'tensor'}, dimensions={0} | all-to-all | bytes 1081344 | tf_op jit(solution)/shard_map/all_to_all | solution.py:85
  51.1 2.8 %collective-permute-start.1 = (bf16[64,4224]{1,0:T(8,128)(2,1)S(1)}, bf16[64,4224]{1,0:T(8,128)(2,1)S(1)}, u32[]{:S(2)}, u32[]{:S(2)}) collective-permute-start(bf16[64,4224]{1,0:T(8,128)(2,1)S(1)} %bitcast.78), channel_id=1, source_target_pairs={{0,3},{1,0},{2,1},{3,2},{4,7},{5,4},{6,5},{7,6},{8,11},{9,8},{10,9... | collective-permute-start | bytes 1622024 | tf_op jit(solution)/shard_map/ppermute | solution.py:40
  53.8 0.8 constant_dynamic-update-slice_fusion.4
  54.7 6.0 %collective-permute-done.1 = bf16[64,4224]{1,0:T(8,128)(2,1)S(1)} collective-permute-done((bf16[64,4224]{1,0:T(8,128)(2,1)S(1)}, bf16[64,4224]{1,0:T(8,128)(2,1)S(1)}, u32[]{:S(2)}, u32[]{:S(2)}) %collective-permute-start.1) | collective-permute-done | bytes 540704 | tf_op jit(solution)/shard_map/ppermute | solution.py:40
  60.7 3.7 %collective-permute-done = bf16[64,4224]{1,0:T(8,128)(2,1)S(1)} collective-permute-done((bf16[64,4224]{1,0:T(8,128)(2,1)S(1)}, bf16[64,4224]{1,0:T(8,128)(2,1)S(1)}, u32[]{:S(2)}, u32[]{:S(2)}) %collective-permute-start) | collective-permute-done | bytes 540704 | tf_op jit(solution)/shard_map/ppermute | solution.py:40
  64.5 2.0 collective-permute-start.2
  66.6 0.8 constant_dynamic-update-slice_fusion.3
  67.4 0.8 constant_dynamic-update-slice_fusion.2
  68.2 2.7 %collective-permute-done.3 = bf16[32,4224]{1,0:T(8,128)(2,1)S(1)} collective-permute-done((bf16[32,4224]{1,0:T(8,128)(2,1)S(1)}, bf16[32,4224]{1,0:T(8,128)(2,1)S(1)}, u32[]{:S(2)}, u32[]{:S(2)}) %collective-permute-start.3) | collective-permute-done | bytes 270368 | tf_op jit(solution)/shard_map/ppermute | solution.py:40
  71.0 1.3 collective-permute-done.2
  72.3 0.7 constant_dynamic-update-slice_fusion.1
  73.0 0.7 constant_dynamic-update-slice_fusion
  73.7 0.7 collective-permute-start.5
  74.5 2.5 %collective-permute-start.4 = (bf16[256,4224]{1,0:T(8,128)(2,1)}, bf16[256,4224]{1,0:T(8,128)(2,1)}, u32[]{:S(2)}, u32[]{:S(2)}) collective-permute-start(bf16[256,4224]{1,0:T(8,128)(2,1)} %constant_dynamic-update-slice_fusion), channel_id=1, source_target_pairs={{0,4},{1,5},{2,6},{3,7},{4,8},{5,9},{6,10},{7,11},{8,12},{9,13},{1... | collective-permute-start | bytes 6488072 | tf_op jit(solution)/shard_map/ppermute | solution.py:40
  77.0 25.0 %collective-permute-done.5 = bf16[256,4224]{1,0:T(8,128)(2,1)} collective-permute-done((bf16[256,4224]{1,0:T(8,128)(2,1)}, bf16[256,4224]{1,0:T(8,128)(2,1)}, u32[]{:S(2)}, u32[]{:S(2)}) %collective-permute-start.5) | collective-permute-done | bytes 2162720 | tf_op jit(solution)/shard_map/ppermute | solution.py:40
  102.0 1.3 slice.89
  103.3 1.3 slice.88
  104.6 3.3 %collective-permute-start.6 = (bf16[128,4224]{1,0:T(8,128)(2,1)S(1)}, bf16[128,4224]{1,0:T(8,128)(2,1)S(1)}, u32[]{:S(2)}, u32[]{:S(2)}) collective-permute-start(bf16[128,4224]{1,0:T(8,128)(2,1)S(1)} %slice.88), channel_id=1, source_target_pairs={{0,4},{1,5},{2,6},{3,7},{4,8},{5,9},{6,10},{7,11},{8,12},{9,13},{1... | collective-permute-start | bytes 3244040 | tf_op jit(solution)/shard_map/ppermute | solution.py:40
  108.0 2.6 %fusion.17 = f32[256,192]{0,1:T(8,128)S(1)} fusion(bf16[256,4224]{1,0:T(8,128)(2,1)} %collective-permute-done.5, bf16[1,192,4096]{2,1,0:T(8,128)(2,1)S(1)} %copy-done.2), kind=kOutput, calls=%fused_computation.28 | convolution fusion | flops 402653184 | bytes 3866624 | tf_op jit(solution)/shard_map/rd,fd->rf/dot_general | solution.py:94
  110.6 2.5 %multiply_convert_fusion.1 = bf16[256,192]{0,1:T(8,128)(2,1)S(1)} fusion(f32[256,192]{0,1:T(8,128)S(1)} %fusion.17, bf16[1,192,4096]{2,1,0:T(8,128)(2,1)S(1)} %copy-done.7, bf16[256,4224]{1,0:T(8,128)(2,1)} %collective-permute-done.5), kind=kOutput, calls=%fused_computation.68 | convolution fusion | flops 402948096 | bytes 3964928 | tf_op jit(solution)/shard_map/rd,fd->rf/dot_general | solution.py:95
  113.1 2.5 %fusion.13 = f32[256,192]{0,1:T(8,128)S(1)} fusion(bf16[256,4224]{1,0:T(8,128)(2,1)} %collective-permute-done.4, bf16[1,192,4096]{2,1,0:T(8,128)(2,1)S(1)} %copy-done.2), kind=kOutput, calls=%fused_computation.24 | convolution fusion | flops 402653184 | bytes 3866624 | tf_op jit(solution)/shard_map/rd,fd->rf/dot_general | solution.py:94
  115.6 5.0 %collective-permute-done.6 = bf16[128,4224]{1,0:T(8,128)(2,1)S(1)} collective-permute-done((bf16[128,4224]{1,0:T(8,128)(2,1)S(1)}, bf16[128,4224]{1,0:T(8,128)(2,1)S(1)}, u32[]{:S(2)}, u32[]{:S(2)}) %collective-permute-start.6) | collective-permute-done | bytes 1081376 | tf_op jit(solution)/shard_map/ppermute | solution.py:40
  120.6 3.7 %collective-permute-done.7 = bf16[128,4224]{1,0:T(8,128)(2,1)S(1)} collective-permute-done((bf16[128,4224]{1,0:T(8,128)(2,1)S(1)}, bf16[128,4224]{1,0:T(8,128)(2,1)S(1)}, u32[]{:S(2)}, u32[]{:S(2)}) %collective-permute-start.7) | collective-permute-done | bytes 1081376 | tf_op jit(solution)/shard_map/ppermute | solution.py:40
  128.0 2.1 collective-permute-start.9
  130.1 2.5 %multiply_convert_fusion = bf16[256,192]{0,1:T(8,128)(2,1)S(1)} fusion(f32[256,192]{0,1:T(8,128)S(1)} %fusion.13, bf16[1,192,4096]{2,1,0:T(8,128)(2,1)S(1)} %copy-done.7, bf16[256,4224]{1,0:T(8,128)(2,1)} %collective-permute-done.4), kind=kOutput, calls=%fused_computation.67 | convolution fusion | flops 402948096 | bytes 3964928 | tf_op jit(solution)/shard_map/rd,fd->rf/dot_general | solution.py:95
  132.6 1.1 fusion.71
  133.7 0.7 fusion.3
  134.5 0.7 fusion.2
  135.3 7.0 %collective-permute-done.8 = bf16[128,4096]{1,0:T(8,128)(2,1)S(1)} collective-permute-done((bf16[128,4096]{1,0:T(8,128)(2,1)S(1)}, bf16[128,4096]{1,0:T(8,128)(2,1)S(1)}, u32[]{:S(2)}, u32[]{:S(2)}) %collective-permute-start.8) | collective-permute-done | bytes 1048608 | tf_op jit(solution)/shard_map/ppermute | solution.py:40
  142.3 1.8 collective-permute-done.9
  144.8 1.0 slice-done
  146.0 1.1 collective-permute-start.11
  147.2 2.5 %fusion.9 = f32[256,192]{0,1:T(8,128)S(1)} fusion(bf16[256,4224]{1,0:T(8,128)(2,1)} %constant_dynamic-update-slice_fusion, bf16[1,192,4096]{2,1,0:T(8,128)(2,1)S(1)} %copy-done.2), kind=kOutput, calls=%fused_computation.20 | convolution fusion | flops 402653184 | bytes 3866624 | tf_op jit(solution)/shard_map/rd,fd->rf/dot_general | solution.py:94
  149.7 2.5 %fusion.43 = bf16[256,192]{0,1:T(8,128)(2,1)S(1)} fusion(bf16[1,192,4096]{2,1,0:T(8,128)(2,1)S(1)} %copy-done.7, bf16[256,4224]{1,0:T(8,128)(2,1)} %constant_dynamic-update-slice_fusion, f32[256,192]{0,1:T(8,128)S(1)} %fusion.9), kind=kOutput, calls=%fused_computation.50 | convolution fusion | flops 402948096 | bytes 3964928 | tf_op jit(solution)/shard_map/rd,fd->rf/dot_general | solution.py:95
  152.2 0.7 fusion.1
  152.9 20.8 %collective-permute-done.10 = bf16[256,4096]{1,0:T(8,128)(2,1)S(1)} collective-permute-done((bf16[256,4096]{1,0:T(8,128)(2,1)S(1)}, bf16[256,4096]{1,0:T(8,128)(2,1)S(1)}, u32[]{:S(2)}, u32[]{:S(2)}) %collective-permute-start.10) | collective-permute-done | bytes 2097184 | tf_op jit(solution)/shard_map/ppermute | solution.py:40
  173.7 2.5 %collective-permute-done.11 = bf16[256,4096]{1,0:T(8,128)(2,1)S(1)} collective-permute-done((bf16[256,4096]{1,0:T(8,128)(2,1)S(1)}, bf16[256,4096]{1,0:T(8,128)(2,1)S(1)}, u32[]{:S(2)}, u32[]{:S(2)}) %collective-permute-start.11) | collective-permute-done | bytes 2097184 | tf_op jit(solution)/shard_map/ppermute | solution.py:40
  176.2 1.0 add_convert_fusion
  177.4 2.0 collective-permute-start.12
  179.4 4.3 %collective-permute-done.13 = bf16[32,4096]{1,0:T(8,128)(2,1)S(1)} collective-permute-done((bf16[32,4096]{1,0:T(8,128)(2,1)S(1)}, bf16[32,4096]{1,0:T(8,128)(2,1)S(1)}, u32[]{:S(2)}, u32[]{:S(2)}) %collective-permute-start.13) | collective-permute-done | bytes 262176 | tf_op jit(solution)/shard_map/ppermute | solution.py:40
  183.7 1.3 collective-permute-done.12
  185.2 0.8 collective-permute-start.14
  186.1 2.6 %collective-permute-start.15 = (bf16[64,4096]{1,0:T(8,128)(2,1)S(1)}, bf16[64,4096]{1,0:T(8,128)(2,1)S(1)}, u32[]{:S(2)}, u32[]{:S(2)}) collective-permute-start(bf16[64,4096]{1,0:T(8,128)(2,1)S(1)} %pad_maximum_fusion.3), channel_id=1, source_target_pairs={{0,3},{1,0},{2,1},{3,2},{4,7},{5,4},{6,5},{7,6},{8,11},{9,8},{10,9... | collective-permute-start | bytes 1572872 | tf_op jit(solution)/shard_map/ppermute | solution.py:40
  188.6 7.0 %collective-permute-done.14 = bf16[64,4096]{1,0:T(8,128)(2,1)S(1)} collective-permute-done((bf16[64,4096]{1,0:T(8,128)(2,1)S(1)}, bf16[64,4096]{1,0:T(8,128)(2,1)S(1)}, u32[]{:S(2)}, u32[]{:S(2)}) %collective-permute-start.14) | collective-permute-done | bytes 524320 | tf_op jit(solution)/shard_map/ppermute | solution.py:40
  195.9 15.7 %all_to_all.28 = bf16[8,8,4096]{2,1,0:T(8,128)(2,1)S(1)} all-to-all(bf16[8,8,4096]{2,1,0:T(8,128)(2,1)S(1)} %fusion.64), channel_id=1, replica_groups=mesh['dp'=2,'tensor'=8,'expert'=16] {'tensor'}, dimensions={0} | all-to-all | bytes 1048576 | tf_op jit(solution)/shard_map/all_to_all | solution.py:22
  (62 shorter events, 6.7 us)
Async XLA Ops:
  0.0 126.8 %copy-start = (bf16[1,192,4096]{2,1,0:T(8,128)(2,1)S(1)}, bf16[1,192,4096]{2,1,0:T(8,128)(2,1)}, u32[]{:S(2)}) copy-start(bf16[1,192,4096]{2,1,0:T(8,128)(2,1)} %param.17) | copy-start | bytes 4718596
  0.0 12.5 %copy-start.5 = (s32[1,8,8]{2,1,0:T(8,128)S(1)}, s32[1,8,8]{2,1,0:T(8,128)}, u32[]{:S(2)}) copy-start(s32[1,8,8]{2,1,0:T(8,128)} %param.14) | copy-start | bytes 772
  0.0 12.6 %copy-start.6 = (s32[1,8,8]{2,1,0:T(8,128)S(1)}, s32[1,8,8]{2,1,0:T(8,128)}, u32[]{:S(2)}) copy-start(s32[1,8,8]{2,1,0:T(8,128)} %param.13) | copy-start | bytes 772
  0.0 30.0 %copy-start.3 = (bf16[1,8,4096]{2,1,0:T(8,128)(2,1)S(1)}, bf16[1,8,4096]{2,1,0:T(8,128)(2,1)}, u32[]{:S(2)}) copy-start(bf16[1,8,4096]{2,1,0:T(8,128)(2,1)} %param.11) | copy-start | bytes 196612
  0.0 30.2 %copy-start.4 = (f32[4096]{0:T(1024)S(1)}, f32[4096]{0:T(1024)}, u32[]{:S(2)}) copy-start(f32[4096]{0:T(1024)} %param.12) | copy-start | bytes 49156
  4.0 26.0 %all-to-all-start = ((bf16[8,8,4096]{2,1,0:T(8,128)(2,1)}), bf16[8,8,4096]{2,1,0:T(8,128)(2,1)S(1)}, u32[]{:S(2)}, u32[]{:S(2)}) async-start(bf16[8,8,4096]{2,1,0:T(8,128)(2,1)} %fusion.6), calls=%async_computation | async-start | bytes 1048576 | tf_op jit(solution)/shard_map/all_to_all | solution.py:22
  51.1 9.6 %collective-permute-start.1 = (bf16[64,4224]{1,0:T(8,128)(2,1)S(1)}, bf16[64,4224]{1,0:T(8,128)(2,1)S(1)}, u32[]{:S(2)}, u32[]{:S(2)}) collective-permute-start(bf16[64,4224]{1,0:T(8,128)(2,1)S(1)} %bitcast.78), channel_id=1, source_target_pairs={{0,3},{1,0},{2,1},{3,2},{4,7},{5,4},{6,5},{7,6},{8,11},{9,8},{10,9... | collective-permute-start | bytes 1622024 | tf_op jit(solution)/shard_map/ppermute | solution.py:40
  53.8 10.6 %collective-permute-start = (bf16[64,4224]{1,0:T(8,128)(2,1)S(1)}, bf16[64,4224]{1,0:T(8,128)(2,1)S(1)}, u32[]{:S(2)}, u32[]{:S(2)}) collective-permute-start(bf16[64,4224]{1,0:T(8,128)(2,1)S(1)} %bitcast.79), channel_id=1, source_target_pairs={{0,1},{1,2},{2,3},{3,0},{4,5},{5,6},{6,7},{7,4},{8,9},{9,10},{10,1... | collective-permute-start | bytes 1622024 | tf_op jit(solution)/shard_map/ppermute | solution.py:40
  64.5 6.5 %collective-permute-start.3 = (bf16[32,4224]{1,0:T(8,128)(2,1)S(1)}, bf16[32,4224]{1,0:T(8,128)(2,1)S(1)}, u32[]{:S(2)}, u32[]{:S(2)}) collective-permute-start(bf16[32,4224]{1,0:T(8,128)(2,1)S(1)} %slice.82), channel_id=1, source_target_pairs={{0,3},{1,0},{2,1},{3,2},{4,7},{5,4},{6,5},{7,6},{8,11},{9,8},{10,9... | collective-permute-start | bytes 811016 | tf_op jit(solution)/shard_map/ppermute | solution.py:40
  64.5 7.7 %collective-permute-start.2 = (bf16[32,4224]{1,0:T(8,128)(2,1)S(1)}, bf16[32,4224]{1,0:T(8,128)(2,1)S(1)}, u32[]{:S(2)}, u32[]{:S(2)}) collective-permute-start(bf16[32,4224]{1,0:T(8,128)(2,1)S(1)} %slice.81), channel_id=1, source_target_pairs={{0,1},{1,2},{2,3},{3,0},{4,5},{5,6},{6,7},{7,4},{8,9},{9,10},{10,1... | collective-permute-start | bytes 811016 | tf_op jit(solution)/shard_map/ppermute | solution.py:40
  73.7 28.3 %collective-permute-start.5 = (bf16[256,4224]{1,0:T(8,128)(2,1)}, bf16[256,4224]{1,0:T(8,128)(2,1)}, u32[]{:S(2)}, u32[]{:S(2)}) collective-permute-start(bf16[256,4224]{1,0:T(8,128)(2,1)} %constant_dynamic-update-slice_fusion), channel_id=1, source_target_pairs={{0,12},{1,13},{2,14},{3,15},{4,0},{5,1},{6,2},{7,3},{8,4},{9,5},{1... | collective-permute-start | bytes 6488072 | tf_op jit(solution)/shard_map/ppermute | solution.py:40
  74.5 27.5 %collective-permute-start.4 = (bf16[256,4224]{1,0:T(8,128)(2,1)}, bf16[256,4224]{1,0:T(8,128)(2,1)}, u32[]{:S(2)}, u32[]{:S(2)}) collective-permute-start(bf16[256,4224]{1,0:T(8,128)(2,1)} %constant_dynamic-update-slice_fusion), channel_id=1, source_target_pairs={{0,4},{1,5},{2,6},{3,7},{4,8},{5,9},{6,10},{7,11},{8,12},{9,13},{1... | collective-permute-start | bytes 6488072 | tf_op jit(solution)/shard_map/ppermute | solution.py:40
  77.0 31.0 %copy-start.2 = (bf16[1,192,4096]{2,1,0:T(8,128)(2,1)S(1)}, bf16[1,192,4096]{2,1,0:T(8,128)(2,1)}, u32[]{:S(2)}) copy-start(bf16[1,192,4096]{2,1,0:T(8,128)(2,1)} %param.15) | copy-start | bytes 4718596
  104.6 16.0 %collective-permute-start.6 = (bf16[128,4224]{1,0:T(8,128)(2,1)S(1)}, bf16[128,4224]{1,0:T(8,128)(2,1)S(1)}, u32[]{:S(2)}, u32[]{:S(2)}) collective-permute-start(bf16[128,4224]{1,0:T(8,128)(2,1)S(1)} %slice.88), channel_id=1, source_target_pairs={{0,4},{1,5},{2,6},{3,7},{4,8},{5,9},{6,10},{7,11},{8,12},{9,13},{1... | collective-permute-start | bytes 3244040 | tf_op jit(solution)/shard_map/ppermute | solution.py:40
  107.9 16.4 %collective-permute-start.7 = (bf16[128,4224]{1,0:T(8,128)(2,1)S(1)}, bf16[128,4224]{1,0:T(8,128)(2,1)S(1)}, u32[]{:S(2)}, u32[]{:S(2)}) collective-permute-start(bf16[128,4224]{1,0:T(8,128)(2,1)S(1)} %slice.89), channel_id=1, source_target_pairs={{0,12},{1,13},{2,14},{3,15},{4,0},{5,1},{6,2},{7,3},{8,4},{9,5},{1... | collective-permute-start | bytes 3244040 | tf_op jit(solution)/shard_map/ppermute | solution.py:40
  108.0 2.6 %copy-start.7 = (bf16[1,192,4096]{2,1,0:T(8,128)(2,1)S(1)}, bf16[1,192,4096]{2,1,0:T(8,128)(2,1)}, u32[]{:S(2)}) copy-start(bf16[1,192,4096]{2,1,0:T(8,128)(2,1)} %param.16) | copy-start | bytes 4718596
  127.3 15.1 %collective-permute-start.8 = (bf16[128,4096]{1,0:T(8,128)(2,1)S(1)}, bf16[128,4096]{1,0:T(8,128)(2,1)S(1)}, u32[]{:S(2)}, u32[]{:S(2)}) collective-permute-start(bf16[128,4096]{1,0:T(8,128)(2,1)S(1)} %fusion.4), channel_id=1, source_target_pairs={{0,4},{1,5},{2,6},{3,7},{4,8},{5,9},{6,10},{7,11},{8,12},{9,13},{1... | collective-permute-start | bytes 3145736 | tf_op jit(solution)/shard_map/ppermute | solution.py:40
  128.0 16.1 %collective-permute-start.9 = (bf16[128,4096]{1,0:T(8,128)(2,1)S(1)}, bf16[128,4096]{1,0:T(8,128)(2,1)S(1)}, u32[]{:S(2)}, u32[]{:S(2)}) collective-permute-start(bf16[128,4096]{1,0:T(8,128)(2,1)S(1)} %fusion.5), channel_id=1, source_target_pairs={{0,12},{1,13},{2,14},{3,15},{4,0},{5,1},{6,2},{7,3},{8,4},{9,5},{1... | collective-permute-start | bytes 3145736 | tf_op jit(solution)/shard_map/ppermute | solution.py:40
  134.4 9.7 %copy-start.1 = (bf16[256,4096]{1,0:T(8,128)(2,1)}, bf16[256,4096]{1,0:T(8,128)(2,1)S(1)}, u32[]{:S(2)}) copy-start(bf16[256,4096]{1,0:T(8,128)(2,1)S(1)} %fusion.3) | copy-start | bytes 6291460
  144.6 1.2 slice-start
  144.8 28.9 %collective-permute-start.10 = (bf16[256,4096]{1,0:T(8,128)(2,1)S(1)}, bf16[256,4096]{1,0:T(8,128)(2,1)S(1)}, u32[]{:S(2)}, u32[]{:S(2)}) collective-permute-start(bf16[256,4096]{1,0:T(8,128)(2,1)S(1)} %pad_maximum_fusion), channel_id=1, source_target_pairs={{0,4},{1,5},{2,6},{3,7},{4,8},{5,9},{6,10},{7,11},{8,12},{9,13},{1... | collective-permute-start | bytes 6291464 | tf_op jit(solution)/shard_map/ppermute | solution.py:40
  146.0 30.1 %collective-permute-start.11 = (bf16[256,4096]{1,0:T(8,128)(2,1)S(1)}, bf16[256,4096]{1,0:T(8,128)(2,1)S(1)}, u32[]{:S(2)}, u32[]{:S(2)}) collective-permute-start(bf16[256,4096]{1,0:T(8,128)(2,1)S(1)} %pad_maximum_fusion.1), channel_id=1, source_target_pairs={{0,12},{1,13},{2,14},{3,15},{4,0},{5,1},{6,2},{7,3},{8,4},{9,5},{1... | collective-permute-start | bytes 6291464 | tf_op jit(solution)/shard_map/ppermute | solution.py:40
  177.3 6.4 %collective-permute-start.13 = (bf16[32,4096]{1,0:T(8,128)(2,1)S(1)}, bf16[32,4096]{1,0:T(8,128)(2,1)S(1)}, u32[]{:S(2)}, u32[]{:S(2)}) collective-permute-start(bf16[32,4096]{1,0:T(8,128)(2,1)S(1)} %get-tuple-element.55), channel_id=1, source_target_pairs={{0,3},{1,0},{2,1},{3,2},{4,7},{5,4},{6,5},{7,6},{8,11},{9,8},{10,9... | collective-permute-start | bytes 786440 | tf_op jit(solution)/shard_map/ppermute | solution.py:40
  177.4 7.7 %collective-permute-start.12 = (bf16[32,4096]{1,0:T(8,128)(2,1)S(1)}, bf16[32,4096]{1,0:T(8,128)(2,1)S(1)}, u32[]{:S(2)}, u32[]{:S(2)}) collective-permute-start(bf16[32,4096]{1,0:T(8,128)(2,1)S(1)} %get-tuple-element.56), channel_id=1, source_target_pairs={{0,1},{1,2},{2,3},{3,0},{4,5},{5,6},{6,7},{7,4},{8,9},{9,10},{10,1... | collective-permute-start | bytes 786440 | tf_op jit(solution)/shard_map/ppermute | solution.py:40
  185.2 10.5 %collective-permute-start.14 = (bf16[64,4096]{1,0:T(8,128)(2,1)S(1)}, bf16[64,4096]{1,0:T(8,128)(2,1)S(1)}, u32[]{:S(2)}, u32[]{:S(2)}) collective-permute-start(bf16[64,4096]{1,0:T(8,128)(2,1)S(1)} %pad_maximum_fusion.2), channel_id=1, source_target_pairs={{0,1},{1,2},{2,3},{3,0},{4,5},{5,6},{6,7},{7,4},{8,9},{9,10},{10,1... | collective-permute-start | bytes 1572872 | tf_op jit(solution)/shard_map/ppermute | solution.py:40
  186.1 9.6 %collective-permute-start.15 = (bf16[64,4096]{1,0:T(8,128)(2,1)S(1)}, bf16[64,4096]{1,0:T(8,128)(2,1)S(1)}, u32[]{:S(2)}, u32[]{:S(2)}) collective-permute-start(bf16[64,4096]{1,0:T(8,128)(2,1)S(1)} %pad_maximum_fusion.3), channel_id=1, source_target_pairs={{0,3},{1,0},{2,1},{3,2},{4,7},{5,4},{6,5},{7,6},{8,11},{9,8},{10,9... | collective-permute-start | bytes 1572872 | tf_op jit(solution)/shard_map/ppermute | solution.py:40

commit v4 on v3

--- a/solution.py
+++ b/solution.py
@@ -11,10 +11,6 @@
 def normalize(hidden, norm_gain):
     mean_square = jnp.mean(hidden * hidden, axis=-1, keepdims=True)
     return (hidden * lax.rsqrt(mean_square + 1e-06) * norm_gain).astype(jnp.bfloat16)
-
-
-def together(*values):
-    return lax.optimization_barrier(values)
 
 
 def reduce_over_tensor(partial):
@@ -40,11 +36,13 @@
     return lax.ppermute(value, ("dp", "expert"), pairs)
 
 
-def spread(block, turn):
-    half = block.shape[0] // 2
-    back, front = together(shift(block, turn, 1), shift(block, turn, -1))
-    far = together(shift(back[:half], turn, 1), shift(front[half:], turn, -1))
-    return back, front, far[0], far[1]
+def send_round(block, turn):
+    return shift(block, turn, 1), shift(block, turn, -1)
+
+
+def send_on(back, front, turn):
+    half = back.shape[0] // 2
+    return shift(back[:half], turn, 1), shift(front[half:], turn, -1)
 
 
 def add(*values):
@@ -56,11 +54,10 @@
 
 def collect(own, back, front, far_low, far_high, turn):
     half = far_low.shape[0]
-    up, down = together(shift(far_low, turn, 1), shift(far_high, turn, -1))
+    up, down = shift(far_low, turn, 1), shift(far_high, turn, -1)
     front = jnp.concatenate([add(front[:half], up).astype(jnp.bfloat16), front[half:]])
     back = jnp.concatenate([back[:half], add(back[half:], down).astype(jnp.bfloat16)])
-    from_back, from_front = together(shift(front, turn, 1), shift(back, turn, -1))
-    return add(own, from_back, from_front)
+    return add(own, shift(front, turn, 1), shift(back, turn, -1))
 
 
 def on_device(
@@ -86,24 +83,41 @@
         jnp.tile(rows, (tensor_count, 1)), "tensor", split_axis=0, concat_axis=0, tiled=True
     )
 
-    def expert(rows):
+    def expert(rows, who):
         x = rows[:, :model_width]
         tail = rows[:, model_width:].astype(jnp.float32)
-        code = jnp.sum(jnp.where(lane == me, tail, 0.0), axis=1, keepdims=True)
+        code = jnp.sum(jnp.where(lane == who, tail, 0.0), axis=1, keepdims=True)
         total = jnp.sum(jnp.where(lane == EXPERTS, tail, 0.0), axis=1, keepdims=True)
         gate_value = jnp.einsum("rd,fd->rf", x, w_gate[0], preferred_element_type=jnp.float32)
         up_value = jnp.einsum("rd,fd->rf", x, w_up[0], preferred_element_type=jnp.float32)
         activated = (jax.nn.silu(gate_value) * up_value).astype(jnp.bfloat16)
         activated = lax.optimization_barrier(activated)
+        scale = code / total
         down = jnp.dot(activated, w_down[0], preferred_element_type=jnp.float32)
-        return (down * (code / total)).astype(jnp.bfloat16)
+        return (down * scale).astype(jnp.bfloat16), scale
 
-    back, front, far_low, far_high = spread(group, 0)
-    line = lax.optimization_barrier(jnp.concatenate([group, back, front, far_low, far_high]))
-    blocks = (line, *spread(line, 1))
-    line_sum = collect(*(expert(block) for block in blocks), 1).astype(jnp.bfloat16)
-    edges = [0, tokens, 2 * tokens, 3 * tokens, 3 * tokens + tokens // 2, 4 * tokens]
-    mixed = collect(*(line_sum[i:j] for i, j in zip(edges[:-1], edges[1:])), 0)
+    def pieces(block):
+        back, front = send_round(block, 1)
+        return (block, back, front, *send_on(back, front, 1))
+
+    back, front = send_round(group, 0)
+    far = send_on(back, front, 0)
+    first = pieces(jnp.concatenate([group, back]))
+    second = pieces(jnp.concatenate([front, *far]))
+    first_out = [expert(block, me) for block in first]
+    late = me + (first_out[4][1][0, 0] < 0.0).astype(jnp.int32)
+    second_out = [expert(block, who) for block, who in zip(second, (me, me, me, late, late))]
+    first_sum = collect(*(out for out, _ in first_out), 1).astype(jnp.bfloat16)
+    second_sum = collect(*(out for out, _ in second_out), 1).astype(jnp.bfloat16)
+    half = tokens // 2
+    mixed = collect(
+        first_sum[:tokens],
+        first_sum[tokens:],
+        second_sum[:tokens],
+        second_sum[tokens : tokens + half],
+        second_sum[tokens + half :],
+        0,
+    )
     layer_out = (hidden + reduce_over_tensor(mixed)).astype(jnp.bfloat16)
     return layer_out[None]
 

time: 213 us -> 205 us (0.962)
  waiting for transfers between devices: 109 us -> 82.3 us
  starting transfers between devices: 28.9 us -> 42 us
  matrix products: 24.5 us -> 28.4 us
    ppermute x16 -> x24, waiting for transfers between devices: 92.3 us -> 65.1 us  [shift(): return lax.ppermute(value, ('dp', 'expert'), pairs)]
    ppermute x16 -> x24, starting transfers between devices: 20.4 us -> 33.4 us  [shift(): return lax.ppermute(value, ('dp', 'expert'), pairs)]
    dot_general x5 -> x10, matrix products: 3.12 us -> 5.02 us  [expert(): down = jnp.dot(activated, w_down[0], preferred_element_type=jnp.float32)]
    dot_general x5 -> x10, matrix products: 8.74 us -> 10.3 us  [expert(): jnp.einsum('rd,fd->rf', x, w_gate[0], preferred_element_type=jnp.float32)]
    dot_general x5 -> x10, matrix products: 8.66 us -> 9.06 us  [expert(): jnp.einsum('rd,fd->rf', x, w_up[0], preferred_element_type=jnp.float32)]
  transfers between devices with their start and end apart: 17 -> 25, of which waited for: 15 -> 11; matrix products, arithmetic and copies ran while one was open for 10% -> 16% of each run, Pallas kernels for 0% -> 0%
where the time goes in v4:
time: 205 us; the launch traced here: 204 us
  waiting for transfers between devices  82.3 us (40%)
  starting transfers between devices  42 us (20%)
  blocking collectives  37.1 us (18%)
  matrix products  28.4 us (14%)
  local copies, waits for them, and re-layouts  7.65 us (4%)
  other arithmetic  5.61 us (3%)
    ppermute x24, waiting for transfers between devices, shift(): return lax.ppermute(value, ('dp', 'expert'), pairs)  65.1 us
    ppermute x24, starting transfers between devices, shift(): return lax.ppermute(value, ('dp', 'expert'), pairs)  33.4 us
    all_to_all x1, blocking collectives, on_device(): lax.all_to_all(jnp.tile(rows, (tensor_count, 1)), 'tensor', split_axis=0,...  21.4 us
    all_to_all x1, waiting for transfers between devices, reduce_over_tensor(): lax.all_to_all(partial.astype(jnp.bfloat16), 'tensor', split_axis=0, conc...  17.2 us
    all_to_all x1, blocking collectives, reduce_over_tensor(): lax.all_to_all(partial.astype(jnp.bfloat16), 'tensor', split_axis=0, conc...  15.7 us
    dot_general x10, matrix products, expert(): jnp.einsum('rd,fd->rf', x, w_gate[0], preferred_element_type=jnp.float32)  10.3 us
    dot_general x10, matrix products, expert(): jnp.einsum('rd,fd->rf', x, w_up[0], preferred_element_type=jnp.float32)  9.06 us
    all_to_all x1, starting transfers between devices, reduce_over_tensor(): lax.all_to_all(partial.astype(jnp.bfloat16), 'tensor', split_axis=0, conc...  8.6 us
  transfers between devices with their start and end apart: 25, of which 11 were waited for; matrix products, arithmetic and copies ran while one was open for 16% of the time, Pallas kernels for 0%

profile of v4, /device:TPU:24, one launch (start us, length us, event | category | flops | bytes accessed | tf_op | source)
XLA Modules:
  0.0 203.8 jit_solution(7596972857807055061)
XLA Ops:
  0.0 4.0 %fusion.12 = bf16[8,8,4096]{2,1,0:T(8,128)(2,1)} fusion(bf16[512,4096]{1,0:T(8,128)(2,1)} %param.10, bf16[1,64,512]{2,1,0:T(8,128)(2,1)} %param.9), kind=kOutput, calls=%fused_computation.23 | convolution fusion | flops 268697600 | bytes 4784128 | tf_op jit(solution)/shard_map/dot_general | solution.py:78
  4.0 8.6 %all-to-all-start = ((bf16[8,8,4096]{2,1,0:T(8,128)(2,1)}), bf16[8,8,4096]{2,1,0:T(8,128)(2,1)S(1)}, u32[]{:S(2)}, u32[]{:S(2)}) async-start(bf16[8,8,4096]{2,1,0:T(8,128)(2,1)} %fusion.12), calls=%async_computation | async-start | bytes 1048576 | tf_op jit(solution)/shard_map/all_to_all | solution.py:18
  12.9 17.2 %all-to-all-done = bf16[8,8,4096]{2,1,0:T(8,128)(2,1)S(1)} async-done(((bf16[8,8,4096]{2,1,0:T(8,128)(2,1)}), bf16[8,8,4096]{2,1,0:T(8,128)(2,1)S(1)}, u32[]{:S(2)}, u32[]{:S(2)}) %all-to-all-start) | async-done | bytes 524320 | tf_op jit(solution)/shard_map/all_to_all | solution.py:18
  30.5 21.4 %all_to_all.27 = bf16[8,8,4224]{2,1,0:T(8,128)(2,1)} all-to-all(bf16[8,8,4224]{2,1,0:T(8,128)(2,1)S(1)} %tile.2), channel_id=1, replica_groups=mesh['dp'=2,'tensor'=8,'expert'=16] {'tensor'}, dimensions={0} | all-to-all | bytes 1081344 | tf_op jit(solution)/shard_map/all_to_all | solution.py:82
  51.9 1.5 collective-permute-start
  53.4 1.7 collective-permute-start.9
  55.1 7.5 %collective-permute-done = bf16[64,4224]{1,0:T(8,128)(2,1)S(1)} collective-permute-done((bf16[64,4224]{1,0:T(8,128)(2,1)}, bf16[64,4224]{1,0:T(8,128)(2,1)S(1)}, u32[]{:S(2)}, u32[]{:S(2)}) %collective-permute-start) | collective-permute-done | bytes 540704 | tf_op jit(solution)/shard_map/ppermute | solution.py:36
  62.6 0.8 copy-done.12
  63.5 1.1 pad_maximum_fusion
  64.6 0.8 collective-permute-start.1
  65.4 2.5 %collective-permute-start.2 = (bf16[128,4224]{1,0:T(8,128)(2,1)S(1)}, bf16[128,4224]{1,0:T(8,128)(2,1)S(1)}, u32[]{:S(2)}, u32[]{:S(2)}) collective-permute-start(bf16[128,4224]{1,0:T(8,128)(2,1)S(1)} %pad_maximum_fusion), channel_id=1, source_target_pairs={{0,4},{1,5},{2,6},{3,7},{4,8},{5,9},{6,10},{7,11},{8,12},{9,13},{1... | collective-permute-start | bytes 3244040 | tf_op jit(solution)/shard_map/ppermute | solution.py:36
  67.9 1.6 collective-permute-start.11
  69.6 1.0 slice.194
  71.2 1.7 fusion.65
  72.9 1.6 multiply_convert_fusion.6
  74.5 6.7 %collective-permute-done.10 = bf16[32,4224]{1,0:T(8,128)(2,1)S(1)} collective-permute-done((bf16[32,4224]{1,0:T(8,128)(2,1)S(1)}, bf16[32,4224]{1,0:T(8,128)(2,1)S(1)}, u32[]{:S(2)}, u32[]{:S(2)}) %collective-permute-start.10) | collective-permute-done | bytes 270368 | tf_op jit(solution)/shard_map/ppermute | solution.py:36
  81.4 2.0 collective-permute-start.12
  87.1 3.5 %collective-permute-start.3 = (bf16[64,4224]{1,0:T(8,128)(2,1)S(1)}, bf16[64,4224]{1,0:T(8,128)(2,1)S(1)}, u32[]{:S(2)}, u32[]{:S(2)}) collective-permute-start(bf16[64,4224]{1,0:T(8,128)(2,1)S(1)} %slice.182), channel_id=1, source_target_pairs={{0,4},{1,5},{2,6},{3,7},{4,8},{5,9},{6,10},{7,11},{8,12},{9,13},{1... | collective-permute-start | bytes 1622024 | tf_op jit(solution)/shard_map/ppermute | solution.py:36
  90.5 6.0 %collective-permute-done.13 = bf16[128,4224]{1,0:T(8,128)(2,1)S(1)} collective-permute-done((bf16[128,4224]{1,0:T(8,128)(2,1)S(1)}, bf16[128,4224]{1,0:T(8,128)(2,1)S(1)}, u32[]{:S(2)}, u32[]{:S(2)}) %collective-permute-start.13) | collective-permute-done | bytes 1081376 | tf_op jit(solution)/shard_map/ppermute | solution.py:36
  97.7 0.9 slice.201
  98.6 2.2 %collective-permute-start.14 = (bf16[64,4224]{1,0:T(8,128)(2,1)}, bf16[64,4224]{1,0:T(8,128)(2,1)}, u32[]{:S(2)}, u32[]{:S(2)}) collective-permute-start(bf16[64,4224]{1,0:T(8,128)(2,1)} %slice.201), channel_id=1, source_target_pairs={{0,4},{1,5},{2,6},{3,7},{4,8},{5,9},{6,10},{7,11},{8,12},{9,13},{1... | collective-permute-start | bytes 1622024 | tf_op jit(solution)/shard_map/ppermute | solution.py:36
  101.9 0.8 slice.209
  102.8 0.9 fusion.91
  108.8 0.8 copy-done.14
  109.8 1.8 fusion.61
  113.2 3.3 %collective-permute-start.4 = (bf16[64,4096]{1,0:T(8,128)(2,1)S(1)}, bf16[64,4096]{1,0:T(8,128)(2,1)S(1)}, u32[]{:S(2)}, u32[]{:S(2)}) collective-permute-start(bf16[64,4096]{1,0:T(8,128)(2,1)S(1)} %fusion.8), channel_id=1, source_target_pairs={{0,4},{1,5},{2,6},{3,7},{4,8},{5,9},{6,10},{7,11},{8,12},{9,13},{1... | collective-permute-start | bytes 1572872 | tf_op jit(solution)/shard_map/ppermute | solution.py:36
  116.5 1.7 fusion.51
  118.2 1.7 multiply_convert_fusion.8
  119.9 1.7 fusion.47
  121.5 1.7 multiply_convert_fusion.7
  123.2 0.9 fusion.111
  124.5 2.3 %collective-permute-start.15 = (bf16[64,4096]{1,0:T(8,128)(2,1)S(1)}, bf16[64,4096]{1,0:T(8,128)(2,1)S(1)}, u32[]{:S(2)}, u32[]{:S(2)}) collective-permute-start(bf16[64,4096]{1,0:T(8,128)(2,1)S(1)} %fusion.10), channel_id=1, source_target_pairs={{0,4},{1,5},{2,6},{3,7},{4,8},{5,9},{6,10},{7,11},{8,12},{9,13},{1... | collective-permute-start | bytes 1572872 | tf_op jit(solution)/shard_map/ppermute | solution.py:36
  128.0 2.9 %collective-permute-start.5 = (bf16[128,4096]{1,0:T(8,128)(2,1)S(1)}, bf16[128,4096]{1,0:T(8,128)(2,1)S(1)}, u32[]{:S(2)}, u32[]{:S(2)}) collective-permute-start(bf16[128,4096]{1,0:T(8,128)(2,1)S(1)} %pad_maximum_fusion.1), channel_id=1, source_target_pairs={{0,4},{1,5},{2,6},{3,7},{4,8},{5,9},{6,10},{7,11},{8,12},{9,13},{1... | collective-permute-start | bytes 3145736 | tf_op jit(solution)/shard_map/ppermute | solution.py:36
  130.9 6.8 %collective-permute-done.18 = bf16[64,4096]{1,0:T(8,128)(2,1)S(1)} collective-permute-done((bf16[64,4096]{1,0:T(8,128)(2,1)S(1)}, bf16[64,4096]{1,0:T(8,128)(2,1)S(1)}, u32[]{:S(2)}, u32[]{:S(2)}) %collective-permute-start.18) | collective-permute-done | bytes 524320 | tf_op jit(solution)/shard_map/ppermute | solution.py:36
  138.2 0.7 slice-done
  139.0 2.6 %collective-permute-start.16 = (bf16[128,4096]{1,0:T(8,128)(2,1)S(1)}, bf16[128,4096]{1,0:T(8,128)(2,1)S(1)}, u32[]{:S(2)}, u32[]{:S(2)}) collective-permute-start(bf16[128,4096]{1,0:T(8,128)(2,1)S(1)} %pad_maximum_fusion.3), channel_id=1, source_target_pairs={{0,4},{1,5},{2,6},{3,7},{4,8},{5,9},{6,10},{7,11},{8,12},{9,13},{1... | collective-permute-start | bytes 3145736 | tf_op jit(solution)/shard_map/ppermute | solution.py:36
  142.0 12.1 %collective-permute-done.19 = bf16[128,4096]{1,0:T(8,128)(2,1)S(1)} collective-permute-done((bf16[128,4096]{1,0:T(8,128)(2,1)S(1)}, bf16[128,4096]{1,0:T(8,128)(2,1)S(1)}, u32[]{:S(2)}, u32[]{:S(2)}) %collective-permute-start.19) | collective-permute-done | bytes 1048608 | tf_op jit(solution)/shard_map/ppermute | solution.py:36
  154.1 2.4 %collective-permute-done.16 = bf16[128,4096]{1,0:T(8,128)(2,1)S(1)} collective-permute-done((bf16[128,4096]{1,0:T(8,128)(2,1)S(1)}, bf16[128,4096]{1,0:T(8,128)(2,1)S(1)}, u32[]{:S(2)}, u32[]{:S(2)}) %collective-permute-start.16) | collective-permute-done | bytes 1048608 | tf_op jit(solution)/shard_map/ppermute | solution.py:36
  156.5 0.8 add_convert_fusion
  157.3 1.6 collective-permute-start.22
  158.9 9.2 %collective-permute-done.8 = bf16[128,4096]{1,0:T(8,128)(2,1)S(1)} collective-permute-done((bf16[128,4096]{1,0:T(8,128)(2,1)S(1)}, bf16[128,4096]{1,0:T(8,128)(2,1)S(1)}, u32[]{:S(2)}, u32[]{:S(2)}) %collective-permute-start.8) | collective-permute-done | bytes 1048608 | tf_op jit(solution)/shard_map/ppermute | solution.py:36
  168.1 0.7 add_convert_fusion.1
  168.9 1.3 collective-permute-start.20
  170.3 2.1 %collective-permute-start.23 = (bf16[64,4096]{1,0:T(8,128)(2,1)S(1)}, bf16[64,4096]{1,0:T(8,128)(2,1)S(1)}, u32[]{:S(2)}, u32[]{:S(2)}) collective-permute-start(bf16[64,4096]{1,0:T(8,128)(2,1)S(1)} %pad_maximum_fusion.6), channel_id=1, source_target_pairs={{0,3},{1,0},{2,1},{3,2},{4,7},{5,4},{6,5},{7,6},{8,11},{9,8},{10,9... | collective-permute-start | bytes 1572872 | tf_op jit(solution)/shard_map/ppermute | solution.py:36
  172.4 4.2 %collective-permute-done.20 = bf16[32,4096]{1,0:T(8,128)(2,1)S(1)} collective-permute-done((bf16[32,4096]{1,0:T(8,128)(2,1)S(1)}, bf16[32,4096]{1,0:T(8,128)(2,1)S(1)}, u32[]{:S(2)}, u32[]{:S(2)}) %collective-permute-start.20) | collective-permute-done | bytes 262176 | tf_op jit(solution)/shard_map/ppermute | solution.py:36
  177.0 3.3 %collective-permute-done.23 = bf16[64,4096]{1,0:T(8,128)(2,1)S(1)} collective-permute-done((bf16[64,4096]{1,0:T(8,128)(2,1)S(1)}, bf16[64,4096]{1,0:T(8,128)(2,1)S(1)}, u32[]{:S(2)}, u32[]{:S(2)}) %collective-permute-start.23) | collective-permute-done | bytes 524320 | tf_op jit(solution)/shard_map/ppermute | solution.py:36
  180.3 6.9 %collective-permute-done.21 = bf16[64,4096]{1,0:T(8,128)(2,1)S(1)} collective-permute-done((bf16[64,4096]{1,0:T(8,128)(2,1)S(1)}, bf16[64,4096]{1,0:T(8,128)(2,1)S(1)}, u32[]{:S(2)}, u32[]{:S(2)}) %collective-permute-start.21) | collective-permute-done | bytes 524320 | tf_op jit(solution)/shard_map/ppermute | solution.py:36
  187.3 15.7 %all_to_all.28 = bf16[8,8,4096]{2,1,0:T(8,128)(2,1)S(1)} all-to-all(bf16[8,8,4096]{2,1,0:T(8,128)(2,1)S(1)} %fusion.78), channel_id=1, replica_groups=mesh['dp'=2,'tensor'=8,'expert'=16] {'tensor'}, dimensions={0} | all-to-all | bytes 1048576 | tf_op jit(solution)/shard_map/all_to_all | solution.py:18
  (135 shorter events, 17.9 us)
Async XLA Ops:
  0.0 103.7 %copy-start = (bf16[1,192,4096]{2,1,0:T(8,128)(2,1)S(1)}, bf16[1,192,4096]{2,1,0:T(8,128)(2,1)}, u32[]{:S(2)}) copy-start(bf16[1,192,4096]{2,1,0:T(8,128)(2,1)} %param.17) | copy-start | bytes 4718596
  0.0 12.6 %copy-start.18 = (s32[1,8,8]{2,1,0:T(8,128)S(1)}, s32[1,8,8]{2,1,0:T(8,128)}, u32[]{:S(2)}) copy-start(s32[1,8,8]{2,1,0:T(8,128)} %param.14) | copy-start | bytes 772
  0.0 12.7 %copy-start.19 = (s32[1,8,8]{2,1,0:T(8,128)S(1)}, s32[1,8,8]{2,1,0:T(8,128)}, u32[]{:S(2)}) copy-start(s32[1,8,8]{2,1,0:T(8,128)} %param.13) | copy-start | bytes 772
  4.0 26.2 %copy-start.16 = (bf16[1,8,4096]{2,1,0:T(8,128)(2,1)S(1)}, bf16[1,8,4096]{2,1,0:T(8,128)(2,1)}, u32[]{:S(2)}) copy-start(bf16[1,8,4096]{2,1,0:T(8,128)(2,1)} %param.11) | copy-start | bytes 196612
  4.0 26.3 %copy-start.17 = (f32[4096]{0:T(1024)S(1)}, f32[4096]{0:T(1024)}, u32[]{:S(2)}) copy-start(f32[4096]{0:T(1024)} %param.12) | copy-start | bytes 49156
  4.0 26.1 %all-to-all-start = ((bf16[8,8,4096]{2,1,0:T(8,128)(2,1)}), bf16[8,8,4096]{2,1,0:T(8,128)(2,1)S(1)}, u32[]{:S(2)}, u32[]{:S(2)}) async-start(bf16[8,8,4096]{2,1,0:T(8,128)(2,1)} %fusion.12), calls=%async_computation | async-start | bytes 1048576 | tf_op jit(solution)/shard_map/all_to_all | solution.py:18
  51.9 10.8 %collective-permute-start = (bf16[64,4224]{1,0:T(8,128)(2,1)}, bf16[64,4224]{1,0:T(8,128)(2,1)S(1)}, u32[]{:S(2)}, u32[]{:S(2)}) collective-permute-start(bf16[64,4224]{1,0:T(8,128)(2,1)} %bitcast.6), channel_id=1, source_target_pairs={{0,1},{1,2},{2,3},{3,0},{4,5},{5,6},{6,7},{7,4},{8,9},{9,10},{10,1... | collective-permute-start | bytes 1622024 | tf_op jit(solution)/shard_map/ppermute | solution.py:36
  53.4 14.6 %collective-permute-start.9 = (bf16[64,4224]{1,0:T(8,128)(2,1)}, bf16[64,4224]{1,0:T(8,128)(2,1)S(1)}, u32[]{:S(2)}, u32[]{:S(2)}) collective-permute-start(bf16[64,4224]{1,0:T(8,128)(2,1)} %bitcast.6), channel_id=1, source_target_pairs={{0,3},{1,0},{2,1},{3,2},{4,7},{5,4},{6,5},{7,6},{8,11},{9,8},{10,9... | collective-permute-start | bytes 1622024 | tf_op jit(solution)/shard_map/ppermute | solution.py:36
  64.6 6.6 %copy-start.1 = (bf16[1,192,4096]{2,1,0:T(8,128)(2,1)S(1)}, bf16[1,192,4096]{2,1,0:T(8,128)(2,1)}, u32[]{:S(2)}) copy-start(bf16[1,192,4096]{2,1,0:T(8,128)(2,1)} %param.15) | copy-start | bytes 4718596
  64.6 6.6 %copy-start.13 = (bf16[64,4224]{1,0:T(8,128)(2,1)S(1)}, bf16[64,4224]{1,0:T(8,128)(2,1)}, u32[]{:S(2)}) copy-start(bf16[64,4224]{1,0:T(8,128)(2,1)} %copy-done.12) | copy-start | bytes 1622020
  64.6 20.0 %collective-permute-start.1 = (bf16[128,4224]{1,0:T(8,128)(2,1)S(1)}, bf16[128,4224]{1,0:T(8,128)(2,1)S(1)}, u32[]{:S(2)}, u32[]{:S(2)}) collective-permute-start(bf16[128,4224]{1,0:T(8,128)(2,1)S(1)} %pad_maximum_fusion), channel_id=1, source_target_pairs={{0,12},{1,13},{2,14},{3,15},{4,0},{5,1},{6,2},{7,3},{8,4},{9,5},{1... | collective-permute-start | bytes 3244040 | tf_op jit(solution)/shard_map/ppermute | solution.py:36
  65.4 20.4 %collective-permute-start.2 = (bf16[128,4224]{1,0:T(8,128)(2,1)S(1)}, bf16[128,4224]{1,0:T(8,128)(2,1)S(1)}, u32[]{:S(2)}, u32[]{:S(2)}) collective-permute-start(bf16[128,4224]{1,0:T(8,128)(2,1)S(1)} %pad_maximum_fusion), channel_id=1, source_target_pairs={{0,4},{1,5},{2,6},{3,7},{4,8},{5,9},{6,10},{7,11},{8,12},{9,13},{1... | collective-permute-start | bytes 3244040 | tf_op jit(solution)/shard_map/ppermute | solution.py:36
  67.9 13.3 %collective-permute-start.11 = (bf16[32,4224]{1,0:T(8,128)(2,1)S(1)}, bf16[32,4224]{1,0:T(8,128)(2,1)S(1)}, u32[]{:S(2)}, u32[]{:S(2)}) collective-permute-start(bf16[32,4224]{1,0:T(8,128)(2,1)S(1)} %slice.195), channel_id=1, source_target_pairs={{0,3},{1,0},{2,1},{3,2},{4,7},{5,4},{6,5},{7,6},{8,11},{9,8},{10,9... | collective-permute-start | bytes 811016 | tf_op jit(solution)/shard_map/ppermute | solution.py:36
  70.5 10.7 %collective-permute-start.10 = (bf16[32,4224]{1,0:T(8,128)(2,1)S(1)}, bf16[32,4224]{1,0:T(8,128)(2,1)S(1)}, u32[]{:S(2)}, u32[]{:S(2)}) collective-permute-start(bf16[32,4224]{1,0:T(8,128)(2,1)S(1)} %slice.194), channel_id=1, source_target_pairs={{0,1},{1,2},{2,3},{3,0},{4,5},{5,6},{6,7},{7,4},{8,9},{9,10},{10,1... | collective-permute-start | bytes 811016 | tf_op jit(solution)/shard_map/ppermute | solution.py:36
  71.2 1.7 copy-start.2
  81.3 15.2 %collective-permute-start.13 = (bf16[128,4224]{1,0:T(8,128)(2,1)S(1)}, bf16[128,4224]{1,0:T(8,128)(2,1)S(1)}, u32[]{:S(2)}, u32[]{:S(2)}) collective-permute-start(bf16[128,4224]{1,0:T(8,128)(2,1)S(1)} %constant_dynamic-update-slice_fusion), channel_id=1, source_target_pairs={{0,4},{1,5},{2,6},{3,7},{4,8},{5,9},{6,10},{7,11},{8,12},{9,13},{1... | collective-permute-start | bytes 3244040 | tf_op jit(solution)/shard_map/ppermute | solution.py:36
  81.4 19.4 %collective-permute-start.12 = (bf16[128,4224]{1,0:T(8,128)(2,1)S(1)}, bf16[128,4224]{1,0:T(8,128)(2,1)S(1)}, u32[]{:S(2)}, u32[]{:S(2)}) collective-permute-start(bf16[128,4224]{1,0:T(8,128)(2,1)S(1)} %constant_dynamic-update-slice_fusion), channel_id=1, source_target_pairs={{0,12},{1,13},{2,14},{3,15},{4,0},{5,1},{6,2},{7,3},{8,4},{9,5},{1... | collective-permute-start | bytes 3244040 | tf_op jit(solution)/shard_map/ppermute | solution.py:36
  85.8 21.4 %collective-permute-start.6 = (bf16[64,4224]{1,0:T(8,128)(2,1)S(1)}, bf16[64,4224]{1,0:T(8,128)(2,1)S(1)}, u32[]{:S(2)}, u32[]{:S(2)}) collective-permute-start(bf16[64,4224]{1,0:T(8,128)(2,1)S(1)} %slice.190), channel_id=1, source_target_pairs={{0,12},{1,13},{2,14},{3,15},{4,0},{5,1},{6,2},{7,3},{8,4},{9,5},{1... | collective-permute-start | bytes 1622024 | tf_op jit(solution)/shard_map/ppermute | solution.py:36
  87.1 21.7 %collective-permute-start.3 = (bf16[64,4224]{1,0:T(8,128)(2,1)S(1)}, bf16[64,4224]{1,0:T(8,128)(2,1)S(1)}, u32[]{:S(2)}, u32[]{:S(2)}) collective-permute-start(bf16[64,4224]{1,0:T(8,128)(2,1)S(1)} %slice.182), channel_id=1, source_target_pairs={{0,4},{1,5},{2,6},{3,7},{4,8},{5,9},{6,10},{7,11},{8,12},{9,13},{1... | collective-permute-start | bytes 1622024 | tf_op jit(solution)/shard_map/ppermute | solution.py:36
  98.6 18.0 %collective-permute-start.14 = (bf16[64,4224]{1,0:T(8,128)(2,1)}, bf16[64,4224]{1,0:T(8,128)(2,1)}, u32[]{:S(2)}, u32[]{:S(2)}) collective-permute-start(bf16[64,4224]{1,0:T(8,128)(2,1)} %slice.201), channel_id=1, source_target_pairs={{0,4},{1,5},{2,6},{3,7},{4,8},{5,9},{6,10},{7,11},{8,12},{9,13},{1... | collective-permute-start | bytes 1622024 | tf_op jit(solution)/shard_map/ppermute | solution.py:36
  102.8 17.1 %collective-permute-start.17 = (bf16[64,4224]{1,0:T(8,128)(2,1)}, bf16[64,4224]{1,0:T(8,128)(2,1)}, u32[]{:S(2)}, u32[]{:S(2)}) collective-permute-start(bf16[64,4224]{1,0:T(8,128)(2,1)} %slice.209), channel_id=1, source_target_pairs={{0,12},{1,13},{2,14},{3,15},{4,0},{5,1},{6,2},{7,3},{8,4},{9,5},{1... | collective-permute-start | bytes 1622024 | tf_op jit(solution)/shard_map/ppermute | solution.py:36
  104.2 1.0 copy-start.4
  105.2 1.0 copy-start.8
  106.2 1.0 copy-start.6
  107.2 1.0 copy-start.10
  108.8 0.8 copy-start.14
  109.8 1.8 copy-start.3
  109.8 1.8 copy-start.15
  112.7 28.9 %collective-permute-start.7 = (bf16[64,4096]{1,0:T(8,128)(2,1)S(1)}, bf16[64,4096]{1,0:T(8,128)(2,1)S(1)}, u32[]{:S(2)}, u32[]{:S(2)}) collective-permute-start(bf16[64,4096]{1,0:T(8,128)(2,1)S(1)} %fusion.9), channel_id=1, source_target_pairs={{0,12},{1,13},{2,14},{3,15},{4,0},{5,1},{6,2},{7,3},{8,4},{9,5},{1... | collective-permute-start | bytes 1572872 | tf_op jit(solution)/shard_map/ppermute | solution.py:36
  113.2 14.1 %collective-permute-start.4 = (bf16[64,4096]{1,0:T(8,128)(2,1)S(1)}, bf16[64,4096]{1,0:T(8,128)(2,1)S(1)}, u32[]{:S(2)}, u32[]{:S(2)}) collective-permute-start(bf16[64,4096]{1,0:T(8,128)(2,1)S(1)} %fusion.8), channel_id=1, source_target_pairs={{0,4},{1,5},{2,6},{3,7},{4,8},{5,9},{6,10},{7,11},{8,12},{9,13},{1... | collective-permute-start | bytes 1572872 | tf_op jit(solution)/shard_map/ppermute | solution.py:36
  124.5 2.9 %copy-start.11 = (bf16[128,4096]{1,0:T(8,128)(2,1)S(1)}, bf16[128,4096]{1,0:T(8,128)(2,1)}, u32[]{:S(2)}) copy-start(bf16[128,4096]{1,0:T(8,128)(2,1)} %copy-done.10) | copy-start | bytes 3145732
  124.5 13.5 %collective-permute-start.15 = (bf16[64,4096]{1,0:T(8,128)(2,1)S(1)}, bf16[64,4096]{1,0:T(8,128)(2,1)S(1)}, u32[]{:S(2)}, u32[]{:S(2)}) collective-permute-start(bf16[64,4096]{1,0:T(8,128)(2,1)S(1)} %fusion.10), channel_id=1, source_target_pairs={{0,4},{1,5},{2,6},{3,7},{4,8},{5,9},{6,10},{7,11},{8,12},{9,13},{1... | collective-permute-start | bytes 1572872 | tf_op jit(solution)/shard_map/ppermute | solution.py:36
  126.8 1.0 slice-start.3
  127.3 10.5 %copy-start.9 = (bf16[128,4096]{1,0:T(8,128)(2,1)S(1)}, bf16[128,4096]{1,0:T(8,128)(2,1)}, u32[]{:S(2)}) copy-start(bf16[128,4096]{1,0:T(8,128)(2,1)} %copy-done.8) | copy-start | bytes 3145732
  127.3 10.5 %collective-permute-start.18 = (bf16[64,4096]{1,0:T(8,128)(2,1)S(1)}, bf16[64,4096]{1,0:T(8,128)(2,1)S(1)}, u32[]{:S(2)}, u32[]{:S(2)}) collective-permute-start(bf16[64,4096]{1,0:T(8,128)(2,1)S(1)} %fusion.11), channel_id=1, source_target_pairs={{0,12},{1,13},{2,14},{3,15},{4,0},{5,1},{6,2},{7,3},{8,4},{9,5},{1... | collective-permute-start | bytes 1572872 | tf_op jit(solution)/shard_map/ppermute | solution.py:36
  127.9 10.0 %slice-start.2 = ((bf16[128,4096]{1,0:T(8,128)(2,1)}), bf16[64,4096]{1,0:T(8,128)(2,1)S(1)}, s32[]{:S(2)}) async-start(bf16[128,4096]{1,0:T(8,128)(2,1)} %copy-done.8), calls=%async_computation.5 | async-start | bytes 1048576 | tf_op jit(solution)/shard_map/slice | solution.py:59
  128.0 10.1 %copy-start.5 = (bf16[128,4096]{1,0:T(8,128)(2,1)S(1)}, bf16[128,4096]{1,0:T(8,128)(2,1)}, u32[]{:S(2)}) copy-start(bf16[128,4096]{1,0:T(8,128)(2,1)} %copy-done.4) | copy-start | bytes 3145732
  128.0 30.9 %collective-permute-start.5 = (bf16[128,4096]{1,0:T(8,128)(2,1)S(1)}, bf16[128,4096]{1,0:T(8,128)(2,1)S(1)}, u32[]{:S(2)}, u32[]{:S(2)}) collective-permute-start(bf16[128,4096]{1,0:T(8,128)(2,1)S(1)} %pad_maximum_fusion.1), channel_id=1, source_target_pairs={{0,4},{1,5},{2,6},{3,7},{4,8},{5,9},{6,10},{7,11},{8,12},{9,13},{1... | collective-permute-start | bytes 3145736 | tf_op jit(solution)/shard_map/ppermute | solution.py:36
  137.9 1.0 slice-start
  138.0 3.7 %copy-start.7 = (bf16[128,4096]{1,0:T(8,128)(2,1)S(1)}, bf16[128,4096]{1,0:T(8,128)(2,1)}, u32[]{:S(2)}) copy-start(bf16[128,4096]{1,0:T(8,128)(2,1)} %copy-done.6) | copy-start | bytes 3145732
  138.0 16.1 %collective-permute-start.19 = (bf16[128,4096]{1,0:T(8,128)(2,1)S(1)}, bf16[128,4096]{1,0:T(8,128)(2,1)S(1)}, u32[]{:S(2)}, u32[]{:S(2)}) collective-permute-start(bf16[128,4096]{1,0:T(8,128)(2,1)S(1)} %pad_maximum_fusion.4), channel_id=1, source_target_pairs={{0,12},{1,13},{2,14},{3,15},{4,0},{5,1},{6,2},{7,3},{8,4},{9,5},{1... | collective-permute-start | bytes 3145736 | tf_op jit(solution)/shard_map/ppermute | solution.py:36
  138.9 2.8 %slice-start.1 = ((bf16[128,4096]{1,0:T(8,128)(2,1)}), bf16[64,4096]{1,0:T(8,128)(2,1)S(1)}, s32[]{:S(2)}) async-start(bf16[128,4096]{1,0:T(8,128)(2,1)} %copy-done.6), calls=%async_computation.4 | async-start | bytes 1048576 | tf_op jit(solution)/shard_map/slice | solution.py:59
  139.0 17.5 %collective-permute-start.16 = (bf16[128,4096]{1,0:T(8,128)(2,1)S(1)}, bf16[128,4096]{1,0:T(8,128)(2,1)S(1)}, u32[]{:S(2)}, u32[]{:S(2)}) collective-permute-start(bf16[128,4096]{1,0:T(8,128)(2,1)S(1)} %pad_maximum_fusion.3), channel_id=1, source_target_pairs={{0,4},{1,5},{2,6},{3,7},{4,8},{5,9},{6,10},{7,11},{8,12},{9,13},{1... | collective-permute-start | bytes 3145736 | tf_op jit(solution)/shard_map/ppermute | solution.py:36
  141.9 26.2 %collective-permute-start.8 = (bf16[128,4096]{1,0:T(8,128)(2,1)S(1)}, bf16[128,4096]{1,0:T(8,128)(2,1)S(1)}, u32[]{:S(2)}, u32[]{:S(2)}) collective-permute-start(bf16[128,4096]{1,0:T(8,128)(2,1)S(1)} %pad_maximum_fusion.2), channel_id=1, source_target_pairs={{0,12},{1,13},{2,14},{3,15},{4,0},{5,1},{6,2},{7,3},{8,4},{9,5},{1... | collective-permute-start | bytes 3145736 | tf_op jit(solution)/shard_map/ppermute | solution.py:36
  157.3 12.9 %collective-permute-start.22 = (bf16[32,4096]{1,0:T(8,128)(2,1)S(1)}, bf16[32,4096]{1,0:T(8,128)(2,1)S(1)}, u32[]{:S(2)}, u32[]{:S(2)}) collective-permute-start(bf16[32,4096]{1,0:T(8,128)(2,1)S(1)} %get-tuple-element.40), channel_id=1, source_target_pairs={{0,3},{1,0},{2,1},{3,2},{4,7},{5,4},{6,5},{7,6},{8,11},{9,8},{10,9... | collective-permute-start | bytes 786440 | tf_op jit(solution)/shard_map/ppermute | solution.py:36
  168.9 7.7 %collective-permute-start.20 = (bf16[32,4096]{1,0:T(8,128)(2,1)S(1)}, bf16[32,4096]{1,0:T(8,128)(2,1)S(1)}, u32[]{:S(2)}, u32[]{:S(2)}) collective-permute-start(bf16[32,4096]{1,0:T(8,128)(2,1)S(1)} %get-tuple-element.39), channel_id=1, source_target_pairs={{0,1},{1,2},{2,3},{3,0},{4,5},{5,6},{6,7},{7,4},{8,9},{9,10},{10,1... | collective-permute-start | bytes 786440 | tf_op jit(solution)/shard_map/ppermute | solution.py:36
  170.3 9.9 %collective-permute-start.23 = (bf16[64,4096]{1,0:T(8,128)(2,1)S(1)}, bf16[64,4096]{1,0:T(8,128)(2,1)S(1)}, u32[]{:S(2)}, u32[]{:S(2)}) collective-permute-start(bf16[64,4096]{1,0:T(8,128)(2,1)S(1)} %pad_maximum_fusion.6), channel_id=1, source_target_pairs={{0,3},{1,0},{2,1},{3,2},{4,7},{5,4},{6,5},{7,6},{8,11},{9,8},{10,9... | collective-permute-start | bytes 1572872 | tf_op jit(solution)/shard_map/ppermute | solution.py:36
  176.7 10.5 %collective-permute-start.21 = (bf16[64,4096]{1,0:T(8,128)(2,1)S(1)}, bf16[64,4096]{1,0:T(8,128)(2,1)S(1)}, u32[]{:S(2)}, u32[]{:S(2)}) collective-permute-start(bf16[64,4096]{1,0:T(8,128)(2,1)S(1)} %pad_maximum_fusion.5), channel_id=1, source_target_pairs={{0,1},{1,2},{2,3},{3,0},{4,5},{5,6},{6,7},{7,4},{8,9},{9,10},{10,1... | collective-permute-start | bytes 1572872 | tf_op jit(solution)/shard_map/ppermute | solution.py:36
  (1 other events, 0.8 us)

commit v5 on v4

--- a/solution.py
+++ b/solution.py
@@ -1,11 +1,16 @@
+import functools
+
 import jax
 import jax.numpy as jnp
 from jax import lax
+from jax.experimental import pallas as pl
+from jax.experimental.pallas import tpu as pltpu
 from jax.sharding import PartitionSpec as P
 
 EXPERTS = 16
 SIDE = 4
 LANES = 128
+CHUNK = 1024
 
 
 def normalize(hidden, norm_gain):
@@ -60,6 +65,47 @@
     return add(own, shift(front, turn, 1), shift(back, turn, -1))
 
 
+def expert_kernel(count, me_ref, *refs):
+    blocks, (gate_ref, up_ref, down_ref), outs = refs[:count], refs[count : count + 3], refs[count + 3 :]
+    width = gate_ref.shape[1]
+    x = jnp.concatenate([block[:, :width] for block in blocks])
+    tail = jnp.concatenate([block[:, width:] for block in blocks]).astype(jnp.float32)
+    lane = lax.broadcasted_iota(jnp.int32, tail.shape, 1)
+    code = jnp.sum(jnp.where(lane == me_ref[0], tail, 0.0), axis=1, keepdims=True)
+    total = jnp.sum(jnp.where(lane == EXPERTS, tail, 0.0), axis=1, keepdims=True)
+    both_last = (((1,), (1,)), ((), ()))
+    gate_value = lax.dot_general(x, gate_ref[...], both_last, preferred_element_type=jnp.float32)
+    up_value = lax.dot_general(x, up_ref[...], both_last, preferred_element_type=jnp.float32)
+    activated = (jax.nn.silu(gate_value) * up_value).astype(jnp.bfloat16)
+    scale = code / total
+    size = outs[0].shape[0]
+    for start in range(0, width, CHUNK):
+        down = jnp.dot(
+            activated, down_ref[:, start : start + CHUNK], preferred_element_type=jnp.float32
+        )
+        result = (down * scale).astype(jnp.bfloat16)
+        for i, out in enumerate(outs):
+            out[:, start : start + CHUNK] = result[i * size : (i + 1) * size]
+
+
+def run_expert(me, blocks, w_gate, w_up, w_down):
+    count, size = len(blocks), blocks[0].shape[0]
+    units, width = w_gate.shape
+    vmem = pl.BlockSpec(memory_space=pltpu.VMEM)
+    return pl.pallas_call(
+        functools.partial(expert_kernel, count),
+        out_shape=[jax.ShapeDtypeStruct((size, width), jnp.bfloat16)] * count,
+        in_specs=[pl.BlockSpec(memory_space=pltpu.SMEM)] + [vmem] * (count + 3),
+        out_specs=[vmem] * count,
+        compiler_params=pltpu.CompilerParams(vmem_limit_bytes=20 << 20),
+        cost_estimate=pl.CostEstimate(
+            flops=6 * count * size * units * width,
+            bytes_accessed=4 * count * size * width + 6 * units * width,
+            transcendentals=count * size * units,
+        ),
+    )(me, *blocks, w_gate, w_up, w_down)
+
+
 def on_device(
     attn_heads, out_proj, residual, norm_gain, expert_ids, weight_codes, w_gate, w_up, w_down
 ):
@@ -83,32 +129,37 @@
         jnp.tile(rows, (tensor_count, 1)), "tensor", split_axis=0, concat_axis=0, tiled=True
     )
 
-    def expert(rows, who):
-        x = rows[:, :model_width]
-        tail = rows[:, model_width:].astype(jnp.float32)
-        code = jnp.sum(jnp.where(lane == who, tail, 0.0), axis=1, keepdims=True)
-        total = jnp.sum(jnp.where(lane == EXPERTS, tail, 0.0), axis=1, keepdims=True)
-        gate_value = jnp.einsum("rd,fd->rf", x, w_gate[0], preferred_element_type=jnp.float32)
-        up_value = jnp.einsum("rd,fd->rf", x, w_up[0], preferred_element_type=jnp.float32)
-        activated = (jax.nn.silu(gate_value) * up_value).astype(jnp.bfloat16)
-        activated = lax.optimization_barrier(activated)
-        scale = code / total
-        down = jnp.dot(activated, w_down[0], preferred_element_type=jnp.float32)
-        return (down * scale).astype(jnp.bfloat16), scale
+    weights = (w_gate[0], w_up[0], w_down[0])
+    who = jnp.reshape(me, (1,)).astype(jnp.int32)
 
-    def pieces(block):
-        back, front = send_round(block, 1)
-        return (block, back, front, *send_on(back, front, 1))
+    def experts(*blocks):
+        return run_expert(who, blocks, *weights)
+
+    def tie(values, others):
+        tied = lax.optimization_barrier((*values, *others))
+        return tied[: len(values)], tied[len(values) :]
 
     back, front = send_round(group, 0)
+    first = jnp.concatenate([group, back])
+    first_near = send_round(first, 1)
     far = send_on(back, front, 0)
-    first = pieces(jnp.concatenate([group, back]))
-    second = pieces(jnp.concatenate([front, *far]))
-    first_out = [expert(block, me) for block in first]
-    late = me + (first_out[4][1][0, 0] < 0.0).astype(jnp.int32)
-    second_out = [expert(block, who) for block, who in zip(second, (me, me, me, late, late))]
-    first_sum = collect(*(out for out, _ in first_out), 1).astype(jnp.bfloat16)
-    second_sum = collect(*(out for out, _ in second_out), 1).astype(jnp.bfloat16)
+    first_own = experts(first)
+    second = jnp.concatenate([front, *far])
+    (second,), first_own = tie((second,), first_own)
+    second_near = send_round(second, 1)
+    second_own = experts(second)
+    first_near, second_own = tie(first_near, second_own)
+    first_far = send_on(*first_near, 1)
+    first_near_out = experts(*first_near)
+    second_near, first_near_out = tie(second_near, first_near_out)
+    second_far = send_on(*second_near, 1)
+    first_far_out = experts(*first_far)
+    second_near, first_far_out = tie(second_near, first_far_out)
+    second_near_out = experts(*second_near)
+    second_far, second_near_out = tie(second_far, second_near_out)
+    second_far_out = experts(*second_far)
+    first_sum = collect(*first_own, *first_near_out, *first_far_out, 1).astype(jnp.bfloat16)
+    second_sum = collect(*second_own, *second_near_out, *second_far_out, 1).astype(jnp.bfloat16)
     half = tokens // 2
     mixed = collect(
         first_sum[:tokens],

time: 205 us -> 187 us (0.912)
  matrix products: 28.4 us -> 3.84 us
  Pallas kernels: 0 us -> 9.91 us
  starting transfers between devices: 42 us -> 36.6 us
  waiting for transfers between devices: 82.3 us -> 87.2 us
  local copies, waits for them, and re-layouts: 7.65 us -> 4.6 us
    dot_general x30 -> x0, matrix products: 24.4 us -> none  [the longest x10 10.3 us: expert(): jnp.einsum('rd,fd->rf', x, w_gate[0], preferred_element_type=jnp.float32)]
    pallas_call x0 -> x6, Pallas kernels: none -> 9.91 us  [run_expert(): pl.pallas_call(functools.partial(expert_kernel, count), out_shape=[jax.Sh...]
    ppermute x24, starting transfers between devices: 33.4 us -> 28.1 us  [shift(): return lax.ppermute(value, ('dp', 'expert'), pairs)]
    ppermute x24, waiting for transfers between devices: 65.1 us -> 70 us  [shift(): return lax.ppermute(value, ('dp', 'expert'), pairs)]
  transfers between devices with their start and end apart: 25 -> 25, of which waited for: 11 -> 17; matrix products, arithmetic and copies ran while one was open for 16% -> 4% of each run, Pallas kernels for 0% -> 5%
where the time goes in v5:
time: 187 us
  waiting for transfers between devices  87.2 us (47%)
  blocking collectives  38.3 us (20%)
  starting transfers between devices  36.6 us (20%)
  Pallas kernels  9.91 us (5%)
  other arithmetic  5.89 us (3%)
  local copies, waits for them, and re-layouts  4.6 us (2%)
  matrix products  3.84 us (2%)
    ppermute x24, waiting for transfers between devices, shift(): return lax.ppermute(value, ('dp', 'expert'), pairs)  70 us
    ppermute x24, starting transfers between devices, shift(): return lax.ppermute(value, ('dp', 'expert'), pairs)  28.1 us
    all_to_all x1, blocking collectives, on_device(): lax.all_to_all(jnp.tile(rows, (tensor_count, 1)), 'tensor', split_axis=0,...  21.6 us
    all_to_all x1, waiting for transfers between devices, reduce_over_tensor(): lax.all_to_all(partial.astype(jnp.bfloat16), 'tensor', split_axis=0, conc...  17.2 us
    all_to_all x1, blocking collectives, reduce_over_tensor(): lax.all_to_all(partial.astype(jnp.bfloat16), 'tensor', split_axis=0, conc...  16.6 us
    pallas_call x6, Pallas kernels, run_expert(): pl.pallas_call(functools.partial(expert_kernel, count), out_shape=[jax.Sh...  9.91 us
    all_to_all x1, starting transfers between devices, reduce_over_tensor(): lax.all_to_all(partial.astype(jnp.bfloat16), 'tensor', split_axis=0, conc...  8.47 us
    dot_general x1, matrix products, on_device(): jnp.dot(attn_heads[0], out_proj, preferred_element_type=jnp.float32)  3.84 us
  transfers between devices with their start and end apart: 25, of which 17 were waited for; matrix products, arithmetic and copies ran while one was open for 4% of the time, Pallas kernels for 5%

profile of v5, /device:TPU:24, one launch (start us, length us, event | category | flops | bytes accessed | tf_op | source)
XLA Modules:
  0.0 186.7 jit_solution(13311967969919037432)
XLA Ops:
  0.0 0.8 copy-done
  0.8 3.8 %fusion = bf16[8,8,4096]{2,1,0:T(8,128)(2,1)} fusion(bf16[512,4096]{1,0:T(8,128)(2,1)} %param.10, bf16[1,64,512]{2,1,0:T(8,128)(2,1)S(1)} %copy-done), kind=kOutput, calls=%fused_computation.1 | convolution fusion | flops 268697600 | bytes 4784128 | tf_op jit(solution)/shard_map/dot_general | solution.py:124
  4.7 8.5 %all-to-all-start = ((bf16[8,8,4096]{2,1,0:T(8,128)(2,1)}), bf16[8,8,4096]{2,1,0:T(8,128)(2,1)S(1)}, u32[]{:S(2)}, u32[]{:S(2)}) async-start(bf16[8,8,4096]{2,1,0:T(8,128)(2,1)} %fusion), calls=%async_computation | async-start | bytes 1048576 | tf_op jit(solution)/shard_map/all_to_all | solution.py:23
  13.5 17.2 %all-to-all-done = bf16[8,8,4096]{2,1,0:T(8,128)(2,1)S(1)} async-done(((bf16[8,8,4096]{2,1,0:T(8,128)(2,1)}), bf16[8,8,4096]{2,1,0:T(8,128)(2,1)S(1)}, u32[]{:S(2)}, u32[]{:S(2)}) %all-to-all-start) | async-done | bytes 524320 | tf_op jit(solution)/shard_map/all_to_all | solution.py:23
  31.1 21.6 %all_to_all.27 = bf16[8,8,4224]{2,1,0:T(8,128)(2,1)} all-to-all(bf16[8,8,4224]{2,1,0:T(8,128)(2,1)S(1)} %tile.2), channel_id=1, replica_groups=mesh['dp'=2,'tensor'=8,'expert'=16] {'tensor'}, dimensions={0} | all-to-all | bytes 1081344 | tf_op jit(solution)/shard_map/all_to_all | solution.py:128
  52.7 1.5 collective-permute-start.1
  54.2 1.7 collective-permute-start
  55.9 7.6 %collective-permute-done.1 = bf16[64,4224]{1,0:T(8,128)(2,1)} collective-permute-done((bf16[64,4224]{1,0:T(8,128)(2,1)}, bf16[64,4224]{1,0:T(8,128)(2,1)}, u32[]{:S(2)}, u32[]{:S(2)}) %collective-permute-start.1) | collective-permute-done | bytes 540704 | tf_op jit(solution)/shard_map/ppermute | solution.py:41
  63.6 1.0 slice.90
  64.9 1.0 slice.91
  65.9 3.0 %collective-permute-start.3 = (bf16[32,4224]{1,0:T(8,128)(2,1)S(1)}, bf16[32,4224]{1,0:T(8,128)(2,1)S(1)}, u32[]{:S(2)}, u32[]{:S(2)}) collective-permute-start(bf16[32,4224]{1,0:T(8,128)(2,1)S(1)} %slice.91), channel_id=1, source_target_pairs={{0,3},{1,0},{2,1},{3,2},{4,7},{5,4},{6,5},{7,6},{8,11},{9,8},{10,9... | collective-permute-start | bytes 811016 | tf_op jit(solution)/shard_map/ppermute | solution.py:41
  68.9 1.3 pad_maximum_fusion.1.refs_0_
  70.5 1.8 collective-permute-start.7
  72.3 1.4 copy-done.3
  73.7 1.5 shard_map.91
  75.3 0.5 collective-permute-done.3
  75.8 1.1 pad_maximum_fusion.refs_0_
  76.9 1.0 collective-permute-start.4
  77.9 1.1 collective-permute-start.5
  79.0 1.5 shard_map.92
  80.5 4.9 %collective-permute-done.6.refs_0_ = bf16[128,4224]{1,0:T(8,128)(2,1)S(1)} collective-permute-done((bf16[128,4224]{1,0:T(8,128)(2,1)S(1)}, bf16[128,4224]{1,0:T(8,128)(2,1)S(1)}, u32[]{:S(2)}, u32[]{:S(2)}) %collective-permute-start.6) | collective-permute-done | bytes 1081376 | tf_op jit(solution)/shard_map/ppermute | solution.py:41
  85.4 1.4 collective-permute-done.7.refs_1_
  87.4 1.9 %collective-permute-start.9 = (bf16[64,4224]{1,0:T(8,128)(2,1)S(1)}, bf16[64,4224]{1,0:T(8,128)(2,1)S(1)}, u32[]{:S(2)}, u32[]{:S(2)}) collective-permute-start(bf16[64,4224]{1,0:T(8,128)(2,1)S(1)} %slice.73), channel_id=1, source_target_pairs={{0,12},{1,13},{2,14},{3,15},{4,0},{5,1},{6,2},{7,3},{8,4},{9,5},{1... | collective-permute-start | bytes 1622024 | tf_op jit(solution)/shard_map/ppermute | solution.py:41
  89.3 1.9 %shard_map.93 = (bf16[128,4096]{1,0:T(8,128)(2,1)S(1)}, bf16[128,4096]{1,0:T(8,128)(2,1)S(1)}) custom-call(s32[1]{0:T(128)} %bitcast.7.me_ref, bf16[128,4224]{1,0:T(8,128)(2,1)S(1)} %collective-permute-done.6.refs_0_, bf16[128,4224]{1,0:T(8,128)(2,1)S(1)} %collective-permute-done.7.refs_1_, bf16[192,4096]{1,0:T(8,128)(2,1)S(1)} %bitcast.29, ...), custom_call_target="tpu_custom_call" | custom-call | flops 1207959552 | bytes 8912896 | tf_op jit(solution)/shard_map/pallas_call | solution.py:95
  91.3 5.8 %collective-permute-done.4.refs_0_ = bf16[128,4224]{1,0:T(8,128)(2,1)S(1)} collective-permute-done((bf16[128,4224]{1,0:T(8,128)(2,1)S(1)}, bf16[128,4224]{1,0:T(8,128)(2,1)S(1)}, u32[]{:S(2)}, u32[]{:S(2)}) %collective-permute-start.4) | collective-permute-done | bytes 1081376 | tf_op jit(solution)/shard_map/ppermute | solution.py:41
  97.0 1.4 collective-permute-done.5.refs_1_
  99.0 1.7 collective-permute-start.15
  100.7 2.1 %collective-permute-done.8.refs_0_ = bf16[64,4224]{1,0:T(8,128)(2,1)S(1)} collective-permute-done((bf16[64,4224]{1,0:T(8,128)(2,1)S(1)}, bf16[64,4224]{1,0:T(8,128)(2,1)S(1)}, u32[]{:S(2)}, u32[]{:S(2)}) %collective-permute-start.8) | collective-permute-done | bytes 540704 | tf_op jit(solution)/shard_map/ppermute | solution.py:41
  102.8 1.4 collective-permute-done.9.refs_1_
  104.3 1.5 shard_map.94
  106.3 1.7 collective-permute-start.12
  108.1 1.9 %shard_map.95 = (bf16[128,4096]{1,0:T(8,128)(2,1)S(1)}, bf16[128,4096]{1,0:T(8,128)(2,1)S(1)}) custom-call(s32[1]{0:T(128)} %bitcast.7.me_ref, bf16[128,4224]{1,0:T(8,128)(2,1)S(1)} %collective-permute-done.4.refs_0_, bf16[128,4224]{1,0:T(8,128)(2,1)S(1)} %collective-permute-done.5.refs_1_, bf16[192,4096]{1,0:T(8,128)(2,1)S(1)} %bitcast.31, ...), custom_call_target="tpu_custom_call" | custom-call | flops 1207959552 | bytes 8912896 | tf_op jit(solution)/shard_map/pallas_call | solution.py:95
  110.1 1.5 shard_map.96
  111.6 1.6 collective-permute-start.16
  113.2 0.6 collective-permute-start.18
  113.8 1.2 collective-permute-done.10
  115.3 1.6 collective-permute-start.11
  116.9 3.9 %collective-permute-done.16 = bf16[64,4096]{1,0:T(8,128)(2,1)S(1)} collective-permute-done((bf16[64,4096]{1,0:T(8,128)(2,1)S(1)}, bf16[64,4096]{1,0:T(8,128)(2,1)S(1)}, u32[]{:S(2)}, u32[]{:S(2)}) %collective-permute-start.16) | collective-permute-done | bytes 524320 | tf_op jit(solution)/shard_map/ppermute | solution.py:41
  121.1 3.0 %collective-permute-start.17 = (bf16[128,4096]{1,0:T(8,128)(2,1)S(1)}, bf16[128,4096]{1,0:T(8,128)(2,1)S(1)}, u32[]{:S(2)}, u32[]{:S(2)}) collective-permute-start(bf16[128,4096]{1,0:T(8,128)(2,1)S(1)} %pad_maximum_fusion.4), channel_id=1, source_target_pairs={{0,4},{1,5},{2,6},{3,7},{4,8},{5,9},{6,10},{7,11},{8,12},{9,13},{1... | collective-permute-start | bytes 3145736 | tf_op jit(solution)/shard_map/ppermute | solution.py:41
  124.7 18.6 %collective-permute-done.17 = bf16[128,4096]{1,0:T(8,128)(2,1)S(1)} collective-permute-done((bf16[128,4096]{1,0:T(8,128)(2,1)S(1)}, bf16[128,4096]{1,0:T(8,128)(2,1)S(1)}, u32[]{:S(2)}, u32[]{:S(2)}) %collective-permute-start.17) | collective-permute-done | bytes 1048608 | tf_op jit(solution)/shard_map/ppermute | solution.py:41
  144.0 8.8 %collective-permute-done.13 = bf16[128,4096]{1,0:T(8,128)(2,1)S(1)} collective-permute-done((bf16[128,4096]{1,0:T(8,128)(2,1)S(1)}, bf16[128,4096]{1,0:T(8,128)(2,1)S(1)}, u32[]{:S(2)}, u32[]{:S(2)}) %collective-permute-start.13) | collective-permute-done | bytes 1048608 | tf_op jit(solution)/shard_map/ppermute | solution.py:41
  153.5 2.1 %collective-permute-start.21 = (bf16[64,4096]{1,0:T(8,128)(2,1)S(1)}, bf16[64,4096]{1,0:T(8,128)(2,1)S(1)}, u32[]{:S(2)}, u32[]{:S(2)}) collective-permute-start(bf16[64,4096]{1,0:T(8,128)(2,1)S(1)} %pad_maximum_fusion.6), channel_id=1, source_target_pairs={{0,1},{1,2},{2,3},{3,0},{4,5},{5,6},{6,7},{7,4},{8,9},{9,10},{10,1... | collective-permute-start | bytes 1572872 | tf_op jit(solution)/shard_map/ppermute | solution.py:41
  155.6 4.2 %collective-permute-done.22 = bf16[32,4096]{1,0:T(8,128)(2,1)S(1)} collective-permute-done((bf16[32,4096]{1,0:T(8,128)(2,1)S(1)}, bf16[32,4096]{1,0:T(8,128)(2,1)S(1)}, u32[]{:S(2)}, u32[]{:S(2)}) %collective-permute-start.22) | collective-permute-done | bytes 262176 | tf_op jit(solution)/shard_map/ppermute | solution.py:41
  159.8 1.3 collective-permute-start.23
  161.1 2.8 %collective-permute-done.21 = bf16[64,4096]{1,0:T(8,128)(2,1)S(1)} collective-permute-done((bf16[64,4096]{1,0:T(8,128)(2,1)S(1)}, bf16[64,4096]{1,0:T(8,128)(2,1)S(1)}, u32[]{:S(2)}, u32[]{:S(2)}) %collective-permute-start.21) | collective-permute-done | bytes 524320 | tf_op jit(solution)/shard_map/ppermute | solution.py:41
  164.0 5.1 %collective-permute-done.23 = bf16[64,4096]{1,0:T(8,128)(2,1)S(1)} collective-permute-done((bf16[64,4096]{1,0:T(8,128)(2,1)S(1)}, bf16[64,4096]{1,0:T(8,128)(2,1)S(1)}, u32[]{:S(2)}, u32[]{:S(2)}) %collective-permute-start.23) | collective-permute-done | bytes 524320 | tf_op jit(solution)/shard_map/ppermute | solution.py:41
  169.3 16.6 %all_to_all.28 = bf16[8,8,4096]{2,1,0:T(8,128)(2,1)S(1)} all-to-all(bf16[8,8,4096]{2,1,0:T(8,128)(2,1)S(1)} %fusion.1), channel_id=1, replica_groups=mesh['dp'=2,'tensor'=8,'expert'=16] {'tensor'}, dimensions={0} | all-to-all | bytes 1048576 | tf_op jit(solution)/shard_map/all_to_all | solution.py:23
  186.0 0.7 fusion.3
  (70 shorter events, 5.7 us)
Async XLA Ops:
  0.0 0.8 copy-start
  0.0 13.1 %copy-start.7 = (s32[1,8,8]{2,1,0:T(8,128)S(1)}, s32[1,8,8]{2,1,0:T(8,128)}, u32[]{:S(2)}) copy-start(s32[1,8,8]{2,1,0:T(8,128)} %param.14) | copy-start | bytes 772
  0.0 13.3 %copy-start.8 = (s32[1,8,8]{2,1,0:T(8,128)S(1)}, s32[1,8,8]{2,1,0:T(8,128)}, u32[]{:S(2)}) copy-start(s32[1,8,8]{2,1,0:T(8,128)} %param.13) | copy-start | bytes 772
  0.0 30.7 %copy-start.5 = (bf16[1,8,4096]{2,1,0:T(8,128)(2,1)S(1)}, bf16[1,8,4096]{2,1,0:T(8,128)(2,1)}, u32[]{:S(2)}) copy-start(bf16[1,8,4096]{2,1,0:T(8,128)(2,1)} %param.11) | copy-start | bytes 196612
  0.0 30.9 %copy-start.6 = (f32[4096]{0:T(1024)S(1)}, f32[4096]{0:T(1024)}, u32[]{:S(2)}) copy-start(f32[4096]{0:T(1024)} %param.12) | copy-start | bytes 49156
  4.7 26.0 %all-to-all-start = ((bf16[8,8,4096]{2,1,0:T(8,128)(2,1)}), bf16[8,8,4096]{2,1,0:T(8,128)(2,1)S(1)}, u32[]{:S(2)}, u32[]{:S(2)}) async-start(bf16[8,8,4096]{2,1,0:T(8,128)(2,1)} %fusion), calls=%async_computation | async-start | bytes 1048576 | tf_op jit(solution)/shard_map/all_to_all | solution.py:23
  31.0 41.3 %copy-start.1 = (bf16[1,192,4096]{2,1,0:T(8,128)(2,1)S(1)}, bf16[1,192,4096]{2,1,0:T(8,128)(2,1)}, u32[]{:S(2)}) copy-start(bf16[1,192,4096]{2,1,0:T(8,128)(2,1)} %param.15) | copy-start | bytes 4718596
  31.0 41.3 %copy-start.2 = (bf16[1,192,4096]{2,1,0:T(8,128)(2,1)S(1)}, bf16[1,192,4096]{2,1,0:T(8,128)(2,1)}, u32[]{:S(2)}) copy-start(bf16[1,192,4096]{2,1,0:T(8,128)(2,1)} %param.16) | copy-start | bytes 4718596
  52.7 10.9 %collective-permute-start.1 = (bf16[64,4224]{1,0:T(8,128)(2,1)}, bf16[64,4224]{1,0:T(8,128)(2,1)}, u32[]{:S(2)}, u32[]{:S(2)}) collective-permute-start(bf16[64,4224]{1,0:T(8,128)(2,1)} %bitcast.6), channel_id=1, source_target_pairs={{0,1},{1,2},{2,3},{3,0},{4,5},{5,6},{6,7},{7,4},{8,9},{9,10},{10,1... | collective-permute-start | bytes 1622024 | tf_op jit(solution)/shard_map/ppermute | solution.py:41
  54.2 10.7 %collective-permute-start = (bf16[64,4224]{1,0:T(8,128)(2,1)}, bf16[64,4224]{1,0:T(8,128)(2,1)}, u32[]{:S(2)}, u32[]{:S(2)}) collective-permute-start(bf16[64,4224]{1,0:T(8,128)(2,1)} %bitcast.6), channel_id=1, source_target_pairs={{0,3},{1,0},{2,1},{3,2},{4,7},{5,4},{6,5},{7,6},{8,11},{9,8},{10,9... | collective-permute-start | bytes 1622024 | tf_op jit(solution)/shard_map/ppermute | solution.py:41
  64.6 10.7 %collective-permute-start.2 = (bf16[32,4224]{1,0:T(8,128)(2,1)S(1)}, bf16[32,4224]{1,0:T(8,128)(2,1)S(1)}, u32[]{:S(2)}, u32[]{:S(2)}) collective-permute-start(bf16[32,4224]{1,0:T(8,128)(2,1)S(1)} %slice.90), channel_id=1, source_target_pairs={{0,1},{1,2},{2,3},{3,0},{4,5},{5,6},{6,7},{7,4},{8,9},{9,10},{10,1... | collective-permute-start | bytes 811016 | tf_op jit(solution)/shard_map/ppermute | solution.py:41
  65.9 9.9 %collective-permute-start.3 = (bf16[32,4224]{1,0:T(8,128)(2,1)S(1)}, bf16[32,4224]{1,0:T(8,128)(2,1)S(1)}, u32[]{:S(2)}, u32[]{:S(2)}) collective-permute-start(bf16[32,4224]{1,0:T(8,128)(2,1)S(1)} %slice.91), channel_id=1, source_target_pairs={{0,3},{1,0},{2,1},{3,2},{4,7},{5,4},{6,5},{7,6},{8,11},{9,8},{10,9... | collective-permute-start | bytes 811016 | tf_op jit(solution)/shard_map/ppermute | solution.py:41
  70.2 15.2 %collective-permute-start.6 = (bf16[128,4224]{1,0:T(8,128)(2,1)S(1)}, bf16[128,4224]{1,0:T(8,128)(2,1)S(1)}, u32[]{:S(2)}, u32[]{:S(2)}) collective-permute-start(bf16[128,4224]{1,0:T(8,128)(2,1)S(1)} %pad_maximum_fusion.1.refs_0_), channel_id=1, source_target_pairs={{0,4},{1,5},{2,6},{3,7},{4,8},{5,9},{6,10},{7,11},{8,12},{9,13},{1... | collective-permute-start | bytes 3244040 | tf_op jit(solution)/shard_map/ppermute | solution.py:41
  70.5 16.4 %collective-permute-start.7 = (bf16[128,4224]{1,0:T(8,128)(2,1)S(1)}, bf16[128,4224]{1,0:T(8,128)(2,1)S(1)}, u32[]{:S(2)}, u32[]{:S(2)}) collective-permute-start(bf16[128,4224]{1,0:T(8,128)(2,1)S(1)} %pad_maximum_fusion.1.refs_0_), channel_id=1, source_target_pairs={{0,12},{1,13},{2,14},{3,15},{4,0},{5,1},{6,2},{7,3},{8,4},{9,5},{1... | collective-permute-start | bytes 3244040 | tf_op jit(solution)/shard_map/ppermute | solution.py:41
  72.3 1.4 copy-start.3
  76.9 20.1 %collective-permute-start.4 = (bf16[128,4224]{1,0:T(8,128)(2,1)S(1)}, bf16[128,4224]{1,0:T(8,128)(2,1)S(1)}, u32[]{:S(2)}, u32[]{:S(2)}) collective-permute-start(bf16[128,4224]{1,0:T(8,128)(2,1)S(1)} %pad_maximum_fusion.refs_0_), channel_id=1, source_target_pairs={{0,4},{1,5},{2,6},{3,7},{4,8},{5,9},{6,10},{7,11},{8,12},{9,13},{1... | collective-permute-start | bytes 3244040 | tf_op jit(solution)/shard_map/ppermute | solution.py:41
  77.9 20.6 %collective-permute-start.5 = (bf16[128,4224]{1,0:T(8,128)(2,1)S(1)}, bf16[128,4224]{1,0:T(8,128)(2,1)S(1)}, u32[]{:S(2)}, u32[]{:S(2)}) collective-permute-start(bf16[128,4224]{1,0:T(8,128)(2,1)S(1)} %pad_maximum_fusion.refs_0_), channel_id=1, source_target_pairs={{0,12},{1,13},{2,14},{3,15},{4,0},{5,1},{6,2},{7,3},{8,4},{9,5},{1... | collective-permute-start | bytes 3244040 | tf_op jit(solution)/shard_map/ppermute | solution.py:41
  86.9 15.9 %collective-permute-start.8 = (bf16[64,4224]{1,0:T(8,128)(2,1)S(1)}, bf16[64,4224]{1,0:T(8,128)(2,1)S(1)}, u32[]{:S(2)}, u32[]{:S(2)}) collective-permute-start(bf16[64,4224]{1,0:T(8,128)(2,1)S(1)} %slice.72), channel_id=1, source_target_pairs={{0,4},{1,5},{2,6},{3,7},{4,8},{5,9},{6,10},{7,11},{8,12},{9,13},{1... | collective-permute-start | bytes 1622024 | tf_op jit(solution)/shard_map/ppermute | solution.py:41
  87.4 16.9 %collective-permute-start.9 = (bf16[64,4224]{1,0:T(8,128)(2,1)S(1)}, bf16[64,4224]{1,0:T(8,128)(2,1)S(1)}, u32[]{:S(2)}, u32[]{:S(2)}) collective-permute-start(bf16[64,4224]{1,0:T(8,128)(2,1)S(1)} %slice.73), channel_id=1, source_target_pairs={{0,12},{1,13},{2,14},{3,15},{4,0},{5,1},{6,2},{7,3},{8,4},{9,5},{1... | collective-permute-start | bytes 1622024 | tf_op jit(solution)/shard_map/ppermute | solution.py:41
  98.5 11.5 %collective-permute-start.14 = (bf16[64,4224]{1,0:T(8,128)(2,1)S(1)}, bf16[64,4224]{1,0:T(8,128)(2,1)S(1)}, u32[]{:S(2)}, u32[]{:S(2)}) collective-permute-start(bf16[64,4224]{1,0:T(8,128)(2,1)S(1)} %slice.78), channel_id=1, source_target_pairs={{0,4},{1,5},{2,6},{3,7},{4,8},{5,9},{6,10},{7,11},{8,12},{9,13},{1... | collective-permute-start | bytes 1622024 | tf_op jit(solution)/shard_map/ppermute | solution.py:41
  99.0 11.1 %collective-permute-start.15 = (bf16[64,4224]{1,0:T(8,128)(2,1)S(1)}, bf16[64,4224]{1,0:T(8,128)(2,1)S(1)}, u32[]{:S(2)}, u32[]{:S(2)}) collective-permute-start(bf16[64,4224]{1,0:T(8,128)(2,1)S(1)} %slice.79), channel_id=1, source_target_pairs={{0,12},{1,13},{2,14},{3,15},{4,0},{5,1},{6,2},{7,3},{8,4},{9,5},{1... | collective-permute-start | bytes 1622024 | tf_op jit(solution)/shard_map/ppermute | solution.py:41
  105.8 9.3 %collective-permute-start.10 = (bf16[64,4096]{1,0:T(8,128)(2,1)S(1)}, bf16[64,4096]{1,0:T(8,128)(2,1)S(1)}, u32[]{:S(2)}, u32[]{:S(2)}) collective-permute-start(bf16[64,4096]{1,0:T(8,128)(2,1)S(1)} %get-tuple-element.41), channel_id=1, source_target_pairs={{0,4},{1,5},{2,6},{3,7},{4,8},{5,9},{6,10},{7,11},{8,12},{9,13},{1... | collective-permute-start | bytes 1572872 | tf_op jit(solution)/shard_map/ppermute | solution.py:41
  106.3 3.8 %copy-start.4 = (bf16[1,192,4096]{2,1,0:T(8,128)(2,1)S(1)}, bf16[1,192,4096]{2,1,0:T(8,128)(2,1)}, u32[]{:S(2)}) copy-start(bf16[1,192,4096]{2,1,0:T(8,128)(2,1)} %param.17) | copy-start | bytes 4718596
  106.3 18.1 %collective-permute-start.12 = (bf16[64,4096]{1,0:T(8,128)(2,1)S(1)}, bf16[64,4096]{1,0:T(8,128)(2,1)S(1)}, u32[]{:S(2)}, u32[]{:S(2)}) collective-permute-start(bf16[64,4096]{1,0:T(8,128)(2,1)S(1)} %get-tuple-element.43), channel_id=1, source_target_pairs={{0,12},{1,13},{2,14},{3,15},{4,0},{5,1},{6,2},{7,3},{8,4},{9,5},{1... | collective-permute-start | bytes 1572872 | tf_op jit(solution)/shard_map/ppermute | solution.py:41
  111.6 9.3 %collective-permute-start.16 = (bf16[64,4096]{1,0:T(8,128)(2,1)S(1)}, bf16[64,4096]{1,0:T(8,128)(2,1)S(1)}, u32[]{:S(2)}, u32[]{:S(2)}) collective-permute-start(bf16[64,4096]{1,0:T(8,128)(2,1)S(1)} %get-tuple-element.52), channel_id=1, source_target_pairs={{0,4},{1,5},{2,6},{3,7},{4,8},{5,9},{6,10},{7,11},{8,12},{9,13},{1... | collective-permute-start | bytes 1572872 | tf_op jit(solution)/shard_map/ppermute | solution.py:41
  113.2 10.9 %collective-permute-start.18 = (bf16[64,4096]{1,0:T(8,128)(2,1)S(1)}, bf16[64,4096]{1,0:T(8,128)(2,1)S(1)}, u32[]{:S(2)}, u32[]{:S(2)}) collective-permute-start(bf16[64,4096]{1,0:T(8,128)(2,1)S(1)} %get-tuple-element.54), channel_id=1, source_target_pairs={{0,12},{1,13},{2,14},{3,15},{4,0},{5,1},{6,2},{7,3},{8,4},{9,5},{1... | collective-permute-start | bytes 1572872 | tf_op jit(solution)/shard_map/ppermute | solution.py:41
  115.3 28.7 %collective-permute-start.11 = (bf16[128,4096]{1,0:T(8,128)(2,1)S(1)}, bf16[128,4096]{1,0:T(8,128)(2,1)S(1)}, u32[]{:S(2)}, u32[]{:S(2)}) collective-permute-start(bf16[128,4096]{1,0:T(8,128)(2,1)S(1)} %pad_maximum_fusion.2), channel_id=1, source_target_pairs={{0,4},{1,5},{2,6},{3,7},{4,8},{5,9},{6,10},{7,11},{8,12},{9,13},{1... | collective-permute-start | bytes 3145736 | tf_op jit(solution)/shard_map/ppermute | solution.py:41
  121.1 22.2 %collective-permute-start.17 = (bf16[128,4096]{1,0:T(8,128)(2,1)S(1)}, bf16[128,4096]{1,0:T(8,128)(2,1)S(1)}, u32[]{:S(2)}, u32[]{:S(2)}) collective-permute-start(bf16[128,4096]{1,0:T(8,128)(2,1)S(1)} %pad_maximum_fusion.4), channel_id=1, source_target_pairs={{0,4},{1,5},{2,6},{3,7},{4,8},{5,9},{6,10},{7,11},{8,12},{9,13},{1... | collective-permute-start | bytes 3145736 | tf_op jit(solution)/shard_map/ppermute | solution.py:41
  124.3 19.0 %collective-permute-start.19 = (bf16[128,4096]{1,0:T(8,128)(2,1)S(1)}, bf16[128,4096]{1,0:T(8,128)(2,1)S(1)}, u32[]{:S(2)}, u32[]{:S(2)}) collective-permute-start(bf16[128,4096]{1,0:T(8,128)(2,1)S(1)} %pad_maximum_fusion.5), channel_id=1, source_target_pairs={{0,12},{1,13},{2,14},{3,15},{4,0},{5,1},{6,2},{7,3},{8,4},{9,5},{1... | collective-permute-start | bytes 3145736 | tf_op jit(solution)/shard_map/ppermute | solution.py:41
  124.6 28.1 %collective-permute-start.13 = (bf16[128,4096]{1,0:T(8,128)(2,1)S(1)}, bf16[128,4096]{1,0:T(8,128)(2,1)S(1)}, u32[]{:S(2)}, u32[]{:S(2)}) collective-permute-start(bf16[128,4096]{1,0:T(8,128)(2,1)S(1)} %pad_maximum_fusion.3), channel_id=1, source_target_pairs={{0,12},{1,13},{2,14},{3,15},{4,0},{5,1},{6,2},{7,3},{8,4},{9,5},{1... | collective-permute-start | bytes 3145736 | tf_op jit(solution)/shard_map/ppermute | solution.py:41
  143.9 9.5 %collective-permute-start.20 = (bf16[32,4096]{1,0:T(8,128)(2,1)S(1)}, bf16[32,4096]{1,0:T(8,128)(2,1)S(1)}, u32[]{:S(2)}, u32[]{:S(2)}) collective-permute-start(bf16[32,4096]{1,0:T(8,128)(2,1)S(1)} %get-tuple-element.55), channel_id=1, source_target_pairs={{0,1},{1,2},{2,3},{3,0},{4,5},{5,6},{6,7},{7,4},{8,9},{9,10},{10,1... | collective-permute-start | bytes 786440 | tf_op jit(solution)/shard_map/ppermute | solution.py:41
  153.3 6.4 %collective-permute-start.22 = (bf16[32,4096]{1,0:T(8,128)(2,1)S(1)}, bf16[32,4096]{1,0:T(8,128)(2,1)S(1)}, u32[]{:S(2)}, u32[]{:S(2)}) collective-permute-start(bf16[32,4096]{1,0:T(8,128)(2,1)S(1)} %get-tuple-element.56), channel_id=1, source_target_pairs={{0,3},{1,0},{2,1},{3,2},{4,7},{5,4},{6,5},{7,6},{8,11},{9,8},{10,9... | collective-permute-start | bytes 786440 | tf_op jit(solution)/shard_map/ppermute | solution.py:41
  153.5 10.5 %collective-permute-start.21 = (bf16[64,4096]{1,0:T(8,128)(2,1)S(1)}, bf16[64,4096]{1,0:T(8,128)(2,1)S(1)}, u32[]{:S(2)}, u32[]{:S(2)}) collective-permute-start(bf16[64,4096]{1,0:T(8,128)(2,1)S(1)} %pad_maximum_fusion.6), channel_id=1, source_target_pairs={{0,1},{1,2},{2,3},{3,0},{4,5},{5,6},{6,7},{7,4},{8,9},{9,10},{10,1... | collective-permute-start | bytes 1572872 | tf_op jit(solution)/shard_map/ppermute | solution.py:41
  159.8 9.3 %collective-permute-start.23 = (bf16[64,4096]{1,0:T(8,128)(2,1)S(1)}, bf16[64,4096]{1,0:T(8,128)(2,1)S(1)}, u32[]{:S(2)}, u32[]{:S(2)}) collective-permute-start(bf16[64,4096]{1,0:T(8,128)(2,1)S(1)} %pad_maximum_fusion.7), channel_id=1, source_target_pairs={{0,3},{1,0},{2,1},{3,2},{4,7},{5,4},{6,5},{7,6},{8,11},{9,8},{10,9... | collective-permute-start | bytes 1572872 | tf_op jit(solution)/shard_map/ppermute | solution.py:41

commit v6 on v5

v6 whole, which is shorter than its diff:
```python
import functools

import jax
import jax.numpy as jnp
from jax import lax
from jax.experimental import pallas as pl
from jax.experimental.pallas import tpu as pltpu
from jax.sharding import PartitionSpec as P

EXPERTS = 16
SIDE = 4
LANES = 128
CHUNK = 1024
GRANT = 8 << 20


def vmem_spec():
    return pl.BlockSpec(memory_space=pltpu.VMEM)


def project_kernel(heads_ref, proj_ref, out_ref):
    out_ref[...] = jnp.dot(
        heads_ref[...], proj_ref[...], preferred_element_type=jnp.float32
    ).astype(jnp.bfloat16)


def project(heads, proj):
    tokens, features = heads.shape
    width = proj.shape[1]
    return pl.pallas_call(
        project_kernel,
        grid=(width // CHUNK,),
        out_shape=jax.ShapeDtypeStruct((tokens, width), jnp.bfloat16),
        in_specs=[
            pl.BlockSpec((tokens, features), lambda i: (0, 0)),
            pl.BlockSpec((features, CHUNK), lambda i: (0, i)),
        ],
        out_specs=pl.BlockSpec((tokens, CHUNK), lambda i: (0, i)),
        compiler_params=pltpu.CompilerParams(vmem_limit_bytes=GRANT),
        cost_estimate=pl.CostEstimate(
            flops=2 * tokens * features * width,
            bytes_accessed=2 * features * width,
            transcendentals=0,
        ),
    )(heads, proj)


def norm_kernel(count, parts_ref, residual_ref, gain_ref, ids_ref, codes_ref, hidden_ref, rows_ref):
    size, width = residual_ref.shape
    hidden = residual_ref[...].astype(jnp.float32)
    attn = parts_ref[:size].astype(jnp.float32)
    for i in range(1, count):
        attn = attn + parts_ref[i * size : (i + 1) * size].astype(jnp.float32)
    hidden = hidden + attn
    hidden_ref[...] = hidden
    mean_square = jnp.mean(hidden * hidden, axis=-1, keepdims=True)
    normed = (hidden * lax.rsqrt(mean_square + 1e-06) * gain_ref[...]).astype(jnp.bfloat16)
    ids, codes = ids_ref[...], codes_ref[...]
    lane = lax.broadcasted_iota(jnp.int32, (size, LANES), 1)
    table = jnp.zeros((size, LANES), jnp.int32)
    for k in range(ids.shape[1]):
        code = codes[:, k : k + 1]
        table = table + jnp.where((lane == ids[:, k : k + 1]) | (lane == EXPERTS), code, 0)
    table = table.astype(jnp.float32).astype(jnp.bfloat16)
    for i in range(count):
        rows_ref[i * size : (i + 1) * size, :width] = normed
        rows_ref[i * size : (i + 1) * size, width:] = table


def normalize(parts, residual, gain, ids, codes, count):
    size, width = residual.shape
    return pl.pallas_call(
        functools.partial(norm_kernel, count),
        out_shape=[
            jax.ShapeDtypeStruct((size, width), jnp.float32),
            jax.ShapeDtypeStruct((count * size, width + LANES), jnp.bfloat16),
        ],
        in_specs=[vmem_spec()] * 5,
        out_specs=[vmem_spec()] * 2,
        compiler_params=pltpu.CompilerParams(vmem_limit_bytes=GRANT),
        cost_estimate=pl.CostEstimate(
            flops=20 * size * width, bytes_accessed=6 * count * size * width, transcendentals=size
        ),
    )(parts, residual, gain, ids, codes)


def swap_over_tensor(value):
    return lax.all_to_all(value, "tensor", split_axis=0, concat_axis=0, tiled=True)


def shift(value, turn, step):
    pairs = []
    for half in range(lax.axis_size("dp")):
        for row in range(SIDE):
            for col in range(SIDE):
                if (half + turn) % 2:
                    to_row, to_col = (row + step) % SIDE, col
                else:
                    to_row, to_col = row, (col + step) % SIDE
                base = half * SIDE * SIDE
                pairs.append((base + row * SIDE + col, base + to_row * SIDE + to_col))
    return lax.ppermute(value, ("dp", "expert"), pairs)


def send_round(block, turn):
    return shift(block, turn, 1), shift(block, turn, -1)


def send_on(back, front, turn):
    half = back.shape[0] // 2
    return shift(back[:half], turn, 1), shift(front[half:], turn, -1)


def add(*values):
    total = values[0].astype(jnp.float32)
    for value in values[1:]:
        total = total + value.astype(jnp.float32)
    return total


def tie(values, others):
    tied = lax.optimization_barrier((*values, *others))
    return tied[: len(values)], tied[len(values) :]


def plus(*values):
    return add(*values).astype(jnp.bfloat16)


def expert_kernel(count, me_ref, *refs):
    blocks, (gate_ref, up_ref, down_ref), outs = refs[:count], refs[count : count + 3], refs[count + 3 :]
    width = gate_ref.shape[1]
    x = jnp.concatenate([block[:, :width] for block in blocks])
    tail = jnp.concatenate([block[:, width:] for block in blocks]).astype(jnp.float32)
    lane = lax.broadcasted_iota(jnp.int32, tail.shape, 1)
    code = jnp.sum(jnp.where(lane == me_ref[0], tail, 0.0), axis=1, keepdims=True)
    total = jnp.sum(jnp.where(lane == EXPERTS, tail, 0.0), axis=1, keepdims=True)
    both_last = (((1,), (1,)), ((), ()))
    gate_value = lax.dot_general(x, gate_ref[...], both_last, preferred_element_type=jnp.float32)
    up_value = lax.dot_general(x, up_ref[...], both_last, preferred_element_type=jnp.float32)
    activated = (jax.nn.silu(gate_value) * up_value).astype(jnp.bfloat16)
    scale = code / total
    size = outs[0].shape[0]
    for start in range(0, width, CHUNK):
        down = jnp.dot(
            activated, down_ref[:, start : start + CHUNK], preferred_element_type=jnp.float32
        )
        result = (down * scale).astype(jnp.bfloat16)
        for i, out in enumerate(outs):
            out[:, start : start + CHUNK] = result[i * size : (i + 1) * size]


def run_expert(me, blocks, size, w_gate, w_up, w_down):
    count = len(blocks)
    pieces = count * blocks[0].shape[0] // size
    units, width = w_gate.shape
    vmem = pl.BlockSpec(memory_space=pltpu.VMEM)
    return pl.pallas_call(
        functools.partial(expert_kernel, count),
        out_shape=[jax.ShapeDtypeStruct((size, width), jnp.bfloat16)] * pieces,
        in_specs=[pl.BlockSpec(memory_space=pltpu.SMEM)] + [vmem] * (count + 3),
        out_specs=[vmem] * pieces,
        compiler_params=pltpu.CompilerParams(vmem_limit_bytes=GRANT),
        cost_estimate=pl.CostEstimate(
            flops=6 * pieces * size * units * width,
            bytes_accessed=4 * pieces * size * width + 6 * units * width,
            transcendentals=pieces * size * units,
        ),
    )(me, *blocks, w_gate, w_up, w_down)


def on_device(
    attn_heads, out_proj, residual, norm_gain, expert_ids, weight_codes, w_gate, w_up, w_down
):
    tensor_count = lax.axis_size("tensor")
    me = lax.axis_index("expert")
    partial = project(attn_heads[0], out_proj)
    hidden, rows = normalize(
        swap_over_tensor(partial),
        residual[0],
        norm_gain[None],
        expert_ids[0],
        weight_codes[0],
        tensor_count,
    )
    group = swap_over_tensor(rows)
    tokens, model_width = partial.shape

    weights = (w_gate[0], w_up[0], w_down[0])
    who = jnp.reshape(me, (1,)).astype(jnp.int32)

    def experts(*blocks):
        return run_expert(who, blocks, tokens, *weights)

    def both(ahead, behind, turn):
        return [shift(ahead, turn, 1), shift(behind, turn, -1)]

    back, front = send_round(group, 0)
    first = jnp.concatenate([group, back])
    first_near = send_round(first, 1)
    far = send_on(back, front, 0)
    first_own = experts(first)
    second = jnp.concatenate([front, *far])
    (second,), first_own = tie((second,), first_own)
    second_near = send_round(second, 1)
    second_own = experts(second)
    first_near, second_own = tie(first_near, second_own)
    first_far = send_on(*first_near, 1)
    a_back_low, a_back_high, a_front_low, a_front_high = experts(*first_near)
    second_near, (a_back_low, a_front_high) = tie(second_near, (a_back_low, a_front_high))
    second_far = send_on(*second_near, 1)
    a_far = experts(*first_far)
    second_near, a_far = tie(second_near, a_far)
    a_up, a_down = both(*a_far, 1)
    b_back_low, b_back_high, b_front_low, b_front_high = experts(*second_near)
    second_far, (b_back_low, b_front_high) = tie(second_far, (b_back_low, b_front_high))
    b_far = experts(*second_far)
    b_up, b_down = both(*b_far, 1)

    a_got = both(a_front_high, a_back_low, 1)
    b_got = both(b_front_high, b_back_low, 1)
    a_late = both(plus(a_front_low, a_up), plus(a_back_high, a_down), 1)
    b_late = both(plus(b_front_low, b_up), plus(b_back_high, b_down), 1)
    far = plus(second_own[1], b_got[0], b_late[1])
    front = plus(second_own[0], b_late[0], b_got[1])
    back = plus(first_own[1], a_got[0], a_late[1])
    own = plus(first_own[0], a_late[0], a_got[1])

    half = tokens // 2
    up, down = both(far[:half], far[half:], 0)
    got = both(front[half:], back[:half], 0)
    late = both(plus(front[:half], up), plus(back[half:], down), 0)
    mixed = jnp.concatenate([plus(own[:half], late[0], got[1]), plus(own[half:], got[0], late[1])])
    parts = swap_over_tensor(mixed).reshape(tensor_count, -1, model_width)
    layer_out = (hidden + jnp.sum(parts.astype(jnp.float32), axis=0)).astype(jnp.bfloat16)
    return layer_out[None]


def solution(mesh):
    return jax.shard_map(
        on_device,
        mesh=mesh,
        in_specs=(
            P(("dp", "expert"), None, "tensor"),
            P("tensor", None),
            P(("dp", "expert"), "tensor", None),
            P(),
            P(("dp", "expert"), "tensor", None),
            P(("dp", "expert"), "tensor", None),
            P("expert", "tensor", None),
            P("expert", "tensor", None),
            P("expert", "tensor", None),
        ),
        out_specs=P(("dp", "expert"), "tensor", None),
        check_vma=False,
    )
```

time: 187 us -> 196 us (1.048)
  blocking collectives: 38.3 us -> 62.8 us
  waiting for transfers between devices: 87.2 us -> 71.3 us
  starting transfers between devices: 36.6 us -> 43.8 us
  matrix products: 3.84 us -> 0 us
  other arithmetic: 5.89 us -> 2.5 us
    all_to_all x2 -> x3, blocking collectives: 38.3 us -> 62.8 us  [swap_over_tensor(): lax.all_to_all(value, 'tensor', split_axis=0, concat_axis=0, tiled=True)]
    all_to_all x1 -> x0, waiting for transfers between devices: 17.2 us -> none  [reduce_over_tensor(): lax.all_to_all(partial.astype(jnp.bfloat16), 'tensor', split_axis=0, conc...]
    ppermute x24 -> x30, starting transfers between devices: 28.1 us -> 43.8 us  [shift(): return lax.ppermute(value, ('dp', 'expert'), pairs)]
    all_to_all x1 -> x0, starting transfers between devices: 8.47 us -> none  [reduce_over_tensor(): lax.all_to_all(partial.astype(jnp.bfloat16), 'tensor', split_axis=0, conc...]
    dot_general x1 -> x0, matrix products: 3.84 us -> none  [on_device(): jnp.dot(attn_heads[0], out_proj, preferred_element_type=jnp.float32)]
    ppermute x24 -> x30, waiting for transfers between devices: 70 us -> 71.3 us  [shift(): return lax.ppermute(value, ('dp', 'expert'), pairs)]
  transfers between devices with their start and end apart: 25 -> 30, of which waited for: 17 -> 18; matrix products, arithmetic and copies ran while one was open for 4% -> 1% of each run, Pallas kernels for 5% -> 5%
where the time goes in v6:
time: 196 us
  waiting for transfers between devices  71.3 us (36%)
  blocking collectives  62.8 us (32%)
  starting transfers between devices  43.8 us (22%)
  Pallas kernels  11.7 us (6%)
  local copies, waits for them, and re-layouts  3.32 us (2%)
  other arithmetic  2.5 us (1%)
    ppermute x30, waiting for transfers between devices, shift(): return lax.ppermute(value, ('dp', 'expert'), pairs)  71.3 us
    all_to_all x3, blocking collectives, swap_over_tensor(): lax.all_to_all(value, 'tensor', split_axis=0, concat_axis=0, tiled=True)  62.8 us
    ppermute x30, starting transfers between devices, shift(): return lax.ppermute(value, ('dp', 'expert'), pairs)  43.8 us
    pallas_call x6, Pallas kernels, run_expert(): pl.pallas_call(functools.partial(expert_kernel, count), out_shape=[jax.Sh...  9.88 us
  transfers between devices with their start and end apart: 30, of which 18 were waited for; matrix products, arithmetic and copies ran while one was open for 1% of the time, Pallas kernels for 5%

profile of v6, /device:TPU:24, one launch (start us, length us, event | category | flops | bytes accessed | tf_op | source)
XLA Modules:
  0.0 195.7 jit_solution(7456900322999154195)
XLA Ops:
  0.0 2.2 %copy-done.3 = bf16[512,4096]{1,0:T(8,128)(2,1)S(1)} copy-done((bf16[512,4096]{1,0:T(8,128)(2,1)S(1)}, bf16[512,4096]{1,0:T(8,128)(2,1)}, u32[]{:S(2)}) %copy-start.3) | copy-done | bytes 4194328
  2.2 0.8 copy-done.4
  3.0 1.6 shard_map.91
  4.6 25.9 %all_to_all.32 = bf16[8,8,4096]{2,1,0:T(8,128)(2,1)S(1)} all-to-all(bf16[8,8,4096]{2,1,0:T(8,128)(2,1)S(1)} %bitcast.35), channel_id=1, replica_groups=mesh['dp'=2,'tensor'=8,'expert'=16] {'tensor'}, dimensions={0} | all-to-all | bytes 1048576 | tf_op jit(solution)/shard_map/all_to_all | solution.py:88
  30.8 18.9 %all_to_all.33 = bf16[8,8,4224]{2,1,0:T(8,128)(2,1)S(1)} all-to-all(bf16[8,8,4224]{2,1,0:T(8,128)(2,1)S(1)} %bitcast.37), channel_id=1, replica_groups=mesh['dp'=2,'tensor'=8,'expert'=16] {'tensor'}, dimensions={0} | all-to-all | bytes 1081344 | tf_op jit(solution)/shard_map/all_to_all | solution.py:88
  49.7 2.8 %collective-permute-start = (bf16[64,4224]{1,0:T(8,128)(2,1)S(1)}, bf16[64,4224]{1,0:T(8,128)(2,1)S(1)}, u32[]{:S(2)}, u32[]{:S(2)}) collective-permute-start(bf16[64,4224]{1,0:T(8,128)(2,1)S(1)} %bitcast.43), channel_id=1, source_target_pairs={{0,3},{1,0},{2,1},{3,2},{4,7},{5,4},{6,5},{7,6},{8,11},{9,8},{10,9... | collective-permute-start | bytes 1622024 | tf_op jit(solution)/shard_map/ppermute | solution.py:102
  52.5 6.9 %collective-permute-done = bf16[64,4224]{1,0:T(8,128)(2,1)S(1)} collective-permute-done((bf16[64,4224]{1,0:T(8,128)(2,1)S(1)}, bf16[64,4224]{1,0:T(8,128)(2,1)S(1)}, u32[]{:S(2)}, u32[]{:S(2)}) %collective-permute-start) | collective-permute-done | bytes 540704 | tf_op jit(solution)/shard_map/ppermute | solution.py:102
  59.4 3.8 %collective-permute-start.3 = (bf16[32,4224]{1,0:T(8,128)(2,1)S(1)}, bf16[32,4224]{1,0:T(8,128)(2,1)S(1)}, u32[]{:S(2)}, u32[]{:S(2)}) collective-permute-start(bf16[32,4224]{1,0:T(8,128)(2,1)S(1)} %slice.57), channel_id=1, source_target_pairs={{0,3},{1,0},{2,1},{3,2},{4,7},{5,4},{6,5},{7,6},{8,11},{9,8},{10,9... | collective-permute-start | bytes 811016 | tf_op jit(solution)/shard_map/ppermute | solution.py:102
  63.7 2.1 %collective-permute-start.5 = (bf16[128,4224]{1,0:T(8,128)(2,1)S(1)}, bf16[128,4224]{1,0:T(8,128)(2,1)S(1)}, u32[]{:S(2)}, u32[]{:S(2)}) collective-permute-start(bf16[128,4224]{1,0:T(8,128)(2,1)S(1)} %pad_maximum_fusion.1.refs_0_), channel_id=1, source_target_pairs={{0,12},{1,13},{2,14},{3,15},{4,0},{5,1},{6,2},{7,3},{8,4},{9,5},{1... | collective-permute-start | bytes 3244040 | tf_op jit(solution)/shard_map/ppermute | solution.py:102
  65.8 1.5 shard_map.93
  67.3 2.8 %collective-permute-done.3 = bf16[32,4224]{1,0:T(8,128)(2,1)S(1)} collective-permute-done((bf16[32,4224]{1,0:T(8,128)(2,1)S(1)}, bf16[32,4224]{1,0:T(8,128)(2,1)S(1)}, u32[]{:S(2)}, u32[]{:S(2)}) %collective-permute-start.3) | collective-permute-done | bytes 270368 | tf_op jit(solution)/shard_map/ppermute | solution.py:102
  70.1 3.8 %collective-permute-done.2 = bf16[32,4224]{1,0:T(8,128)(2,1)S(1)} collective-permute-done((bf16[32,4224]{1,0:T(8,128)(2,1)S(1)}, bf16[32,4224]{1,0:T(8,128)(2,1)S(1)}, u32[]{:S(2)}, u32[]{:S(2)}) %collective-permute-start.2) | collective-permute-done | bytes 270368 | tf_op jit(solution)/shard_map/ppermute | solution.py:102
  74.3 2.1 %collective-permute-start.7 = (bf16[128,4224]{1,0:T(8,128)(2,1)S(1)}, bf16[128,4224]{1,0:T(8,128)(2,1)S(1)}, u32[]{:S(2)}, u32[]{:S(2)}) collective-permute-start(bf16[128,4224]{1,0:T(8,128)(2,1)S(1)} %pad_maximum_fusion.refs_0_), channel_id=1, source_target_pairs={{0,12},{1,13},{2,14},{3,15},{4,0},{5,1},{6,2},{7,3},{8,4},{9,5},{1... | collective-permute-start | bytes 3244040 | tf_op jit(solution)/shard_map/ppermute | solution.py:102
  76.4 1.5 shard_map.94
  77.9 0.9 collective-permute-done.4.refs_0_
  78.8 1.6 collective-permute-done.5.refs_1_
  80.5 2.1 %collective-permute-start.8 = (bf16[64,4224]{1,0:T(8,128)(2,1)S(1)}, bf16[64,4224]{1,0:T(8,128)(2,1)S(1)}, u32[]{:S(2)}, u32[]{:S(2)}) collective-permute-start(bf16[64,4224]{1,0:T(8,128)(2,1)S(1)} %slice.44), channel_id=1, source_target_pairs={{0,4},{1,5},{2,6},{3,7},{4,8},{5,9},{6,10},{7,11},{8,12},{9,13},{1... | collective-permute-start | bytes 1622024 | tf_op jit(solution)/shard_map/ppermute | solution.py:102
  82.9 1.9 shard_map.95
  84.8 5.6 %collective-permute-done.6.refs_0_ = bf16[128,4224]{1,0:T(8,128)(2,1)S(1)} collective-permute-done((bf16[128,4224]{1,0:T(8,128)(2,1)S(1)}, bf16[128,4224]{1,0:T(8,128)(2,1)S(1)}, u32[]{:S(2)}, u32[]{:S(2)}) %collective-permute-start.6) | collective-permute-done | bytes 1081376 | tf_op jit(solution)/shard_map/ppermute | solution.py:102
  90.4 1.6 collective-permute-done.7.refs_1_
  92.1 2.1 %collective-permute-start.13 = (bf16[64,4224]{1,0:T(8,128)(2,1)S(1)}, bf16[64,4224]{1,0:T(8,128)(2,1)S(1)}, u32[]{:S(2)}, u32[]{:S(2)}) collective-permute-start(bf16[64,4224]{1,0:T(8,128)(2,1)S(1)} %slice.47), channel_id=1, source_target_pairs={{0,4},{1,5},{2,6},{3,7},{4,8},{5,9},{6,10},{7,11},{8,12},{9,13},{1... | collective-permute-start | bytes 1622024 | tf_op jit(solution)/shard_map/ppermute | solution.py:102
  94.3 1.9 collective-permute-done.8.refs_0_
  96.2 1.6 collective-permute-done.9.refs_1_
  97.8 1.5 shard_map.96
  99.4 0.5 collective-permute-start.24
  99.9 2.8 %collective-permute-start.23 = (bf16[64,4096]{1,0:T(8,128)(2,1)S(1)}, bf16[64,4096]{1,0:T(8,128)(2,1)S(1)}, u32[]{:S(2)}, u32[]{:S(2)}) collective-permute-start(bf16[64,4096]{1,0:T(8,128)(2,1)S(1)} %get-tuple-element.76), channel_id=1, source_target_pairs={{0,4},{1,5},{2,6},{3,7},{4,8},{5,9},{6,10},{7,11},{8,12},{9,13},{1... | collective-permute-start | bytes 1572872 | tf_op jit(solution)/shard_map/ppermute | solution.py:102
  102.7 1.9 shard_map.97
  104.6 3.3 %collective-permute-start.10 = (bf16[64,4096]{1,0:T(8,128)(2,1)S(1)}, bf16[64,4096]{1,0:T(8,128)(2,1)S(1)}, u32[]{:S(2)}, u32[]{:S(2)}) collective-permute-start(bf16[64,4096]{1,0:T(8,128)(2,1)S(1)} %get-tuple-element.59), channel_id=1, source_target_pairs={{0,4},{1,5},{2,6},{3,7},{4,8},{5,9},{6,10},{7,11},{8,12},{9,13},{1... | collective-permute-start | bytes 1572872 | tf_op jit(solution)/shard_map/ppermute | solution.py:102
  107.9 1.5 shard_map.98
  109.5 1.0 collective-permute-done.24
  110.5 2.3 %collective-permute-start.18 = (bf16[64,4096]{1,0:T(8,128)(2,1)S(1)}, bf16[64,4096]{1,0:T(8,128)(2,1)S(1)}, u32[]{:S(2)}, u32[]{:S(2)}) collective-permute-start(bf16[64,4096]{1,0:T(8,128)(2,1)S(1)} %get-tuple-element.72), channel_id=1, source_target_pairs={{0,4},{1,5},{2,6},{3,7},{4,8},{5,9},{6,10},{7,11},{8,12},{9,13},{1... | collective-permute-start | bytes 1572872 | tf_op jit(solution)/shard_map/ppermute | solution.py:102
  112.9 2.1 %collective-permute-done.10 = bf16[64,4096]{1,0:T(8,128)(2,1)S(1)} collective-permute-done((bf16[64,4096]{1,0:T(8,128)(2,1)S(1)}, bf16[64,4096]{1,0:T(8,128)(2,1)S(1)}, u32[]{:S(2)}, u32[]{:S(2)}) %collective-permute-start.10) | collective-permute-done | bytes 524320 | tf_op jit(solution)/shard_map/ppermute | solution.py:102
  115.0 1.7 collective-permute-start.17
  116.8 5.0 %collective-permute-done.19 = bf16[64,4096]{1,0:T(8,128)(2,1)S(1)} collective-permute-done((bf16[64,4096]{1,0:T(8,128)(2,1)S(1)}, bf16[64,4096]{1,0:T(8,128)(2,1)S(1)}, u32[]{:S(2)}, u32[]{:S(2)}) %collective-permute-start.19) | collective-permute-done | bytes 524320 | tf_op jit(solution)/shard_map/ppermute | solution.py:102
  121.7 0.8 collective-permute-start.15
  122.6 8.3 %collective-permute-done.15 = bf16[64,4096]{1,0:T(8,128)(2,1)S(1)} collective-permute-done((bf16[64,4096]{1,0:T(8,128)(2,1)S(1)}, bf16[64,4096]{1,0:T(8,128)(2,1)S(1)}, u32[]{:S(2)}, u32[]{:S(2)}) %collective-permute-start.15) | collective-permute-done | bytes 524320 | tf_op jit(solution)/shard_map/ppermute | solution.py:102
  131.1 3.3 %collective-permute-start.11 = (bf16[64,4096]{1,0:T(8,128)(2,1)S(1)}, bf16[64,4096]{1,0:T(8,128)(2,1)S(1)}, u32[]{:S(2)}, u32[]{:S(2)}) collective-permute-start(bf16[64,4096]{1,0:T(8,128)(2,1)S(1)} %add_convert_fusion.7), channel_id=1, source_target_pairs={{0,4},{1,5},{2,6},{3,7},{4,8},{5,9},{6,10},{7,11},{8,12},{9,13},{1... | collective-permute-start | bytes 1572872 | tf_op jit(solution)/shard_map/ppermute | solution.py:102
  134.4 6.9 %collective-permute-done.25 = bf16[64,4096]{1,0:T(8,128)(2,1)S(1)} collective-permute-done((bf16[64,4096]{1,0:T(8,128)(2,1)S(1)}, bf16[64,4096]{1,0:T(8,128)(2,1)S(1)}, u32[]{:S(2)}, u32[]{:S(2)}) %collective-permute-start.25) | collective-permute-done | bytes 524320 | tf_op jit(solution)/shard_map/ppermute | solution.py:102
  141.5 3.3 %collective-permute-start.16 = (bf16[64,4096]{1,0:T(8,128)(2,1)S(1)}, bf16[64,4096]{1,0:T(8,128)(2,1)S(1)}, u32[]{:S(2)}, u32[]{:S(2)}) collective-permute-start(bf16[64,4096]{1,0:T(8,128)(2,1)S(1)} %add_convert_fusion.5), channel_id=1, source_target_pairs={{0,4},{1,5},{2,6},{3,7},{4,8},{5,9},{6,10},{7,11},{8,12},{9,13},{1... | collective-permute-start | bytes 1572872 | tf_op jit(solution)/shard_map/ppermute | solution.py:102
  144.8 10.6 %collective-permute-done.20 = bf16[64,4096]{1,0:T(8,128)(2,1)S(1)} collective-permute-done((bf16[64,4096]{1,0:T(8,128)(2,1)S(1)}, bf16[64,4096]{1,0:T(8,128)(2,1)S(1)}, u32[]{:S(2)}, u32[]{:S(2)}) %collective-permute-start.20) | collective-permute-done | bytes 524320 | tf_op jit(solution)/shard_map/ppermute | solution.py:102
  155.4 3.0 %collective-permute-start.26 = (bf16[32,4096]{1,0:T(8,128)(2,1)S(1)}, bf16[32,4096]{1,0:T(8,128)(2,1)S(1)}, u32[]{:S(2)}, u32[]{:S(2)}) collective-permute-start(bf16[32,4096]{1,0:T(8,128)(2,1)S(1)} %slice.61), channel_id=1, source_target_pairs={{0,3},{1,0},{2,1},{3,2},{4,7},{5,4},{6,5},{7,6},{8,11},{9,8},{10,9... | collective-permute-start | bytes 786440 | tf_op jit(solution)/shard_map/ppermute | solution.py:102
  158.8 3.2 %collective-permute-start.28 = (bf16[32,4096]{1,0:T(8,128)(2,1)S(1)}, bf16[32,4096]{1,0:T(8,128)(2,1)S(1)}, u32[]{:S(2)}, u32[]{:S(2)}) collective-permute-start(bf16[32,4096]{1,0:T(8,128)(2,1)S(1)} %get-tuple-element.82), channel_id=1, source_target_pairs={{0,3},{1,0},{2,1},{3,2},{4,7},{5,4},{6,5},{7,6},{8,11},{9,8},{10,9... | collective-permute-start | bytes 786440 | tf_op jit(solution)/shard_map/ppermute | solution.py:102
  162.2 4.1 %collective-permute-done.21 = bf16[32,4096]{1,0:T(8,128)(2,1)S(1)} collective-permute-done((bf16[32,4096]{1,0:T(8,128)(2,1)S(1)}, bf16[32,4096]{1,0:T(8,128)(2,1)S(1)}, u32[]{:S(2)}, u32[]{:S(2)}) %collective-permute-start.21) | collective-permute-done | bytes 262176 | tf_op jit(solution)/shard_map/ppermute | solution.py:102
  166.6 3.3 %collective-permute-start.29 = (bf16[32,4096]{1,0:T(8,128)(2,1)S(1)}, bf16[32,4096]{1,0:T(8,128)(2,1)S(1)}, u32[]{:S(2)}, u32[]{:S(2)}) collective-permute-start(bf16[32,4096]{1,0:T(8,128)(2,1)S(1)} %add_convert_fusion.9), channel_id=1, source_target_pairs={{0,3},{1,0},{2,1},{3,2},{4,7},{5,4},{6,5},{7,6},{8,11},{9,8},{10,9... | collective-permute-start | bytes 786440 | tf_op jit(solution)/shard_map/ppermute | solution.py:102
  170.1 3.8 %collective-permute-done.27 = bf16[32,4096]{1,0:T(8,128)(2,1)S(1)} collective-permute-done((bf16[32,4096]{1,0:T(8,128)(2,1)S(1)}, bf16[32,4096]{1,0:T(8,128)(2,1)S(1)}, u32[]{:S(2)}, u32[]{:S(2)}) %collective-permute-start.27) | collective-permute-done | bytes 262176 | tf_op jit(solution)/shard_map/ppermute | solution.py:102
  174.0 2.8 %collective-permute-done.22 = bf16[32,4096]{1,0:T(8,128)(2,1)S(1)} collective-permute-done((bf16[32,4096]{1,0:T(8,128)(2,1)S(1)}, bf16[32,4096]{1,0:T(8,128)(2,1)S(1)}, u32[]{:S(2)}, u32[]{:S(2)}) %collective-permute-start.22) | collective-permute-done | bytes 262176 | tf_op jit(solution)/shard_map/ppermute | solution.py:102
  177.0 17.9 %all_to_all.34 = bf16[8,8,4096]{2,1,0:T(8,128)(2,1)S(1)} all-to-all(bf16[8,8,4096]{2,1,0:T(8,128)(2,1)S(1)} %maximum_bitcast_fusion), channel_id=1, replica_groups=mesh['dp'=2,'tensor'=8,'expert'=16] {'tensor'}, dimensions={0} | all-to-all | bytes 1048576 | tf_op jit(solution)/shard_map/all_to_all | solution.py:88
  195.0 0.7 fusion
  (66 shorter events, 3.7 us)
Async XLA Ops:
  0.0 2.2 %copy-start.3 = (bf16[512,4096]{1,0:T(8,128)(2,1)S(1)}, bf16[512,4096]{1,0:T(8,128)(2,1)}, u32[]{:S(2)}) copy-start(bf16[512,4096]{1,0:T(8,128)(2,1)} %proj_ref.1) | copy-start | bytes 12582916
  2.2 0.8 copy-start.4
  3.0 27.5 %copy-start.6 = (f32[4096]{0:T(1024)S(1)}, f32[4096]{0:T(1024)}, u32[]{:S(2)}) copy-start(f32[4096]{0:T(1024)} %param.12) | copy-start | bytes 49156
  3.0 27.5 %copy-start.7 = (s32[1,8,8]{2,1,0:T(8,128)S(1)}, s32[1,8,8]{2,1,0:T(8,128)}, u32[]{:S(2)}) copy-start(s32[1,8,8]{2,1,0:T(8,128)} %param.13) | copy-start | bytes 772
  3.0 27.5 %copy-start.8 = (s32[1,8,8]{2,1,0:T(8,128)S(1)}, s32[1,8,8]{2,1,0:T(8,128)}, u32[]{:S(2)}) copy-start(s32[1,8,8]{2,1,0:T(8,128)} %param.14) | copy-start | bytes 772
  4.6 25.9 %copy-start.5 = (bf16[1,8,4096]{2,1,0:T(8,128)(2,1)S(1)}, bf16[1,8,4096]{2,1,0:T(8,128)(2,1)}, u32[]{:S(2)}) copy-start(bf16[1,8,4096]{2,1,0:T(8,128)(2,1)} %param.11) | copy-start | bytes 196612
  30.5 35.3 %copy-start.2 = (bf16[1,192,4096]{2,1,0:T(8,128)(2,1)S(1)}, bf16[1,192,4096]{2,1,0:T(8,128)(2,1)}, u32[]{:S(2)}) copy-start(bf16[1,192,4096]{2,1,0:T(8,128)(2,1)} %param.17) | copy-start | bytes 4718596
  49.7 9.6 %collective-permute-start = (bf16[64,4224]{1,0:T(8,128)(2,1)S(1)}, bf16[64,4224]{1,0:T(8,128)(2,1)S(1)}, u32[]{:S(2)}, u32[]{:S(2)}) collective-permute-start(bf16[64,4224]{1,0:T(8,128)(2,1)S(1)} %bitcast.43), channel_id=1, source_target_pairs={{0,3},{1,0},{2,1},{3,2},{4,7},{5,4},{6,5},{7,6},{8,11},{9,8},{10,9... | collective-permute-start | bytes 1622024 | tf_op jit(solution)/shard_map/ppermute | solution.py:102
  52.5 10.7 %collective-permute-start.1 = (bf16[64,4224]{1,0:T(8,128)(2,1)S(1)}, bf16[64,4224]{1,0:T(8,128)(2,1)S(1)}, u32[]{:S(2)}, u32[]{:S(2)}) collective-permute-start(bf16[64,4224]{1,0:T(8,128)(2,1)S(1)} %bitcast.44), channel_id=1, source_target_pairs={{0,1},{1,2},{2,3},{3,0},{4,5},{5,6},{6,7},{7,4},{8,9},{9,10},{10,1... | collective-permute-start | bytes 1622024 | tf_op jit(solution)/shard_map/ppermute | solution.py:102
  59.4 6.4 %copy-start.1 = (bf16[1,192,4096]{2,1,0:T(8,128)(2,1)S(1)}, bf16[1,192,4096]{2,1,0:T(8,128)(2,1)}, u32[]{:S(2)}) copy-start(bf16[1,192,4096]{2,1,0:T(8,128)(2,1)} %param.16) | copy-start | bytes 4718596
  59.4 10.7 %collective-permute-start.3 = (bf16[32,4224]{1,0:T(8,128)(2,1)S(1)}, bf16[32,4224]{1,0:T(8,128)(2,1)S(1)}, u32[]{:S(2)}, u32[]{:S(2)}) collective-permute-start(bf16[32,4224]{1,0:T(8,128)(2,1)S(1)} %slice.57), channel_id=1, source_target_pairs={{0,3},{1,0},{2,1},{3,2},{4,7},{5,4},{6,5},{7,6},{8,11},{9,8},{10,9... | collective-permute-start | bytes 811016 | tf_op jit(solution)/shard_map/ppermute | solution.py:102
  63.2 2.6 %copy-start = (bf16[1,192,4096]{2,1,0:T(8,128)(2,1)S(1)}, bf16[1,192,4096]{2,1,0:T(8,128)(2,1)}, u32[]{:S(2)}) copy-start(bf16[1,192,4096]{2,1,0:T(8,128)(2,1)} %param.15) | copy-start | bytes 4718596
  63.2 10.7 %collective-permute-start.2 = (bf16[32,4224]{1,0:T(8,128)(2,1)S(1)}, bf16[32,4224]{1,0:T(8,128)(2,1)S(1)}, u32[]{:S(2)}, u32[]{:S(2)}) collective-permute-start(bf16[32,4224]{1,0:T(8,128)(2,1)S(1)} %slice.56), channel_id=1, source_target_pairs={{0,1},{1,2},{2,3},{3,0},{4,5},{5,6},{6,7},{7,4},{8,9},{9,10},{10,1... | collective-permute-start | bytes 811016 | tf_op jit(solution)/shard_map/ppermute | solution.py:102
  63.4 15.5 %collective-permute-start.4 = (bf16[128,4224]{1,0:T(8,128)(2,1)S(1)}, bf16[128,4224]{1,0:T(8,128)(2,1)S(1)}, u32[]{:S(2)}, u32[]{:S(2)}) collective-permute-start(bf16[128,4224]{1,0:T(8,128)(2,1)S(1)} %pad_maximum_fusion.1.refs_0_), channel_id=1, source_target_pairs={{0,4},{1,5},{2,6},{3,7},{4,8},{5,9},{6,10},{7,11},{8,12},{9,13},{1... | collective-permute-start | bytes 3244040 | tf_op jit(solution)/shard_map/ppermute | solution.py:102
  63.7 16.8 %collective-permute-start.5 = (bf16[128,4224]{1,0:T(8,128)(2,1)S(1)}, bf16[128,4224]{1,0:T(8,128)(2,1)S(1)}, u32[]{:S(2)}, u32[]{:S(2)}) collective-permute-start(bf16[128,4224]{1,0:T(8,128)(2,1)S(1)} %pad_maximum_fusion.1.refs_0_), channel_id=1, source_target_pairs={{0,12},{1,13},{2,14},{3,15},{4,0},{5,1},{6,2},{7,3},{8,4},{9,5},{1... | collective-permute-start | bytes 3244040 | tf_op jit(solution)/shard_map/ppermute | solution.py:102
  74.0 16.4 %collective-permute-start.6 = (bf16[128,4224]{1,0:T(8,128)(2,1)S(1)}, bf16[128,4224]{1,0:T(8,128)(2,1)S(1)}, u32[]{:S(2)}, u32[]{:S(2)}) collective-permute-start(bf16[128,4224]{1,0:T(8,128)(2,1)S(1)} %pad_maximum_fusion.refs_0_), channel_id=1, source_target_pairs={{0,4},{1,5},{2,6},{3,7},{4,8},{5,9},{6,10},{7,11},{8,12},{9,13},{1... | collective-permute-start | bytes 3244040 | tf_op jit(solution)/shard_map/ppermute | solution.py:102
  74.3 17.8 %collective-permute-start.7 = (bf16[128,4224]{1,0:T(8,128)(2,1)S(1)}, bf16[128,4224]{1,0:T(8,128)(2,1)S(1)}, u32[]{:S(2)}, u32[]{:S(2)}) collective-permute-start(bf16[128,4224]{1,0:T(8,128)(2,1)S(1)} %pad_maximum_fusion.refs_0_), channel_id=1, source_target_pairs={{0,12},{1,13},{2,14},{3,15},{4,0},{5,1},{6,2},{7,3},{8,4},{9,5},{1... | collective-permute-start | bytes 3244040 | tf_op jit(solution)/shard_map/ppermute | solution.py:102
  80.5 15.7 %collective-permute-start.8 = (bf16[64,4224]{1,0:T(8,128)(2,1)S(1)}, bf16[64,4224]{1,0:T(8,128)(2,1)S(1)}, u32[]{:S(2)}, u32[]{:S(2)}) collective-permute-start(bf16[64,4224]{1,0:T(8,128)(2,1)S(1)} %slice.44), channel_id=1, source_target_pairs={{0,4},{1,5},{2,6},{3,7},{4,8},{5,9},{6,10},{7,11},{8,12},{9,13},{1... | collective-permute-start | bytes 1622024 | tf_op jit(solution)/shard_map/ppermute | solution.py:102
  82.6 15.2 %collective-permute-start.9 = (bf16[64,4224]{1,0:T(8,128)(2,1)S(1)}, bf16[64,4224]{1,0:T(8,128)(2,1)S(1)}, u32[]{:S(2)}, u32[]{:S(2)}) collective-permute-start(bf16[64,4224]{1,0:T(8,128)(2,1)S(1)} %slice.45), channel_id=1, source_target_pairs={{0,12},{1,13},{2,14},{3,15},{4,0},{5,1},{6,2},{7,3},{8,4},{9,5},{1... | collective-permute-start | bytes 1622024 | tf_op jit(solution)/shard_map/ppermute | solution.py:102
  92.1 12.5 %collective-permute-start.13 = (bf16[64,4224]{1,0:T(8,128)(2,1)S(1)}, bf16[64,4224]{1,0:T(8,128)(2,1)S(1)}, u32[]{:S(2)}, u32[]{:S(2)}) collective-permute-start(bf16[64,4224]{1,0:T(8,128)(2,1)S(1)} %slice.47), channel_id=1, source_target_pairs={{0,4},{1,5},{2,6},{3,7},{4,8},{5,9},{6,10},{7,11},{8,12},{9,13},{1... | collective-permute-start | bytes 1622024 | tf_op jit(solution)/shard_map/ppermute | solution.py:102
  94.2 13.7 %collective-permute-start.14 = (bf16[64,4224]{1,0:T(8,128)(2,1)S(1)}, bf16[64,4224]{1,0:T(8,128)(2,1)S(1)}, u32[]{:S(2)}, u32[]{:S(2)}) collective-permute-start(bf16[64,4224]{1,0:T(8,128)(2,1)S(1)} %slice.48), channel_id=1, source_target_pairs={{0,12},{1,13},{2,14},{3,15},{4,0},{5,1},{6,2},{7,3},{8,4},{9,5},{1... | collective-permute-start | bytes 1622024 | tf_op jit(solution)/shard_map/ppermute | solution.py:102
  99.4 11.1 %collective-permute-start.24 = (bf16[64,4096]{1,0:T(8,128)(2,1)S(1)}, bf16[64,4096]{1,0:T(8,128)(2,1)S(1)}, u32[]{:S(2)}, u32[]{:S(2)}) collective-permute-start(bf16[64,4096]{1,0:T(8,128)(2,1)S(1)} %get-tuple-element.78), channel_id=1, source_target_pairs={{0,12},{1,13},{2,14},{3,15},{4,0},{5,1},{6,2},{7,3},{8,4},{9,5},{1... | collective-permute-start | bytes 1572872 | tf_op jit(solution)/shard_map/ppermute | solution.py:102
  99.9 31.1 %collective-permute-start.23 = (bf16[64,4096]{1,0:T(8,128)(2,1)S(1)}, bf16[64,4096]{1,0:T(8,128)(2,1)S(1)}, u32[]{:S(2)}, u32[]{:S(2)}) collective-permute-start(bf16[64,4096]{1,0:T(8,128)(2,1)S(1)} %get-tuple-element.76), channel_id=1, source_target_pairs={{0,4},{1,5},{2,6},{3,7},{4,8},{5,9},{6,10},{7,11},{8,12},{9,13},{1... | collective-permute-start | bytes 1572872 | tf_op jit(solution)/shard_map/ppermute | solution.py:102
  102.7 63.9 %collective-permute-start.12 = (bf16[64,4096]{1,0:T(8,128)(2,1)S(1)}, bf16[64,4096]{1,0:T(8,128)(2,1)S(1)}, u32[]{:S(2)}, u32[]{:S(2)}) collective-permute-start(bf16[64,4096]{1,0:T(8,128)(2,1)S(1)} %get-tuple-element.60), channel_id=1, source_target_pairs={{0,12},{1,13},{2,14},{3,15},{4,0},{5,1},{6,2},{7,3},{8,4},{9,5},{1... | collective-permute-start | bytes 1572872 | tf_op jit(solution)/shard_map/ppermute | solution.py:102
  104.6 10.4 %collective-permute-start.10 = (bf16[64,4096]{1,0:T(8,128)(2,1)S(1)}, bf16[64,4096]{1,0:T(8,128)(2,1)S(1)}, u32[]{:S(2)}, u32[]{:S(2)}) collective-permute-start(bf16[64,4096]{1,0:T(8,128)(2,1)S(1)} %get-tuple-element.59), channel_id=1, source_target_pairs={{0,4},{1,5},{2,6},{3,7},{4,8},{5,9},{6,10},{7,11},{8,12},{9,13},{1... | collective-permute-start | bytes 1572872 | tf_op jit(solution)/shard_map/ppermute | solution.py:102
  109.4 12.3 %collective-permute-start.19 = (bf16[64,4096]{1,0:T(8,128)(2,1)S(1)}, bf16[64,4096]{1,0:T(8,128)(2,1)S(1)}, u32[]{:S(2)}, u32[]{:S(2)}) collective-permute-start(bf16[64,4096]{1,0:T(8,128)(2,1)S(1)} %get-tuple-element.74), channel_id=1, source_target_pairs={{0,12},{1,13},{2,14},{3,15},{4,0},{5,1},{6,2},{7,3},{8,4},{9,5},{1... | collective-permute-start | bytes 1572872 | tf_op jit(solution)/shard_map/ppermute | solution.py:102
  110.5 31.0 %collective-permute-start.18 = (bf16[64,4096]{1,0:T(8,128)(2,1)S(1)}, bf16[64,4096]{1,0:T(8,128)(2,1)S(1)}, u32[]{:S(2)}, u32[]{:S(2)}) collective-permute-start(bf16[64,4096]{1,0:T(8,128)(2,1)S(1)} %get-tuple-element.72), channel_id=1, source_target_pairs={{0,4},{1,5},{2,6},{3,7},{4,8},{5,9},{6,10},{7,11},{8,12},{9,13},{1... | collective-permute-start | bytes 1572872 | tf_op jit(solution)/shard_map/ppermute | solution.py:102
  115.0 43.7 %collective-permute-start.17 = (bf16[64,4096]{1,0:T(8,128)(2,1)S(1)}, bf16[64,4096]{1,0:T(8,128)(2,1)S(1)}, u32[]{:S(2)}, u32[]{:S(2)}) collective-permute-start(bf16[64,4096]{1,0:T(8,128)(2,1)S(1)} %get-tuple-element.70), channel_id=1, source_target_pairs={{0,12},{1,13},{2,14},{3,15},{4,0},{5,1},{6,2},{7,3},{8,4},{9,5},{1... | collective-permute-start | bytes 1572872 | tf_op jit(solution)/shard_map/ppermute | solution.py:102
  121.7 9.2 %collective-permute-start.15 = (bf16[64,4096]{1,0:T(8,128)(2,1)S(1)}, bf16[64,4096]{1,0:T(8,128)(2,1)S(1)}, u32[]{:S(2)}, u32[]{:S(2)}) collective-permute-start(bf16[64,4096]{1,0:T(8,128)(2,1)S(1)} %get-tuple-element.69), channel_id=1, source_target_pairs={{0,4},{1,5},{2,6},{3,7},{4,8},{5,9},{6,10},{7,11},{8,12},{9,13},{1... | collective-permute-start | bytes 1572872 | tf_op jit(solution)/shard_map/ppermute | solution.py:102
  130.9 10.4 %collective-permute-start.25 = (bf16[64,4096]{1,0:T(8,128)(2,1)S(1)}, bf16[64,4096]{1,0:T(8,128)(2,1)S(1)}, u32[]{:S(2)}, u32[]{:S(2)}) collective-permute-start(bf16[64,4096]{1,0:T(8,128)(2,1)S(1)} %add_convert_fusion.1), channel_id=1, source_target_pairs={{0,12},{1,13},{2,14},{3,15},{4,0},{5,1},{6,2},{7,3},{8,4},{9,5},{1... | collective-permute-start | bytes 1572872 | tf_op jit(solution)/shard_map/ppermute | solution.py:102
  131.1 38.9 %collective-permute-start.11 = (bf16[64,4096]{1,0:T(8,128)(2,1)S(1)}, bf16[64,4096]{1,0:T(8,128)(2,1)S(1)}, u32[]{:S(2)}, u32[]{:S(2)}) collective-permute-start(bf16[64,4096]{1,0:T(8,128)(2,1)S(1)} %add_convert_fusion.7), channel_id=1, source_target_pairs={{0,4},{1,5},{2,6},{3,7},{4,8},{5,9},{6,10},{7,11},{8,12},{9,13},{1... | collective-permute-start | bytes 1572872 | tf_op jit(solution)/shard_map/ppermute | solution.py:102
  141.3 14.1 %collective-permute-start.20 = (bf16[64,4096]{1,0:T(8,128)(2,1)S(1)}, bf16[64,4096]{1,0:T(8,128)(2,1)S(1)}, u32[]{:S(2)}, u32[]{:S(2)}) collective-permute-start(bf16[64,4096]{1,0:T(8,128)(2,1)S(1)} %add_convert_fusion.3), channel_id=1, source_target_pairs={{0,12},{1,13},{2,14},{3,15},{4,0},{5,1},{6,2},{7,3},{8,4},{9,5},{1... | collective-permute-start | bytes 1572872 | tf_op jit(solution)/shard_map/ppermute | solution.py:102
  141.5 17.3 %collective-permute-start.16 = (bf16[64,4096]{1,0:T(8,128)(2,1)S(1)}, bf16[64,4096]{1,0:T(8,128)(2,1)S(1)}, u32[]{:S(2)}, u32[]{:S(2)}) collective-permute-start(bf16[64,4096]{1,0:T(8,128)(2,1)S(1)} %add_convert_fusion.5), channel_id=1, source_target_pairs={{0,4},{1,5},{2,6},{3,7},{4,8},{5,9},{6,10},{7,11},{8,12},{9,13},{1... | collective-permute-start | bytes 1572872 | tf_op jit(solution)/shard_map/ppermute | solution.py:102
  155.4 14.7 %collective-permute-start.26 = (bf16[32,4096]{1,0:T(8,128)(2,1)S(1)}, bf16[32,4096]{1,0:T(8,128)(2,1)S(1)}, u32[]{:S(2)}, u32[]{:S(2)}) collective-permute-start(bf16[32,4096]{1,0:T(8,128)(2,1)S(1)} %slice.61), channel_id=1, source_target_pairs={{0,3},{1,0},{2,1},{3,2},{4,7},{5,4},{6,5},{7,6},{8,11},{9,8},{10,9... | collective-permute-start | bytes 786440 | tf_op jit(solution)/shard_map/ppermute | solution.py:102
  158.7 7.7 %collective-permute-start.21 = (bf16[32,4096]{1,0:T(8,128)(2,1)S(1)}, bf16[32,4096]{1,0:T(8,128)(2,1)S(1)}, u32[]{:S(2)}, u32[]{:S(2)}) collective-permute-start(bf16[32,4096]{1,0:T(8,128)(2,1)S(1)} %get-tuple-element.81), channel_id=1, source_target_pairs={{0,1},{1,2},{2,3},{3,0},{4,5},{5,6},{6,7},{7,4},{8,9},{9,10},{10,1... | collective-permute-start | bytes 786440 | tf_op jit(solution)/shard_map/ppermute | solution.py:102
  158.8 7.6 %collective-permute-start.28 = (bf16[32,4096]{1,0:T(8,128)(2,1)S(1)}, bf16[32,4096]{1,0:T(8,128)(2,1)S(1)}, u32[]{:S(2)}, u32[]{:S(2)}) collective-permute-start(bf16[32,4096]{1,0:T(8,128)(2,1)S(1)} %get-tuple-element.82), channel_id=1, source_target_pairs={{0,3},{1,0},{2,1},{3,2},{4,7},{5,4},{6,5},{7,6},{8,11},{9,8},{10,9... | collective-permute-start | bytes 786440 | tf_op jit(solution)/shard_map/ppermute | solution.py:102
  166.4 7.6 %collective-permute-start.27 = (bf16[32,4096]{1,0:T(8,128)(2,1)S(1)}, bf16[32,4096]{1,0:T(8,128)(2,1)S(1)}, u32[]{:S(2)}, u32[]{:S(2)}) collective-permute-start(bf16[32,4096]{1,0:T(8,128)(2,1)S(1)} %slice.63), channel_id=1, source_target_pairs={{0,1},{1,2},{2,3},{3,0},{4,5},{5,6},{6,7},{7,4},{8,9},{9,10},{10,1... | collective-permute-start | bytes 786440 | tf_op jit(solution)/shard_map/ppermute | solution.py:102
  166.5 10.3 %collective-permute-start.22 = (bf16[32,4096]{1,0:T(8,128)(2,1)S(1)}, bf16[32,4096]{1,0:T(8,128)(2,1)S(1)}, u32[]{:S(2)}, u32[]{:S(2)}) collective-permute-start(bf16[32,4096]{1,0:T(8,128)(2,1)S(1)} %add_convert_fusion.11), channel_id=1, source_target_pairs={{0,1},{1,2},{2,3},{3,0},{4,5},{5,6},{6,7},{7,4},{8,9},{9,10},{10,1... | collective-permute-start | bytes 786440 | tf_op jit(solution)/shard_map/ppermute | solution.py:102
  166.6 10.1 %collective-permute-start.29 = (bf16[32,4096]{1,0:T(8,128)(2,1)S(1)}, bf16[32,4096]{1,0:T(8,128)(2,1)S(1)}, u32[]{:S(2)}, u32[]{:S(2)}) collective-permute-start(bf16[32,4096]{1,0:T(8,128)(2,1)S(1)} %add_convert_fusion.9), channel_id=1, source_target_pairs={{0,3},{1,0},{2,1},{3,2},{4,7},{5,4},{6,5},{7,6},{8,11},{9,8},{10,9... | collective-permute-start | bytes 786440 | tf_op jit(solution)/shard_map/ppermute | solution.py:102

commit v7 on v6

--- a/solution.py
+++ b/solution.py
@@ -12,6 +12,7 @@
 LANES = 128
 CHUNK = 1024
 GRANT = 8 << 20
+STREAM = 62 << 20
 
 
 def vmem_spec():
@@ -36,7 +37,7 @@
             pl.BlockSpec((features, CHUNK), lambda i: (0, i)),
         ],
         out_specs=pl.BlockSpec((tokens, CHUNK), lambda i: (0, i)),
-        compiler_params=pltpu.CompilerParams(vmem_limit_bytes=GRANT),
+        compiler_params=pltpu.CompilerParams(vmem_limit_bytes=STREAM),
         cost_estimate=pl.CostEstimate(
             flops=2 * tokens * features * width,
             bytes_accessed=2 * features * width,
@@ -123,8 +124,32 @@
     return tied[: len(values)], tied[len(values) :]
 
 
-def plus(*values):
-    return add(*values).astype(jnp.bfloat16)
+def join(back, front, up, down):
+    half = up.shape[0]
+    front = jnp.concatenate([add(front[:half], up).astype(jnp.bfloat16), front[half:]])
+    back = jnp.concatenate([back[:half], add(back[half:], down).astype(jnp.bfloat16)])
+    return front, back
+
+
+def pair_kernel(own_ref, back_ref, front_ref, pair_ref, low_ref, high_ref):
+    size, half = own_ref.shape[0], low_ref.shape[0]
+    pair_ref[:size] = own_ref[...]
+    pair_ref[size:] = back_ref[...]
+    low_ref[...] = back_ref[:half]
+    high_ref[...] = front_ref[half:]
+
+
+def pair(own, back, front):
+    size, width = own.shape
+    shapes = [(2 * size, width), (size // 2, width), (size // 2, width)]
+    return pl.pallas_call(
+        pair_kernel,
+        out_shape=[jax.ShapeDtypeStruct(shape, own.dtype) for shape in shapes],
+        in_specs=[vmem_spec()] * 3,
+        out_specs=[vmem_spec()] * 3,
+        compiler_params=pltpu.CompilerParams(vmem_limit_bytes=GRANT),
+        cost_estimate=pl.CostEstimate(flops=0, bytes_accessed=12 * size * width, transcendentals=0),
+    )(own, back, front)
 
 
 def expert_kernel(count, me_ref, *refs):
@@ -150,21 +175,20 @@
             out[:, start : start + CHUNK] = result[i * size : (i + 1) * size]
 
 
-def run_expert(me, blocks, size, w_gate, w_up, w_down):
-    count = len(blocks)
-    pieces = count * blocks[0].shape[0] // size
+def run_expert(me, blocks, w_gate, w_up, w_down):
+    count, size = len(blocks), blocks[0].shape[0]
     units, width = w_gate.shape
     vmem = pl.BlockSpec(memory_space=pltpu.VMEM)
     return pl.pallas_call(
         functools.partial(expert_kernel, count),
-        out_shape=[jax.ShapeDtypeStruct((size, width), jnp.bfloat16)] * pieces,
+        out_shape=[jax.ShapeDtypeStruct((size, width), jnp.bfloat16)] * count,
         in_specs=[pl.BlockSpec(memory_space=pltpu.SMEM)] + [vmem] * (count + 3),
-        out_specs=[vmem] * pieces,
+        out_specs=[vmem] * count,
         compiler_params=pltpu.CompilerParams(vmem_limit_bytes=GRANT),
         cost_estimate=pl.CostEstimate(
-            flops=6 * pieces * size * units * width,
-            bytes_accessed=4 * pieces * size * width + 6 * units * width,
-            transcendentals=pieces * size * units,
+            flops=6 * count * size * units * width,
+            bytes_accessed=4 * count * size * width + 6 * units * width,
+            transcendentals=count * size * units,
         ),
     )(me, *blocks, w_gate, w_up, w_down)
 
@@ -173,8 +197,9 @@
     attn_heads, out_proj, residual, norm_gain, expert_ids, weight_codes, w_gate, w_up, w_down
 ):
     tensor_count = lax.axis_size("tensor")
-    me = lax.axis_index("expert")
-    partial = project(attn_heads[0], out_proj)
+    who = jnp.reshape(lax.axis_index("expert"), (1,)).astype(jnp.int32)
+    (heads,), (who,) = tie((attn_heads[0],), (who,))
+    partial = project(heads, out_proj)
     hidden, rows = normalize(
         swap_over_tensor(partial),
         residual[0],
@@ -187,18 +212,17 @@
     tokens, model_width = partial.shape
 
     weights = (w_gate[0], w_up[0], w_down[0])
-    who = jnp.reshape(me, (1,)).astype(jnp.int32)
 
     def experts(*blocks):
-        return run_expert(who, blocks, tokens, *weights)
+        return run_expert(who, blocks, *weights)
 
     def both(ahead, behind, turn):
-        return [shift(ahead, turn, 1), shift(behind, turn, -1)]
+        return shift(ahead, turn, 1), shift(behind, turn, -1)
 
     back, front = send_round(group, 0)
-    first = jnp.concatenate([group, back])
+    first, low, high = pair(group, back, front)
     first_near = send_round(first, 1)
-    far = send_on(back, front, 0)
+    far = both(low, high, 0)
     first_own = experts(first)
     second = jnp.concatenate([front, *far])
     (second,), first_own = tie((second,), first_own)
@@ -206,31 +230,31 @@
     second_own = experts(second)
     first_near, second_own = tie(first_near, second_own)
     first_far = send_on(*first_near, 1)
-    a_back_low, a_back_high, a_front_low, a_front_high = experts(*first_near)
-    second_near, (a_back_low, a_front_high) = tie(second_near, (a_back_low, a_front_high))
+    first_near_out = experts(*first_near)
+    second_near, first_near_out = tie(second_near, first_near_out)
     second_far = send_on(*second_near, 1)
-    a_far = experts(*first_far)
-    second_near, a_far = tie(second_near, a_far)
-    a_up, a_down = both(*a_far, 1)
-    b_back_low, b_back_high, b_front_low, b_front_high = experts(*second_near)
-    second_far, (b_back_low, b_front_high) = tie(second_far, (b_back_low, b_front_high))
-    b_far = experts(*second_far)
-    b_up, b_down = both(*b_far, 1)
-
-    a_got = both(a_front_high, a_back_low, 1)
-    b_got = both(b_front_high, b_back_low, 1)
-    a_late = both(plus(a_front_low, a_up), plus(a_back_high, a_down), 1)
-    b_late = both(plus(b_front_low, b_up), plus(b_back_high, b_down), 1)
-    far = plus(second_own[1], b_got[0], b_late[1])
-    front = plus(second_own[0], b_late[0], b_got[1])
-    back = plus(first_own[1], a_got[0], a_late[1])
-    own = plus(first_own[0], a_late[0], a_got[1])
+    first_far_out = experts(*first_far)
+    second_far, first_far_out = tie(second_far, first_far_out)
+    second_far_out = experts(*second_far)
+    first_up = both(*first_far_out, 1)
+    second_up = both(*second_far_out, 1)
+    first_up, first_own = tie(first_up, first_own)
+    first_send = join(*first_near_out, *first_up)
+    second_near, first_send = tie(second_near, first_send)
+    second_near_out = experts(*second_near)
+    second_send = join(*second_near_out, *second_up)
+    first_got = both(*first_send, 1)
+    second_got = both(*second_send, 1)
+    first_sum = add(*first_own, *first_got).astype(jnp.bfloat16)
+    (first_sum,), second_own = tie((first_sum,), second_own)
+    second_sum = add(*second_own, *second_got).astype(jnp.bfloat16)
 
     half = tokens // 2
-    up, down = both(far[:half], far[half:], 0)
-    got = both(front[half:], back[:half], 0)
-    late = both(plus(front[:half], up), plus(back[half:], down), 0)
-    mixed = jnp.concatenate([plus(own[:half], late[0], got[1]), plus(own[half:], got[0], late[1])])
+    far_low, far_high = second_sum[tokens : tokens + half], second_sum[tokens + half :]
+    up = both(far_low, far_high, 0)
+    front, back = join(first_sum[tokens:], second_sum[:tokens], *up)
+    got = both(front, back, 0)
+    mixed = add(first_sum[:tokens], *got).astype(jnp.bfloat16)
     parts = swap_over_tensor(mixed).reshape(tensor_count, -1, model_width)
     layer_out = (hidden + jnp.sum(parts.astype(jnp.float32), axis=0)).astype(jnp.bfloat16)
     return layer_out[None]

time: 196 us -> 187 us (0.954)
  starting transfers between devices: 43.8 us -> 31.2 us
  Pallas kernels: 11.7 us -> 14.8 us
  local copies, waits for them, and re-layouts: 3.32 us -> 0.39 us
  waiting for transfers between devices: 71.3 us -> 73.5 us
    ppermute x30 -> x24, starting transfers between devices: 43.8 us -> 31.2 us  [shift(): return lax.ppermute(value, ('dp', 'expert'), pairs)]
    unnamed x18 -> x14, local copies, waits for them, and re-layouts: 3.06 us -> 0.03 us
    pallas_call x1, Pallas kernels: 1.56 us -> 4.58 us  [project(): pl.pallas_call(project_kernel, grid=(width // CHUNK,), out_shape=jax.Shap...]
    ppermute x30 -> x24, waiting for transfers between devices: 71.3 us -> 73.5 us  [shift(): return lax.ppermute(value, ('dp', 'expert'), pairs)]
  transfers between devices with their start and end apart: 30 -> 24, of which waited for: 18 -> 19; matrix products, arithmetic and copies ran while one was open for 1% -> 1% of each run, Pallas kernels for 5% -> 5%
where the time goes in v7:
time: 187 us; the launch traced here: 186 us
  waiting for transfers between devices  73.5 us (39%)
  blocking collectives  62.5 us (33%)
  starting transfers between devices  31.2 us (17%)
  Pallas kernels  14.8 us (8%)
  other arithmetic  2.95 us (2%)
    ppermute x24, waiting for transfers between devices, shift(): return lax.ppermute(value, ('dp', 'expert'), pairs)  73.5 us
    all_to_all x3, blocking collectives, swap_over_tensor(): lax.all_to_all(value, 'tensor', split_axis=0, concat_axis=0, tiled=True)  62.5 us
    ppermute x24, starting transfers between devices, shift(): return lax.ppermute(value, ('dp', 'expert'), pairs)  31.2 us
    pallas_call x6, Pallas kernels, run_expert(): pl.pallas_call(functools.partial(expert_kernel, count), out_shape=[jax.Sh...  9.86 us
    pallas_call x1, Pallas kernels, project(): pl.pallas_call(project_kernel, grid=(width // CHUNK,), out_shape=jax.Shap...  4.58 us
  transfers between devices with their start and end apart: 24, of which 19 were waited for; matrix products, arithmetic and copies ran while one was open for 1% of the time, Pallas kernels for 5%

profile of v7, /device:TPU:24, one launch (start us, length us, event | category | flops | bytes accessed | tf_op | source)
XLA Modules:
  0.0 185.6 jit_solution(833648478216331235)
XLA Ops:
  0.0 4.6 %shard_map.91 = bf16[64,4096]{1,0:T(8,128)(2,1)} custom-call(bf16[64,512]{1,0:T(8,128)(2,1)} %bitcast.45, bf16[512,4096]{1,0:T(8,128)(2,1)} %proj_ref.1), custom_call_target="tpu_custom_call" | custom-call | flops 268435456 | bytes 4194304 | tf_op jit(solution)/shard_map/pallas_call | solution.py:31
  4.6 26.2 %all_to_all.31 = bf16[8,8,4096]{2,1,0:T(8,128)(2,1)S(1)} all-to-all(bf16[8,8,4096]{2,1,0:T(8,128)(2,1)} %bitcast.44), channel_id=1, replica_groups=mesh['dp'=2,'tensor'=8,'expert'=16] {'tensor'}, dimensions={0} | all-to-all | bytes 1048576 | tf_op jit(solution)/shard_map/all_to_all | solution.py:89
  31.1 18.8 %all_to_all.32 = bf16[8,8,4224]{2,1,0:T(8,128)(2,1)S(1)} all-to-all(bf16[8,8,4224]{2,1,0:T(8,128)(2,1)S(1)} %bitcast.39), channel_id=1, replica_groups=mesh['dp'=2,'tensor'=8,'expert'=16] {'tensor'}, dimensions={0} | all-to-all | bytes 1081344 | tf_op jit(solution)/shard_map/all_to_all | solution.py:89
  49.9 2.8 %collective-permute-start = (bf16[64,4224]{1,0:T(8,128)(2,1)S(1)}, bf16[64,4224]{1,0:T(8,128)(2,1)S(1)}, u32[]{:S(2)}, u32[]{:S(2)}) collective-permute-start(bf16[64,4224]{1,0:T(8,128)(2,1)S(1)} %bitcast.35), channel_id=1, source_target_pairs={{0,3},{1,0},{2,1},{3,2},{4,7},{5,4},{6,5},{7,6},{8,11},{9,8},{10,9... | collective-permute-start | bytes 1622024 | tf_op jit(solution)/shard_map/ppermute | solution.py:103
  52.7 6.9 %collective-permute-done.front_ref = bf16[64,4224]{1,0:T(8,128)(2,1)S(1)} collective-permute-done((bf16[64,4224]{1,0:T(8,128)(2,1)S(1)}, bf16[64,4224]{1,0:T(8,128)(2,1)S(1)}, u32[]{:S(2)}, u32[]{:S(2)}) %collective-permute-start) | collective-permute-done | bytes 540704 | tf_op jit(solution)/shard_map/ppermute | solution.py:103
  59.5 3.7 %collective-permute-done.1.back_ref = bf16[64,4224]{1,0:T(8,128)(2,1)S(1)} collective-permute-done((bf16[64,4224]{1,0:T(8,128)(2,1)S(1)}, bf16[64,4224]{1,0:T(8,128)(2,1)S(1)}, u32[]{:S(2)}, u32[]{:S(2)}) %collective-permute-start.1) | collective-permute-done | bytes 540704 | tf_op jit(solution)/shard_map/ppermute | solution.py:103
  63.4 3.2 %collective-permute-start.3 = (bf16[32,4224]{1,0:T(8,128)(2,1)S(1)}, bf16[32,4224]{1,0:T(8,128)(2,1)S(1)}, u32[]{:S(2)}, u32[]{:S(2)}) collective-permute-start(bf16[32,4224]{1,0:T(8,128)(2,1)S(1)} %get-tuple-element.46), channel_id=1, source_target_pairs={{0,3},{1,0},{2,1},{3,2},{4,7},{5,4},{6,5},{7,6},{8,11},{9,8},{10,9... | collective-permute-start | bytes 811016 | tf_op jit(solution)/shard_map/ppermute | solution.py:103
  66.9 2.3 %collective-permute-start.7 = (bf16[128,4224]{1,0:T(8,128)(2,1)S(1)}, bf16[128,4224]{1,0:T(8,128)(2,1)S(1)}, u32[]{:S(2)}, u32[]{:S(2)}) collective-permute-start(bf16[128,4224]{1,0:T(8,128)(2,1)S(1)} %get-tuple-element.48.refs_0_), channel_id=1, source_target_pairs={{0,12},{1,13},{2,14},{3,15},{4,0},{5,1},{6,2},{7,3},{8,4},{9,5},{1... | collective-permute-start | bytes 3244040 | tf_op jit(solution)/shard_map/ppermute | solution.py:103
  69.2 1.5 shard_map.94
  70.7 3.3 %collective-permute-done.2 = bf16[32,4224]{1,0:T(8,128)(2,1)S(1)} collective-permute-done((bf16[32,4224]{1,0:T(8,128)(2,1)S(1)}, bf16[32,4224]{1,0:T(8,128)(2,1)S(1)}, u32[]{:S(2)}, u32[]{:S(2)}) %collective-permute-start.2) | collective-permute-done | bytes 270368 | tf_op jit(solution)/shard_map/ppermute | solution.py:103
  74.4 2.4 %collective-permute-start.5 = (bf16[128,4224]{1,0:T(8,128)(2,1)S(1)}, bf16[128,4224]{1,0:T(8,128)(2,1)S(1)}, u32[]{:S(2)}, u32[]{:S(2)}) collective-permute-start(bf16[128,4224]{1,0:T(8,128)(2,1)S(1)} %pad_maximum_fusion.refs_0_), channel_id=1, source_target_pairs={{0,12},{1,13},{2,14},{3,15},{4,0},{5,1},{6,2},{7,3},{8,4},{9,5},{1... | collective-permute-start | bytes 3244040 | tf_op jit(solution)/shard_map/ppermute | solution.py:103
  76.9 1.5 shard_map.95
  78.4 4.0 %collective-permute-done.6.refs_0_ = bf16[128,4224]{1,0:T(8,128)(2,1)S(1)} collective-permute-done((bf16[128,4224]{1,0:T(8,128)(2,1)S(1)}, bf16[128,4224]{1,0:T(8,128)(2,1)S(1)}, u32[]{:S(2)}, u32[]{:S(2)}) %collective-permute-start.6) | collective-permute-done | bytes 1081376 | tf_op jit(solution)/shard_map/ppermute | solution.py:103
  82.3 0.9 collective-permute-done.7.refs_1_
  83.3 1.8 collective-permute-start.10
  85.1 0.5 collective-permute-start.11
  85.7 1.9 %shard_map.96 = (bf16[128,4096]{1,0:T(8,128)(2,1)S(1)}, bf16[128,4096]{1,0:T(8,128)(2,1)S(1)}) custom-call(s32[1]{0:T(128)} %bitcast.1.me_ref, bf16[128,4224]{1,0:T(8,128)(2,1)S(1)} %collective-permute-done.6.refs_0_, bf16[128,4224]{1,0:T(8,128)(2,1)S(1)} %collective-permute-done.7.refs_1_, bf16[192,4096]{1,0:T(8,128)(2,1)S(1)} %bitcast.19, ...), custom_call_target="tpu_custom_call" | custom-call | flops 1207959552 | bytes 8912896 | tf_op jit(solution)/shard_map/pallas_call | solution.py:182
  87.6 6.3 %collective-permute-done.4.refs_0_ = bf16[128,4224]{1,0:T(8,128)(2,1)S(1)} collective-permute-done((bf16[128,4224]{1,0:T(8,128)(2,1)S(1)}, bf16[128,4224]{1,0:T(8,128)(2,1)S(1)}, u32[]{:S(2)}, u32[]{:S(2)}) %collective-permute-start.4) | collective-permute-done | bytes 1081376 | tf_op jit(solution)/shard_map/ppermute | solution.py:103
  93.9 0.9 collective-permute-done.5.refs_1_
  94.9 1.8 collective-permute-start.8
  96.7 0.4 collective-permute-start.9
  97.1 2.6 %collective-permute-done.10.refs_0_ = bf16[64,4224]{1,0:T(8,128)(2,1)S(1)} collective-permute-done((bf16[64,4224]{1,0:T(8,128)(2,1)S(1)}, bf16[64,4224]{1,0:T(8,128)(2,1)S(1)}, u32[]{:S(2)}, u32[]{:S(2)}) %collective-permute-start.10) | collective-permute-done | bytes 540704 | tf_op jit(solution)/shard_map/ppermute | solution.py:103
  99.7 0.9 collective-permute-done.11.refs_1_
  100.6 1.5 shard_map.97
  102.2 3.4 %collective-permute-done.8.refs_0_ = bf16[64,4224]{1,0:T(8,128)(2,1)S(1)} collective-permute-done((bf16[64,4224]{1,0:T(8,128)(2,1)S(1)}, bf16[64,4224]{1,0:T(8,128)(2,1)S(1)}, u32[]{:S(2)}, u32[]{:S(2)}) %collective-permute-start.8) | collective-permute-done | bytes 540704 | tf_op jit(solution)/shard_map/ppermute | solution.py:103
  105.5 1.8 collective-permute-done.9.refs_1_
  107.4 0.8 collective-permute-start.12
  108.2 1.2 collective-permute-start.13
  109.5 1.5 shard_map.99
  111.0 2.1 %collective-permute-start.16 = (bf16[64,4096]{1,0:T(8,128)(2,1)S(1)}, bf16[64,4096]{1,0:T(8,128)(2,1)S(1)}, u32[]{:S(2)}, u32[]{:S(2)}) collective-permute-start(bf16[64,4096]{1,0:T(8,128)(2,1)S(1)} %get-tuple-element.76), channel_id=1, source_target_pairs={{0,4},{1,5},{2,6},{3,7},{4,8},{5,9},{6,10},{7,11},{8,12},{9,13},{1... | collective-permute-start | bytes 1572872 | tf_op jit(solution)/shard_map/ppermute | solution.py:103
  113.1 3.5 %collective-permute-done.12 = bf16[64,4096]{1,0:T(8,128)(2,1)S(1)} collective-permute-done((bf16[64,4096]{1,0:T(8,128)(2,1)S(1)}, bf16[64,4096]{1,0:T(8,128)(2,1)S(1)}, u32[]{:S(2)}, u32[]{:S(2)}) %collective-permute-start.12) | collective-permute-done | bytes 524320 | tf_op jit(solution)/shard_map/ppermute | solution.py:103
  116.6 2.0 %collective-permute-done.13 = bf16[64,4096]{1,0:T(8,128)(2,1)S(1)} collective-permute-done((bf16[64,4096]{1,0:T(8,128)(2,1)S(1)}, bf16[64,4096]{1,0:T(8,128)(2,1)S(1)}, u32[]{:S(2)}, u32[]{:S(2)}) %collective-permute-start.13) | collective-permute-done | bytes 524320 | tf_op jit(solution)/shard_map/ppermute | solution.py:103
  119.0 0.9 collective-permute-start.14
  119.9 1.2 collective-permute-start.15
  121.1 1.9 %shard_map.98 = (bf16[128,4096]{1,0:T(8,128)(2,1)S(1)}, bf16[128,4096]{1,0:T(8,128)(2,1)S(1)}) custom-call(s32[1]{0:T(128)} %bitcast.1.me_ref, bf16[128,4224]{1,0:T(8,128)(2,1)S(1)} %collective-permute-done.4.refs_0_, bf16[128,4224]{1,0:T(8,128)(2,1)S(1)} %collective-permute-done.5.refs_1_, bf16[192,4096]{1,0:T(8,128)(2,1)S(1)} %bitcast.22, ...), custom_call_target="tpu_custom_call" | custom-call | flops 1207959552 | bytes 8912896 | tf_op jit(solution)/shard_map/pallas_call | solution.py:182
  123.3 2.3 %collective-permute-start.17 = (bf16[128,4096]{1,0:T(8,128)(2,1)S(1)}, bf16[128,4096]{1,0:T(8,128)(2,1)S(1)}, u32[]{:S(2)}, u32[]{:S(2)}) collective-permute-start(bf16[128,4096]{1,0:T(8,128)(2,1)S(1)} %pad_maximum_fusion.3), channel_id=1, source_target_pairs={{0,4},{1,5},{2,6},{3,7},{4,8},{5,9},{6,10},{7,11},{8,12},{9,13},{1... | collective-permute-start | bytes 3145736 | tf_op jit(solution)/shard_map/ppermute | solution.py:103
  126.0 7.9 %collective-permute-done.14 = bf16[128,4096]{1,0:T(8,128)(2,1)S(1)} collective-permute-done((bf16[128,4096]{1,0:T(8,128)(2,1)S(1)}, bf16[128,4096]{1,0:T(8,128)(2,1)S(1)}, u32[]{:S(2)}, u32[]{:S(2)}) %collective-permute-start.14) | collective-permute-done | bytes 1048608 | tf_op jit(solution)/shard_map/ppermute | solution.py:103
  133.9 2.0 %collective-permute-done.15 = bf16[128,4096]{1,0:T(8,128)(2,1)S(1)} collective-permute-done((bf16[128,4096]{1,0:T(8,128)(2,1)S(1)}, bf16[128,4096]{1,0:T(8,128)(2,1)S(1)}, u32[]{:S(2)}, u32[]{:S(2)}) %collective-permute-start.15) | collective-permute-done | bytes 1048608 | tf_op jit(solution)/shard_map/ppermute | solution.py:103
  135.9 0.5 add_convert_fusion.1
  136.4 11.6 %collective-permute-done.17 = bf16[128,4096]{1,0:T(8,128)(2,1)S(1)} collective-permute-done((bf16[128,4096]{1,0:T(8,128)(2,1)S(1)}, bf16[128,4096]{1,0:T(8,128)(2,1)S(1)}, u32[]{:S(2)}, u32[]{:S(2)}) %collective-permute-start.17) | collective-permute-done | bytes 1048608 | tf_op jit(solution)/shard_map/ppermute | solution.py:103
  147.9 0.5 collective-permute-done.19
  148.5 0.5 add_convert_fusion
  149.1 3.2 %collective-permute-start.22 = (bf16[32,4096]{1,0:T(8,128)(2,1)S(1)}, bf16[32,4096]{1,0:T(8,128)(2,1)S(1)}, u32[]{:S(2)}, u32[]{:S(2)}) collective-permute-start(bf16[32,4096]{1,0:T(8,128)(2,1)S(1)} %get-tuple-element.80), channel_id=1, source_target_pairs={{0,3},{1,0},{2,1},{3,2},{4,7},{5,4},{6,5},{7,6},{8,11},{9,8},{10,9... | collective-permute-start | bytes 786440 | tf_op jit(solution)/shard_map/ppermute | solution.py:103
  152.3 4.3 %collective-permute-done.20 = bf16[32,4096]{1,0:T(8,128)(2,1)S(1)} collective-permute-done((bf16[32,4096]{1,0:T(8,128)(2,1)S(1)}, bf16[32,4096]{1,0:T(8,128)(2,1)S(1)}, u32[]{:S(2)}, u32[]{:S(2)}) %collective-permute-start.20) | collective-permute-done | bytes 262176 | tf_op jit(solution)/shard_map/ppermute | solution.py:103
  157.0 3.3 %collective-permute-start.23 = (bf16[64,4096]{1,0:T(8,128)(2,1)S(1)}, bf16[64,4096]{1,0:T(8,128)(2,1)S(1)}, u32[]{:S(2)}, u32[]{:S(2)}) collective-permute-start(bf16[64,4096]{1,0:T(8,128)(2,1)S(1)} %pad_maximum_fusion.6), channel_id=1, source_target_pairs={{0,3},{1,0},{2,1},{3,2},{4,7},{5,4},{6,5},{7,6},{8,11},{9,8},{10,9... | collective-permute-start | bytes 1572872 | tf_op jit(solution)/shard_map/ppermute | solution.py:103
  160.3 7.0 %collective-permute-done.21 = bf16[64,4096]{1,0:T(8,128)(2,1)S(1)} collective-permute-done((bf16[64,4096]{1,0:T(8,128)(2,1)S(1)}, bf16[64,4096]{1,0:T(8,128)(2,1)S(1)}, u32[]{:S(2)}, u32[]{:S(2)}) %collective-permute-start.21) | collective-permute-done | bytes 524320 | tf_op jit(solution)/shard_map/ppermute | solution.py:103
  167.5 17.5 %all_to_all.33 = bf16[8,8,4096]{2,1,0:T(8,128)(2,1)S(1)} all-to-all(bf16[8,8,4096]{2,1,0:T(8,128)(2,1)S(1)} %fusion), channel_id=1, replica_groups=mesh['dp'=2,'tensor'=8,'expert'=16] {'tensor'}, dimensions={0} | all-to-all | bytes 1048576 | tf_op jit(solution)/shard_map/all_to_all | solution.py:89
  185.0 0.7 fusion.1
  (53 shorter events, 3.0 us)
Async XLA Ops:
  0.0 30.8 %copy-start.3 = (bf16[1,8,4096]{2,1,0:T(8,128)(2,1)S(1)}, bf16[1,8,4096]{2,1,0:T(8,128)(2,1)}, u32[]{:S(2)}) copy-start(bf16[1,8,4096]{2,1,0:T(8,128)(2,1)} %param.11) | copy-start | bytes 196612
  0.0 30.8 %copy-start.4 = (f32[4096]{0:T(1024)S(1)}, f32[4096]{0:T(1024)}, u32[]{:S(2)}) copy-start(f32[4096]{0:T(1024)} %param.12) | copy-start | bytes 49156
  0.0 30.8 %copy-start.5 = (s32[1,8,8]{2,1,0:T(8,128)S(1)}, s32[1,8,8]{2,1,0:T(8,128)}, u32[]{:S(2)}) copy-start(s32[1,8,8]{2,1,0:T(8,128)} %param.13) | copy-start | bytes 772
  0.0 30.8 %copy-start.6 = (s32[1,8,8]{2,1,0:T(8,128)S(1)}, s32[1,8,8]{2,1,0:T(8,128)}, u32[]{:S(2)}) copy-start(s32[1,8,8]{2,1,0:T(8,128)} %param.14) | copy-start | bytes 772
  0.0 69.2 %copy-start.2 = (bf16[1,192,4096]{2,1,0:T(8,128)(2,1)S(1)}, bf16[1,192,4096]{2,1,0:T(8,128)(2,1)}, u32[]{:S(2)}) copy-start(bf16[1,192,4096]{2,1,0:T(8,128)(2,1)} %param.17) | copy-start | bytes 4718596
  4.6 64.6 %copy-start = (bf16[1,192,4096]{2,1,0:T(8,128)(2,1)S(1)}, bf16[1,192,4096]{2,1,0:T(8,128)(2,1)}, u32[]{:S(2)}) copy-start(bf16[1,192,4096]{2,1,0:T(8,128)(2,1)} %param.15) | copy-start | bytes 4718596
  4.6 64.6 %copy-start.1 = (bf16[1,192,4096]{2,1,0:T(8,128)(2,1)S(1)}, bf16[1,192,4096]{2,1,0:T(8,128)(2,1)}, u32[]{:S(2)}) copy-start(bf16[1,192,4096]{2,1,0:T(8,128)(2,1)} %param.16) | copy-start | bytes 4718596
  49.9 9.6 %collective-permute-start = (bf16[64,4224]{1,0:T(8,128)(2,1)S(1)}, bf16[64,4224]{1,0:T(8,128)(2,1)S(1)}, u32[]{:S(2)}, u32[]{:S(2)}) collective-permute-start(bf16[64,4224]{1,0:T(8,128)(2,1)S(1)} %bitcast.35), channel_id=1, source_target_pairs={{0,3},{1,0},{2,1},{3,2},{4,7},{5,4},{6,5},{7,6},{8,11},{9,8},{10,9... | collective-permute-start | bytes 1622024 | tf_op jit(solution)/shard_map/ppermute | solution.py:103
  52.7 10.6 %collective-permute-start.1 = (bf16[64,4224]{1,0:T(8,128)(2,1)S(1)}, bf16[64,4224]{1,0:T(8,128)(2,1)S(1)}, u32[]{:S(2)}, u32[]{:S(2)}) collective-permute-start(bf16[64,4224]{1,0:T(8,128)(2,1)S(1)} %bitcast.36), channel_id=1, source_target_pairs={{0,1},{1,2},{2,3},{3,0},{4,5},{5,6},{6,7},{7,4},{8,9},{9,10},{10,1... | collective-permute-start | bytes 1622024 | tf_op jit(solution)/shard_map/ppermute | solution.py:103
  63.3 10.7 %collective-permute-start.2 = (bf16[32,4224]{1,0:T(8,128)(2,1)S(1)}, bf16[32,4224]{1,0:T(8,128)(2,1)S(1)}, u32[]{:S(2)}, u32[]{:S(2)}) collective-permute-start(bf16[32,4224]{1,0:T(8,128)(2,1)S(1)} %get-tuple-element.45), channel_id=1, source_target_pairs={{0,1},{1,2},{2,3},{3,0},{4,5},{5,6},{6,7},{7,4},{8,9},{9,10},{10,1... | collective-permute-start | bytes 811016 | tf_op jit(solution)/shard_map/ppermute | solution.py:103
  63.4 10.6 %collective-permute-start.3 = (bf16[32,4224]{1,0:T(8,128)(2,1)S(1)}, bf16[32,4224]{1,0:T(8,128)(2,1)S(1)}, u32[]{:S(2)}, u32[]{:S(2)}) collective-permute-start(bf16[32,4224]{1,0:T(8,128)(2,1)S(1)} %get-tuple-element.46), channel_id=1, source_target_pairs={{0,3},{1,0},{2,1},{3,2},{4,7},{5,4},{6,5},{7,6},{8,11},{9,8},{10,9... | collective-permute-start | bytes 811016 | tf_op jit(solution)/shard_map/ppermute | solution.py:103
  66.7 15.7 %collective-permute-start.6 = (bf16[128,4224]{1,0:T(8,128)(2,1)S(1)}, bf16[128,4224]{1,0:T(8,128)(2,1)S(1)}, u32[]{:S(2)}, u32[]{:S(2)}) collective-permute-start(bf16[128,4224]{1,0:T(8,128)(2,1)S(1)} %get-tuple-element.48.refs_0_), channel_id=1, source_target_pairs={{0,4},{1,5},{2,6},{3,7},{4,8},{5,9},{6,10},{7,11},{8,12},{9,13},{1... | collective-permute-start | bytes 3244040 | tf_op jit(solution)/shard_map/ppermute | solution.py:103
  66.9 16.4 %collective-permute-start.7 = (bf16[128,4224]{1,0:T(8,128)(2,1)S(1)}, bf16[128,4224]{1,0:T(8,128)(2,1)S(1)}, u32[]{:S(2)}, u32[]{:S(2)}) collective-permute-start(bf16[128,4224]{1,0:T(8,128)(2,1)S(1)} %get-tuple-element.48.refs_0_), channel_id=1, source_target_pairs={{0,12},{1,13},{2,14},{3,15},{4,0},{5,1},{6,2},{7,3},{8,4},{9,5},{1... | collective-permute-start | bytes 3244040 | tf_op jit(solution)/shard_map/ppermute | solution.py:103
  74.1 19.8 %collective-permute-start.4 = (bf16[128,4224]{1,0:T(8,128)(2,1)S(1)}, bf16[128,4224]{1,0:T(8,128)(2,1)S(1)}, u32[]{:S(2)}, u32[]{:S(2)}) collective-permute-start(bf16[128,4224]{1,0:T(8,128)(2,1)S(1)} %pad_maximum_fusion.refs_0_), channel_id=1, source_target_pairs={{0,4},{1,5},{2,6},{3,7},{4,8},{5,9},{6,10},{7,11},{8,12},{9,13},{1... | collective-permute-start | bytes 3244040 | tf_op jit(solution)/shard_map/ppermute | solution.py:103
  74.4 20.4 %collective-permute-start.5 = (bf16[128,4224]{1,0:T(8,128)(2,1)S(1)}, bf16[128,4224]{1,0:T(8,128)(2,1)S(1)}, u32[]{:S(2)}, u32[]{:S(2)}) collective-permute-start(bf16[128,4224]{1,0:T(8,128)(2,1)S(1)} %pad_maximum_fusion.refs_0_), channel_id=1, source_target_pairs={{0,12},{1,13},{2,14},{3,15},{4,0},{5,1},{6,2},{7,3},{8,4},{9,5},{1... | collective-permute-start | bytes 3244040 | tf_op jit(solution)/shard_map/ppermute | solution.py:103
  83.3 16.4 %collective-permute-start.10 = (bf16[64,4224]{1,0:T(8,128)(2,1)S(1)}, bf16[64,4224]{1,0:T(8,128)(2,1)S(1)}, u32[]{:S(2)}, u32[]{:S(2)}) collective-permute-start(bf16[64,4224]{1,0:T(8,128)(2,1)S(1)} %slice.65), channel_id=1, source_target_pairs={{0,4},{1,5},{2,6},{3,7},{4,8},{5,9},{6,10},{7,11},{8,12},{9,13},{1... | collective-permute-start | bytes 1622024 | tf_op jit(solution)/shard_map/ppermute | solution.py:103
  85.1 15.5 %collective-permute-start.11 = (bf16[64,4224]{1,0:T(8,128)(2,1)S(1)}, bf16[64,4224]{1,0:T(8,128)(2,1)S(1)}, u32[]{:S(2)}, u32[]{:S(2)}) collective-permute-start(bf16[64,4224]{1,0:T(8,128)(2,1)S(1)} %slice.66), channel_id=1, source_target_pairs={{0,12},{1,13},{2,14},{3,15},{4,0},{5,1},{6,2},{7,3},{8,4},{9,5},{1... | collective-permute-start | bytes 1622024 | tf_op jit(solution)/shard_map/ppermute | solution.py:103
  94.9 10.7 %collective-permute-start.8 = (bf16[64,4224]{1,0:T(8,128)(2,1)S(1)}, bf16[64,4224]{1,0:T(8,128)(2,1)S(1)}, u32[]{:S(2)}, u32[]{:S(2)}) collective-permute-start(bf16[64,4224]{1,0:T(8,128)(2,1)S(1)} %slice.63), channel_id=1, source_target_pairs={{0,4},{1,5},{2,6},{3,7},{4,8},{5,9},{6,10},{7,11},{8,12},{9,13},{1... | collective-permute-start | bytes 1622024 | tf_op jit(solution)/shard_map/ppermute | solution.py:103
  96.7 10.6 %collective-permute-start.9 = (bf16[64,4224]{1,0:T(8,128)(2,1)S(1)}, bf16[64,4224]{1,0:T(8,128)(2,1)S(1)}, u32[]{:S(2)}, u32[]{:S(2)}) collective-permute-start(bf16[64,4224]{1,0:T(8,128)(2,1)S(1)} %slice.64), channel_id=1, source_target_pairs={{0,12},{1,13},{2,14},{3,15},{4,0},{5,1},{6,2},{7,3},{8,4},{9,5},{1... | collective-permute-start | bytes 1622024 | tf_op jit(solution)/shard_map/ppermute | solution.py:103
  107.4 9.2 %collective-permute-start.12 = (bf16[64,4096]{1,0:T(8,128)(2,1)S(1)}, bf16[64,4096]{1,0:T(8,128)(2,1)S(1)}, u32[]{:S(2)}, u32[]{:S(2)}) collective-permute-start(bf16[64,4096]{1,0:T(8,128)(2,1)S(1)} %get-tuple-element.58), channel_id=1, source_target_pairs={{0,4},{1,5},{2,6},{3,7},{4,8},{5,9},{6,10},{7,11},{8,12},{9,13},{1... | collective-permute-start | bytes 1572872 | tf_op jit(solution)/shard_map/ppermute | solution.py:103
  108.2 10.4 %collective-permute-start.13 = (bf16[64,4096]{1,0:T(8,128)(2,1)S(1)}, bf16[64,4096]{1,0:T(8,128)(2,1)S(1)}, u32[]{:S(2)}, u32[]{:S(2)}) collective-permute-start(bf16[64,4096]{1,0:T(8,128)(2,1)S(1)} %get-tuple-element.59), channel_id=1, source_target_pairs={{0,12},{1,13},{2,14},{3,15},{4,0},{5,1},{6,2},{7,3},{8,4},{9,5},{1... | collective-permute-start | bytes 1572872 | tf_op jit(solution)/shard_map/ppermute | solution.py:103
  111.0 12.0 %collective-permute-start.16 = (bf16[64,4096]{1,0:T(8,128)(2,1)S(1)}, bf16[64,4096]{1,0:T(8,128)(2,1)S(1)}, u32[]{:S(2)}, u32[]{:S(2)}) collective-permute-start(bf16[64,4096]{1,0:T(8,128)(2,1)S(1)} %get-tuple-element.76), channel_id=1, source_target_pairs={{0,4},{1,5},{2,6},{3,7},{4,8},{5,9},{6,10},{7,11},{8,12},{9,13},{1... | collective-permute-start | bytes 1572872 | tf_op jit(solution)/shard_map/ppermute | solution.py:103
  113.1 12.5 %collective-permute-start.18 = (bf16[64,4096]{1,0:T(8,128)(2,1)S(1)}, bf16[64,4096]{1,0:T(8,128)(2,1)S(1)}, u32[]{:S(2)}, u32[]{:S(2)}) collective-permute-start(bf16[64,4096]{1,0:T(8,128)(2,1)S(1)} %get-tuple-element.78), channel_id=1, source_target_pairs={{0,12},{1,13},{2,14},{3,15},{4,0},{5,1},{6,2},{7,3},{8,4},{9,5},{1... | collective-permute-start | bytes 1572872 | tf_op jit(solution)/shard_map/ppermute | solution.py:103
  119.0 14.9 %collective-permute-start.14 = (bf16[128,4096]{1,0:T(8,128)(2,1)S(1)}, bf16[128,4096]{1,0:T(8,128)(2,1)S(1)}, u32[]{:S(2)}, u32[]{:S(2)}) collective-permute-start(bf16[128,4096]{1,0:T(8,128)(2,1)S(1)} %pad_maximum_fusion.1), channel_id=1, source_target_pairs={{0,4},{1,5},{2,6},{3,7},{4,8},{5,9},{6,10},{7,11},{8,12},{9,13},{1... | collective-permute-start | bytes 3145736 | tf_op jit(solution)/shard_map/ppermute | solution.py:103
  119.9 16.0 %collective-permute-start.15 = (bf16[128,4096]{1,0:T(8,128)(2,1)S(1)}, bf16[128,4096]{1,0:T(8,128)(2,1)S(1)}, u32[]{:S(2)}, u32[]{:S(2)}) collective-permute-start(bf16[128,4096]{1,0:T(8,128)(2,1)S(1)} %pad_maximum_fusion.2), channel_id=1, source_target_pairs={{0,12},{1,13},{2,14},{3,15},{4,0},{5,1},{6,2},{7,3},{8,4},{9,5},{1... | collective-permute-start | bytes 3145736 | tf_op jit(solution)/shard_map/ppermute | solution.py:103
  123.3 24.6 %collective-permute-start.17 = (bf16[128,4096]{1,0:T(8,128)(2,1)S(1)}, bf16[128,4096]{1,0:T(8,128)(2,1)S(1)}, u32[]{:S(2)}, u32[]{:S(2)}) collective-permute-start(bf16[128,4096]{1,0:T(8,128)(2,1)S(1)} %pad_maximum_fusion.3), channel_id=1, source_target_pairs={{0,4},{1,5},{2,6},{3,7},{4,8},{5,9},{6,10},{7,11},{8,12},{9,13},{1... | collective-permute-start | bytes 3145736 | tf_op jit(solution)/shard_map/ppermute | solution.py:103
  125.8 22.6 %collective-permute-start.19 = (bf16[128,4096]{1,0:T(8,128)(2,1)S(1)}, bf16[128,4096]{1,0:T(8,128)(2,1)S(1)}, u32[]{:S(2)}, u32[]{:S(2)}) collective-permute-start(bf16[128,4096]{1,0:T(8,128)(2,1)S(1)} %pad_maximum_fusion.4), channel_id=1, source_target_pairs={{0,12},{1,13},{2,14},{3,15},{4,0},{5,1},{6,2},{7,3},{8,4},{9,5},{1... | collective-permute-start | bytes 3145736 | tf_op jit(solution)/shard_map/ppermute | solution.py:103
  149.0 7.7 %collective-permute-start.20 = (bf16[32,4096]{1,0:T(8,128)(2,1)S(1)}, bf16[32,4096]{1,0:T(8,128)(2,1)S(1)}, u32[]{:S(2)}, u32[]{:S(2)}) collective-permute-start(bf16[32,4096]{1,0:T(8,128)(2,1)S(1)} %get-tuple-element.79), channel_id=1, source_target_pairs={{0,1},{1,2},{2,3},{3,0},{4,5},{5,6},{6,7},{7,4},{8,9},{9,10},{10,1... | collective-permute-start | bytes 786440 | tf_op jit(solution)/shard_map/ppermute | solution.py:103
  149.1 7.8 %collective-permute-start.22 = (bf16[32,4096]{1,0:T(8,128)(2,1)S(1)}, bf16[32,4096]{1,0:T(8,128)(2,1)S(1)}, u32[]{:S(2)}, u32[]{:S(2)}) collective-permute-start(bf16[32,4096]{1,0:T(8,128)(2,1)S(1)} %get-tuple-element.80), channel_id=1, source_target_pairs={{0,3},{1,0},{2,1},{3,2},{4,7},{5,4},{6,5},{7,6},{8,11},{9,8},{10,9... | collective-permute-start | bytes 786440 | tf_op jit(solution)/shard_map/ppermute | solution.py:103
  156.8 10.5 %collective-permute-start.21 = (bf16[64,4096]{1,0:T(8,128)(2,1)S(1)}, bf16[64,4096]{1,0:T(8,128)(2,1)S(1)}, u32[]{:S(2)}, u32[]{:S(2)}) collective-permute-start(bf16[64,4096]{1,0:T(8,128)(2,1)S(1)} %pad_maximum_fusion.5), channel_id=1, source_target_pairs={{0,1},{1,2},{2,3},{3,0},{4,5},{5,6},{6,7},{7,4},{8,9},{9,10},{10,1... | collective-permute-start | bytes 1572872 | tf_op jit(solution)/shard_map/ppermute | solution.py:103
  157.0 10.3 %collective-permute-start.23 = (bf16[64,4096]{1,0:T(8,128)(2,1)S(1)}, bf16[64,4096]{1,0:T(8,128)(2,1)S(1)}, u32[]{:S(2)}, u32[]{:S(2)}) collective-permute-start(bf16[64,4096]{1,0:T(8,128)(2,1)S(1)} %pad_maximum_fusion.6), channel_id=1, source_target_pairs={{0,3},{1,0},{2,1},{3,2},{4,7},{5,4},{6,5},{7,6},{8,11},{9,8},{10,9... | collective-permute-start | bytes 1572872 | tf_op jit(solution)/shard_map/ppermute | solution.py:103

commit v8 on v7

--- a/solution.py
+++ b/solution.py
@@ -8,9 +8,11 @@
 from jax.sharding import PartitionSpec as P
 
 EXPERTS = 16
+TOP_TOKENS, CAP = 8, 6
 SIDE = 4
 LANES = 128
 CHUNK = 1024
+STRIPE = 512
 GRANT = 8 << 20
 STREAM = 62 << 20
 
@@ -19,24 +21,39 @@
     return pl.BlockSpec(memory_space=pltpu.VMEM)
 
 
-def project_kernel(heads_ref, proj_ref, out_ref):
-    out_ref[...] = jnp.dot(
-        heads_ref[...], proj_ref[...], preferred_element_type=jnp.float32
-    ).astype(jnp.bfloat16)
+def project_kernel(heads_hbm, proj_hbm, out_ref, heads_ref, proj_ref, sems):
+    count, _, size = proj_ref.shape
+    copies = [pltpu.make_async_copy(heads_hbm, heads_ref, sems.at[count])]
+    for i in range(count):
+        columns = pl.ds(i * size, size)
+        copies.append(
+            pltpu.make_async_copy(proj_hbm.at[:, columns], proj_ref.at[i], sems.at[i])
+        )
+    for copy in copies:
+        copy.start()
+    copies[0].wait()
+    heads = heads_ref[...]
+    for i in range(count):
+        copies[i + 1].wait()
+        out_ref[:, i * size : (i + 1) * size] = jnp.dot(
+            heads, proj_ref[i], preferred_element_type=jnp.float32
+        ).astype(jnp.bfloat16)
 
 
 def project(heads, proj):
     tokens, features = heads.shape
     width = proj.shape[1]
+    count = width // STRIPE
     return pl.pallas_call(
         project_kernel,
-        grid=(width // CHUNK,),
         out_shape=jax.ShapeDtypeStruct((tokens, width), jnp.bfloat16),
-        in_specs=[
-            pl.BlockSpec((tokens, features), lambda i: (0, 0)),
-            pl.BlockSpec((features, CHUNK), lambda i: (0, i)),
+        in_specs=[pl.BlockSpec(memory_space=pl.ANY)] * 2,
+        out_specs=vmem_spec(),
+        scratch_shapes=[
+            pltpu.VMEM((tokens, features), jnp.bfloat16),
+            pltpu.VMEM((count, features, STRIPE), jnp.bfloat16),
+            pltpu.SemaphoreType.DMA((count + 1,)),
         ],
-        out_specs=pl.BlockSpec((tokens, CHUNK), lambda i: (0, i)),
         compiler_params=pltpu.CompilerParams(vmem_limit_bytes=STREAM),
         cost_estimate=pl.CostEstimate(
             flops=2 * tokens * features * width,
@@ -124,11 +141,96 @@
     return tied[: len(values)], tied[len(values) :]
 
 
-def join(back, front, up, down):
-    half = up.shape[0]
-    front = jnp.concatenate([add(front[:half], up).astype(jnp.bfloat16), front[half:]])
-    back = jnp.concatenate([back[:half], add(back[half:], down).astype(jnp.bfloat16)])
-    return front, back
+def packing(tail, expert, slots):
+    rows = tail.shape[0]
+    named = jnp.where(tail.astype(jnp.float32) > 0.0, 1.0, 0.0).astype(jnp.bfloat16)
+    square = (rows, rows)
+    below = lax.broadcasted_iota(jnp.int32, square, 0) > lax.broadcasted_iota(jnp.int32, square, 1)
+    before = jnp.dot(
+        jnp.where(below, 1.0, 0.0).astype(jnp.bfloat16), named, preferred_element_type=jnp.float32
+    ).astype(jnp.bfloat16)
+    lane = lax.broadcasted_iota(jnp.int32, (8, tail.shape[1]), 1)
+    pick = jnp.where(lane == expert, 1.0, 0.0).astype(jnp.bfloat16)
+    both_last = (((1,), (1,)), ((), ()))
+    is_named = lax.dot_general(pick, named, both_last, preferred_element_type=jnp.float32)
+    place = lax.dot_general(pick, before, both_last, preferred_element_type=jnp.float32)
+    slot = lax.broadcasted_iota(jnp.int32, (slots, rows), 0).astype(jnp.float32)
+    fills = (slot == place[:1]) & (is_named[:1] > 0.5)
+    return jnp.where(fills, 1.0, 0.0).astype(jnp.bfloat16)
+
+
+def pack_kernel(me_ref, dp_ref, back_ref, front_ref, low_ref, high_ref, low_hot_ref, high_hot_ref):
+    slots, width = low_ref.shape
+    half = back_ref.shape[0] // 2
+    me = me_ref[0]
+    row, col = me // SIDE, me % SIDE
+    first = dp_ref[0] == 0
+    ahead = jnp.where(first, (row + 1) % SIDE * SIDE + col, row * SIDE + (col + 1) % SIDE)
+    behind = jnp.where(
+        first, (row + SIDE - 1) % SIDE * SIDE + col, row * SIDE + (col + SIDE - 1) % SIDE
+    )
+    tail = width - LANES
+    low_hot = packing(back_ref[:half, tail:], ahead, slots)
+    high_hot = packing(front_ref[half:, tail:], behind, slots)
+    low_hot_ref[...] = low_hot
+    high_hot_ref[...] = high_hot
+    low_ref[...] = jnp.dot(
+        low_hot, back_ref[:half, :], preferred_element_type=jnp.float32
+    ).astype(jnp.bfloat16)
+    high_ref[...] = jnp.dot(
+        high_hot, front_ref[half:, :], preferred_element_type=jnp.float32
+    ).astype(jnp.bfloat16)
+
+
+def pack(me, dp, back, front):
+    rows, width = back.shape
+    half = rows // 2
+    slots = half // TOP_TOKENS * CAP
+    smem = pl.BlockSpec(memory_space=pltpu.SMEM)
+    return pl.pallas_call(
+        pack_kernel,
+        out_shape=[jax.ShapeDtypeStruct((slots, width), jnp.bfloat16)] * 2
+        + [jax.ShapeDtypeStruct((slots, half), jnp.bfloat16)] * 2,
+        in_specs=[smem] * 2 + [vmem_spec()] * 2,
+        out_specs=[vmem_spec()] * 4,
+        compiler_params=pltpu.CompilerParams(vmem_limit_bytes=GRANT),
+        cost_estimate=pl.CostEstimate(
+            flops=2 * rows * slots * width, bytes_accessed=4 * rows * width, transcendentals=0
+        ),
+    )(me, dp, back, front)
+
+
+def join_kernel(
+    _, back_ref, front_ref, low_ref, high_ref, low_hot_ref, high_hot_ref, to_front_ref, to_back_ref
+):
+    half = back_ref.shape[0] // 2
+    first = (((0,), (0,)), ((), ()))
+
+    def unpacked(hot_ref, value_ref):
+        return lax.dot_general(
+            hot_ref[...], value_ref[...], first, preferred_element_type=jnp.float32
+        )
+
+    low = back_ref[:half, :].astype(jnp.float32) + unpacked(low_hot_ref, low_ref)
+    high = front_ref[half:, :].astype(jnp.float32) + unpacked(high_hot_ref, high_ref)
+    to_back_ref[:half, :] = low.astype(jnp.bfloat16)
+    to_back_ref[half:, :] = back_ref[half:, :]
+    to_front_ref[:half, :] = front_ref[:half, :]
+    to_front_ref[half:, :] = high.astype(jnp.bfloat16)
+
+
+def join(after, back, front, low, high, low_hot, high_hot):
+    rows, width = back.shape
+    return pl.pallas_call(
+        join_kernel,
+        out_shape=[jax.ShapeDtypeStruct((rows, width), jnp.bfloat16)] * 2,
+        in_specs=[pl.BlockSpec(memory_space=pl.ANY)] + [vmem_spec()] * 6,
+        out_specs=[vmem_spec()] * 2,
+        compiler_params=pltpu.CompilerParams(vmem_limit_bytes=GRANT),
+        cost_estimate=pl.CostEstimate(
+            flops=2 * rows * low.shape[0] * width, bytes_accessed=10 * rows * width, transcendentals=0
+        ),
+    )(after, back, front, low, high, low_hot, high_hot)
 
 
 def pair_kernel(own_ref, back_ref, front_ref, pair_ref, low_ref, high_ref):
@@ -152,7 +254,7 @@
     )(own, back, front)
 
 
-def expert_kernel(count, me_ref, *refs):
+def expert_kernel(count, me_ref, _, *refs):
     blocks, (gate_ref, up_ref, down_ref), outs = refs[:count], refs[count : count + 3], refs[count + 3 :]
     width = gate_ref.shape[1]
     x = jnp.concatenate([block[:, :width] for block in blocks])
@@ -164,7 +266,7 @@
     gate_value = lax.dot_general(x, gate_ref[...], both_last, preferred_element_type=jnp.float32)
     up_value = lax.dot_general(x, up_ref[...], both_last, preferred_element_type=jnp.float32)
     activated = (jax.nn.silu(gate_value) * up_value).astype(jnp.bfloat16)
-    scale = code / total
+    scale = code / jnp.maximum(total, 1.0)
     size = outs[0].shape[0]
     for start in range(0, width, CHUNK):
         down = jnp.dot(
@@ -175,14 +277,15 @@
             out[:, start : start + CHUNK] = result[i * size : (i + 1) * size]
 
 
-def run_expert(me, blocks, w_gate, w_up, w_down):
+def run_expert(me, after, blocks, w_gate, w_up, w_down):
     count, size = len(blocks), blocks[0].shape[0]
     units, width = w_gate.shape
     vmem = pl.BlockSpec(memory_space=pltpu.VMEM)
     return pl.pallas_call(
         functools.partial(expert_kernel, count),
         out_shape=[jax.ShapeDtypeStruct((size, width), jnp.bfloat16)] * count,
-        in_specs=[pl.BlockSpec(memory_space=pltpu.SMEM)] + [vmem] * (count + 3),
+        in_specs=[pl.BlockSpec(memory_space=pltpu.SMEM), pl.BlockSpec(memory_space=pl.ANY)]
+        + [vmem] * (count + 3),
         out_specs=[vmem] * count,
         compiler_params=pltpu.CompilerParams(vmem_limit_bytes=GRANT),
         cost_estimate=pl.CostEstimate(
@@ -190,7 +293,7 @@
             bytes_accessed=4 * count * size * width + 6 * units * width,
             transcendentals=count * size * units,
         ),
-    )(me, *blocks, w_gate, w_up, w_down)
+    )(me, after, *blocks, w_gate, w_up, w_down)
 
 
 def on_device(
@@ -198,7 +301,8 @@
 ):
     tensor_count = lax.axis_size("tensor")
     who = jnp.reshape(lax.axis_index("expert"), (1,)).astype(jnp.int32)
-    (heads,), (who,) = tie((attn_heads[0],), (who,))
+    side = jnp.reshape(lax.axis_index("dp"), (1,)).astype(jnp.int32)
+    (heads,), (who, side) = tie((attn_heads[0],), (who, side))
     partial = project(heads, out_proj)
     hidden, rows = normalize(
         swap_over_tensor(partial),
@@ -213,8 +317,8 @@
 
     weights = (w_gate[0], w_up[0], w_down[0])
 
-    def experts(*blocks):
-        return run_expert(who, blocks, *weights)
+    def experts(*blocks, after):
+        return run_expert(who, after, blocks, *weights)
 
     def both(ahead, behind, turn):
         return shift(ahead, turn, 1), shift(behind, turn, -1)
@@ -223,26 +327,25 @@
     first, low, high = pair(group, back, front)
     first_near = send_round(first, 1)
     far = both(low, high, 0)
-    first_own = experts(first)
+    first_own = experts(first, after=low)
     second = jnp.concatenate([front, *far])
     (second,), first_own = tie((second,), first_own)
     second_near = send_round(second, 1)
-    second_own = experts(second)
+    second_own = experts(second, after=first_own[0])
     first_near, second_own = tie(first_near, second_own)
-    first_far = send_on(*first_near, 1)
-    first_near_out = experts(*first_near)
+    low, high, *first_hot = pack(who, side, *first_near)
+    first_far = both(low, high, 1)
+    first_near_out = experts(*first_near, after=low)
     second_near, first_near_out = tie(second_near, first_near_out)
-    second_far = send_on(*second_near, 1)
-    first_far_out = experts(*first_far)
-    second_far, first_far_out = tie(second_far, first_far_out)
-    second_far_out = experts(*second_far)
-    first_up = both(*first_far_out, 1)
-    second_up = both(*second_far_out, 1)
-    first_up, first_own = tie(first_up, first_own)
-    first_send = join(*first_near_out, *first_up)
-    second_near, first_send = tie(second_near, first_send)
-    second_near_out = experts(*second_near)
-    second_send = join(*second_near_out, *second_up)
+    low, high, *second_hot = pack(who, side, *second_near)
+    second_far = both(low, high, 1)
+    first_far_low, first_far_high = experts(*first_far, after=high)
+    first_down = both(first_far_high, first_far_low, 1)[::-1]
+    second_far_low, second_far_high = experts(*second_far, after=first_far_low)
+    second_down = both(second_far_high, second_far_low, 1)[::-1]
+    second_near_out = experts(*second_near, after=second_far_low)
+    first_send = join(second_near_out[0], *first_near_out, *first_down, *first_hot)
+    second_send = join(first_send[1], *second_near_out, *second_down, *second_hot)
     first_got = both(*first_send, 1)
     second_got = both(*second_send, 1)
     first_sum = add(*first_own, *first_got).astype(jnp.bfloat16)
@@ -250,9 +353,10 @@
     second_sum = add(*second_own, *second_got).astype(jnp.bfloat16)
 
     half = tokens // 2
-    far_low, far_high = second_sum[tokens : tokens + half], second_sum[tokens + half :]
-    up = both(far_low, far_high, 0)
-    front, back = join(first_sum[tokens:], second_sum[:tokens], *up)
+    up, down = both(second_sum[tokens : tokens + half], second_sum[tokens + half :], 0)
+    front, back = second_sum[:tokens], first_sum[tokens:]
+    front = jnp.concatenate([add(front[:half], up).astype(jnp.bfloat16), front[half:]])
+    back = jnp.concatenate([back[:half], add(back[half:], down).astype(jnp.bfloat16)])
     got = both(front, back, 0)
     mixed = add(first_sum[:tokens], *got).astype(jnp.bfloat16)
     parts = swap_over_tensor(mixed).reshape(tensor_count, -1, model_width)

time: 187 us -> 189 us (1.011)
  starting transfers between devices: 31.2 us -> 36.7 us
  waiting for transfers between devices: 73.5 us -> 71.2 us
    ppermute x24, starting transfers between devices: 31.2 us -> 36.7 us  [shift(): return lax.ppermute(value, ('dp', 'expert'), pairs)]
    ppermute x24, waiting for transfers between devices: 73.5 us -> 71.2 us  [shift(): return lax.ppermute(value, ('dp', 'expert'), pairs)]
    pallas_call x1 -> x5, Pallas kernels: 4.58 us -> 5.9 us  [the longest x1 3.74 us: project(): pl.pallas_call(project_kernel, out_shape=jax.ShapeDtypeStruct((tokens, wi...]
  transfers between devices with their start and end apart: 24 -> 24, of which waited for: 19 -> 17; matrix products, arithmetic and copies ran while one was open for 1% -> 0% of each run, Pallas kernels for 5% -> 6%
where the time goes in v8:
time: 189 us; the launch traced here: 187 us
  waiting for transfers between devices  71.2 us (38%)
  blocking collectives  60.9 us (32%)
  starting transfers between devices  36.7 us (19%)
  Pallas kernels  16 us (8%)
  other arithmetic  2.14 us (1%)
    ppermute x24, waiting for transfers between devices, shift(): return lax.ppermute(value, ('dp', 'expert'), pairs)  71.2 us
    all_to_all x3, blocking collectives, swap_over_tensor(): lax.all_to_all(value, 'tensor', split_axis=0, concat_axis=0, tiled=True)  60.9 us
    ppermute x24, starting transfers between devices, shift(): return lax.ppermute(value, ('dp', 'expert'), pairs)  36.7 us
    pallas_call x6, Pallas kernels, run_expert(): pl.pallas_call(functools.partial(expert_kernel, count), out_shape=[jax.Sh...  9.78 us
  transfers between devices with their start and end apart: 24, of which 17 were waited for; matrix products, arithmetic and copies ran while one was open for 0% of the time, Pallas kernels for 6%

profile of v8, /device:TPU:24, one launch (start us, length us, event | category | flops | bytes accessed | tf_op | source)
XLA Modules:
  0.0 187.4 jit_solution(15444073921697547262)
XLA Ops:
  0.0 3.7 %shard_map.91 = bf16[64,4096]{1,0:T(8,128)(2,1)} custom-call(bf16[64,512]{1,0:T(8,128)(2,1)} %bitcast.46, bf16[512,4096]{1,0:T(8,128)(2,1)} %proj_hbm.1), custom_call_target="tpu_custom_call" | custom-call | flops 268435456 | bytes 4194304 | tf_op jit(solution)/shard_map/pallas_call | solution.py:47
  3.8 26.2 %all_to_all.31 = bf16[8,8,4096]{2,1,0:T(8,128)(2,1)S(1)} all-to-all(bf16[8,8,4096]{2,1,0:T(8,128)(2,1)} %bitcast.45), channel_id=1, replica_groups=mesh['dp'=2,'tensor'=8,'expert'=16] {'tensor'}, dimensions={0} | all-to-all | bytes 1048576 | tf_op jit(solution)/shard_map/all_to_all | solution.py:106
  30.3 18.8 %all_to_all.32 = bf16[8,8,4224]{2,1,0:T(8,128)(2,1)S(1)} all-to-all(bf16[8,8,4224]{2,1,0:T(8,128)(2,1)S(1)} %bitcast.40), channel_id=1, replica_groups=mesh['dp'=2,'tensor'=8,'expert'=16] {'tensor'}, dimensions={0} | all-to-all | bytes 1081344 | tf_op jit(solution)/shard_map/all_to_all | solution.py:106
  49.1 1.5 collective-permute-start.1
  50.6 1.7 collective-permute-start
  52.3 7.3 %collective-permute-done.1.back_ref = bf16[64,4224]{1,0:T(8,128)(2,1)S(1)} collective-permute-done((bf16[64,4224]{1,0:T(8,128)(2,1)S(1)}, bf16[64,4224]{1,0:T(8,128)(2,1)S(1)}, u32[]{:S(2)}, u32[]{:S(2)}) %collective-permute-start.1) | collective-permute-done | bytes 540704 | tf_op jit(solution)/shard_map/ppermute | solution.py:120
  60.1 3.0 %collective-permute-start.3 = (bf16[32,4224]{1,0:T(8,128)(2,1)S(1)}, bf16[32,4224]{1,0:T(8,128)(2,1)S(1)}, u32[]{:S(2)}, u32[]{:S(2)}) collective-permute-start(bf16[32,4224]{1,0:T(8,128)(2,1)S(1)} %get-tuple-element.48), channel_id=1, source_target_pairs={{0,3},{1,0},{2,1},{3,2},{4,7},{5,4},{6,5},{7,6},{8,11},{9,8},{10,9... | collective-permute-start | bytes 811016 | tf_op jit(solution)/shard_map/ppermute | solution.py:120
  63.1 0.7 collective-permute-start.7
  63.8 2.5 %collective-permute-start.6 = (bf16[128,4224]{1,0:T(8,128)(2,1)S(1)}, bf16[128,4224]{1,0:T(8,128)(2,1)S(1)}, u32[]{:S(2)}, u32[]{:S(2)}) collective-permute-start(bf16[128,4224]{1,0:T(8,128)(2,1)S(1)} %get-tuple-element.50.refs_0_), channel_id=1, source_target_pairs={{0,4},{1,5},{2,6},{3,7},{4,8},{5,9},{6,10},{7,11},{8,12},{9,13},{1... | collective-permute-start | bytes 3244040 | tf_op jit(solution)/shard_map/ppermute | solution.py:120
  66.3 1.5 shard_map.94._
  67.9 2.2 %collective-permute-done.3 = bf16[32,4224]{1,0:T(8,128)(2,1)S(1)} collective-permute-done((bf16[32,4224]{1,0:T(8,128)(2,1)S(1)}, bf16[32,4224]{1,0:T(8,128)(2,1)S(1)}, u32[]{:S(2)}, u32[]{:S(2)}) %collective-permute-start.3) | collective-permute-done | bytes 270368 | tf_op jit(solution)/shard_map/ppermute | solution.py:120
  70.0 3.7 %collective-permute-done.2 = bf16[32,4224]{1,0:T(8,128)(2,1)S(1)} collective-permute-done((bf16[32,4224]{1,0:T(8,128)(2,1)S(1)}, bf16[32,4224]{1,0:T(8,128)(2,1)S(1)}, u32[]{:S(2)}, u32[]{:S(2)}) %collective-permute-start.2) | collective-permute-done | bytes 270368 | tf_op jit(solution)/shard_map/ppermute | solution.py:120
  73.8 0.8 collective-permute-start.5
  74.6 2.5 %collective-permute-start.4 = (bf16[128,4224]{1,0:T(8,128)(2,1)S(1)}, bf16[128,4224]{1,0:T(8,128)(2,1)S(1)}, u32[]{:S(2)}, u32[]{:S(2)}) collective-permute-start(bf16[128,4224]{1,0:T(8,128)(2,1)S(1)} %pad_maximum_fusion.refs_0_), channel_id=1, source_target_pairs={{0,4},{1,5},{2,6},{3,7},{4,8},{5,9},{6,10},{7,11},{8,12},{9,13},{1... | collective-permute-start | bytes 3244040 | tf_op jit(solution)/shard_map/ppermute | solution.py:120
  77.1 1.5 shard_map.95
  78.6 0.8 collective-permute-done.7.front_ref.refs_1_
  79.5 0.6 shard_map.96
  80.2 3.5 %collective-permute-start.8 = (bf16[48,4224]{1,0:T(8,128)(2,1)S(1)}, bf16[48,4224]{1,0:T(8,128)(2,1)S(1)}, u32[]{:S(2)}, u32[]{:S(2)}) collective-permute-start(bf16[48,4224]{1,0:T(8,128)(2,1)S(1)} %get-tuple-element.56._), channel_id=1, source_target_pairs={{0,4},{1,5},{2,6},{3,7},{4,8},{5,9},{6,10},{7,11},{8,12},{9,13},{1... | collective-permute-start | bytes 1216520 | tf_op jit(solution)/shard_map/ppermute | solution.py:120
  83.7 1.9 %shard_map.97 = (bf16[128,4096]{1,0:T(8,128)(2,1)S(1)}, bf16[128,4096]{1,0:T(8,128)(2,1)S(1)}) custom-call(s32[1]{0:T(128)} %bitcast.1.me_ref, bf16[48,4224]{1,0:T(8,128)(2,1)S(1)} %get-tuple-element.56._, bf16[128,4224]{1,0:T(8,128)(2,1)S(1)} %collective-permute-done.6.back_ref.refs_0_, bf16[128,4224]{1,0:T(8,128)(2,1)S(1)} %collective-permute-done.7.front_ref.refs_1_, ...), custom_call_target="tpu_custom_call" | custom-call | flops 1207959552 | bytes 8912896 | tf_op jit(solution)/shard_map/pallas_call | solution.py:284
  85.6 5.5 %collective-permute-done.5.front_ref.refs_1_ = bf16[128,4224]{1,0:T(8,128)(2,1)S(1)} collective-permute-done((bf16[128,4224]{1,0:T(8,128)(2,1)S(1)}, bf16[128,4224]{1,0:T(8,128)(2,1)S(1)}, u32[]{:S(2)}, u32[]{:S(2)}) %collective-permute-start.5) | collective-permute-done | bytes 1081376 | tf_op jit(solution)/shard_map/ppermute | solution.py:120
  91.0 0.6 shard_map.98
  91.7 3.3 %collective-permute-start.10 = (bf16[48,4224]{1,0:T(8,128)(2,1)S(1)}, bf16[48,4224]{1,0:T(8,128)(2,1)S(1)}, u32[]{:S(2)}, u32[]{:S(2)}) collective-permute-start(bf16[48,4224]{1,0:T(8,128)(2,1)S(1)} %get-tuple-element.64), channel_id=1, source_target_pairs={{0,4},{1,5},{2,6},{3,7},{4,8},{5,9},{6,10},{7,11},{8,12},{9,13},{1... | collective-permute-start | bytes 1216520 | tf_op jit(solution)/shard_map/ppermute | solution.py:120
  95.0 0.4 collective-permute-done.9.refs_1_
  95.4 1.5 shard_map.99
  96.9 3.3 %collective-permute-start.13 = (bf16[48,4096]{1,0:T(8,128)(2,1)S(1)}, bf16[48,4096]{1,0:T(8,128)(2,1)S(1)}, u32[]{:S(2)}, u32[]{:S(2)}) collective-permute-start(bf16[48,4096]{1,0:T(8,128)(2,1)S(1)} %get-tuple-element.69), channel_id=1, source_target_pairs={{0,4},{1,5},{2,6},{3,7},{4,8},{5,9},{6,10},{7,11},{8,12},{9,13},{1... | collective-permute-start | bytes 1179656 | tf_op jit(solution)/shard_map/ppermute | solution.py:120
  100.4 3.7 %collective-permute-done.11.refs_1_ = bf16[48,4224]{1,0:T(8,128)(2,1)S(1)} collective-permute-done((bf16[48,4224]{1,0:T(8,128)(2,1)S(1)}, bf16[48,4224]{1,0:T(8,128)(2,1)S(1)}, u32[]{:S(2)}, u32[]{:S(2)}) %collective-permute-start.11) | collective-permute-done | bytes 405536 | tf_op jit(solution)/shard_map/ppermute | solution.py:120
  104.1 1.5 shard_map.100
  105.6 1.9 %shard_map.101 = (bf16[128,4096]{1,0:T(8,128)(2,1)S(1)}, bf16[128,4096]{1,0:T(8,128)(2,1)S(1)}) custom-call(s32[1]{0:T(128)} %bitcast.1.me_ref, bf16[48,4096]{1,0:T(8,128)(2,1)S(1)} %get-tuple-element.65._, bf16[128,4224]{1,0:T(8,128)(2,1)S(1)} %collective-permute-done.4.back_ref.refs_0_, bf16[128,4224]{1,0:T(8,128)(2,1)S(1)} %collective-permute-done.5.front_ref.refs_1_, ...), custom_call_target="tpu_custom_call" | custom-call | flops 1207959552 | bytes 8912896 | tf_op jit(solution)/shard_map/pallas_call | solution.py:284
  107.5 1.7 collective-permute-done.12.low_ref
  109.2 0.5 shard_map.102
  109.7 2.0 %collective-permute-start.15 = (bf16[128,4096]{1,0:T(8,128)(2,1)S(1)}, bf16[128,4096]{1,0:T(8,128)(2,1)S(1)}, u32[]{:S(2)}, u32[]{:S(2)}) collective-permute-start(bf16[128,4096]{1,0:T(8,128)(2,1)S(1)} %get-tuple-element.73._), channel_id=1, source_target_pairs={{0,12},{1,13},{2,14},{3,15},{4,0},{5,1},{6,2},{7,3},{8,4},{9,5},{1... | collective-permute-start | bytes 3145736 | tf_op jit(solution)/shard_map/ppermute | solution.py:120
  111.7 1.3 collective-permute-start.17
  113.0 0.7 collective-permute-start.16
  113.8 15.0 %collective-permute-done.17.high_ref = bf16[48,4096]{1,0:T(8,128)(2,1)S(1)} collective-permute-done((bf16[48,4096]{1,0:T(8,128)(2,1)S(1)}, bf16[48,4096]{1,0:T(8,128)(2,1)S(1)}, u32[]{:S(2)}, u32[]{:S(2)}) %collective-permute-start.17) | collective-permute-done | bytes 393248 | tf_op jit(solution)/shard_map/ppermute | solution.py:120
  128.7 1.3 collective-permute-done.16.low_ref
  130.0 0.5 shard_map.103
  130.6 2.0 %collective-permute-start.19 = (bf16[128,4096]{1,0:T(8,128)(2,1)S(1)}, bf16[128,4096]{1,0:T(8,128)(2,1)S(1)}, u32[]{:S(2)}, u32[]{:S(2)}) collective-permute-start(bf16[128,4096]{1,0:T(8,128)(2,1)S(1)} %get-tuple-element.82), channel_id=1, source_target_pairs={{0,12},{1,13},{2,14},{3,15},{4,0},{5,1},{6,2},{7,3},{8,4},{9,5},{1... | collective-permute-start | bytes 3145736 | tf_op jit(solution)/shard_map/ppermute | solution.py:120
  132.6 0.5 add_convert_fusion.1
  133.1 13.5 %collective-permute-done.18 = bf16[128,4096]{1,0:T(8,128)(2,1)S(1)} collective-permute-done((bf16[128,4096]{1,0:T(8,128)(2,1)S(1)}, bf16[128,4096]{1,0:T(8,128)(2,1)S(1)}, u32[]{:S(2)}, u32[]{:S(2)}) %collective-permute-start.18) | collective-permute-done | bytes 1048608 | tf_op jit(solution)/shard_map/ppermute | solution.py:120
  146.6 1.5 collective-permute-done.19
  148.1 0.5 add_convert_fusion
  148.7 3.5 %collective-permute-start.22 = (bf16[32,4096]{1,0:T(8,128)(2,1)S(1)}, bf16[32,4096]{1,0:T(8,128)(2,1)S(1)}, u32[]{:S(2)}, u32[]{:S(2)}) collective-permute-start(bf16[32,4096]{1,0:T(8,128)(2,1)S(1)} %get-tuple-element.84), channel_id=1, source_target_pairs={{0,3},{1,0},{2,1},{3,2},{4,7},{5,4},{6,5},{7,6},{8,11},{9,8},{10,9... | collective-permute-start | bytes 786440 | tf_op jit(solution)/shard_map/ppermute | solution.py:120
  152.3 3.8 %collective-permute-done.22 = bf16[32,4096]{1,0:T(8,128)(2,1)S(1)} collective-permute-done((bf16[32,4096]{1,0:T(8,128)(2,1)S(1)}, bf16[32,4096]{1,0:T(8,128)(2,1)S(1)}, u32[]{:S(2)}, u32[]{:S(2)}) %collective-permute-start.22) | collective-permute-done | bytes 262176 | tf_op jit(solution)/shard_map/ppermute | solution.py:120
  156.2 3.8 %collective-permute-start.23 = (bf16[64,4096]{1,0:T(8,128)(2,1)S(1)}, bf16[64,4096]{1,0:T(8,128)(2,1)S(1)}, u32[]{:S(2)}, u32[]{:S(2)}) collective-permute-start(bf16[64,4096]{1,0:T(8,128)(2,1)S(1)} %pad_maximum_fusion.2), channel_id=1, source_target_pairs={{0,3},{1,0},{2,1},{3,2},{4,7},{5,4},{6,5},{7,6},{8,11},{9,8},{10,9... | collective-permute-start | bytes 1572872 | tf_op jit(solution)/shard_map/ppermute | solution.py:120
  160.1 6.5 %collective-permute-done.23 = bf16[64,4096]{1,0:T(8,128)(2,1)S(1)} collective-permute-done((bf16[64,4096]{1,0:T(8,128)(2,1)S(1)}, bf16[64,4096]{1,0:T(8,128)(2,1)S(1)}, u32[]{:S(2)}, u32[]{:S(2)}) %collective-permute-start.23) | collective-permute-done | bytes 524320 | tf_op jit(solution)/shard_map/ppermute | solution.py:120
  166.6 3.9 %collective-permute-done.21 = bf16[64,4096]{1,0:T(8,128)(2,1)S(1)} collective-permute-done((bf16[64,4096]{1,0:T(8,128)(2,1)S(1)}, bf16[64,4096]{1,0:T(8,128)(2,1)S(1)}, u32[]{:S(2)}, u32[]{:S(2)}) %collective-permute-start.21) | collective-permute-done | bytes 524320 | tf_op jit(solution)/shard_map/ppermute | solution.py:120
  170.7 15.9 %all_to_all.33 = bf16[8,8,4096]{2,1,0:T(8,128)(2,1)S(1)} all-to-all(bf16[8,8,4096]{2,1,0:T(8,128)(2,1)S(1)} %fusion), channel_id=1, replica_groups=mesh['dp'=2,'tensor'=8,'expert'=16] {'tensor'}, dimensions={0} | all-to-all | bytes 1048576 | tf_op jit(solution)/shard_map/all_to_all | solution.py:106
  186.7 0.7 fusion.1
  (42 shorter events, 1.9 us)
Async XLA Ops:
  0.0 30.0 %copy-start.3 = (bf16[1,8,4096]{2,1,0:T(8,128)(2,1)S(1)}, bf16[1,8,4096]{2,1,0:T(8,128)(2,1)}, u32[]{:S(2)}) copy-start(bf16[1,8,4096]{2,1,0:T(8,128)(2,1)} %param.11) | copy-start | bytes 196612
  0.0 30.0 %copy-start.4 = (f32[4096]{0:T(1024)S(1)}, f32[4096]{0:T(1024)}, u32[]{:S(2)}) copy-start(f32[4096]{0:T(1024)} %param.12) | copy-start | bytes 49156
  0.0 30.0 %copy-start.5 = (s32[1,8,8]{2,1,0:T(8,128)S(1)}, s32[1,8,8]{2,1,0:T(8,128)}, u32[]{:S(2)}) copy-start(s32[1,8,8]{2,1,0:T(8,128)} %param.13) | copy-start | bytes 772
  0.0 30.0 %copy-start.6 = (s32[1,8,8]{2,1,0:T(8,128)S(1)}, s32[1,8,8]{2,1,0:T(8,128)}, u32[]{:S(2)}) copy-start(s32[1,8,8]{2,1,0:T(8,128)} %param.14) | copy-start | bytes 772
  0.0 66.3 %copy-start.2 = (bf16[1,192,4096]{2,1,0:T(8,128)(2,1)S(1)}, bf16[1,192,4096]{2,1,0:T(8,128)(2,1)}, u32[]{:S(2)}) copy-start(bf16[1,192,4096]{2,1,0:T(8,128)(2,1)} %param.17) | copy-start | bytes 4718596
  3.8 62.6 %copy-start = (bf16[1,192,4096]{2,1,0:T(8,128)(2,1)S(1)}, bf16[1,192,4096]{2,1,0:T(8,128)(2,1)}, u32[]{:S(2)}) copy-start(bf16[1,192,4096]{2,1,0:T(8,128)(2,1)} %param.15) | copy-start | bytes 4718596
  3.8 62.6 %copy-start.1 = (bf16[1,192,4096]{2,1,0:T(8,128)(2,1)S(1)}, bf16[1,192,4096]{2,1,0:T(8,128)(2,1)}, u32[]{:S(2)}) copy-start(bf16[1,192,4096]{2,1,0:T(8,128)(2,1)} %param.16) | copy-start | bytes 4718596
  49.1 10.6 %collective-permute-start.1 = (bf16[64,4224]{1,0:T(8,128)(2,1)S(1)}, bf16[64,4224]{1,0:T(8,128)(2,1)S(1)}, u32[]{:S(2)}, u32[]{:S(2)}) collective-permute-start(bf16[64,4224]{1,0:T(8,128)(2,1)S(1)} %bitcast.36), channel_id=1, source_target_pairs={{0,1},{1,2},{2,3},{3,0},{4,5},{5,6},{6,7},{7,4},{8,9},{9,10},{10,1... | collective-permute-start | bytes 1622024 | tf_op jit(solution)/shard_map/ppermute | solution.py:120
  50.6 9.4 %collective-permute-start = (bf16[64,4224]{1,0:T(8,128)(2,1)S(1)}, bf16[64,4224]{1,0:T(8,128)(2,1)S(1)}, u32[]{:S(2)}, u32[]{:S(2)}) collective-permute-start(bf16[64,4224]{1,0:T(8,128)(2,1)S(1)} %bitcast.37), channel_id=1, source_target_pairs={{0,3},{1,0},{2,1},{3,2},{4,7},{5,4},{6,5},{7,6},{8,11},{9,8},{10,9... | collective-permute-start | bytes 1622024 | tf_op jit(solution)/shard_map/ppermute | solution.py:120
  60.1 10.0 %collective-permute-start.3 = (bf16[32,4224]{1,0:T(8,128)(2,1)S(1)}, bf16[32,4224]{1,0:T(8,128)(2,1)S(1)}, u32[]{:S(2)}, u32[]{:S(2)}) collective-permute-start(bf16[32,4224]{1,0:T(8,128)(2,1)S(1)} %get-tuple-element.48), channel_id=1, source_target_pairs={{0,3},{1,0},{2,1},{3,2},{4,7},{5,4},{6,5},{7,6},{8,11},{9,8},{10,9... | collective-permute-start | bytes 811016 | tf_op jit(solution)/shard_map/ppermute | solution.py:120
  63.1 10.6 %collective-permute-start.2 = (bf16[32,4224]{1,0:T(8,128)(2,1)S(1)}, bf16[32,4224]{1,0:T(8,128)(2,1)S(1)}, u32[]{:S(2)}, u32[]{:S(2)}) collective-permute-start(bf16[32,4224]{1,0:T(8,128)(2,1)S(1)} %get-tuple-element.47._), channel_id=1, source_target_pairs={{0,1},{1,2},{2,3},{3,0},{4,5},{5,6},{6,7},{7,4},{8,9},{9,10},{10,1... | collective-permute-start | bytes 811016 | tf_op jit(solution)/shard_map/ppermute | solution.py:120
  63.1 16.4 %collective-permute-start.7 = (bf16[128,4224]{1,0:T(8,128)(2,1)S(1)}, bf16[128,4224]{1,0:T(8,128)(2,1)S(1)}, u32[]{:S(2)}, u32[]{:S(2)}) collective-permute-start(bf16[128,4224]{1,0:T(8,128)(2,1)S(1)} %get-tuple-element.50.refs_0_), channel_id=1, source_target_pairs={{0,12},{1,13},{2,14},{3,15},{4,0},{5,1},{6,2},{7,3},{8,4},{9,5},{1... | collective-permute-start | bytes 3244040 | tf_op jit(solution)/shard_map/ppermute | solution.py:120
  63.8 15.6 %collective-permute-start.6 = (bf16[128,4224]{1,0:T(8,128)(2,1)S(1)}, bf16[128,4224]{1,0:T(8,128)(2,1)S(1)}, u32[]{:S(2)}, u32[]{:S(2)}) collective-permute-start(bf16[128,4224]{1,0:T(8,128)(2,1)S(1)} %get-tuple-element.50.refs_0_), channel_id=1, source_target_pairs={{0,4},{1,5},{2,6},{3,7},{4,8},{5,9},{6,10},{7,11},{8,12},{9,13},{1... | collective-permute-start | bytes 3244040 | tf_op jit(solution)/shard_map/ppermute | solution.py:120
  73.8 17.2 %collective-permute-start.5 = (bf16[128,4224]{1,0:T(8,128)(2,1)S(1)}, bf16[128,4224]{1,0:T(8,128)(2,1)S(1)}, u32[]{:S(2)}, u32[]{:S(2)}) collective-permute-start(bf16[128,4224]{1,0:T(8,128)(2,1)S(1)} %pad_maximum_fusion.refs_0_), channel_id=1, source_target_pairs={{0,12},{1,13},{2,14},{3,15},{4,0},{5,1},{6,2},{7,3},{8,4},{9,5},{1... | collective-permute-start | bytes 3244040 | tf_op jit(solution)/shard_map/ppermute | solution.py:120
  74.6 16.4 %collective-permute-start.4 = (bf16[128,4224]{1,0:T(8,128)(2,1)S(1)}, bf16[128,4224]{1,0:T(8,128)(2,1)S(1)}, u32[]{:S(2)}, u32[]{:S(2)}) collective-permute-start(bf16[128,4224]{1,0:T(8,128)(2,1)S(1)} %pad_maximum_fusion.refs_0_), channel_id=1, source_target_pairs={{0,4},{1,5},{2,6},{3,7},{4,8},{5,9},{6,10},{7,11},{8,12},{9,13},{1... | collective-permute-start | bytes 3244040 | tf_op jit(solution)/shard_map/ppermute | solution.py:120
  80.1 15.3 %collective-permute-start.9 = (bf16[48,4224]{1,0:T(8,128)(2,1)S(1)}, bf16[48,4224]{1,0:T(8,128)(2,1)S(1)}, u32[]{:S(2)}, u32[]{:S(2)}) collective-permute-start(bf16[48,4224]{1,0:T(8,128)(2,1)S(1)} %get-tuple-element.62), channel_id=1, source_target_pairs={{0,12},{1,13},{2,14},{3,15},{4,0},{5,1},{6,2},{7,3},{8,4},{9,5},{1... | collective-permute-start | bytes 1216520 | tf_op jit(solution)/shard_map/ppermute | solution.py:120
  80.2 15.2 %collective-permute-start.8 = (bf16[48,4224]{1,0:T(8,128)(2,1)S(1)}, bf16[48,4224]{1,0:T(8,128)(2,1)S(1)}, u32[]{:S(2)}, u32[]{:S(2)}) collective-permute-start(bf16[48,4224]{1,0:T(8,128)(2,1)S(1)} %get-tuple-element.56._), channel_id=1, source_target_pairs={{0,4},{1,5},{2,6},{3,7},{4,8},{5,9},{6,10},{7,11},{8,12},{9,13},{1... | collective-permute-start | bytes 1216520 | tf_op jit(solution)/shard_map/ppermute | solution.py:120
  91.7 8.7 %collective-permute-start.10 = (bf16[48,4224]{1,0:T(8,128)(2,1)S(1)}, bf16[48,4224]{1,0:T(8,128)(2,1)S(1)}, u32[]{:S(2)}, u32[]{:S(2)}) collective-permute-start(bf16[48,4224]{1,0:T(8,128)(2,1)S(1)} %get-tuple-element.64), channel_id=1, source_target_pairs={{0,4},{1,5},{2,6},{3,7},{4,8},{5,9},{6,10},{7,11},{8,12},{9,13},{1... | collective-permute-start | bytes 1216520 | tf_op jit(solution)/shard_map/ppermute | solution.py:120
  95.0 9.1 %collective-permute-start.11 = (bf16[48,4224]{1,0:T(8,128)(2,1)S(1)}, bf16[48,4224]{1,0:T(8,128)(2,1)S(1)}, u32[]{:S(2)}, u32[]{:S(2)}) collective-permute-start(bf16[48,4224]{1,0:T(8,128)(2,1)S(1)} %get-tuple-element.61._), channel_id=1, source_target_pairs={{0,12},{1,13},{2,14},{3,15},{4,0},{5,1},{6,2},{7,3},{8,4},{9,5},{1... | collective-permute-start | bytes 1216520 | tf_op jit(solution)/shard_map/ppermute | solution.py:120
  96.9 10.6 %collective-permute-start.13 = (bf16[48,4096]{1,0:T(8,128)(2,1)S(1)}, bf16[48,4096]{1,0:T(8,128)(2,1)S(1)}, u32[]{:S(2)}, u32[]{:S(2)}) collective-permute-start(bf16[48,4096]{1,0:T(8,128)(2,1)S(1)} %get-tuple-element.69), channel_id=1, source_target_pairs={{0,4},{1,5},{2,6},{3,7},{4,8},{5,9},{6,10},{7,11},{8,12},{9,13},{1... | collective-permute-start | bytes 1179656 | tf_op jit(solution)/shard_map/ppermute | solution.py:120
  100.2 9.0 %collective-permute-start.12 = (bf16[48,4096]{1,0:T(8,128)(2,1)S(1)}, bf16[48,4096]{1,0:T(8,128)(2,1)S(1)}, u32[]{:S(2)}, u32[]{:S(2)}) collective-permute-start(bf16[48,4096]{1,0:T(8,128)(2,1)S(1)} %get-tuple-element.63._), channel_id=1, source_target_pairs={{0,12},{1,13},{2,14},{3,15},{4,0},{5,1},{6,2},{7,3},{8,4},{9,5},{1... | collective-permute-start | bytes 1179656 | tf_op jit(solution)/shard_map/ppermute | solution.py:120
  109.6 23.0 %collective-permute-start.14 = (bf16[128,4096]{1,0:T(8,128)(2,1)S(1)}, bf16[128,4096]{1,0:T(8,128)(2,1)S(1)}, u32[]{:S(2)}, u32[]{:S(2)}) collective-permute-start(bf16[128,4096]{1,0:T(8,128)(2,1)S(1)} %get-tuple-element.72), channel_id=1, source_target_pairs={{0,4},{1,5},{2,6},{3,7},{4,8},{5,9},{6,10},{7,11},{8,12},{9,13},{1... | collective-permute-start | bytes 3145736 | tf_op jit(solution)/shard_map/ppermute | solution.py:120
  109.7 22.9 %collective-permute-start.15 = (bf16[128,4096]{1,0:T(8,128)(2,1)S(1)}, bf16[128,4096]{1,0:T(8,128)(2,1)S(1)}, u32[]{:S(2)}, u32[]{:S(2)}) collective-permute-start(bf16[128,4096]{1,0:T(8,128)(2,1)S(1)} %get-tuple-element.73._), channel_id=1, source_target_pairs={{0,12},{1,13},{2,14},{3,15},{4,0},{5,1},{6,2},{7,3},{8,4},{9,5},{1... | collective-permute-start | bytes 3145736 | tf_op jit(solution)/shard_map/ppermute | solution.py:120
  111.7 17.0 %collective-permute-start.17 = (bf16[48,4096]{1,0:T(8,128)(2,1)S(1)}, bf16[48,4096]{1,0:T(8,128)(2,1)S(1)}, u32[]{:S(2)}, u32[]{:S(2)}) collective-permute-start(bf16[48,4096]{1,0:T(8,128)(2,1)S(1)} %get-tuple-element.78), channel_id=1, source_target_pairs={{0,4},{1,5},{2,6},{3,7},{4,8},{5,9},{6,10},{7,11},{8,12},{9,13},{1... | collective-permute-start | bytes 1179656 | tf_op jit(solution)/shard_map/ppermute | solution.py:120
  113.0 17.0 %collective-permute-start.16 = (bf16[48,4096]{1,0:T(8,128)(2,1)S(1)}, bf16[48,4096]{1,0:T(8,128)(2,1)S(1)}, u32[]{:S(2)}, u32[]{:S(2)}) collective-permute-start(bf16[48,4096]{1,0:T(8,128)(2,1)S(1)} %get-tuple-element.65._), channel_id=1, source_target_pairs={{0,12},{1,13},{2,14},{3,15},{4,0},{5,1},{6,2},{7,3},{8,4},{9,5},{1... | collective-permute-start | bytes 1179656 | tf_op jit(solution)/shard_map/ppermute | solution.py:120
  130.5 16.1 %collective-permute-start.18 = (bf16[128,4096]{1,0:T(8,128)(2,1)S(1)}, bf16[128,4096]{1,0:T(8,128)(2,1)S(1)}, u32[]{:S(2)}, u32[]{:S(2)}) collective-permute-start(bf16[128,4096]{1,0:T(8,128)(2,1)S(1)} %get-tuple-element.81), channel_id=1, source_target_pairs={{0,4},{1,5},{2,6},{3,7},{4,8},{5,9},{6,10},{7,11},{8,12},{9,13},{1... | collective-permute-start | bytes 3145736 | tf_op jit(solution)/shard_map/ppermute | solution.py:120
  130.6 17.5 %collective-permute-start.19 = (bf16[128,4096]{1,0:T(8,128)(2,1)S(1)}, bf16[128,4096]{1,0:T(8,128)(2,1)S(1)}, u32[]{:S(2)}, u32[]{:S(2)}) collective-permute-start(bf16[128,4096]{1,0:T(8,128)(2,1)S(1)} %get-tuple-element.82), channel_id=1, source_target_pairs={{0,12},{1,13},{2,14},{3,15},{4,0},{5,1},{6,2},{7,3},{8,4},{9,5},{1... | collective-permute-start | bytes 3145736 | tf_op jit(solution)/shard_map/ppermute | solution.py:120
  148.7 7.4 %collective-permute-start.22 = (bf16[32,4096]{1,0:T(8,128)(2,1)S(1)}, bf16[32,4096]{1,0:T(8,128)(2,1)S(1)}, u32[]{:S(2)}, u32[]{:S(2)}) collective-permute-start(bf16[32,4096]{1,0:T(8,128)(2,1)S(1)} %get-tuple-element.84), channel_id=1, source_target_pairs={{0,3},{1,0},{2,1},{3,2},{4,7},{5,4},{6,5},{7,6},{8,11},{9,8},{10,9... | collective-permute-start | bytes 786440 | tf_op jit(solution)/shard_map/ppermute | solution.py:120
  152.2 7.8 %collective-permute-start.20 = (bf16[32,4096]{1,0:T(8,128)(2,1)S(1)}, bf16[32,4096]{1,0:T(8,128)(2,1)S(1)}, u32[]{:S(2)}, u32[]{:S(2)}) collective-permute-start(bf16[32,4096]{1,0:T(8,128)(2,1)S(1)} %get-tuple-element.83), channel_id=1, source_target_pairs={{0,1},{1,2},{2,3},{3,0},{4,5},{5,6},{6,7},{7,4},{8,9},{9,10},{10,1... | collective-permute-start | bytes 786440 | tf_op jit(solution)/shard_map/ppermute | solution.py:120
  156.2 10.5 %collective-permute-start.23 = (bf16[64,4096]{1,0:T(8,128)(2,1)S(1)}, bf16[64,4096]{1,0:T(8,128)(2,1)S(1)}, u32[]{:S(2)}, u32[]{:S(2)}) collective-permute-start(bf16[64,4096]{1,0:T(8,128)(2,1)S(1)} %pad_maximum_fusion.2), channel_id=1, source_target_pairs={{0,3},{1,0},{2,1},{3,2},{4,7},{5,4},{6,5},{7,6},{8,11},{9,8},{10,9... | collective-permute-start | bytes 1572872 | tf_op jit(solution)/shard_map/ppermute | solution.py:120
  160.1 10.5 %collective-permute-start.21 = (bf16[64,4096]{1,0:T(8,128)(2,1)S(1)}, bf16[64,4096]{1,0:T(8,128)(2,1)S(1)}, u32[]{:S(2)}, u32[]{:S(2)}) collective-permute-start(bf16[64,4096]{1,0:T(8,128)(2,1)S(1)} %pad_maximum_fusion.1), channel_id=1, source_target_pairs={{0,1},{1,2},{2,3},{3,0},{4,5},{5,6},{6,7},{7,4},{8,9},{9,10},{10,1... | collective-permute-start | bytes 1572872 | tf_op jit(solution)/shard_map/ppermute | solution.py:120

commit v9 on v8

--- a/solution.py
+++ b/solution.py
@@ -233,6 +233,50 @@
     )(after, back, front, low, high, low_hot, high_hot)
 
 
+def total_kernel(own_ref, a_ref, b_ref, *outs):
+    start = 0
+    for out in outs:
+        rows = pl.ds(start, out.shape[0])
+        out[...] = add(own_ref[rows, :], a_ref[rows, :], b_ref[rows, :]).astype(jnp.bfloat16)
+        start += out.shape[0]
+
+
+def total(own, got, sizes):
+    rows, width = own.shape
+    return pl.pallas_call(
+        total_kernel,
+        out_shape=[jax.ShapeDtypeStruct((size, width), jnp.bfloat16) for size in sizes],
+        in_specs=[vmem_spec()] * 3,
+        out_specs=[vmem_spec()] * len(sizes),
+        compiler_params=pltpu.CompilerParams(vmem_limit_bytes=GRANT),
+        cost_estimate=pl.CostEstimate(
+            flops=2 * rows * width, bytes_accessed=8 * rows * width, transcendentals=0
+        ),
+    )(own, *got)
+
+
+def join_last_kernel(front_ref, back_ref, up_ref, down_ref, to_front_ref, to_back_ref):
+    half = up_ref.shape[0]
+    to_front_ref[:half, :] = add(front_ref[:half, :], up_ref[...]).astype(jnp.bfloat16)
+    to_front_ref[half:, :] = front_ref[half:, :]
+    to_back_ref[:half, :] = back_ref[:half, :]
+    to_back_ref[half:, :] = add(back_ref[half:, :], down_ref[...]).astype(jnp.bfloat16)
+
+
+def join_last(front, back, up, down):
+    rows, width = front.shape
+    return pl.pallas_call(
+        join_last_kernel,
+        out_shape=[jax.ShapeDtypeStruct((rows, width), jnp.bfloat16)] * 2,
+        in_specs=[vmem_spec()] * 4,
+        out_specs=[vmem_spec()] * 2,
+        compiler_params=pltpu.CompilerParams(vmem_limit_bytes=GRANT),
+        cost_estimate=pl.CostEstimate(
+            flops=rows * width, bytes_accessed=10 * rows * width, transcendentals=0
+        ),
+    )(front, back, up, down)
+
+
 def pair_kernel(own_ref, back_ref, front_ref, pair_ref, low_ref, high_ref):
     size, half = own_ref.shape[0], low_ref.shape[0]
     pair_ref[:size] = own_ref[...]
@@ -344,21 +388,16 @@
     second_far_low, second_far_high = experts(*second_far, after=first_far_low)
     second_down = both(second_far_high, second_far_low, 1)[::-1]
     second_near_out = experts(*second_near, after=second_far_low)
+    first_down, second_down = tie(first_down, second_down)
     first_send = join(second_near_out[0], *first_near_out, *first_down, *first_hot)
     second_send = join(first_send[1], *second_near_out, *second_down, *second_hot)
     first_got = both(*first_send, 1)
     second_got = both(*second_send, 1)
-    first_sum = add(*first_own, *first_got).astype(jnp.bfloat16)
-    (first_sum,), second_own = tie((first_sum,), second_own)
-    second_sum = add(*second_own, *second_got).astype(jnp.bfloat16)
-
+    own, back = total(first_own[0], first_got, (tokens, tokens))
     half = tokens // 2
-    up, down = both(second_sum[tokens : tokens + half], second_sum[tokens + half :], 0)
-    front, back = second_sum[:tokens], first_sum[tokens:]
-    front = jnp.concatenate([add(front[:half], up).astype(jnp.bfloat16), front[half:]])
-    back = jnp.concatenate([back[:half], add(back[half:], down).astype(jnp.bfloat16)])
-    got = both(front, back, 0)
-    mixed = add(first_sum[:tokens], *got).astype(jnp.bfloat16)
+    front, low, high = total(second_own[0], second_got, (tokens, half, half))
+    got = both(*join_last(front, back, *both(low, high, 0)), 0)
+    mixed = add(own, *got).astype(jnp.bfloat16)
     parts = swap_over_tensor(mixed).reshape(tensor_count, -1, model_width)
     layer_out = (hidden + jnp.sum(parts.astype(jnp.float32), axis=0)).astype(jnp.bfloat16)
     return layer_out[None]

time: 189 us -> 180 us (0.952)
  waiting for transfers between devices: 71.2 us -> 63.4 us
    ppermute x24, waiting for transfers between devices: 71.2 us -> 63.4 us  [shift(): return lax.ppermute(value, ('dp', 'expert'), pairs)]
  transfers between devices with their start and end apart: 24 -> 24, of which waited for: 17 -> 16; matrix products, arithmetic and copies ran while one was open for 0% -> 0% of each run, Pallas kernels for 6% -> 7%
where the time goes in v9:
time: 180 us; the launch traced here: 179 us
  waiting for transfers between devices  63.4 us (35%)
  blocking collectives  61 us (34%)
  starting transfers between devices  36 us (20%)
  Pallas kernels  16.9 us (9%)
    ppermute x24, waiting for transfers between devices, shift(): return lax.ppermute(value, ('dp', 'expert'), pairs)  63.4 us
    all_to_all x3, blocking collectives, swap_over_tensor(): lax.all_to_all(value, 'tensor', split_axis=0, concat_axis=0, tiled=True)  61 us
    ppermute x24, starting transfers between devices, shift(): return lax.ppermute(value, ('dp', 'expert'), pairs)  36 us
    pallas_call x6, Pallas kernels, run_expert(): pl.pallas_call(functools.partial(expert_kernel, count), out_shape=[jax.Sh...  9.77 us
    pallas_call x1, Pallas kernels, project(): pl.pallas_call(project_kernel, out_shape=jax.ShapeDtypeStruct((tokens, wi...  3.73 us
  transfers between devices with their start and end apart: 24, of which 16 were waited for; matrix products, arithmetic and copies ran while one was open for 0% of the time, Pallas kernels for 7%

profile of v9, /device:TPU:24, one launch (start us, length us, event | category | flops | bytes accessed | tf_op | source)
XLA Modules:
  0.0 178.6 jit_solution(8402224180597006702)
XLA Ops:
  0.0 3.7 %shard_map.91 = bf16[64,4096]{1,0:T(8,128)(2,1)} custom-call(bf16[64,512]{1,0:T(8,128)(2,1)} %bitcast.46, bf16[512,4096]{1,0:T(8,128)(2,1)} %proj_hbm.1), custom_call_target="tpu_custom_call" | custom-call | flops 268435456 | bytes 4194304 | tf_op jit(solution)/shard_map/pallas_call | solution.py:47
  3.8 26.1 %all_to_all.31 = bf16[8,8,4096]{2,1,0:T(8,128)(2,1)S(1)} all-to-all(bf16[8,8,4096]{2,1,0:T(8,128)(2,1)} %bitcast.45), channel_id=1, replica_groups=mesh['dp'=2,'tensor'=8,'expert'=16] {'tensor'}, dimensions={0} | all-to-all | bytes 1048576 | tf_op jit(solution)/shard_map/all_to_all | solution.py:106
  30.2 18.9 %all_to_all.32 = bf16[8,8,4224]{2,1,0:T(8,128)(2,1)S(1)} all-to-all(bf16[8,8,4224]{2,1,0:T(8,128)(2,1)S(1)} %bitcast.40), channel_id=1, replica_groups=mesh['dp'=2,'tensor'=8,'expert'=16] {'tensor'}, dimensions={0} | all-to-all | bytes 1081344 | tf_op jit(solution)/shard_map/all_to_all | solution.py:106
  49.1 1.5 collective-permute-start.1
  50.6 1.7 collective-permute-start
  52.3 7.3 %collective-permute-done.1.back_ref = bf16[64,4224]{1,0:T(8,128)(2,1)S(1)} collective-permute-done((bf16[64,4224]{1,0:T(8,128)(2,1)S(1)}, bf16[64,4224]{1,0:T(8,128)(2,1)S(1)}, u32[]{:S(2)}, u32[]{:S(2)}) %collective-permute-start.1) | collective-permute-done | bytes 540704 | tf_op jit(solution)/shard_map/ppermute | solution.py:120
  59.7 0.3 collective-permute-done.front_ref
  60.0 3.0 %collective-permute-start.3 = (bf16[32,4224]{1,0:T(8,128)(2,1)S(1)}, bf16[32,4224]{1,0:T(8,128)(2,1)S(1)}, u32[]{:S(2)}, u32[]{:S(2)}) collective-permute-start(bf16[32,4224]{1,0:T(8,128)(2,1)S(1)} %get-tuple-element.57), channel_id=1, source_target_pairs={{0,3},{1,0},{2,1},{3,2},{4,7},{5,4},{6,5},{7,6},{8,11},{9,8},{10,9... | collective-permute-start | bytes 811016 | tf_op jit(solution)/shard_map/ppermute | solution.py:120
  63.1 0.7 collective-permute-start.7
  63.8 2.5 %collective-permute-start.6 = (bf16[128,4224]{1,0:T(8,128)(2,1)S(1)}, bf16[128,4224]{1,0:T(8,128)(2,1)S(1)}, u32[]{:S(2)}, u32[]{:S(2)}) collective-permute-start(bf16[128,4224]{1,0:T(8,128)(2,1)S(1)} %get-tuple-element.59.refs_0_), channel_id=1, source_target_pairs={{0,4},{1,5},{2,6},{3,7},{4,8},{5,9},{6,10},{7,11},{8,12},{9,13},{1... | collective-permute-start | bytes 3244040 | tf_op jit(solution)/shard_map/ppermute | solution.py:120
  66.3 1.5 shard_map.94._.own_ref
  67.8 2.2 %collective-permute-done.3 = bf16[32,4224]{1,0:T(8,128)(2,1)S(1)} collective-permute-done((bf16[32,4224]{1,0:T(8,128)(2,1)S(1)}, bf16[32,4224]{1,0:T(8,128)(2,1)S(1)}, u32[]{:S(2)}, u32[]{:S(2)}) %collective-permute-start.3) | collective-permute-done | bytes 270368 | tf_op jit(solution)/shard_map/ppermute | solution.py:120
  70.0 3.7 %collective-permute-done.2 = bf16[32,4224]{1,0:T(8,128)(2,1)S(1)} collective-permute-done((bf16[32,4224]{1,0:T(8,128)(2,1)S(1)}, bf16[32,4224]{1,0:T(8,128)(2,1)S(1)}, u32[]{:S(2)}, u32[]{:S(2)}) %collective-permute-start.2) | collective-permute-done | bytes 270368 | tf_op jit(solution)/shard_map/ppermute | solution.py:120
  73.8 0.8 collective-permute-start.5
  74.6 2.5 %collective-permute-start.4 = (bf16[128,4224]{1,0:T(8,128)(2,1)S(1)}, bf16[128,4224]{1,0:T(8,128)(2,1)S(1)}, u32[]{:S(2)}, u32[]{:S(2)}) collective-permute-start(bf16[128,4224]{1,0:T(8,128)(2,1)S(1)} %pad_maximum_fusion.refs_0_), channel_id=1, source_target_pairs={{0,4},{1,5},{2,6},{3,7},{4,8},{5,9},{6,10},{7,11},{8,12},{9,13},{1... | collective-permute-start | bytes 3244040 | tf_op jit(solution)/shard_map/ppermute | solution.py:120
  77.1 1.5 shard_map.95.own_ref
  78.6 0.8 collective-permute-done.7.front_ref.refs_1_
  79.4 0.6 shard_map.96
  80.1 3.5 %collective-permute-start.8 = (bf16[48,4224]{1,0:T(8,128)(2,1)S(1)}, bf16[48,4224]{1,0:T(8,128)(2,1)S(1)}, u32[]{:S(2)}, u32[]{:S(2)}) collective-permute-start(bf16[48,4224]{1,0:T(8,128)(2,1)S(1)} %get-tuple-element.65._), channel_id=1, source_target_pairs={{0,4},{1,5},{2,6},{3,7},{4,8},{5,9},{6,10},{7,11},{8,12},{9,13},{1... | collective-permute-start | bytes 1216520 | tf_op jit(solution)/shard_map/ppermute | solution.py:120
  83.6 1.9 %shard_map.97 = (bf16[128,4096]{1,0:T(8,128)(2,1)S(1)}, bf16[128,4096]{1,0:T(8,128)(2,1)S(1)}) custom-call(s32[1]{0:T(128)} %bitcast.1.me_ref, bf16[48,4224]{1,0:T(8,128)(2,1)S(1)} %get-tuple-element.65._, bf16[128,4224]{1,0:T(8,128)(2,1)S(1)} %collective-permute-done.6.back_ref.refs_0_, bf16[128,4224]{1,0:T(8,128)(2,1)S(1)} %collective-permute-done.7.front_ref.refs_1_, ...), custom_call_target="tpu_custom_call" | custom-call | flops 1207959552 | bytes 8912896 | tf_op jit(solution)/shard_map/pallas_call | solution.py:328
  85.6 5.5 %collective-permute-done.5.front_ref.refs_1_ = bf16[128,4224]{1,0:T(8,128)(2,1)S(1)} collective-permute-done((bf16[128,4224]{1,0:T(8,128)(2,1)S(1)}, bf16[128,4224]{1,0:T(8,128)(2,1)S(1)}, u32[]{:S(2)}, u32[]{:S(2)}) %collective-permute-start.5) | collective-permute-done | bytes 1081376 | tf_op jit(solution)/shard_map/ppermute | solution.py:120
  91.0 0.6 shard_map.98
  91.7 3.3 %collective-permute-start.10 = (bf16[48,4224]{1,0:T(8,128)(2,1)S(1)}, bf16[48,4224]{1,0:T(8,128)(2,1)S(1)}, u32[]{:S(2)}, u32[]{:S(2)}) collective-permute-start(bf16[48,4224]{1,0:T(8,128)(2,1)S(1)} %get-tuple-element.73), channel_id=1, source_target_pairs={{0,4},{1,5},{2,6},{3,7},{4,8},{5,9},{6,10},{7,11},{8,12},{9,13},{1... | collective-permute-start | bytes 1216520 | tf_op jit(solution)/shard_map/ppermute | solution.py:120
  95.0 0.4 collective-permute-done.9.refs_1_
  95.4 1.5 shard_map.99
  96.9 3.3 %collective-permute-start.13 = (bf16[48,4096]{1,0:T(8,128)(2,1)S(1)}, bf16[48,4096]{1,0:T(8,128)(2,1)S(1)}, u32[]{:S(2)}, u32[]{:S(2)}) collective-permute-start(bf16[48,4096]{1,0:T(8,128)(2,1)S(1)} %get-tuple-element.78), channel_id=1, source_target_pairs={{0,4},{1,5},{2,6},{3,7},{4,8},{5,9},{6,10},{7,11},{8,12},{9,13},{1... | collective-permute-start | bytes 1179656 | tf_op jit(solution)/shard_map/ppermute | solution.py:120
  100.4 3.7 %collective-permute-done.11.refs_1_ = bf16[48,4224]{1,0:T(8,128)(2,1)S(1)} collective-permute-done((bf16[48,4224]{1,0:T(8,128)(2,1)S(1)}, bf16[48,4224]{1,0:T(8,128)(2,1)S(1)}, u32[]{:S(2)}, u32[]{:S(2)}) %collective-permute-start.11) | collective-permute-done | bytes 405536 | tf_op jit(solution)/shard_map/ppermute | solution.py:120
  104.1 1.5 shard_map.100
  105.6 2.0 %collective-permute-start.14 = (bf16[48,4096]{1,0:T(8,128)(2,1)S(1)}, bf16[48,4096]{1,0:T(8,128)(2,1)S(1)}, u32[]{:S(2)}, u32[]{:S(2)}) collective-permute-start(bf16[48,4096]{1,0:T(8,128)(2,1)S(1)} %get-tuple-element.74._), channel_id=1, source_target_pairs={{0,12},{1,13},{2,14},{3,15},{4,0},{5,1},{6,2},{7,3},{8,4},{9,5},{1... | collective-permute-start | bytes 1179656 | tf_op jit(solution)/shard_map/ppermute | solution.py:120
  107.7 1.9 %shard_map.101 = (bf16[128,4096]{1,0:T(8,128)(2,1)S(1)}, bf16[128,4096]{1,0:T(8,128)(2,1)S(1)}) custom-call(s32[1]{0:T(128)} %bitcast.1.me_ref, bf16[48,4096]{1,0:T(8,128)(2,1)S(1)} %get-tuple-element.74._, bf16[128,4224]{1,0:T(8,128)(2,1)S(1)} %collective-permute-done.4.back_ref.refs_0_, bf16[128,4224]{1,0:T(8,128)(2,1)S(1)} %collective-permute-done.5.front_ref.refs_1_, ...), custom_call_target="tpu_custom_call" | custom-call | flops 1207959552 | bytes 8912896 | tf_op jit(solution)/shard_map/pallas_call | solution.py:328
  109.6 3.8 %collective-permute-done.15.high_ref = bf16[48,4096]{1,0:T(8,128)(2,1)S(1)} collective-permute-done((bf16[48,4096]{1,0:T(8,128)(2,1)S(1)}, bf16[48,4096]{1,0:T(8,128)(2,1)S(1)}, u32[]{:S(2)}, u32[]{:S(2)}) %collective-permute-start.15) | collective-permute-done | bytes 393248 | tf_op jit(solution)/shard_map/ppermute | solution.py:120
  113.4 1.3 collective-permute-done.14.low_ref
  114.7 0.5 shard_map.102
  115.2 0.5 shard_map.104
  115.8 2.0 %collective-permute-start.19 = (bf16[128,4096]{1,0:T(8,128)(2,1)S(1)}, bf16[128,4096]{1,0:T(8,128)(2,1)S(1)}, u32[]{:S(2)}, u32[]{:S(2)}) collective-permute-start(bf16[128,4096]{1,0:T(8,128)(2,1)S(1)} %get-tuple-element.94), channel_id=1, source_target_pairs={{0,12},{1,13},{2,14},{3,15},{4,0},{5,1},{6,2},{7,3},{8,4},{9,5},{1... | collective-permute-start | bytes 3145736 | tf_op jit(solution)/shard_map/ppermute | solution.py:120
  117.8 1.5 collective-permute-start.16
  119.3 0.5 collective-permute-start.17
  119.8 12.4 %collective-permute-done.18.a_ref = bf16[128,4096]{1,0:T(8,128)(2,1)S(1)} collective-permute-done((bf16[128,4096]{1,0:T(8,128)(2,1)S(1)}, bf16[128,4096]{1,0:T(8,128)(2,1)S(1)}, u32[]{:S(2)}, u32[]{:S(2)}) %collective-permute-start.18) | collective-permute-done | bytes 1048608 | tf_op jit(solution)/shard_map/ppermute | solution.py:120
  132.2 1.7 collective-permute-done.19.b_ref
  134.0 0.4 shard_map.105
  134.4 3.3 %collective-permute-start.21 = (bf16[32,4096]{1,0:T(8,128)(2,1)S(1)}, bf16[32,4096]{1,0:T(8,128)(2,1)S(1)}, u32[]{:S(2)}, u32[]{:S(2)}) collective-permute-start(bf16[32,4096]{1,0:T(8,128)(2,1)S(1)} %get-tuple-element.98), channel_id=1, source_target_pairs={{0,3},{1,0},{2,1},{3,2},{4,7},{5,4},{6,5},{7,6},{8,11},{9,8},{10,9... | collective-permute-start | bytes 786440 | tf_op jit(solution)/shard_map/ppermute | solution.py:120
  137.7 11.1 %collective-permute-done.16.a_ref = bf16[128,4096]{1,0:T(8,128)(2,1)S(1)} collective-permute-done((bf16[128,4096]{1,0:T(8,128)(2,1)S(1)}, bf16[128,4096]{1,0:T(8,128)(2,1)S(1)}, u32[]{:S(2)}, u32[]{:S(2)}) %collective-permute-start.16) | collective-permute-done | bytes 1048608 | tf_op jit(solution)/shard_map/ppermute | solution.py:120
  148.9 1.7 collective-permute-done.17.b_ref
  150.6 0.4 shard_map.103
  151.3 3.3 %collective-permute-start.23 = (bf16[64,4096]{1,0:T(8,128)(2,1)S(1)}, bf16[64,4096]{1,0:T(8,128)(2,1)S(1)}, u32[]{:S(2)}, u32[]{:S(2)}) collective-permute-start(bf16[64,4096]{1,0:T(8,128)(2,1)S(1)} %get-tuple-element.100), channel_id=1, source_target_pairs={{0,3},{1,0},{2,1},{3,2},{4,7},{5,4},{6,5},{7,6},{8,11},{9,8},{10,9... | collective-permute-start | bytes 1572872 | tf_op jit(solution)/shard_map/ppermute | solution.py:120
  154.6 7.1 %collective-permute-done.22 = bf16[64,4096]{1,0:T(8,128)(2,1)S(1)} collective-permute-done((bf16[64,4096]{1,0:T(8,128)(2,1)S(1)}, bf16[64,4096]{1,0:T(8,128)(2,1)S(1)}, u32[]{:S(2)}, u32[]{:S(2)}) %collective-permute-start.22) | collective-permute-done | bytes 524320 | tf_op jit(solution)/shard_map/ppermute | solution.py:120
  161.9 16.0 %all_to_all.33 = bf16[8,8,4096]{2,1,0:T(8,128)(2,1)S(1)} all-to-all(bf16[8,8,4096]{2,1,0:T(8,128)(2,1)S(1)} %fusion), channel_id=1, replica_groups=mesh['dp'=2,'tensor'=8,'expert'=16] {'tensor'}, dimensions={0} | all-to-all | bytes 1048576 | tf_op jit(solution)/shard_map/all_to_all | solution.py:106
  178.0 0.7 fusion.1
  (37 shorter events, 1.5 us)
Async XLA Ops:
  0.0 29.9 %copy-start.4 = (f32[4096]{0:T(1024)S(1)}, f32[4096]{0:T(1024)}, u32[]{:S(2)}) copy-start(f32[4096]{0:T(1024)} %param.12) | copy-start | bytes 49156
  0.0 29.9 %copy-start.5 = (s32[1,8,8]{2,1,0:T(8,128)S(1)}, s32[1,8,8]{2,1,0:T(8,128)}, u32[]{:S(2)}) copy-start(s32[1,8,8]{2,1,0:T(8,128)} %param.13) | copy-start | bytes 772
  0.0 29.9 %copy-start.6 = (s32[1,8,8]{2,1,0:T(8,128)S(1)}, s32[1,8,8]{2,1,0:T(8,128)}, u32[]{:S(2)}) copy-start(s32[1,8,8]{2,1,0:T(8,128)} %param.14) | copy-start | bytes 772
  0.0 66.3 %copy-start.2 = (bf16[1,192,4096]{2,1,0:T(8,128)(2,1)S(1)}, bf16[1,192,4096]{2,1,0:T(8,128)(2,1)}, u32[]{:S(2)}) copy-start(bf16[1,192,4096]{2,1,0:T(8,128)(2,1)} %param.17) | copy-start | bytes 4718596
  3.8 26.1 %copy-start.3 = (bf16[1,8,4096]{2,1,0:T(8,128)(2,1)S(1)}, bf16[1,8,4096]{2,1,0:T(8,128)(2,1)}, u32[]{:S(2)}) copy-start(bf16[1,8,4096]{2,1,0:T(8,128)(2,1)} %param.11) | copy-start | bytes 196612
  29.9 36.4 %copy-start.1 = (bf16[1,192,4096]{2,1,0:T(8,128)(2,1)S(1)}, bf16[1,192,4096]{2,1,0:T(8,128)(2,1)}, u32[]{:S(2)}) copy-start(bf16[1,192,4096]{2,1,0:T(8,128)(2,1)} %param.16) | copy-start | bytes 4718596
  49.1 17.2 %copy-start = (bf16[1,192,4096]{2,1,0:T(8,128)(2,1)S(1)}, bf16[1,192,4096]{2,1,0:T(8,128)(2,1)}, u32[]{:S(2)}) copy-start(bf16[1,192,4096]{2,1,0:T(8,128)(2,1)} %param.15) | copy-start | bytes 4718596
  49.1 10.6 %collective-permute-start.1 = (bf16[64,4224]{1,0:T(8,128)(2,1)S(1)}, bf16[64,4224]{1,0:T(8,128)(2,1)S(1)}, u32[]{:S(2)}, u32[]{:S(2)}) collective-permute-start(bf16[64,4224]{1,0:T(8,128)(2,1)S(1)} %bitcast.36), channel_id=1, source_target_pairs={{0,1},{1,2},{2,3},{3,0},{4,5},{5,6},{6,7},{7,4},{8,9},{9,10},{10,1... | collective-permute-start | bytes 1622024 | tf_op jit(solution)/shard_map/ppermute | solution.py:120
  50.6 9.4 %collective-permute-start = (bf16[64,4224]{1,0:T(8,128)(2,1)S(1)}, bf16[64,4224]{1,0:T(8,128)(2,1)S(1)}, u32[]{:S(2)}, u32[]{:S(2)}) collective-permute-start(bf16[64,4224]{1,0:T(8,128)(2,1)S(1)} %bitcast.37), channel_id=1, source_target_pairs={{0,3},{1,0},{2,1},{3,2},{4,7},{5,4},{6,5},{7,6},{8,11},{9,8},{10,9... | collective-permute-start | bytes 1622024 | tf_op jit(solution)/shard_map/ppermute | solution.py:120
  60.0 10.0 %collective-permute-start.3 = (bf16[32,4224]{1,0:T(8,128)(2,1)S(1)}, bf16[32,4224]{1,0:T(8,128)(2,1)S(1)}, u32[]{:S(2)}, u32[]{:S(2)}) collective-permute-start(bf16[32,4224]{1,0:T(8,128)(2,1)S(1)} %get-tuple-element.57), channel_id=1, source_target_pairs={{0,3},{1,0},{2,1},{3,2},{4,7},{5,4},{6,5},{7,6},{8,11},{9,8},{10,9... | collective-permute-start | bytes 811016 | tf_op jit(solution)/shard_map/ppermute | solution.py:120
  63.1 10.6 %collective-permute-start.2 = (bf16[32,4224]{1,0:T(8,128)(2,1)S(1)}, bf16[32,4224]{1,0:T(8,128)(2,1)S(1)}, u32[]{:S(2)}, u32[]{:S(2)}) collective-permute-start(bf16[32,4224]{1,0:T(8,128)(2,1)S(1)} %get-tuple-element.56._), channel_id=1, source_target_pairs={{0,1},{1,2},{2,3},{3,0},{4,5},{5,6},{6,7},{7,4},{8,9},{9,10},{10,1... | collective-permute-start | bytes 811016 | tf_op jit(solution)/shard_map/ppermute | solution.py:120
  63.1 16.4 %collective-permute-start.7 = (bf16[128,4224]{1,0:T(8,128)(2,1)S(1)}, bf16[128,4224]{1,0:T(8,128)(2,1)S(1)}, u32[]{:S(2)}, u32[]{:S(2)}) collective-permute-start(bf16[128,4224]{1,0:T(8,128)(2,1)S(1)} %get-tuple-element.59.refs_0_), channel_id=1, source_target_pairs={{0,12},{1,13},{2,14},{3,15},{4,0},{5,1},{6,2},{7,3},{8,4},{9,5},{1... | collective-permute-start | bytes 3244040 | tf_op jit(solution)/shard_map/ppermute | solution.py:120
  63.8 15.6 %collective-permute-start.6 = (bf16[128,4224]{1,0:T(8,128)(2,1)S(1)}, bf16[128,4224]{1,0:T(8,128)(2,1)S(1)}, u32[]{:S(2)}, u32[]{:S(2)}) collective-permute-start(bf16[128,4224]{1,0:T(8,128)(2,1)S(1)} %get-tuple-element.59.refs_0_), channel_id=1, source_target_pairs={{0,4},{1,5},{2,6},{3,7},{4,8},{5,9},{6,10},{7,11},{8,12},{9,13},{1... | collective-permute-start | bytes 3244040 | tf_op jit(solution)/shard_map/ppermute | solution.py:120
  73.8 17.2 %collective-permute-start.5 = (bf16[128,4224]{1,0:T(8,128)(2,1)S(1)}, bf16[128,4224]{1,0:T(8,128)(2,1)S(1)}, u32[]{:S(2)}, u32[]{:S(2)}) collective-permute-start(bf16[128,4224]{1,0:T(8,128)(2,1)S(1)} %pad_maximum_fusion.refs_0_), channel_id=1, source_target_pairs={{0,12},{1,13},{2,14},{3,15},{4,0},{5,1},{6,2},{7,3},{8,4},{9,5},{1... | collective-permute-start | bytes 3244040 | tf_op jit(solution)/shard_map/ppermute | solution.py:120
  74.6 16.4 %collective-permute-start.4 = (bf16[128,4224]{1,0:T(8,128)(2,1)S(1)}, bf16[128,4224]{1,0:T(8,128)(2,1)S(1)}, u32[]{:S(2)}, u32[]{:S(2)}) collective-permute-start(bf16[128,4224]{1,0:T(8,128)(2,1)S(1)} %pad_maximum_fusion.refs_0_), channel_id=1, source_target_pairs={{0,4},{1,5},{2,6},{3,7},{4,8},{5,9},{6,10},{7,11},{8,12},{9,13},{1... | collective-permute-start | bytes 3244040 | tf_op jit(solution)/shard_map/ppermute | solution.py:120
  80.1 15.3 %collective-permute-start.9 = (bf16[48,4224]{1,0:T(8,128)(2,1)S(1)}, bf16[48,4224]{1,0:T(8,128)(2,1)S(1)}, u32[]{:S(2)}, u32[]{:S(2)}) collective-permute-start(bf16[48,4224]{1,0:T(8,128)(2,1)S(1)} %get-tuple-element.71), channel_id=1, source_target_pairs={{0,12},{1,13},{2,14},{3,15},{4,0},{5,1},{6,2},{7,3},{8,4},{9,5},{1... | collective-permute-start | bytes 1216520 | tf_op jit(solution)/shard_map/ppermute | solution.py:120
  80.1 15.2 %collective-permute-start.8 = (bf16[48,4224]{1,0:T(8,128)(2,1)S(1)}, bf16[48,4224]{1,0:T(8,128)(2,1)S(1)}, u32[]{:S(2)}, u32[]{:S(2)}) collective-permute-start(bf16[48,4224]{1,0:T(8,128)(2,1)S(1)} %get-tuple-element.65._), channel_id=1, source_target_pairs={{0,4},{1,5},{2,6},{3,7},{4,8},{5,9},{6,10},{7,11},{8,12},{9,13},{1... | collective-permute-start | bytes 1216520 | tf_op jit(solution)/shard_map/ppermute | solution.py:120
  91.7 8.7 %collective-permute-start.10 = (bf16[48,4224]{1,0:T(8,128)(2,1)S(1)}, bf16[48,4224]{1,0:T(8,128)(2,1)S(1)}, u32[]{:S(2)}, u32[]{:S(2)}) collective-permute-start(bf16[48,4224]{1,0:T(8,128)(2,1)S(1)} %get-tuple-element.73), channel_id=1, source_target_pairs={{0,4},{1,5},{2,6},{3,7},{4,8},{5,9},{6,10},{7,11},{8,12},{9,13},{1... | collective-permute-start | bytes 1216520 | tf_op jit(solution)/shard_map/ppermute | solution.py:120
  95.0 9.1 %collective-permute-start.11 = (bf16[48,4224]{1,0:T(8,128)(2,1)S(1)}, bf16[48,4224]{1,0:T(8,128)(2,1)S(1)}, u32[]{:S(2)}, u32[]{:S(2)}) collective-permute-start(bf16[48,4224]{1,0:T(8,128)(2,1)S(1)} %get-tuple-element.70._), channel_id=1, source_target_pairs={{0,12},{1,13},{2,14},{3,15},{4,0},{5,1},{6,2},{7,3},{8,4},{9,5},{1... | collective-permute-start | bytes 1216520 | tf_op jit(solution)/shard_map/ppermute | solution.py:120
  96.9 12.7 %collective-permute-start.13 = (bf16[48,4096]{1,0:T(8,128)(2,1)S(1)}, bf16[48,4096]{1,0:T(8,128)(2,1)S(1)}, u32[]{:S(2)}, u32[]{:S(2)}) collective-permute-start(bf16[48,4096]{1,0:T(8,128)(2,1)S(1)} %get-tuple-element.78), channel_id=1, source_target_pairs={{0,4},{1,5},{2,6},{3,7},{4,8},{5,9},{6,10},{7,11},{8,12},{9,13},{1... | collective-permute-start | bytes 1179656 | tf_op jit(solution)/shard_map/ppermute | solution.py:120
  100.2 9.4 %collective-permute-start.12 = (bf16[48,4096]{1,0:T(8,128)(2,1)S(1)}, bf16[48,4096]{1,0:T(8,128)(2,1)S(1)}, u32[]{:S(2)}, u32[]{:S(2)}) collective-permute-start(bf16[48,4096]{1,0:T(8,128)(2,1)S(1)} %get-tuple-element.72._), channel_id=1, source_target_pairs={{0,12},{1,13},{2,14},{3,15},{4,0},{5,1},{6,2},{7,3},{8,4},{9,5},{1... | collective-permute-start | bytes 1179656 | tf_op jit(solution)/shard_map/ppermute | solution.py:120
  105.6 7.9 %collective-permute-start.15 = (bf16[48,4096]{1,0:T(8,128)(2,1)S(1)}, bf16[48,4096]{1,0:T(8,128)(2,1)S(1)}, u32[]{:S(2)}, u32[]{:S(2)}) collective-permute-start(bf16[48,4096]{1,0:T(8,128)(2,1)S(1)} %get-tuple-element.79), channel_id=1, source_target_pairs={{0,4},{1,5},{2,6},{3,7},{4,8},{5,9},{6,10},{7,11},{8,12},{9,13},{1... | collective-permute-start | bytes 1179656 | tf_op jit(solution)/shard_map/ppermute | solution.py:120
  105.6 9.1 %collective-permute-start.14 = (bf16[48,4096]{1,0:T(8,128)(2,1)S(1)}, bf16[48,4096]{1,0:T(8,128)(2,1)S(1)}, u32[]{:S(2)}, u32[]{:S(2)}) collective-permute-start(bf16[48,4096]{1,0:T(8,128)(2,1)S(1)} %get-tuple-element.74._), channel_id=1, source_target_pairs={{0,12},{1,13},{2,14},{3,15},{4,0},{5,1},{6,2},{7,3},{8,4},{9,5},{1... | collective-permute-start | bytes 1179656 | tf_op jit(solution)/shard_map/ppermute | solution.py:120
  115.7 16.6 %collective-permute-start.18 = (bf16[128,4096]{1,0:T(8,128)(2,1)S(1)}, bf16[128,4096]{1,0:T(8,128)(2,1)S(1)}, u32[]{:S(2)}, u32[]{:S(2)}) collective-permute-start(bf16[128,4096]{1,0:T(8,128)(2,1)S(1)} %get-tuple-element.93), channel_id=1, source_target_pairs={{0,4},{1,5},{2,6},{3,7},{4,8},{5,9},{6,10},{7,11},{8,12},{9,13},{1... | collective-permute-start | bytes 3145736 | tf_op jit(solution)/shard_map/ppermute | solution.py:120
  115.8 18.2 %collective-permute-start.19 = (bf16[128,4096]{1,0:T(8,128)(2,1)S(1)}, bf16[128,4096]{1,0:T(8,128)(2,1)S(1)}, u32[]{:S(2)}, u32[]{:S(2)}) collective-permute-start(bf16[128,4096]{1,0:T(8,128)(2,1)S(1)} %get-tuple-element.94), channel_id=1, source_target_pairs={{0,12},{1,13},{2,14},{3,15},{4,0},{5,1},{6,2},{7,3},{8,4},{9,5},{1... | collective-permute-start | bytes 3145736 | tf_op jit(solution)/shard_map/ppermute | solution.py:120
  117.8 31.1 %collective-permute-start.16 = (bf16[128,4096]{1,0:T(8,128)(2,1)S(1)}, bf16[128,4096]{1,0:T(8,128)(2,1)S(1)}, u32[]{:S(2)}, u32[]{:S(2)}) collective-permute-start(bf16[128,4096]{1,0:T(8,128)(2,1)S(1)} %get-tuple-element.84), channel_id=1, source_target_pairs={{0,4},{1,5},{2,6},{3,7},{4,8},{5,9},{6,10},{7,11},{8,12},{9,13},{1... | collective-permute-start | bytes 3145736 | tf_op jit(solution)/shard_map/ppermute | solution.py:120
  119.3 31.3 %collective-permute-start.17 = (bf16[128,4096]{1,0:T(8,128)(2,1)S(1)}, bf16[128,4096]{1,0:T(8,128)(2,1)S(1)}, u32[]{:S(2)}, u32[]{:S(2)}) collective-permute-start(bf16[128,4096]{1,0:T(8,128)(2,1)S(1)} %get-tuple-element.85._), channel_id=1, source_target_pairs={{0,12},{1,13},{2,14},{3,15},{4,0},{5,1},{6,2},{7,3},{8,4},{9,5},{1... | collective-permute-start | bytes 3145736 | tf_op jit(solution)/shard_map/ppermute | solution.py:120
  134.3 16.7 %collective-permute-start.20 = (bf16[32,4096]{1,0:T(8,128)(2,1)S(1)}, bf16[32,4096]{1,0:T(8,128)(2,1)S(1)}, u32[]{:S(2)}, u32[]{:S(2)}) collective-permute-start(bf16[32,4096]{1,0:T(8,128)(2,1)S(1)} %get-tuple-element.97), channel_id=1, source_target_pairs={{0,1},{1,2},{2,3},{3,0},{4,5},{5,6},{6,7},{7,4},{8,9},{9,10},{10,1... | collective-permute-start | bytes 786440 | tf_op jit(solution)/shard_map/ppermute | solution.py:120
  134.4 16.6 %collective-permute-start.21 = (bf16[32,4096]{1,0:T(8,128)(2,1)S(1)}, bf16[32,4096]{1,0:T(8,128)(2,1)S(1)}, u32[]{:S(2)}, u32[]{:S(2)}) collective-permute-start(bf16[32,4096]{1,0:T(8,128)(2,1)S(1)} %get-tuple-element.98), channel_id=1, source_target_pairs={{0,3},{1,0},{2,1},{3,2},{4,7},{5,4},{6,5},{7,6},{8,11},{9,8},{10,9... | collective-permute-start | bytes 786440 | tf_op jit(solution)/shard_map/ppermute | solution.py:120
  151.2 10.5 %collective-permute-start.22 = (bf16[64,4096]{1,0:T(8,128)(2,1)S(1)}, bf16[64,4096]{1,0:T(8,128)(2,1)S(1)}, u32[]{:S(2)}, u32[]{:S(2)}) collective-permute-start(bf16[64,4096]{1,0:T(8,128)(2,1)S(1)} %get-tuple-element.99), channel_id=1, source_target_pairs={{0,1},{1,2},{2,3},{3,0},{4,5},{5,6},{6,7},{7,4},{8,9},{9,10},{10,1... | collective-permute-start | bytes 1572872 | tf_op jit(solution)/shard_map/ppermute | solution.py:120
  151.3 10.4 %collective-permute-start.23 = (bf16[64,4096]{1,0:T(8,128)(2,1)S(1)}, bf16[64,4096]{1,0:T(8,128)(2,1)S(1)}, u32[]{:S(2)}, u32[]{:S(2)}) collective-permute-start(bf16[64,4096]{1,0:T(8,128)(2,1)S(1)} %get-tuple-element.100), channel_id=1, source_target_pairs={{0,3},{1,0},{2,1},{3,2},{4,7},{5,4},{6,5},{7,6},{8,11},{9,8},{10,9... | collective-permute-start | bytes 1572872 | tf_op jit(solution)/shard_map/ppermute | solution.py:120

commit v10 on v9

--- a/solution.py
+++ b/solution.py
@@ -120,15 +120,6 @@
     return lax.ppermute(value, ("dp", "expert"), pairs)
 
 
-def send_round(block, turn):
-    return shift(block, turn, 1), shift(block, turn, -1)
-
-
-def send_on(back, front, turn):
-    half = back.shape[0] // 2
-    return shift(back[:half], turn, 1), shift(front[half:], turn, -1)
-
-
 def add(*values):
     total = values[0].astype(jnp.float32)
     for value in values[1:]:
@@ -159,33 +150,73 @@
     return jnp.where(fills, 1.0, 0.0).astype(jnp.bfloat16)
 
 
-def pack_kernel(me_ref, dp_ref, back_ref, front_ref, low_ref, high_ref, low_hot_ref, high_hot_ref):
-    slots, width = low_ref.shape
-    half = back_ref.shape[0] // 2
-    me = me_ref[0]
-    row, col = me // SIDE, me % SIDE
+def beside(me_ref, dp_ref):
+    row, col = me_ref[0] // SIDE, me_ref[0] % SIDE
     first = dp_ref[0] == 0
     ahead = jnp.where(first, (row + 1) % SIDE * SIDE + col, row * SIDE + (col + 1) % SIDE)
-    behind = jnp.where(
-        first, (row + SIDE - 1) % SIDE * SIDE + col, row * SIDE + (col + SIDE - 1) % SIDE
-    )
-    tail = width - LANES
+    back_row, back_col = (row + SIDE - 1) % SIDE, (col + SIDE - 1) % SIDE
+    return ahead, jnp.where(first, back_row * SIDE + col, row * SIDE + back_col)
+
+
+def chosen(hot, rows):
+    return jnp.dot(hot, rows, preferred_element_type=jnp.float32).astype(jnp.bfloat16)
+
+
+def unpacked(hot_ref, value):
+    over_slots = (((0,), (0,)), ((), ()))
+    return lax.dot_general(hot_ref[...], value, over_slots, preferred_element_type=jnp.float32)
+
+
+def line_kernel(me_ref, dp_ref, _, low_ref, *refs):
+    *highs, line_ref, to_ahead_ref, to_behind_ref, ahead_hot_ref, behind_hot_ref = refs
+    slots, half = ahead_hot_ref.shape
+    ahead, behind = beside(me_ref, dp_ref)
+    tail = low_ref.shape[1] - LANES
+    low, high = low_ref[...], jnp.concatenate([ref[...] for ref in highs])
+    ahead_hot = packing(high[:, tail:], ahead, slots)
+    behind_hot = packing(low[:, tail:], behind, slots)
+    line_ref[:half, :] = low
+    line_ref[half:, :] = high
+    to_ahead_ref[:half, :] = low
+    to_ahead_ref[half:, :] = chosen(ahead_hot, high)
+    to_behind_ref[:slots, :] = chosen(behind_hot, low)
+    to_behind_ref[slots:, :] = high
+    ahead_hot_ref[...] = ahead_hot
+    behind_hot_ref[...] = behind_hot
+
+
+def make_line(me, dp, after, low, *highs):
+    half, width = low.shape
+    slots = half // TOP_TOKENS * CAP
+    smem = pl.BlockSpec(memory_space=pltpu.SMEM)
+    shapes = [(2 * half, width)] + [(half + slots, width)] * 2 + [(slots, half)] * 2
+    return pl.pallas_call(
+        line_kernel,
+        out_shape=[jax.ShapeDtypeStruct(shape, jnp.bfloat16) for shape in shapes],
+        in_specs=[smem] * 2 + [pl.BlockSpec(memory_space=pl.ANY)] + [vmem_spec()] * (1 + len(highs)),
+        out_specs=[vmem_spec()] * 5,
+        compiler_params=pltpu.CompilerParams(vmem_limit_bytes=GRANT),
+        cost_estimate=pl.CostEstimate(
+            flops=4 * half * slots * width, bytes_accessed=12 * half * width, transcendentals=0
+        ),
+    )(me, dp, after, low, *highs)
+
+
+def pack_kernel(me_ref, dp_ref, back_ref, front_ref, low_ref, high_ref, low_hot_ref, high_hot_ref):
+    slots, half = low_hot_ref.shape
+    ahead, behind = beside(me_ref, dp_ref)
+    tail = low_ref.shape[1] - LANES
     low_hot = packing(back_ref[:half, tail:], ahead, slots)
-    high_hot = packing(front_ref[half:, tail:], behind, slots)
+    high_hot = packing(front_ref[slots:, tail:], behind, slots)
     low_hot_ref[...] = low_hot
     high_hot_ref[...] = high_hot
-    low_ref[...] = jnp.dot(
-        low_hot, back_ref[:half, :], preferred_element_type=jnp.float32
-    ).astype(jnp.bfloat16)
-    high_ref[...] = jnp.dot(
-        high_hot, front_ref[half:, :], preferred_element_type=jnp.float32
-    ).astype(jnp.bfloat16)
-
-
-def pack(me, dp, back, front):
+    low_ref[...] = chosen(low_hot, back_ref[:half, :])
+    high_ref[...] = chosen(high_hot, front_ref[slots:, :])
+
+
+def pack(me, dp, half, back, front):
     rows, width = back.shape
-    half = rows // 2
-    slots = half // TOP_TOKENS * CAP
+    slots = rows - half
     smem = pl.BlockSpec(memory_space=pltpu.SMEM)
     return pl.pallas_call(
         pack_kernel,
@@ -195,7 +226,7 @@
         out_specs=[vmem_spec()] * 4,
         compiler_params=pltpu.CompilerParams(vmem_limit_bytes=GRANT),
         cost_estimate=pl.CostEstimate(
-            flops=2 * rows * slots * width, bytes_accessed=4 * rows * width, transcendentals=0
+            flops=4 * half * slots * width, bytes_accessed=4 * rows * width, transcendentals=0
         ),
     )(me, dp, back, front)
 
@@ -203,20 +234,13 @@
 def join_kernel(
     _, back_ref, front_ref, low_ref, high_ref, low_hot_ref, high_hot_ref, to_front_ref, to_back_ref
 ):
-    half = back_ref.shape[0] // 2
-    first = (((0,), (0,)), ((), ()))
-
-    def unpacked(hot_ref, value_ref):
-        return lax.dot_general(
-            hot_ref[...], value_ref[...], first, preferred_element_type=jnp.float32
-        )
-
-    low = back_ref[:half, :].astype(jnp.float32) + unpacked(low_hot_ref, low_ref)
-    high = front_ref[half:, :].astype(jnp.float32) + unpacked(high_hot_ref, high_ref)
+    slots, half = low_hot_ref.shape
+    low = back_ref[:half, :].astype(jnp.float32) + unpacked(low_hot_ref, low_ref[...])
+    high = front_ref[slots:, :].astype(jnp.float32) + unpacked(high_hot_ref, high_ref[...])
     to_back_ref[:half, :] = low.astype(jnp.bfloat16)
     to_back_ref[half:, :] = back_ref[half:, :]
-    to_front_ref[:half, :] = front_ref[:half, :]
-    to_front_ref[half:, :] = high.astype(jnp.bfloat16)
+    to_front_ref[:slots, :] = front_ref[:slots, :]
+    to_front_ref[slots:, :] = high.astype(jnp.bfloat16)
 
 
 def join(after, back, front, low, high, low_hot, high_hot):
@@ -233,26 +257,29 @@
     )(after, back, front, low, high, low_hot, high_hot)
 
 
-def total_kernel(own_ref, a_ref, b_ref, *outs):
-    start = 0
-    for out in outs:
-        rows = pl.ds(start, out.shape[0])
-        out[...] = add(own_ref[rows, :], a_ref[rows, :], b_ref[rows, :]).astype(jnp.bfloat16)
-        start += out.shape[0]
-
-
-def total(own, got, sizes):
+def total_kernel(own_ref, back_ref, front_ref, ahead_hot_ref, behind_hot_ref, low_ref, *highs):
+    slots, half = ahead_hot_ref.shape
+    low = add(own_ref[:half, :], front_ref[:half, :]) + unpacked(behind_hot_ref, back_ref[:slots, :])
+    low_ref[...] = low.astype(jnp.bfloat16)
+    high = add(own_ref[half:, :], back_ref[slots:, :]) + unpacked(ahead_hot_ref, front_ref[half:, :])
+    high = high.astype(jnp.bfloat16)
+    size = highs[0].shape[0]
+    for i, out in enumerate(highs):
+        out[...] = high[i * size : (i + 1) * size]
+
+
+def total(own, got, hots, sizes):
     rows, width = own.shape
     return pl.pallas_call(
         total_kernel,
         out_shape=[jax.ShapeDtypeStruct((size, width), jnp.bfloat16) for size in sizes],
-        in_specs=[vmem_spec()] * 3,
+        in_specs=[vmem_spec()] * 5,
         out_specs=[vmem_spec()] * len(sizes),
         compiler_params=pltpu.CompilerParams(vmem_limit_bytes=GRANT),
         cost_estimate=pl.CostEstimate(
             flops=2 * rows * width, bytes_accessed=8 * rows * width, transcendentals=0
         ),
-    )(own, *got)
+    )(own, *got, *hots)
 
 
 def join_last_kernel(front_ref, back_ref, up_ref, down_ref, to_front_ref, to_back_ref):
@@ -275,27 +302,6 @@
             flops=rows * width, bytes_accessed=10 * rows * width, transcendentals=0
         ),
     )(front, back, up, down)
-
-
-def pair_kernel(own_ref, back_ref, front_ref, pair_ref, low_ref, high_ref):
-    size, half = own_ref.shape[0], low_ref.shape[0]
-    pair_ref[:size] = own_ref[...]
-    pair_ref[size:] = back_ref[...]
-    low_ref[...] = back_ref[:half]
-    high_ref[...] = front_ref[half:]
-
-
-def pair(own, back, front):
-    size, width = own.shape
-    shapes = [(2 * size, width), (size // 2, width), (size // 2, width)]
-    return pl.pallas_call(
-        pair_kernel,
-        out_shape=[jax.ShapeDtypeStruct(shape, own.dtype) for shape in shapes],
-        in_specs=[vmem_spec()] * 3,
-        out_specs=[vmem_spec()] * 3,
-        compiler_params=pltpu.CompilerParams(vmem_limit_bytes=GRANT),
-        cost_estimate=pl.CostEstimate(flops=0, bytes_accessed=12 * size * width, transcendentals=0),
-    )(own, back, front)
 
 
 def expert_kernel(count, me_ref, _, *refs):
@@ -367,21 +373,23 @@
     def both(ahead, behind, turn):
         return shift(ahead, turn, 1), shift(behind, turn, -1)
 
-    back, front = send_round(group, 0)
-    first, low, high = pair(group, back, front)
-    first_near = send_round(first, 1)
-    far = both(low, high, 0)
-    first_own = experts(first, after=low)
-    second = jnp.concatenate([front, *far])
-    (second,), first_own = tie((second,), first_own)
-    second_near = send_round(second, 1)
+    half = tokens // 2
+    back, front = both(group, group, 0)
+    first, *first_sent, first_ahead, first_behind = make_line(who, side, front, group, back)
+    first_near = both(*first_sent, 1)
+    far = both(back[:half], front[half:], 0)
+    first_own = experts(first, after=back)
+    second, *second_sent, second_ahead, second_behind = make_line(
+        who, side, first_own[0], front, *far
+    )
+    second_near = both(*second_sent, 1)
     second_own = experts(second, after=first_own[0])
     first_near, second_own = tie(first_near, second_own)
-    low, high, *first_hot = pack(who, side, *first_near)
+    low, high, *first_hot = pack(who, side, tokens, *first_near)
     first_far = both(low, high, 1)
     first_near_out = experts(*first_near, after=low)
     second_near, first_near_out = tie(second_near, first_near_out)
-    low, high, *second_hot = pack(who, side, *second_near)
+    low, high, *second_hot = pack(who, side, tokens, *second_near)
     second_far = both(low, high, 1)
     first_far_low, first_far_high = experts(*first_far, after=high)
     first_down = both(first_far_high, first_far_low, 1)[::-1]
@@ -393,9 +401,9 @@
     second_send = join(first_send[1], *second_near_out, *second_down, *second_hot)
     first_got = both(*first_send, 1)
     second_got = both(*second_send, 1)
-    own, back = total(first_own[0], first_got, (tokens, tokens))
-    half = tokens // 2
-    front, low, high = total(second_own[0], second_got, (tokens, half, half))
+    own, back = total(first_own[0], first_got, (first_ahead, first_behind), (tokens, tokens))
+    hots = (second_ahead, second_behind)
+    front, low, high = total(second_own[0], second_got, hots, (tokens, half, half))
     got = both(*join_last(front, back, *both(low, high, 0)), 0)
     mixed = add(own, *got).astype(jnp.bfloat16)
     parts = swap_over_tensor(mixed).reshape(tensor_count, -1, model_width)

time: 180 us -> 174 us (0.967)
  starting transfers between devices: 36 us -> 31.2 us
    ppermute x24, starting transfers between devices: 36 us -> 31.2 us  [shift(): return lax.ppermute(value, ('dp', 'expert'), pairs)]
where the time goes in v10:
time: 174 us; the launch traced here: 173 us
  waiting for transfers between devices  62.1 us (36%)
  blocking collectives  61 us (35%)
  starting transfers between devices  31.2 us (18%)
  Pallas kernels  17.9 us (10%)
    ppermute x24, waiting for transfers between devices, shift(): return lax.ppermute(value, ('dp', 'expert'), pairs)  62.1 us
    all_to_all x3, blocking collectives, swap_over_tensor(): lax.all_to_all(value, 'tensor', split_axis=0, concat_axis=0, tiled=True)  61 us
    ppermute x24, starting transfers between devices, shift(): return lax.ppermute(value, ('dp', 'expert'), pairs)  31.2 us
    pallas_call x6, Pallas kernels, run_expert(): pl.pallas_call(functools.partial(expert_kernel, count), out_shape=[jax.Sh...  9.39 us
    pallas_call x1, Pallas kernels, project(): pl.pallas_call(project_kernel, out_shape=jax.ShapeDtypeStruct((tokens, wi...  3.67 us
  transfers between devices with their start and end apart: 24, of which 16 were waited for; matrix products, arithmetic and copies ran while one was open for 0% of the time, Pallas kernels for 7%

profile of v10, /device:TPU:24, one launch (start us, length us, event | category | flops | bytes accessed | tf_op | source)
XLA Modules:
  0.0 173.4 jit_solution(7067247611863902921)
XLA Ops:
  0.0 3.7 %shard_map.91 = bf16[64,4096]{1,0:T(8,128)(2,1)} custom-call(bf16[64,512]{1,0:T(8,128)(2,1)} %bitcast.46, bf16[512,4096]{1,0:T(8,128)(2,1)} %proj_hbm.1), custom_call_target="tpu_custom_call" | custom-call | flops 268435456 | bytes 4194304 | tf_op jit(solution)/shard_map/pallas_call | solution.py:47
  3.7 26.1 %all_to_all.31 = bf16[8,8,4096]{2,1,0:T(8,128)(2,1)S(1)} all-to-all(bf16[8,8,4096]{2,1,0:T(8,128)(2,1)} %bitcast.45), channel_id=1, replica_groups=mesh['dp'=2,'tensor'=8,'expert'=16] {'tensor'}, dimensions={0} | all-to-all | bytes 1048576 | tf_op jit(solution)/shard_map/all_to_all | solution.py:106
  30.1 18.9 %all_to_all.32 = bf16[8,8,4224]{2,1,0:T(8,128)(2,1)S(1)} all-to-all(bf16[8,8,4224]{2,1,0:T(8,128)(2,1)S(1)} %bitcast.40), channel_id=1, replica_groups=mesh['dp'=2,'tensor'=8,'expert'=16] {'tensor'}, dimensions={0} | all-to-all | bytes 1081344 | tf_op jit(solution)/shard_map/all_to_all | solution.py:106
  49.0 2.8 %collective-permute-start.1 = (bf16[64,4224]{1,0:T(8,128)(2,1)S(1)}, bf16[64,4224]{1,0:T(8,128)(2,1)S(1)}, u32[]{:S(2)}, u32[]{:S(2)}) collective-permute-start(bf16[64,4224]{1,0:T(8,128)(2,1)S(1)} %bitcast.36), channel_id=1, source_target_pairs={{0,3},{1,0},{2,1},{3,2},{4,7},{5,4},{6,5},{7,6},{8,11},{9,8},{10,9... | collective-permute-start | bytes 1622024 | tf_op jit(solution)/shard_map/ppermute | solution.py:120
  51.8 6.9 %collective-permute-done.1._.low_ref = bf16[64,4224]{1,0:T(8,128)(2,1)S(1)} collective-permute-done((bf16[64,4224]{1,0:T(8,128)(2,1)S(1)}, bf16[64,4224]{1,0:T(8,128)(2,1)S(1)}, u32[]{:S(2)}, u32[]{:S(2)}) %collective-permute-start.1) | collective-permute-done | bytes 540704 | tf_op jit(solution)/shard_map/ppermute | solution.py:120
  58.7 3.8 %collective-permute-start.3 = (bf16[32,4224]{1,0:T(8,128)(2,1)S(1)}, bf16[32,4224]{1,0:T(8,128)(2,1)S(1)}, u32[]{:S(2)}, u32[]{:S(2)}) collective-permute-start(bf16[32,4224]{1,0:T(8,128)(2,1)S(1)} %slice.9), channel_id=1, source_target_pairs={{0,3},{1,0},{2,1},{3,2},{4,7},{5,4},{6,5},{7,6},{8,11},{9,8},{10,9... | collective-permute-start | bytes 811016 | tf_op jit(solution)/shard_map/ppermute | solution.py:120
  62.6 0.6 shard_map.93
  63.5 1.8 %collective-permute-start.7 = (bf16[112,4224]{1,0:T(8,128)(2,1)S(1)}, bf16[112,4224]{1,0:T(8,128)(2,1)S(1)}, u32[]{:S(2)}, u32[]{:S(2)}) collective-permute-start(bf16[112,4224]{1,0:T(8,128)(2,1)S(1)} %get-tuple-element.67), channel_id=1, source_target_pairs={{0,12},{1,13},{2,14},{3,15},{4,0},{5,1},{6,2},{7,3},{8,4},{9,5},{1... | collective-permute-start | bytes 2838536 | tf_op jit(solution)/shard_map/ppermute | solution.py:120
  65.3 1.5 shard_map.94._.own_ref
  66.8 2.5 %collective-permute-done.3.refs_1_ = bf16[32,4224]{1,0:T(8,128)(2,1)S(1)} collective-permute-done((bf16[32,4224]{1,0:T(8,128)(2,1)S(1)}, bf16[32,4224]{1,0:T(8,128)(2,1)S(1)}, u32[]{:S(2)}, u32[]{:S(2)}) %collective-permute-start.3) | collective-permute-done | bytes 270368 | tf_op jit(solution)/shard_map/ppermute | solution.py:120
  69.4 3.8 %collective-permute-done.2.refs_0_ = bf16[32,4224]{1,0:T(8,128)(2,1)S(1)} collective-permute-done((bf16[32,4224]{1,0:T(8,128)(2,1)S(1)}, bf16[32,4224]{1,0:T(8,128)(2,1)S(1)}, u32[]{:S(2)}, u32[]{:S(2)}) %collective-permute-start.2) | collective-permute-done | bytes 270368 | tf_op jit(solution)/shard_map/ppermute | solution.py:120
  73.2 0.6 shard_map.95
  74.1 1.8 %collective-permute-start.5 = (bf16[112,4224]{1,0:T(8,128)(2,1)S(1)}, bf16[112,4224]{1,0:T(8,128)(2,1)S(1)}, u32[]{:S(2)}, u32[]{:S(2)}) collective-permute-start(bf16[112,4224]{1,0:T(8,128)(2,1)S(1)} %get-tuple-element.65), channel_id=1, source_target_pairs={{0,12},{1,13},{2,14},{3,15},{4,0},{5,1},{6,2},{7,3},{8,4},{9,5},{1... | collective-permute-start | bytes 2838536 | tf_op jit(solution)/shard_map/ppermute | solution.py:120
  75.9 1.5 shard_map.96.own_ref
  77.4 1.0 collective-permute-done.7.front_ref.refs_1_
  78.4 0.6 shard_map.97
  79.0 0.8 collective-permute-start.9
  79.8 2.5 %collective-permute-start.8 = (bf16[48,4224]{1,0:T(8,128)(2,1)S(1)}, bf16[48,4224]{1,0:T(8,128)(2,1)S(1)}, u32[]{:S(2)}, u32[]{:S(2)}) collective-permute-start(bf16[48,4224]{1,0:T(8,128)(2,1)S(1)} %get-tuple-element.71._), channel_id=1, source_target_pairs={{0,4},{1,5},{2,6},{3,7},{4,8},{5,9},{6,10},{7,11},{8,12},{9,13},{1... | collective-permute-start | bytes 1216520 | tf_op jit(solution)/shard_map/ppermute | solution.py:120
  82.3 1.7 shard_map.98
  84.1 3.5 %collective-permute-done.4.back_ref.refs_0_ = bf16[112,4224]{1,0:T(8,128)(2,1)S(1)} collective-permute-done((bf16[112,4224]{1,0:T(8,128)(2,1)S(1)}, bf16[112,4224]{1,0:T(8,128)(2,1)S(1)}, u32[]{:S(2)}, u32[]{:S(2)}) %collective-permute-start.4) | collective-permute-done | bytes 946208 | tf_op jit(solution)/shard_map/ppermute | solution.py:120
  87.6 1.4 collective-permute-done.5.front_ref.refs_1_
  89.0 0.6 shard_map.99
  89.6 2.0 %collective-permute-start.10 = (bf16[48,4224]{1,0:T(8,128)(2,1)S(1)}, bf16[48,4224]{1,0:T(8,128)(2,1)S(1)}, u32[]{:S(2)}, u32[]{:S(2)}) collective-permute-start(bf16[48,4224]{1,0:T(8,128)(2,1)S(1)} %get-tuple-element.79), channel_id=1, source_target_pairs={{0,4},{1,5},{2,6},{3,7},{4,8},{5,9},{6,10},{7,11},{8,12},{9,13},{1... | collective-permute-start | bytes 1216520 | tf_op jit(solution)/shard_map/ppermute | solution.py:120
  91.7 1.6 collective-permute-done.9.refs_1_
  93.4 1.5 shard_map.100
  94.8 2.0 %collective-permute-start.13 = (bf16[48,4096]{1,0:T(8,128)(2,1)S(1)}, bf16[48,4096]{1,0:T(8,128)(2,1)S(1)}, u32[]{:S(2)}, u32[]{:S(2)}) collective-permute-start(bf16[48,4096]{1,0:T(8,128)(2,1)S(1)} %get-tuple-element.84), channel_id=1, source_target_pairs={{0,4},{1,5},{2,6},{3,7},{4,8},{5,9},{6,10},{7,11},{8,12},{9,13},{1... | collective-permute-start | bytes 1179656 | tf_op jit(solution)/shard_map/ppermute | solution.py:120
  96.9 0.7 collective-permute-done.10.refs_0_
  97.6 3.1 %collective-permute-done.11.refs_1_ = bf16[48,4224]{1,0:T(8,128)(2,1)S(1)} collective-permute-done((bf16[48,4224]{1,0:T(8,128)(2,1)S(1)}, bf16[48,4224]{1,0:T(8,128)(2,1)S(1)}, u32[]{:S(2)}, u32[]{:S(2)}) %collective-permute-start.11) | collective-permute-done | bytes 405536 | tf_op jit(solution)/shard_map/ppermute | solution.py:120
  100.8 1.5 shard_map.101
  102.3 2.0 %collective-permute-start.14 = (bf16[48,4096]{1,0:T(8,128)(2,1)S(1)}, bf16[48,4096]{1,0:T(8,128)(2,1)S(1)}, u32[]{:S(2)}, u32[]{:S(2)}) collective-permute-start(bf16[48,4096]{1,0:T(8,128)(2,1)S(1)} %get-tuple-element.80._), channel_id=1, source_target_pairs={{0,12},{1,13},{2,14},{3,15},{4,0},{5,1},{6,2},{7,3},{8,4},{9,5},{1... | collective-permute-start | bytes 1179656 | tf_op jit(solution)/shard_map/ppermute | solution.py:120
  104.3 1.7 shard_map.102
  106.1 4.0 %collective-permute-done.15.high_ref = bf16[48,4096]{1,0:T(8,128)(2,1)S(1)} collective-permute-done((bf16[48,4096]{1,0:T(8,128)(2,1)S(1)}, bf16[48,4096]{1,0:T(8,128)(2,1)S(1)}, u32[]{:S(2)}, u32[]{:S(2)}) %collective-permute-start.15) | collective-permute-done | bytes 393248 | tf_op jit(solution)/shard_map/ppermute | solution.py:120
  110.1 1.3 collective-permute-done.14.low_ref
  111.9 0.5 shard_map.105
  112.4 2.0 %collective-permute-start.19 = (bf16[112,4096]{1,0:T(8,128)(2,1)S(1)}, bf16[112,4096]{1,0:T(8,128)(2,1)S(1)}, u32[]{:S(2)}, u32[]{:S(2)}) collective-permute-start(bf16[112,4096]{1,0:T(8,128)(2,1)S(1)} %get-tuple-element.102), channel_id=1, source_target_pairs={{0,12},{1,13},{2,14},{3,15},{4,0},{5,1},{6,2},{7,3},{8,4},{9,5},{1... | collective-permute-start | bytes 2752520 | tf_op jit(solution)/shard_map/ppermute | solution.py:120
  114.4 1.3 collective-permute-start.16
  115.7 0.7 collective-permute-start.17
  116.5 12.1 %collective-permute-done.18.back_ref = bf16[112,4096]{1,0:T(8,128)(2,1)S(1)} collective-permute-done((bf16[112,4096]{1,0:T(8,128)(2,1)S(1)}, bf16[112,4096]{1,0:T(8,128)(2,1)S(1)}, u32[]{:S(2)}, u32[]{:S(2)}) %collective-permute-start.18) | collective-permute-done | bytes 917536 | tf_op jit(solution)/shard_map/ppermute | solution.py:120
  128.6 1.3 collective-permute-done.19.front_ref
  129.9 0.5 shard_map.106
  130.5 3.2 %collective-permute-start.21 = (bf16[32,4096]{1,0:T(8,128)(2,1)S(1)}, bf16[32,4096]{1,0:T(8,128)(2,1)S(1)}, u32[]{:S(2)}, u32[]{:S(2)}) collective-permute-start(bf16[32,4096]{1,0:T(8,128)(2,1)S(1)} %get-tuple-element.108), channel_id=1, source_target_pairs={{0,3},{1,0},{2,1},{3,2},{4,7},{5,4},{6,5},{7,6},{8,11},{9,8},{10,9... | collective-permute-start | bytes 786440 | tf_op jit(solution)/shard_map/ppermute | solution.py:120
  133.7 10.3 %collective-permute-done.16.back_ref = bf16[112,4096]{1,0:T(8,128)(2,1)S(1)} collective-permute-done((bf16[112,4096]{1,0:T(8,128)(2,1)S(1)}, bf16[112,4096]{1,0:T(8,128)(2,1)S(1)}, u32[]{:S(2)}, u32[]{:S(2)}) %collective-permute-start.16) | collective-permute-done | bytes 917536 | tf_op jit(solution)/shard_map/ppermute | solution.py:120
  144.1 1.3 collective-permute-done.17.front_ref
  145.4 0.5 shard_map.104
  146.1 3.2 %collective-permute-start.23 = (bf16[64,4096]{1,0:T(8,128)(2,1)S(1)}, bf16[64,4096]{1,0:T(8,128)(2,1)S(1)}, u32[]{:S(2)}, u32[]{:S(2)}) collective-permute-start(bf16[64,4096]{1,0:T(8,128)(2,1)S(1)} %get-tuple-element.110), channel_id=1, source_target_pairs={{0,3},{1,0},{2,1},{3,2},{4,7},{5,4},{6,5},{7,6},{8,11},{9,8},{10,9... | collective-permute-start | bytes 1572872 | tf_op jit(solution)/shard_map/ppermute | solution.py:120
  149.4 7.2 %collective-permute-done.22 = bf16[64,4096]{1,0:T(8,128)(2,1)S(1)} collective-permute-done((bf16[64,4096]{1,0:T(8,128)(2,1)S(1)}, bf16[64,4096]{1,0:T(8,128)(2,1)S(1)}, u32[]{:S(2)}, u32[]{:S(2)}) %collective-permute-start.22) | collective-permute-done | bytes 524320 | tf_op jit(solution)/shard_map/ppermute | solution.py:120
  156.7 16.0 %all_to_all.33 = bf16[8,8,4096]{2,1,0:T(8,128)(2,1)S(1)} all-to-all(bf16[8,8,4096]{2,1,0:T(8,128)(2,1)S(1)} %fusion), channel_id=1, replica_groups=mesh['dp'=2,'tensor'=8,'expert'=16] {'tensor'}, dimensions={0} | all-to-all | bytes 1048576 | tf_op jit(solution)/shard_map/all_to_all | solution.py:106
  172.8 0.7 fusion.1
  (39 shorter events, 2.4 us)
Async XLA Ops:
  0.0 29.8 %copy-start.3 = (bf16[1,8,4096]{2,1,0:T(8,128)(2,1)S(1)}, bf16[1,8,4096]{2,1,0:T(8,128)(2,1)}, u32[]{:S(2)}) copy-start(bf16[1,8,4096]{2,1,0:T(8,128)(2,1)} %param.11) | copy-start | bytes 196612
  0.0 29.8 %copy-start.4 = (f32[4096]{0:T(1024)S(1)}, f32[4096]{0:T(1024)}, u32[]{:S(2)}) copy-start(f32[4096]{0:T(1024)} %param.12) | copy-start | bytes 49156
  0.0 29.8 %copy-start.5 = (s32[1,8,8]{2,1,0:T(8,128)S(1)}, s32[1,8,8]{2,1,0:T(8,128)}, u32[]{:S(2)}) copy-start(s32[1,8,8]{2,1,0:T(8,128)} %param.13) | copy-start | bytes 772
  0.0 29.8 %copy-start.6 = (s32[1,8,8]{2,1,0:T(8,128)S(1)}, s32[1,8,8]{2,1,0:T(8,128)}, u32[]{:S(2)}) copy-start(s32[1,8,8]{2,1,0:T(8,128)} %param.14) | copy-start | bytes 772
  3.7 61.6 %copy-start.2 = (bf16[1,192,4096]{2,1,0:T(8,128)(2,1)S(1)}, bf16[1,192,4096]{2,1,0:T(8,128)(2,1)}, u32[]{:S(2)}) copy-start(bf16[1,192,4096]{2,1,0:T(8,128)(2,1)} %param.17) | copy-start | bytes 4718596
  30.1 35.2 %copy-start.1 = (bf16[1,192,4096]{2,1,0:T(8,128)(2,1)S(1)}, bf16[1,192,4096]{2,1,0:T(8,128)(2,1)}, u32[]{:S(2)}) copy-start(bf16[1,192,4096]{2,1,0:T(8,128)(2,1)} %param.16) | copy-start | bytes 4718596
  49.0 16.3 %copy-start = (bf16[1,192,4096]{2,1,0:T(8,128)(2,1)S(1)}, bf16[1,192,4096]{2,1,0:T(8,128)(2,1)}, u32[]{:S(2)}) copy-start(bf16[1,192,4096]{2,1,0:T(8,128)(2,1)} %param.15) | copy-start | bytes 4718596
  49.0 9.6 %collective-permute-start.1 = (bf16[64,4224]{1,0:T(8,128)(2,1)S(1)}, bf16[64,4224]{1,0:T(8,128)(2,1)S(1)}, u32[]{:S(2)}, u32[]{:S(2)}) collective-permute-start(bf16[64,4224]{1,0:T(8,128)(2,1)S(1)} %bitcast.36), channel_id=1, source_target_pairs={{0,3},{1,0},{2,1},{3,2},{4,7},{5,4},{6,5},{7,6},{8,11},{9,8},{10,9... | collective-permute-start | bytes 1622024 | tf_op jit(solution)/shard_map/ppermute | solution.py:120
  51.8 10.7 %collective-permute-start = (bf16[64,4224]{1,0:T(8,128)(2,1)S(1)}, bf16[64,4224]{1,0:T(8,128)(2,1)S(1)}, u32[]{:S(2)}, u32[]{:S(2)}) collective-permute-start(bf16[64,4224]{1,0:T(8,128)(2,1)S(1)} %bitcast.37), channel_id=1, source_target_pairs={{0,1},{1,2},{2,3},{3,0},{4,5},{5,6},{6,7},{7,4},{8,9},{9,10},{10,1... | collective-permute-start | bytes 1622024 | tf_op jit(solution)/shard_map/ppermute | solution.py:120
  58.7 10.7 %collective-permute-start.3 = (bf16[32,4224]{1,0:T(8,128)(2,1)S(1)}, bf16[32,4224]{1,0:T(8,128)(2,1)S(1)}, u32[]{:S(2)}, u32[]{:S(2)}) collective-permute-start(bf16[32,4224]{1,0:T(8,128)(2,1)S(1)} %slice.9), channel_id=1, source_target_pairs={{0,3},{1,0},{2,1},{3,2},{4,7},{5,4},{6,5},{7,6},{8,11},{9,8},{10,9... | collective-permute-start | bytes 811016 | tf_op jit(solution)/shard_map/ppermute | solution.py:120
  62.5 10.7 %collective-permute-start.2 = (bf16[32,4224]{1,0:T(8,128)(2,1)S(1)}, bf16[32,4224]{1,0:T(8,128)(2,1)S(1)}, u32[]{:S(2)}, u32[]{:S(2)}) collective-permute-start(bf16[32,4224]{1,0:T(8,128)(2,1)S(1)} %slice.8), channel_id=1, source_target_pairs={{0,1},{1,2},{2,3},{3,0},{4,5},{5,6},{6,7},{7,4},{8,9},{9,10},{10,1... | collective-permute-start | bytes 811016 | tf_op jit(solution)/shard_map/ppermute | solution.py:120
  63.2 14.2 %collective-permute-start.6 = (bf16[112,4224]{1,0:T(8,128)(2,1)S(1)}, bf16[112,4224]{1,0:T(8,128)(2,1)S(1)}, u32[]{:S(2)}, u32[]{:S(2)}) collective-permute-start(bf16[112,4224]{1,0:T(8,128)(2,1)S(1)} %get-tuple-element.66), channel_id=1, source_target_pairs={{0,4},{1,5},{2,6},{3,7},{4,8},{5,9},{6,10},{7,11},{8,12},{9,13},{1... | collective-permute-start | bytes 2838536 | tf_op jit(solution)/shard_map/ppermute | solution.py:120
  63.5 14.9 %collective-permute-start.7 = (bf16[112,4224]{1,0:T(8,128)(2,1)S(1)}, bf16[112,4224]{1,0:T(8,128)(2,1)S(1)}, u32[]{:S(2)}, u32[]{:S(2)}) collective-permute-start(bf16[112,4224]{1,0:T(8,128)(2,1)S(1)} %get-tuple-element.67), channel_id=1, source_target_pairs={{0,12},{1,13},{2,14},{3,15},{4,0},{5,1},{6,2},{7,3},{8,4},{9,5},{1... | collective-permute-start | bytes 2838536 | tf_op jit(solution)/shard_map/ppermute | solution.py:120
  73.8 13.8 %collective-permute-start.4 = (bf16[112,4224]{1,0:T(8,128)(2,1)S(1)}, bf16[112,4224]{1,0:T(8,128)(2,1)S(1)}, u32[]{:S(2)}, u32[]{:S(2)}) collective-permute-start(bf16[112,4224]{1,0:T(8,128)(2,1)S(1)} %get-tuple-element.64), channel_id=1, source_target_pairs={{0,4},{1,5},{2,6},{3,7},{4,8},{5,9},{6,10},{7,11},{8,12},{9,13},{1... | collective-permute-start | bytes 2838536 | tf_op jit(solution)/shard_map/ppermute | solution.py:120
  74.1 14.9 %collective-permute-start.5 = (bf16[112,4224]{1,0:T(8,128)(2,1)S(1)}, bf16[112,4224]{1,0:T(8,128)(2,1)S(1)}, u32[]{:S(2)}, u32[]{:S(2)}) collective-permute-start(bf16[112,4224]{1,0:T(8,128)(2,1)S(1)} %get-tuple-element.65), channel_id=1, source_target_pairs={{0,12},{1,13},{2,14},{3,15},{4,0},{5,1},{6,2},{7,3},{8,4},{9,5},{1... | collective-permute-start | bytes 2838536 | tf_op jit(solution)/shard_map/ppermute | solution.py:120
  79.0 14.3 %collective-permute-start.9 = (bf16[48,4224]{1,0:T(8,128)(2,1)S(1)}, bf16[48,4224]{1,0:T(8,128)(2,1)S(1)}, u32[]{:S(2)}, u32[]{:S(2)}) collective-permute-start(bf16[48,4224]{1,0:T(8,128)(2,1)S(1)} %get-tuple-element.77), channel_id=1, source_target_pairs={{0,12},{1,13},{2,14},{3,15},{4,0},{5,1},{6,2},{7,3},{8,4},{9,5},{1... | collective-permute-start | bytes 1216520 | tf_op jit(solution)/shard_map/ppermute | solution.py:120
  79.8 13.5 %collective-permute-start.8 = (bf16[48,4224]{1,0:T(8,128)(2,1)S(1)}, bf16[48,4224]{1,0:T(8,128)(2,1)S(1)}, u32[]{:S(2)}, u32[]{:S(2)}) collective-permute-start(bf16[48,4224]{1,0:T(8,128)(2,1)S(1)} %get-tuple-element.71._), channel_id=1, source_target_pairs={{0,4},{1,5},{2,6},{3,7},{4,8},{5,9},{6,10},{7,11},{8,12},{9,13},{1... | collective-permute-start | bytes 1216520 | tf_op jit(solution)/shard_map/ppermute | solution.py:120
  89.6 8.0 %collective-permute-start.10 = (bf16[48,4224]{1,0:T(8,128)(2,1)S(1)}, bf16[48,4224]{1,0:T(8,128)(2,1)S(1)}, u32[]{:S(2)}, u32[]{:S(2)}) collective-permute-start(bf16[48,4224]{1,0:T(8,128)(2,1)S(1)} %get-tuple-element.79), channel_id=1, source_target_pairs={{0,4},{1,5},{2,6},{3,7},{4,8},{5,9},{6,10},{7,11},{8,12},{9,13},{1... | collective-permute-start | bytes 1216520 | tf_op jit(solution)/shard_map/ppermute | solution.py:120
  91.6 9.1 %collective-permute-start.11 = (bf16[48,4224]{1,0:T(8,128)(2,1)S(1)}, bf16[48,4224]{1,0:T(8,128)(2,1)S(1)}, u32[]{:S(2)}, u32[]{:S(2)}) collective-permute-start(bf16[48,4224]{1,0:T(8,128)(2,1)S(1)} %get-tuple-element.76._), channel_id=1, source_target_pairs={{0,12},{1,13},{2,14},{3,15},{4,0},{5,1},{6,2},{7,3},{8,4},{9,5},{1... | collective-permute-start | bytes 1216520 | tf_op jit(solution)/shard_map/ppermute | solution.py:120
  94.8 11.2 %collective-permute-start.13 = (bf16[48,4096]{1,0:T(8,128)(2,1)S(1)}, bf16[48,4096]{1,0:T(8,128)(2,1)S(1)}, u32[]{:S(2)}, u32[]{:S(2)}) collective-permute-start(bf16[48,4096]{1,0:T(8,128)(2,1)S(1)} %get-tuple-element.84), channel_id=1, source_target_pairs={{0,4},{1,5},{2,6},{3,7},{4,8},{5,9},{6,10},{7,11},{8,12},{9,13},{1... | collective-permute-start | bytes 1179656 | tf_op jit(solution)/shard_map/ppermute | solution.py:120
  96.8 9.2 %collective-permute-start.12 = (bf16[48,4096]{1,0:T(8,128)(2,1)S(1)}, bf16[48,4096]{1,0:T(8,128)(2,1)S(1)}, u32[]{:S(2)}, u32[]{:S(2)}) collective-permute-start(bf16[48,4096]{1,0:T(8,128)(2,1)S(1)} %get-tuple-element.78._), channel_id=1, source_target_pairs={{0,12},{1,13},{2,14},{3,15},{4,0},{5,1},{6,2},{7,3},{8,4},{9,5},{1... | collective-permute-start | bytes 1179656 | tf_op jit(solution)/shard_map/ppermute | solution.py:120
  102.2 7.9 %collective-permute-start.15 = (bf16[48,4096]{1,0:T(8,128)(2,1)S(1)}, bf16[48,4096]{1,0:T(8,128)(2,1)S(1)}, u32[]{:S(2)}, u32[]{:S(2)}) collective-permute-start(bf16[48,4096]{1,0:T(8,128)(2,1)S(1)} %get-tuple-element.85), channel_id=1, source_target_pairs={{0,4},{1,5},{2,6},{3,7},{4,8},{5,9},{6,10},{7,11},{8,12},{9,13},{1... | collective-permute-start | bytes 1179656 | tf_op jit(solution)/shard_map/ppermute | solution.py:120
  102.3 9.1 %collective-permute-start.14 = (bf16[48,4096]{1,0:T(8,128)(2,1)S(1)}, bf16[48,4096]{1,0:T(8,128)(2,1)S(1)}, u32[]{:S(2)}, u32[]{:S(2)}) collective-permute-start(bf16[48,4096]{1,0:T(8,128)(2,1)S(1)} %get-tuple-element.80._), channel_id=1, source_target_pairs={{0,12},{1,13},{2,14},{3,15},{4,0},{5,1},{6,2},{7,3},{8,4},{9,5},{1... | collective-permute-start | bytes 1179656 | tf_op jit(solution)/shard_map/ppermute | solution.py:120
  112.3 16.3 %collective-permute-start.18 = (bf16[112,4096]{1,0:T(8,128)(2,1)S(1)}, bf16[112,4096]{1,0:T(8,128)(2,1)S(1)}, u32[]{:S(2)}, u32[]{:S(2)}) collective-permute-start(bf16[112,4096]{1,0:T(8,128)(2,1)S(1)} %get-tuple-element.101), channel_id=1, source_target_pairs={{0,4},{1,5},{2,6},{3,7},{4,8},{5,9},{6,10},{7,11},{8,12},{9,13},{1... | collective-permute-start | bytes 2752520 | tf_op jit(solution)/shard_map/ppermute | solution.py:120
  112.4 17.5 %collective-permute-start.19 = (bf16[112,4096]{1,0:T(8,128)(2,1)S(1)}, bf16[112,4096]{1,0:T(8,128)(2,1)S(1)}, u32[]{:S(2)}, u32[]{:S(2)}) collective-permute-start(bf16[112,4096]{1,0:T(8,128)(2,1)S(1)} %get-tuple-element.102), channel_id=1, source_target_pairs={{0,12},{1,13},{2,14},{3,15},{4,0},{5,1},{6,2},{7,3},{8,4},{9,5},{1... | collective-permute-start | bytes 2752520 | tf_op jit(solution)/shard_map/ppermute | solution.py:120
  114.4 29.6 %collective-permute-start.16 = (bf16[112,4096]{1,0:T(8,128)(2,1)S(1)}, bf16[112,4096]{1,0:T(8,128)(2,1)S(1)}, u32[]{:S(2)}, u32[]{:S(2)}) collective-permute-start(bf16[112,4096]{1,0:T(8,128)(2,1)S(1)} %get-tuple-element.90), channel_id=1, source_target_pairs={{0,4},{1,5},{2,6},{3,7},{4,8},{5,9},{6,10},{7,11},{8,12},{9,13},{1... | collective-permute-start | bytes 2752520 | tf_op jit(solution)/shard_map/ppermute | solution.py:120
  115.7 29.6 %collective-permute-start.17 = (bf16[112,4096]{1,0:T(8,128)(2,1)S(1)}, bf16[112,4096]{1,0:T(8,128)(2,1)S(1)}, u32[]{:S(2)}, u32[]{:S(2)}) collective-permute-start(bf16[112,4096]{1,0:T(8,128)(2,1)S(1)} %get-tuple-element.91._), channel_id=1, source_target_pairs={{0,12},{1,13},{2,14},{3,15},{4,0},{5,1},{6,2},{7,3},{8,4},{9,5},{1... | collective-permute-start | bytes 2752520 | tf_op jit(solution)/shard_map/ppermute | solution.py:120
  130.4 15.5 %collective-permute-start.20 = (bf16[32,4096]{1,0:T(8,128)(2,1)S(1)}, bf16[32,4096]{1,0:T(8,128)(2,1)S(1)}, u32[]{:S(2)}, u32[]{:S(2)}) collective-permute-start(bf16[32,4096]{1,0:T(8,128)(2,1)S(1)} %get-tuple-element.107), channel_id=1, source_target_pairs={{0,1},{1,2},{2,3},{3,0},{4,5},{5,6},{6,7},{7,4},{8,9},{9,10},{10,1... | collective-permute-start | bytes 786440 | tf_op jit(solution)/shard_map/ppermute | solution.py:120
  130.5 15.4 %collective-permute-start.21 = (bf16[32,4096]{1,0:T(8,128)(2,1)S(1)}, bf16[32,4096]{1,0:T(8,128)(2,1)S(1)}, u32[]{:S(2)}, u32[]{:S(2)}) collective-permute-start(bf16[32,4096]{1,0:T(8,128)(2,1)S(1)} %get-tuple-element.108), channel_id=1, source_target_pairs={{0,3},{1,0},{2,1},{3,2},{4,7},{5,4},{6,5},{7,6},{8,11},{9,8},{10,9... | collective-permute-start | bytes 786440 | tf_op jit(solution)/shard_map/ppermute | solution.py:120
  146.0 10.5 %collective-permute-start.22 = (bf16[64,4096]{1,0:T(8,128)(2,1)S(1)}, bf16[64,4096]{1,0:T(8,128)(2,1)S(1)}, u32[]{:S(2)}, u32[]{:S(2)}) collective-permute-start(bf16[64,4096]{1,0:T(8,128)(2,1)S(1)} %get-tuple-element.109), channel_id=1, source_target_pairs={{0,1},{1,2},{2,3},{3,0},{4,5},{5,6},{6,7},{7,4},{8,9},{9,10},{10,1... | collective-permute-start | bytes 1572872 | tf_op jit(solution)/shard_map/ppermute | solution.py:120
  146.1 10.4 %collective-permute-start.23 = (bf16[64,4096]{1,0:T(8,128)(2,1)S(1)}, bf16[64,4096]{1,0:T(8,128)(2,1)S(1)}, u32[]{:S(2)}, u32[]{:S(2)}) collective-permute-start(bf16[64,4096]{1,0:T(8,128)(2,1)S(1)} %get-tuple-element.110), channel_id=1, source_target_pairs={{0,3},{1,0},{2,1},{3,2},{4,7},{5,4},{6,5},{7,6},{8,11},{9,8},{10,9... | collective-permute-start | bytes 1572872 | tf_op jit(solution)/shard_map/ppermute | solution.py:120

commit v11 on v10

--- a/solution.py
+++ b/solution.py
@@ -202,7 +202,9 @@
     )(me, dp, after, low, *highs)
 
 
-def pack_kernel(me_ref, dp_ref, back_ref, front_ref, low_ref, high_ref, low_hot_ref, high_hot_ref):
+def pack_kernel(
+    me_ref, dp_ref, _, back_ref, front_ref, low_ref, high_ref, low_hot_ref, high_hot_ref
+):
     slots, half = low_hot_ref.shape
     ahead, behind = beside(me_ref, dp_ref)
     tail = low_ref.shape[1] - LANES
@@ -214,7 +216,7 @@
     high_ref[...] = chosen(high_hot, front_ref[slots:, :])
 
 
-def pack(me, dp, half, back, front):
+def pack(me, dp, half, after, back, front):
     rows, width = back.shape
     slots = rows - half
     smem = pl.BlockSpec(memory_space=pltpu.SMEM)
@@ -222,13 +224,13 @@
         pack_kernel,
         out_shape=[jax.ShapeDtypeStruct((slots, width), jnp.bfloat16)] * 2
         + [jax.ShapeDtypeStruct((slots, half), jnp.bfloat16)] * 2,
-        in_specs=[smem] * 2 + [vmem_spec()] * 2,
+        in_specs=[smem] * 2 + [pl.BlockSpec(memory_space=pl.ANY)] + [vmem_spec()] * 2,
         out_specs=[vmem_spec()] * 4,
         compiler_params=pltpu.CompilerParams(vmem_limit_bytes=GRANT),
         cost_estimate=pl.CostEstimate(
             flops=4 * half * slots * width, bytes_accessed=4 * rows * width, transcendentals=0
         ),
-    )(me, dp, back, front)
+    )(me, dp, after, back, front)
 
 
 def join_kernel(
@@ -383,13 +385,12 @@
         who, side, first_own[0], front, *far
     )
     second_near = both(*second_sent, 1)
-    second_own = experts(second, after=first_own[0])
-    first_near, second_own = tie(first_near, second_own)
-    low, high, *first_hot = pack(who, side, tokens, *first_near)
+    first_near_out = experts(*first_near, after=first_own[0])
+    second_own = experts(second, after=first_near_out[0])
+    low, high, *first_hot = pack(who, side, tokens, second_own[0], *first_near)
     first_far = both(low, high, 1)
-    first_near_out = experts(*first_near, after=low)
     second_near, first_near_out = tie(second_near, first_near_out)
-    low, high, *second_hot = pack(who, side, tokens, *second_near)
+    low, high, *second_hot = pack(who, side, tokens, low, *second_near)
     second_far = both(low, high, 1)
     first_far_low, first_far_high = experts(*first_far, after=high)
     first_down = both(first_far_high, first_far_low, 1)[::-1]

time: 174 us -> 174 us (level)
  transfers between devices with their start and end apart: 24 -> 24, of which waited for: 16 -> 17; matrix products, arithmetic and copies ran while one was open for 0% -> 0% of each run, Pallas kernels for 7% -> 7%
where the time goes in v11:
time: 174 us; the launch traced here: 173 us
  waiting for transfers between devices  61.6 us (35%)
  blocking collectives  61.3 us (35%)
  starting transfers between devices  31.4 us (18%)
  Pallas kernels  17.9 us (10%)
    ppermute x24, waiting for transfers between devices, shift(): return lax.ppermute(value, ('dp', 'expert'), pairs)  61.6 us
    all_to_all x3, blocking collectives, swap_over_tensor(): lax.all_to_all(value, 'tensor', split_axis=0, concat_axis=0, tiled=True)  61.3 us
    ppermute x24, starting transfers between devices, shift(): return lax.ppermute(value, ('dp', 'expert'), pairs)  31.4 us
    pallas_call x6, Pallas kernels, run_expert(): pl.pallas_call(functools.partial(expert_kernel, count), out_shape=[jax.Sh...  9.4 us
    pallas_call x1, Pallas kernels, project(): pl.pallas_call(project_kernel, out_shape=jax.ShapeDtypeStruct((tokens, wi...  3.67 us
  transfers between devices with their start and end apart: 24, of which 17 were waited for; matrix products, arithmetic and copies ran while one was open for 0% of the time, Pallas kernels for 7%

profile of v11, /device:TPU:24, one launch (start us, length us, event | category | flops | bytes accessed | tf_op | source)
XLA Modules:
  0.0 173.4 jit_solution(15649757358036118622)
XLA Ops:
  0.0 3.7 %shard_map.91 = bf16[64,4096]{1,0:T(8,128)(2,1)} custom-call(bf16[64,512]{1,0:T(8,128)(2,1)} %bitcast.46, bf16[512,4096]{1,0:T(8,128)(2,1)} %proj_hbm.1), custom_call_target="tpu_custom_call" | custom-call | flops 268435456 | bytes 4194304 | tf_op jit(solution)/shard_map/pallas_call | solution.py:47
  3.7 26.1 %all_to_all.31 = bf16[8,8,4096]{2,1,0:T(8,128)(2,1)S(1)} all-to-all(bf16[8,8,4096]{2,1,0:T(8,128)(2,1)} %bitcast.45), channel_id=1, replica_groups=mesh['dp'=2,'tensor'=8,'expert'=16] {'tensor'}, dimensions={0} | all-to-all | bytes 1048576 | tf_op jit(solution)/shard_map/all_to_all | solution.py:106
  30.1 18.9 %all_to_all.32 = bf16[8,8,4224]{2,1,0:T(8,128)(2,1)S(1)} all-to-all(bf16[8,8,4224]{2,1,0:T(8,128)(2,1)S(1)} %bitcast.40), channel_id=1, replica_groups=mesh['dp'=2,'tensor'=8,'expert'=16] {'tensor'}, dimensions={0} | all-to-all | bytes 1081344 | tf_op jit(solution)/shard_map/all_to_all | solution.py:106
  49.0 2.8 %collective-permute-start.1 = (bf16[64,4224]{1,0:T(8,128)(2,1)S(1)}, bf16[64,4224]{1,0:T(8,128)(2,1)S(1)}, u32[]{:S(2)}, u32[]{:S(2)}) collective-permute-start(bf16[64,4224]{1,0:T(8,128)(2,1)S(1)} %bitcast.36), channel_id=1, source_target_pairs={{0,3},{1,0},{2,1},{3,2},{4,7},{5,4},{6,5},{7,6},{8,11},{9,8},{10,9... | collective-permute-start | bytes 1622024 | tf_op jit(solution)/shard_map/ppermute | solution.py:120
  51.8 6.9 %collective-permute-done.1._.low_ref = bf16[64,4224]{1,0:T(8,128)(2,1)S(1)} collective-permute-done((bf16[64,4224]{1,0:T(8,128)(2,1)S(1)}, bf16[64,4224]{1,0:T(8,128)(2,1)S(1)}, u32[]{:S(2)}, u32[]{:S(2)}) %collective-permute-start.1) | collective-permute-done | bytes 540704 | tf_op jit(solution)/shard_map/ppermute | solution.py:120
  58.7 3.8 %collective-permute-start.5 = (bf16[32,4224]{1,0:T(8,128)(2,1)S(1)}, bf16[32,4224]{1,0:T(8,128)(2,1)S(1)}, u32[]{:S(2)}, u32[]{:S(2)}) collective-permute-start(bf16[32,4224]{1,0:T(8,128)(2,1)S(1)} %slice.9), channel_id=1, source_target_pairs={{0,3},{1,0},{2,1},{3,2},{4,7},{5,4},{6,5},{7,6},{8,11},{9,8},{10,9... | collective-permute-start | bytes 811016 | tf_op jit(solution)/shard_map/ppermute | solution.py:120
  62.6 0.6 shard_map.93
  63.5 1.8 %collective-permute-start.3 = (bf16[112,4224]{1,0:T(8,128)(2,1)S(1)}, bf16[112,4224]{1,0:T(8,128)(2,1)S(1)}, u32[]{:S(2)}, u32[]{:S(2)}) collective-permute-start(bf16[112,4224]{1,0:T(8,128)(2,1)S(1)} %get-tuple-element.62), channel_id=1, source_target_pairs={{0,12},{1,13},{2,14},{3,15},{4,0},{5,1},{6,2},{7,3},{8,4},{9,5},{1... | collective-permute-start | bytes 2838536 | tf_op jit(solution)/shard_map/ppermute | solution.py:120
  65.3 1.5 shard_map.94._.own_ref
  66.8 2.5 %collective-permute-done.5.refs_1_ = bf16[32,4224]{1,0:T(8,128)(2,1)S(1)} collective-permute-done((bf16[32,4224]{1,0:T(8,128)(2,1)S(1)}, bf16[32,4224]{1,0:T(8,128)(2,1)S(1)}, u32[]{:S(2)}, u32[]{:S(2)}) %collective-permute-start.5) | collective-permute-done | bytes 270368 | tf_op jit(solution)/shard_map/ppermute | solution.py:120
  69.4 3.8 %collective-permute-done.4.refs_0_ = bf16[32,4224]{1,0:T(8,128)(2,1)S(1)} collective-permute-done((bf16[32,4224]{1,0:T(8,128)(2,1)S(1)}, bf16[32,4224]{1,0:T(8,128)(2,1)S(1)}, u32[]{:S(2)}, u32[]{:S(2)}) %collective-permute-start.4) | collective-permute-done | bytes 270368 | tf_op jit(solution)/shard_map/ppermute | solution.py:120
  73.2 0.6 shard_map.96
  74.1 1.8 %collective-permute-start.7 = (bf16[112,4224]{1,0:T(8,128)(2,1)S(1)}, bf16[112,4224]{1,0:T(8,128)(2,1)S(1)}, u32[]{:S(2)}, u32[]{:S(2)}) collective-permute-start(bf16[112,4224]{1,0:T(8,128)(2,1)S(1)} %get-tuple-element.67), channel_id=1, source_target_pairs={{0,12},{1,13},{2,14},{3,15},{4,0},{5,1},{6,2},{7,3},{8,4},{9,5},{1... | collective-permute-start | bytes 2838536 | tf_op jit(solution)/shard_map/ppermute | solution.py:120
  75.9 1.1 collective-permute-done.2.refs_0_.back_ref
  77.0 1.4 collective-permute-done.3.refs_1_.front_ref
  78.4 1.7 shard_map.95
  80.1 1.5 shard_map.97._.own_ref
  81.6 0.6 shard_map.98
  82.3 0.9 collective-permute-start.9
  83.1 2.6 %collective-permute-start.8 = (bf16[48,4224]{1,0:T(8,128)(2,1)S(1)}, bf16[48,4224]{1,0:T(8,128)(2,1)S(1)}, u32[]{:S(2)}, u32[]{:S(2)}) collective-permute-start(bf16[48,4224]{1,0:T(8,128)(2,1)S(1)} %get-tuple-element.65._), channel_id=1, source_target_pairs={{0,4},{1,5},{2,6},{3,7},{4,8},{5,9},{6,10},{7,11},{8,12},{9,13},{1... | collective-permute-start | bytes 1216520 | tf_op jit(solution)/shard_map/ppermute | solution.py:120
  85.8 1.8 %collective-permute-done.6.back_ref.refs_0_ = bf16[112,4224]{1,0:T(8,128)(2,1)S(1)} collective-permute-done((bf16[112,4224]{1,0:T(8,128)(2,1)S(1)}, bf16[112,4224]{1,0:T(8,128)(2,1)S(1)}, u32[]{:S(2)}, u32[]{:S(2)}) %collective-permute-start.6) | collective-permute-done | bytes 946208 | tf_op jit(solution)/shard_map/ppermute | solution.py:120
  87.6 1.4 collective-permute-done.7.front_ref.refs_1_
  89.0 0.6 shard_map.99
  89.6 2.0 %collective-permute-start.10 = (bf16[48,4224]{1,0:T(8,128)(2,1)S(1)}, bf16[48,4224]{1,0:T(8,128)(2,1)S(1)}, u32[]{:S(2)}, u32[]{:S(2)}) collective-permute-start(bf16[48,4224]{1,0:T(8,128)(2,1)S(1)} %get-tuple-element.74), channel_id=1, source_target_pairs={{0,4},{1,5},{2,6},{3,7},{4,8},{5,9},{6,10},{7,11},{8,12},{9,13},{1... | collective-permute-start | bytes 1216520 | tf_op jit(solution)/shard_map/ppermute | solution.py:120
  91.8 1.6 collective-permute-done.9.refs_1_
  93.4 1.5 shard_map.100
  94.9 2.0 %collective-permute-start.13 = (bf16[48,4096]{1,0:T(8,128)(2,1)S(1)}, bf16[48,4096]{1,0:T(8,128)(2,1)S(1)}, u32[]{:S(2)}, u32[]{:S(2)}) collective-permute-start(bf16[48,4096]{1,0:T(8,128)(2,1)S(1)} %get-tuple-element.79), channel_id=1, source_target_pairs={{0,4},{1,5},{2,6},{3,7},{4,8},{5,9},{6,10},{7,11},{8,12},{9,13},{1... | collective-permute-start | bytes 1179656 | tf_op jit(solution)/shard_map/ppermute | solution.py:120
  97.0 0.7 collective-permute-done.10.refs_0_
  97.6 3.1 %collective-permute-done.11.refs_1_ = bf16[48,4224]{1,0:T(8,128)(2,1)S(1)} collective-permute-done((bf16[48,4224]{1,0:T(8,128)(2,1)S(1)}, bf16[48,4224]{1,0:T(8,128)(2,1)S(1)}, u32[]{:S(2)}, u32[]{:S(2)}) %collective-permute-start.11) | collective-permute-done | bytes 405536 | tf_op jit(solution)/shard_map/ppermute | solution.py:120
  100.8 1.5 shard_map.101
  102.3 2.0 %collective-permute-start.14 = (bf16[48,4096]{1,0:T(8,128)(2,1)S(1)}, bf16[48,4096]{1,0:T(8,128)(2,1)S(1)}, u32[]{:S(2)}, u32[]{:S(2)}) collective-permute-start(bf16[48,4096]{1,0:T(8,128)(2,1)S(1)} %get-tuple-element.75._), channel_id=1, source_target_pairs={{0,12},{1,13},{2,14},{3,15},{4,0},{5,1},{6,2},{7,3},{8,4},{9,5},{1... | collective-permute-start | bytes 1179656 | tf_op jit(solution)/shard_map/ppermute | solution.py:120
  104.3 1.7 shard_map.102
  106.1 4.0 %collective-permute-done.15.high_ref = bf16[48,4096]{1,0:T(8,128)(2,1)S(1)} collective-permute-done((bf16[48,4096]{1,0:T(8,128)(2,1)S(1)}, bf16[48,4096]{1,0:T(8,128)(2,1)S(1)}, u32[]{:S(2)}, u32[]{:S(2)}) %collective-permute-start.15) | collective-permute-done | bytes 393248 | tf_op jit(solution)/shard_map/ppermute | solution.py:120
  110.1 1.3 collective-permute-done.14.low_ref
  112.4 2.0 %collective-permute-start.19 = (bf16[112,4096]{1,0:T(8,128)(2,1)S(1)}, bf16[112,4096]{1,0:T(8,128)(2,1)S(1)}, u32[]{:S(2)}, u32[]{:S(2)}) collective-permute-start(bf16[112,4096]{1,0:T(8,128)(2,1)S(1)} %get-tuple-element.96), channel_id=1, source_target_pairs={{0,12},{1,13},{2,14},{3,15},{4,0},{5,1},{6,2},{7,3},{8,4},{9,5},{1... | collective-permute-start | bytes 2752520 | tf_op jit(solution)/shard_map/ppermute | solution.py:120
  114.4 1.3 collective-permute-start.16
  115.7 0.7 collective-permute-start.17
  116.5 12.0 %collective-permute-done.18.back_ref = bf16[112,4096]{1,0:T(8,128)(2,1)S(1)} collective-permute-done((bf16[112,4096]{1,0:T(8,128)(2,1)S(1)}, bf16[112,4096]{1,0:T(8,128)(2,1)S(1)}, u32[]{:S(2)}, u32[]{:S(2)}) %collective-permute-start.18) | collective-permute-done | bytes 917536 | tf_op jit(solution)/shard_map/ppermute | solution.py:120
  128.5 1.3 collective-permute-done.19.front_ref
  129.8 0.5 shard_map.106
  130.4 3.2 %collective-permute-start.21 = (bf16[32,4096]{1,0:T(8,128)(2,1)S(1)}, bf16[32,4096]{1,0:T(8,128)(2,1)S(1)}, u32[]{:S(2)}, u32[]{:S(2)}) collective-permute-start(bf16[32,4096]{1,0:T(8,128)(2,1)S(1)} %get-tuple-element.102), channel_id=1, source_target_pairs={{0,3},{1,0},{2,1},{3,2},{4,7},{5,4},{6,5},{7,6},{8,11},{9,8},{10,9... | collective-permute-start | bytes 786440 | tf_op jit(solution)/shard_map/ppermute | solution.py:120
  133.6 10.1 %collective-permute-done.16.back_ref = bf16[112,4096]{1,0:T(8,128)(2,1)S(1)} collective-permute-done((bf16[112,4096]{1,0:T(8,128)(2,1)S(1)}, bf16[112,4096]{1,0:T(8,128)(2,1)S(1)}, u32[]{:S(2)}, u32[]{:S(2)}) %collective-permute-start.16) | collective-permute-done | bytes 917536 | tf_op jit(solution)/shard_map/ppermute | solution.py:120
  143.7 1.3 collective-permute-done.17.front_ref
  145.0 0.5 shard_map.104
  145.8 3.2 %collective-permute-start.23 = (bf16[64,4096]{1,0:T(8,128)(2,1)S(1)}, bf16[64,4096]{1,0:T(8,128)(2,1)S(1)}, u32[]{:S(2)}, u32[]{:S(2)}) collective-permute-start(bf16[64,4096]{1,0:T(8,128)(2,1)S(1)} %get-tuple-element.104), channel_id=1, source_target_pairs={{0,3},{1,0},{2,1},{3,2},{4,7},{5,4},{6,5},{7,6},{8,11},{9,8},{10,9... | collective-permute-start | bytes 1572872 | tf_op jit(solution)/shard_map/ppermute | solution.py:120
  149.1 7.2 %collective-permute-done.22 = bf16[64,4096]{1,0:T(8,128)(2,1)S(1)} collective-permute-done((bf16[64,4096]{1,0:T(8,128)(2,1)S(1)}, bf16[64,4096]{1,0:T(8,128)(2,1)S(1)}, u32[]{:S(2)}, u32[]{:S(2)}) %collective-permute-start.22) | collective-permute-done | bytes 524320 | tf_op jit(solution)/shard_map/ppermute | solution.py:120
  156.4 16.3 %all_to_all.33 = bf16[8,8,4096]{2,1,0:T(8,128)(2,1)S(1)} all-to-all(bf16[8,8,4096]{2,1,0:T(8,128)(2,1)S(1)} %fusion), channel_id=1, replica_groups=mesh['dp'=2,'tensor'=8,'expert'=16] {'tensor'}, dimensions={0} | all-to-all | bytes 1048576 | tf_op jit(solution)/shard_map/all_to_all | solution.py:106
  172.8 0.7 fusion.1
  (39 shorter events, 2.9 us)
Async XLA Ops:
  0.0 29.8 %copy-start.3 = (bf16[1,8,4096]{2,1,0:T(8,128)(2,1)S(1)}, bf16[1,8,4096]{2,1,0:T(8,128)(2,1)}, u32[]{:S(2)}) copy-start(bf16[1,8,4096]{2,1,0:T(8,128)(2,1)} %param.11) | copy-start | bytes 196612
  0.0 29.8 %copy-start.4 = (f32[4096]{0:T(1024)S(1)}, f32[4096]{0:T(1024)}, u32[]{:S(2)}) copy-start(f32[4096]{0:T(1024)} %param.12) | copy-start | bytes 49156
  0.0 29.8 %copy-start.5 = (s32[1,8,8]{2,1,0:T(8,128)S(1)}, s32[1,8,8]{2,1,0:T(8,128)}, u32[]{:S(2)}) copy-start(s32[1,8,8]{2,1,0:T(8,128)} %param.13) | copy-start | bytes 772
  0.0 29.8 %copy-start.6 = (s32[1,8,8]{2,1,0:T(8,128)S(1)}, s32[1,8,8]{2,1,0:T(8,128)}, u32[]{:S(2)}) copy-start(s32[1,8,8]{2,1,0:T(8,128)} %param.14) | copy-start | bytes 772
  3.7 61.6 %copy-start.2 = (bf16[1,192,4096]{2,1,0:T(8,128)(2,1)S(1)}, bf16[1,192,4096]{2,1,0:T(8,128)(2,1)}, u32[]{:S(2)}) copy-start(bf16[1,192,4096]{2,1,0:T(8,128)(2,1)} %param.17) | copy-start | bytes 4718596
  30.1 35.2 %copy-start.1 = (bf16[1,192,4096]{2,1,0:T(8,128)(2,1)S(1)}, bf16[1,192,4096]{2,1,0:T(8,128)(2,1)}, u32[]{:S(2)}) copy-start(bf16[1,192,4096]{2,1,0:T(8,128)(2,1)} %param.16) | copy-start | bytes 4718596
  49.0 16.3 %copy-start = (bf16[1,192,4096]{2,1,0:T(8,128)(2,1)S(1)}, bf16[1,192,4096]{2,1,0:T(8,128)(2,1)}, u32[]{:S(2)}) copy-start(bf16[1,192,4096]{2,1,0:T(8,128)(2,1)} %param.15) | copy-start | bytes 4718596
  49.0 9.6 %collective-permute-start.1 = (bf16[64,4224]{1,0:T(8,128)(2,1)S(1)}, bf16[64,4224]{1,0:T(8,128)(2,1)S(1)}, u32[]{:S(2)}, u32[]{:S(2)}) collective-permute-start(bf16[64,4224]{1,0:T(8,128)(2,1)S(1)} %bitcast.36), channel_id=1, source_target_pairs={{0,3},{1,0},{2,1},{3,2},{4,7},{5,4},{6,5},{7,6},{8,11},{9,8},{10,9... | collective-permute-start | bytes 1622024 | tf_op jit(solution)/shard_map/ppermute | solution.py:120
  51.8 10.7 %collective-permute-start = (bf16[64,4224]{1,0:T(8,128)(2,1)S(1)}, bf16[64,4224]{1,0:T(8,128)(2,1)S(1)}, u32[]{:S(2)}, u32[]{:S(2)}) collective-permute-start(bf16[64,4224]{1,0:T(8,128)(2,1)S(1)} %bitcast.37), channel_id=1, source_target_pairs={{0,1},{1,2},{2,3},{3,0},{4,5},{5,6},{6,7},{7,4},{8,9},{9,10},{10,1... | collective-permute-start | bytes 1622024 | tf_op jit(solution)/shard_map/ppermute | solution.py:120
  58.7 10.7 %collective-permute-start.5 = (bf16[32,4224]{1,0:T(8,128)(2,1)S(1)}, bf16[32,4224]{1,0:T(8,128)(2,1)S(1)}, u32[]{:S(2)}, u32[]{:S(2)}) collective-permute-start(bf16[32,4224]{1,0:T(8,128)(2,1)S(1)} %slice.9), channel_id=1, source_target_pairs={{0,3},{1,0},{2,1},{3,2},{4,7},{5,4},{6,5},{7,6},{8,11},{9,8},{10,9... | collective-permute-start | bytes 811016 | tf_op jit(solution)/shard_map/ppermute | solution.py:120
  62.5 10.7 %collective-permute-start.4 = (bf16[32,4224]{1,0:T(8,128)(2,1)S(1)}, bf16[32,4224]{1,0:T(8,128)(2,1)S(1)}, u32[]{:S(2)}, u32[]{:S(2)}) collective-permute-start(bf16[32,4224]{1,0:T(8,128)(2,1)S(1)} %slice.8), channel_id=1, source_target_pairs={{0,1},{1,2},{2,3},{3,0},{4,5},{5,6},{6,7},{7,4},{8,9},{9,10},{10,1... | collective-permute-start | bytes 811016 | tf_op jit(solution)/shard_map/ppermute | solution.py:120
  63.2 13.8 %collective-permute-start.2 = (bf16[112,4224]{1,0:T(8,128)(2,1)S(1)}, bf16[112,4224]{1,0:T(8,128)(2,1)S(1)}, u32[]{:S(2)}, u32[]{:S(2)}) collective-permute-start(bf16[112,4224]{1,0:T(8,128)(2,1)S(1)} %get-tuple-element.61), channel_id=1, source_target_pairs={{0,4},{1,5},{2,6},{3,7},{4,8},{5,9},{6,10},{7,11},{8,12},{9,13},{1... | collective-permute-start | bytes 2838536 | tf_op jit(solution)/shard_map/ppermute | solution.py:120
  63.5 14.9 %collective-permute-start.3 = (bf16[112,4224]{1,0:T(8,128)(2,1)S(1)}, bf16[112,4224]{1,0:T(8,128)(2,1)S(1)}, u32[]{:S(2)}, u32[]{:S(2)}) collective-permute-start(bf16[112,4224]{1,0:T(8,128)(2,1)S(1)} %get-tuple-element.62), channel_id=1, source_target_pairs={{0,12},{1,13},{2,14},{3,15},{4,0},{5,1},{6,2},{7,3},{8,4},{9,5},{1... | collective-permute-start | bytes 2838536 | tf_op jit(solution)/shard_map/ppermute | solution.py:120
  73.8 13.8 %collective-permute-start.6 = (bf16[112,4224]{1,0:T(8,128)(2,1)S(1)}, bf16[112,4224]{1,0:T(8,128)(2,1)S(1)}, u32[]{:S(2)}, u32[]{:S(2)}) collective-permute-start(bf16[112,4224]{1,0:T(8,128)(2,1)S(1)} %get-tuple-element.66), channel_id=1, source_target_pairs={{0,4},{1,5},{2,6},{3,7},{4,8},{5,9},{6,10},{7,11},{8,12},{9,13},{1... | collective-permute-start | bytes 2838536 | tf_op jit(solution)/shard_map/ppermute | solution.py:120
  74.1 14.9 %collective-permute-start.7 = (bf16[112,4224]{1,0:T(8,128)(2,1)S(1)}, bf16[112,4224]{1,0:T(8,128)(2,1)S(1)}, u32[]{:S(2)}, u32[]{:S(2)}) collective-permute-start(bf16[112,4224]{1,0:T(8,128)(2,1)S(1)} %get-tuple-element.67), channel_id=1, source_target_pairs={{0,12},{1,13},{2,14},{3,15},{4,0},{5,1},{6,2},{7,3},{8,4},{9,5},{1... | collective-permute-start | bytes 2838536 | tf_op jit(solution)/shard_map/ppermute | solution.py:120
  82.3 11.1 %collective-permute-start.9 = (bf16[48,4224]{1,0:T(8,128)(2,1)S(1)}, bf16[48,4224]{1,0:T(8,128)(2,1)S(1)}, u32[]{:S(2)}, u32[]{:S(2)}) collective-permute-start(bf16[48,4224]{1,0:T(8,128)(2,1)S(1)} %get-tuple-element.72), channel_id=1, source_target_pairs={{0,12},{1,13},{2,14},{3,15},{4,0},{5,1},{6,2},{7,3},{8,4},{9,5},{1... | collective-permute-start | bytes 1216520 | tf_op jit(solution)/shard_map/ppermute | solution.py:120
  83.1 10.2 %collective-permute-start.8 = (bf16[48,4224]{1,0:T(8,128)(2,1)S(1)}, bf16[48,4224]{1,0:T(8,128)(2,1)S(1)}, u32[]{:S(2)}, u32[]{:S(2)}) collective-permute-start(bf16[48,4224]{1,0:T(8,128)(2,1)S(1)} %get-tuple-element.65._), channel_id=1, source_target_pairs={{0,4},{1,5},{2,6},{3,7},{4,8},{5,9},{6,10},{7,11},{8,12},{9,13},{1... | collective-permute-start | bytes 1216520 | tf_op jit(solution)/shard_map/ppermute | solution.py:120
  89.6 8.0 %collective-permute-start.10 = (bf16[48,4224]{1,0:T(8,128)(2,1)S(1)}, bf16[48,4224]{1,0:T(8,128)(2,1)S(1)}, u32[]{:S(2)}, u32[]{:S(2)}) collective-permute-start(bf16[48,4224]{1,0:T(8,128)(2,1)S(1)} %get-tuple-element.74), channel_id=1, source_target_pairs={{0,4},{1,5},{2,6},{3,7},{4,8},{5,9},{6,10},{7,11},{8,12},{9,13},{1... | collective-permute-start | bytes 1216520 | tf_op jit(solution)/shard_map/ppermute | solution.py:120
  91.6 9.1 %collective-permute-start.11 = (bf16[48,4224]{1,0:T(8,128)(2,1)S(1)}, bf16[48,4224]{1,0:T(8,128)(2,1)S(1)}, u32[]{:S(2)}, u32[]{:S(2)}) collective-permute-start(bf16[48,4224]{1,0:T(8,128)(2,1)S(1)} %get-tuple-element.71._), channel_id=1, source_target_pairs={{0,12},{1,13},{2,14},{3,15},{4,0},{5,1},{6,2},{7,3},{8,4},{9,5},{1... | collective-permute-start | bytes 1216520 | tf_op jit(solution)/shard_map/ppermute | solution.py:120
  94.9 11.2 %collective-permute-start.13 = (bf16[48,4096]{1,0:T(8,128)(2,1)S(1)}, bf16[48,4096]{1,0:T(8,128)(2,1)S(1)}, u32[]{:S(2)}, u32[]{:S(2)}) collective-permute-start(bf16[48,4096]{1,0:T(8,128)(2,1)S(1)} %get-tuple-element.79), channel_id=1, source_target_pairs={{0,4},{1,5},{2,6},{3,7},{4,8},{5,9},{6,10},{7,11},{8,12},{9,13},{1... | collective-permute-start | bytes 1179656 | tf_op jit(solution)/shard_map/ppermute | solution.py:120
  96.9 9.2 %collective-permute-start.12 = (bf16[48,4096]{1,0:T(8,128)(2,1)S(1)}, bf16[48,4096]{1,0:T(8,128)(2,1)S(1)}, u32[]{:S(2)}, u32[]{:S(2)}) collective-permute-start(bf16[48,4096]{1,0:T(8,128)(2,1)S(1)} %get-tuple-element.73._), channel_id=1, source_target_pairs={{0,12},{1,13},{2,14},{3,15},{4,0},{5,1},{6,2},{7,3},{8,4},{9,5},{1... | collective-permute-start | bytes 1179656 | tf_op jit(solution)/shard_map/ppermute | solution.py:120
  102.2 7.9 %collective-permute-start.15 = (bf16[48,4096]{1,0:T(8,128)(2,1)S(1)}, bf16[48,4096]{1,0:T(8,128)(2,1)S(1)}, u32[]{:S(2)}, u32[]{:S(2)}) collective-permute-start(bf16[48,4096]{1,0:T(8,128)(2,1)S(1)} %get-tuple-element.80), channel_id=1, source_target_pairs={{0,4},{1,5},{2,6},{3,7},{4,8},{5,9},{6,10},{7,11},{8,12},{9,13},{1... | collective-permute-start | bytes 1179656 | tf_op jit(solution)/shard_map/ppermute | solution.py:120
  102.3 9.1 %collective-permute-start.14 = (bf16[48,4096]{1,0:T(8,128)(2,1)S(1)}, bf16[48,4096]{1,0:T(8,128)(2,1)S(1)}, u32[]{:S(2)}, u32[]{:S(2)}) collective-permute-start(bf16[48,4096]{1,0:T(8,128)(2,1)S(1)} %get-tuple-element.75._), channel_id=1, source_target_pairs={{0,12},{1,13},{2,14},{3,15},{4,0},{5,1},{6,2},{7,3},{8,4},{9,5},{1... | collective-permute-start | bytes 1179656 | tf_op jit(solution)/shard_map/ppermute | solution.py:120
  112.3 16.1 %collective-permute-start.18 = (bf16[112,4096]{1,0:T(8,128)(2,1)S(1)}, bf16[112,4096]{1,0:T(8,128)(2,1)S(1)}, u32[]{:S(2)}, u32[]{:S(2)}) collective-permute-start(bf16[112,4096]{1,0:T(8,128)(2,1)S(1)} %get-tuple-element.95), channel_id=1, source_target_pairs={{0,4},{1,5},{2,6},{3,7},{4,8},{5,9},{6,10},{7,11},{8,12},{9,13},{1... | collective-permute-start | bytes 2752520 | tf_op jit(solution)/shard_map/ppermute | solution.py:120
  112.4 17.3 %collective-permute-start.19 = (bf16[112,4096]{1,0:T(8,128)(2,1)S(1)}, bf16[112,4096]{1,0:T(8,128)(2,1)S(1)}, u32[]{:S(2)}, u32[]{:S(2)}) collective-permute-start(bf16[112,4096]{1,0:T(8,128)(2,1)S(1)} %get-tuple-element.96), channel_id=1, source_target_pairs={{0,12},{1,13},{2,14},{3,15},{4,0},{5,1},{6,2},{7,3},{8,4},{9,5},{1... | collective-permute-start | bytes 2752520 | tf_op jit(solution)/shard_map/ppermute | solution.py:120
  114.4 29.3 %collective-permute-start.16 = (bf16[112,4096]{1,0:T(8,128)(2,1)S(1)}, bf16[112,4096]{1,0:T(8,128)(2,1)S(1)}, u32[]{:S(2)}, u32[]{:S(2)}) collective-permute-start(bf16[112,4096]{1,0:T(8,128)(2,1)S(1)} %get-tuple-element.85), channel_id=1, source_target_pairs={{0,4},{1,5},{2,6},{3,7},{4,8},{5,9},{6,10},{7,11},{8,12},{9,13},{1... | collective-permute-start | bytes 2752520 | tf_op jit(solution)/shard_map/ppermute | solution.py:120
  115.7 29.3 %collective-permute-start.17 = (bf16[112,4096]{1,0:T(8,128)(2,1)S(1)}, bf16[112,4096]{1,0:T(8,128)(2,1)S(1)}, u32[]{:S(2)}, u32[]{:S(2)}) collective-permute-start(bf16[112,4096]{1,0:T(8,128)(2,1)S(1)} %get-tuple-element.86._), channel_id=1, source_target_pairs={{0,12},{1,13},{2,14},{3,15},{4,0},{5,1},{6,2},{7,3},{8,4},{9,5},{1... | collective-permute-start | bytes 2752520 | tf_op jit(solution)/shard_map/ppermute | solution.py:120
  130.3 15.3 %collective-permute-start.20 = (bf16[32,4096]{1,0:T(8,128)(2,1)S(1)}, bf16[32,4096]{1,0:T(8,128)(2,1)S(1)}, u32[]{:S(2)}, u32[]{:S(2)}) collective-permute-start(bf16[32,4096]{1,0:T(8,128)(2,1)S(1)} %get-tuple-element.101), channel_id=1, source_target_pairs={{0,1},{1,2},{2,3},{3,0},{4,5},{5,6},{6,7},{7,4},{8,9},{9,10},{10,1... | collective-permute-start | bytes 786440 | tf_op jit(solution)/shard_map/ppermute | solution.py:120
  130.4 15.2 %collective-permute-start.21 = (bf16[32,4096]{1,0:T(8,128)(2,1)S(1)}, bf16[32,4096]{1,0:T(8,128)(2,1)S(1)}, u32[]{:S(2)}, u32[]{:S(2)}) collective-permute-start(bf16[32,4096]{1,0:T(8,128)(2,1)S(1)} %get-tuple-element.102), channel_id=1, source_target_pairs={{0,3},{1,0},{2,1},{3,2},{4,7},{5,4},{6,5},{7,6},{8,11},{9,8},{10,9... | collective-permute-start | bytes 786440 | tf_op jit(solution)/shard_map/ppermute | solution.py:120
  145.7 10.5 %collective-permute-start.22 = (bf16[64,4096]{1,0:T(8,128)(2,1)S(1)}, bf16[64,4096]{1,0:T(8,128)(2,1)S(1)}, u32[]{:S(2)}, u32[]{:S(2)}) collective-permute-start(bf16[64,4096]{1,0:T(8,128)(2,1)S(1)} %get-tuple-element.103), channel_id=1, source_target_pairs={{0,1},{1,2},{2,3},{3,0},{4,5},{5,6},{6,7},{7,4},{8,9},{9,10},{10,1... | collective-permute-start | bytes 1572872 | tf_op jit(solution)/shard_map/ppermute | solution.py:120
  145.8 10.4 %collective-permute-start.23 = (bf16[64,4096]{1,0:T(8,128)(2,1)S(1)}, bf16[64,4096]{1,0:T(8,128)(2,1)S(1)}, u32[]{:S(2)}, u32[]{:S(2)}) collective-permute-start(bf16[64,4096]{1,0:T(8,128)(2,1)S(1)} %get-tuple-element.104), channel_id=1, source_target_pairs={{0,3},{1,0},{2,1},{3,2},{4,7},{5,4},{6,5},{7,6},{8,11},{9,8},{10,9... | collective-permute-start | bytes 1572872 | tf_op jit(solution)/shard_map/ppermute | solution.py:120

commit v12 on v11

--- a/solution.py
+++ b/solution.py
@@ -12,7 +12,7 @@
 SIDE = 4
 LANES = 128
 CHUNK = 1024
-STRIPE = 512
+STRIPE = 1024
 GRANT = 8 << 20
 STREAM = 62 << 20
 
@@ -398,8 +398,8 @@
     second_down = both(second_far_high, second_far_low, 1)[::-1]
     second_near_out = experts(*second_near, after=second_far_low)
     first_down, second_down = tie(first_down, second_down)
-    first_send = join(second_near_out[0], *first_near_out, *first_down, *first_hot)
-    second_send = join(first_send[1], *second_near_out, *second_down, *second_hot)
+    second_send = join(second_near_out[0], *second_near_out, *second_down, *second_hot)
+    first_send = join(second_send[0], *first_near_out, *first_down, *first_hot)
     first_got = both(*first_send, 1)
     second_got = both(*second_send, 1)
     own, back = total(first_own[0], first_got, (first_ahead, first_behind), (tokens, tokens))

time: 174 us -> 176 us (1.011)
  the two profiles are of different devices: /device:TPU:24 before, /device:TPU:6 now
where the time goes in v12:
time: 176 us
  blocking collectives  61.1 us (35%)
  waiting for transfers between devices  59.4 us (34%)
  starting transfers between devices  36.8 us (21%)
  Pallas kernels  17.6 us (10%)
    all_to_all x3, blocking collectives, swap_over_tensor(): lax.all_to_all(value, 'tensor', split_axis=0, concat_axis=0, tiled=True)  61.1 us
    ppermute x24, waiting for transfers between devices, shift(): return lax.ppermute(value, ('dp', 'expert'), pairs)  59.4 us
    ppermute x24, starting transfers between devices, shift(): return lax.ppermute(value, ('dp', 'expert'), pairs)  36.8 us
    pallas_call x6, Pallas kernels, run_expert(): pl.pallas_call(functools.partial(expert_kernel, count), out_shape=[jax.Sh...  9.38 us
  transfers between devices with their start and end apart: 24, of which 15 were waited for; matrix products, arithmetic and copies ran while one was open for 0% of the time, Pallas kernels for 8%

profile of v12, /device:TPU:6, one launch (start us, length us, event | category | flops | bytes accessed | tf_op | source)
XLA Modules:
  0.0 176.1 jit_solution(15970215816049730654)
XLA Ops:
  0.0 3.4 %shard_map.91 = bf16[64,4096]{1,0:T(8,128)(2,1)} custom-call(bf16[64,512]{1,0:T(8,128)(2,1)} %bitcast.46, bf16[512,4096]{1,0:T(8,128)(2,1)} %proj_hbm.1), custom_call_target="tpu_custom_call" | custom-call | flops 268435456 | bytes 4194304 | tf_op jit(solution)/shard_map/pallas_call | solution.py:47
  3.4 26.1 %all_to_all.31 = bf16[8,8,4096]{2,1,0:T(8,128)(2,1)S(1)} all-to-all(bf16[8,8,4096]{2,1,0:T(8,128)(2,1)} %bitcast.45), channel_id=1, replica_groups=mesh['dp'=2,'tensor'=8,'expert'=16] {'tensor'}, dimensions={0} | all-to-all | bytes 1048576 | tf_op jit(solution)/shard_map/all_to_all | solution.py:106
  29.8 18.9 %all_to_all.32 = bf16[8,8,4224]{2,1,0:T(8,128)(2,1)S(1)} all-to-all(bf16[8,8,4224]{2,1,0:T(8,128)(2,1)S(1)} %bitcast.40), channel_id=1, replica_groups=mesh['dp'=2,'tensor'=8,'expert'=16] {'tensor'}, dimensions={0} | all-to-all | bytes 1081344 | tf_op jit(solution)/shard_map/all_to_all | solution.py:106
  48.8 0.8 collective-permute-start.1
  49.6 2.4 %collective-permute-start = (bf16[64,4224]{1,0:T(8,128)(2,1)S(1)}, bf16[64,4224]{1,0:T(8,128)(2,1)S(1)}, u32[]{:S(2)}, u32[]{:S(2)}) collective-permute-start(bf16[64,4224]{1,0:T(8,128)(2,1)S(1)} %bitcast.37), channel_id=1, source_target_pairs={{0,1},{1,2},{2,3},{3,0},{4,5},{5,6},{6,7},{7,4},{8,9},{9,10},{10,1... | collective-permute-start | bytes 1622024 | tf_op jit(solution)/shard_map/ppermute | solution.py:120
  52.0 7.3 %collective-permute-done.1._.low_ref = bf16[64,4224]{1,0:T(8,128)(2,1)S(1)} collective-permute-done((bf16[64,4224]{1,0:T(8,128)(2,1)S(1)}, bf16[64,4224]{1,0:T(8,128)(2,1)S(1)}, u32[]{:S(2)}, u32[]{:S(2)}) %collective-permute-start.1) | collective-permute-done | bytes 540704 | tf_op jit(solution)/shard_map/ppermute | solution.py:120
  59.5 3.3 %collective-permute-start.4 = (bf16[32,4224]{1,0:T(8,128)(2,1)S(1)}, bf16[32,4224]{1,0:T(8,128)(2,1)S(1)}, u32[]{:S(2)}, u32[]{:S(2)}) collective-permute-start(bf16[32,4224]{1,0:T(8,128)(2,1)S(1)} %slice.8), channel_id=1, source_target_pairs={{0,1},{1,2},{2,3},{3,0},{4,5},{5,6},{6,7},{7,4},{8,9},{9,10},{10,1... | collective-permute-start | bytes 811016 | tf_op jit(solution)/shard_map/ppermute | solution.py:120
  62.8 0.6 shard_map.93
  63.4 3.2 %collective-permute-start.2 = (bf16[112,4224]{1,0:T(8,128)(2,1)S(1)}, bf16[112,4224]{1,0:T(8,128)(2,1)S(1)}, u32[]{:S(2)}, u32[]{:S(2)}) collective-permute-start(bf16[112,4224]{1,0:T(8,128)(2,1)S(1)} %get-tuple-element.61), channel_id=1, source_target_pairs={{0,4},{1,5},{2,6},{3,7},{4,8},{5,9},{6,10},{7,11},{8,12},{9,13},{1... | collective-permute-start | bytes 2838536 | tf_op jit(solution)/shard_map/ppermute | solution.py:120
  66.7 1.5 shard_map.94._.own_ref
  68.2 1.8 %collective-permute-done.5.refs_1_ = bf16[32,4224]{1,0:T(8,128)(2,1)S(1)} collective-permute-done((bf16[32,4224]{1,0:T(8,128)(2,1)S(1)}, bf16[32,4224]{1,0:T(8,128)(2,1)S(1)}, u32[]{:S(2)}, u32[]{:S(2)}) %collective-permute-start.5) | collective-permute-done | bytes 270368 | tf_op jit(solution)/shard_map/ppermute | solution.py:120
  70.0 0.6 shard_map.96
  70.7 2.9 %collective-permute-start.6 = (bf16[112,4224]{1,0:T(8,128)(2,1)S(1)}, bf16[112,4224]{1,0:T(8,128)(2,1)S(1)}, u32[]{:S(2)}, u32[]{:S(2)}) collective-permute-start(bf16[112,4224]{1,0:T(8,128)(2,1)S(1)} %get-tuple-element.66), channel_id=1, source_target_pairs={{0,4},{1,5},{2,6},{3,7},{4,8},{5,9},{6,10},{7,11},{8,12},{9,13},{1... | collective-permute-start | bytes 2838536 | tf_op jit(solution)/shard_map/ppermute | solution.py:120
  74.0 4.4 %collective-permute-done.2.refs_0_.back_ref = bf16[112,4224]{1,0:T(8,128)(2,1)S(1)} collective-permute-done((bf16[112,4224]{1,0:T(8,128)(2,1)S(1)}, bf16[112,4224]{1,0:T(8,128)(2,1)S(1)}, u32[]{:S(2)}, u32[]{:S(2)}) %collective-permute-start.2) | collective-permute-done | bytes 946208 | tf_op jit(solution)/shard_map/ppermute | solution.py:120
  78.4 1.9 %collective-permute-done.3.refs_1_.front_ref = bf16[112,4224]{1,0:T(8,128)(2,1)S(1)} collective-permute-done((bf16[112,4224]{1,0:T(8,128)(2,1)S(1)}, bf16[112,4224]{1,0:T(8,128)(2,1)S(1)}, u32[]{:S(2)}, u32[]{:S(2)}) %collective-permute-start.3) | collective-permute-done | bytes 946208 | tf_op jit(solution)/shard_map/ppermute | solution.py:120
  80.3 1.7 shard_map.95
  82.0 1.5 shard_map.97._.own_ref
  83.6 0.6 shard_map.98
  84.2 1.6 collective-permute-start.9
  85.8 0.7 collective-permute-start.8
  86.5 2.1 %collective-permute-done.6.back_ref.refs_0_ = bf16[112,4224]{1,0:T(8,128)(2,1)S(1)} collective-permute-done((bf16[112,4224]{1,0:T(8,128)(2,1)S(1)}, bf16[112,4224]{1,0:T(8,128)(2,1)S(1)}, u32[]{:S(2)}, u32[]{:S(2)}) %collective-permute-start.6) | collective-permute-done | bytes 946208 | tf_op jit(solution)/shard_map/ppermute | solution.py:120
  88.5 1.9 %collective-permute-done.7.front_ref.refs_1_ = bf16[112,4224]{1,0:T(8,128)(2,1)S(1)} collective-permute-done((bf16[112,4224]{1,0:T(8,128)(2,1)S(1)}, bf16[112,4224]{1,0:T(8,128)(2,1)S(1)}, u32[]{:S(2)}, u32[]{:S(2)}) %collective-permute-start.7) | collective-permute-done | bytes 946208 | tf_op jit(solution)/shard_map/ppermute | solution.py:120
  90.4 0.6 shard_map.99
  91.1 1.0 collective-permute-start.10
  92.1 2.3 %collective-permute-start.11 = (bf16[48,4224]{1,0:T(8,128)(2,1)S(1)}, bf16[48,4224]{1,0:T(8,128)(2,1)S(1)}, u32[]{:S(2)}, u32[]{:S(2)}) collective-permute-start(bf16[48,4224]{1,0:T(8,128)(2,1)S(1)} %get-tuple-element.71._), channel_id=1, source_target_pairs={{0,12},{1,13},{2,14},{3,15},{4,0},{5,1},{6,2},{7,3},{8,4},{9,5},{1... | collective-permute-start | bytes 1216520 | tf_op jit(solution)/shard_map/ppermute | solution.py:120
  94.9 1.5 shard_map.100
  96.3 1.0 collective-permute-start.13
  97.3 2.3 %collective-permute-start.12 = (bf16[48,4096]{1,0:T(8,128)(2,1)S(1)}, bf16[48,4096]{1,0:T(8,128)(2,1)S(1)}, u32[]{:S(2)}, u32[]{:S(2)}) collective-permute-start(bf16[48,4096]{1,0:T(8,128)(2,1)S(1)} %get-tuple-element.73._), channel_id=1, source_target_pairs={{0,12},{1,13},{2,14},{3,15},{4,0},{5,1},{6,2},{7,3},{8,4},{9,5},{1... | collective-permute-start | bytes 1179656 | tf_op jit(solution)/shard_map/ppermute | solution.py:120
  99.7 0.6 collective-permute-done.10.refs_0_
  100.3 1.5 shard_map.101
  101.9 3.2 %collective-permute-start.14 = (bf16[48,4096]{1,0:T(8,128)(2,1)S(1)}, bf16[48,4096]{1,0:T(8,128)(2,1)S(1)}, u32[]{:S(2)}, u32[]{:S(2)}) collective-permute-start(bf16[48,4096]{1,0:T(8,128)(2,1)S(1)} %get-tuple-element.75._), channel_id=1, source_target_pairs={{0,12},{1,13},{2,14},{3,15},{4,0},{5,1},{6,2},{7,3},{8,4},{9,5},{1... | collective-permute-start | bytes 1179656 | tf_op jit(solution)/shard_map/ppermute | solution.py:120
  105.1 1.7 shard_map.102
  106.9 3.9 %collective-permute-done.15.high_ref = bf16[48,4096]{1,0:T(8,128)(2,1)S(1)} collective-permute-done((bf16[48,4096]{1,0:T(8,128)(2,1)S(1)}, bf16[48,4096]{1,0:T(8,128)(2,1)S(1)}, u32[]{:S(2)}, u32[]{:S(2)}) %collective-permute-start.15) | collective-permute-done | bytes 393248 | tf_op jit(solution)/shard_map/ppermute | solution.py:120
  111.3 3.4 %collective-permute-start.19 = (bf16[112,4096]{1,0:T(8,128)(2,1)S(1)}, bf16[112,4096]{1,0:T(8,128)(2,1)S(1)}, u32[]{:S(2)}, u32[]{:S(2)}) collective-permute-start(bf16[112,4096]{1,0:T(8,128)(2,1)S(1)} %get-tuple-element.96), channel_id=1, source_target_pairs={{0,12},{1,13},{2,14},{3,15},{4,0},{5,1},{6,2},{7,3},{8,4},{9,5},{1... | collective-permute-start | bytes 2752520 | tf_op jit(solution)/shard_map/ppermute | solution.py:120
  115.6 3.1 %collective-permute-start.17 = (bf16[112,4096]{1,0:T(8,128)(2,1)S(1)}, bf16[112,4096]{1,0:T(8,128)(2,1)S(1)}, u32[]{:S(2)}, u32[]{:S(2)}) collective-permute-start(bf16[112,4096]{1,0:T(8,128)(2,1)S(1)} %get-tuple-element.92), channel_id=1, source_target_pairs={{0,12},{1,13},{2,14},{3,15},{4,0},{5,1},{6,2},{7,3},{8,4},{9,5},{1... | collective-permute-start | bytes 2752520 | tf_op jit(solution)/shard_map/ppermute | solution.py:120
  118.8 9.2 %collective-permute-done.19.front_ref = bf16[112,4096]{1,0:T(8,128)(2,1)S(1)} collective-permute-done((bf16[112,4096]{1,0:T(8,128)(2,1)S(1)}, bf16[112,4096]{1,0:T(8,128)(2,1)S(1)}, u32[]{:S(2)}, u32[]{:S(2)}) %collective-permute-start.19) | collective-permute-done | bytes 917536 | tf_op jit(solution)/shard_map/ppermute | solution.py:120
  128.0 4.1 %collective-permute-done.18.back_ref = bf16[112,4096]{1,0:T(8,128)(2,1)S(1)} collective-permute-done((bf16[112,4096]{1,0:T(8,128)(2,1)S(1)}, bf16[112,4096]{1,0:T(8,128)(2,1)S(1)}, u32[]{:S(2)}, u32[]{:S(2)}) %collective-permute-start.18) | collective-permute-done | bytes 917536 | tf_op jit(solution)/shard_map/ppermute | solution.py:120
  132.1 0.5 shard_map.106
  132.6 0.6 collective-permute-start.20
  133.2 1.5 collective-permute-start.21
  134.7 12.8 %collective-permute-done.16.back_ref = bf16[112,4096]{1,0:T(8,128)(2,1)S(1)} collective-permute-done((bf16[112,4096]{1,0:T(8,128)(2,1)S(1)}, bf16[112,4096]{1,0:T(8,128)(2,1)S(1)}, u32[]{:S(2)}, u32[]{:S(2)}) %collective-permute-start.16) | collective-permute-done | bytes 917536 | tf_op jit(solution)/shard_map/ppermute | solution.py:120
  147.5 0.5 shard_map.105
  148.2 0.5 collective-permute-start.22
  148.8 1.6 collective-permute-start.23
  150.4 7.2 %collective-permute-done.22 = bf16[64,4096]{1,0:T(8,128)(2,1)S(1)} collective-permute-done((bf16[64,4096]{1,0:T(8,128)(2,1)S(1)}, bf16[64,4096]{1,0:T(8,128)(2,1)S(1)}, u32[]{:S(2)}, u32[]{:S(2)}) %collective-permute-start.22) | collective-permute-done | bytes 524320 | tf_op jit(solution)/shard_map/ppermute | solution.py:120
  157.5 1.6 collective-permute-done.23
  159.3 16.0 %all_to_all.33 = bf16[8,8,4096]{2,1,0:T(8,128)(2,1)S(1)} all-to-all(bf16[8,8,4096]{2,1,0:T(8,128)(2,1)S(1)} %fusion), channel_id=1, replica_groups=mesh['dp'=2,'tensor'=8,'expert'=16] {'tensor'}, dimensions={0} | all-to-all | bytes 1048576 | tf_op jit(solution)/shard_map/all_to_all | solution.py:106
  175.5 0.7 fusion.1
  (39 shorter events, 3.4 us)
Async XLA Ops:
  0.0 29.5 %copy-start.3 = (bf16[1,8,4096]{2,1,0:T(8,128)(2,1)S(1)}, bf16[1,8,4096]{2,1,0:T(8,128)(2,1)}, u32[]{:S(2)}) copy-start(bf16[1,8,4096]{2,1,0:T(8,128)(2,1)} %param.11) | copy-start | bytes 196612
  0.0 29.5 %copy-start.4 = (f32[4096]{0:T(1024)S(1)}, f32[4096]{0:T(1024)}, u32[]{:S(2)}) copy-start(f32[4096]{0:T(1024)} %param.12) | copy-start | bytes 49156
  0.0 29.5 %copy-start.5 = (s32[1,8,8]{2,1,0:T(8,128)S(1)}, s32[1,8,8]{2,1,0:T(8,128)}, u32[]{:S(2)}) copy-start(s32[1,8,8]{2,1,0:T(8,128)} %param.13) | copy-start | bytes 772
  0.0 29.5 %copy-start.6 = (s32[1,8,8]{2,1,0:T(8,128)S(1)}, s32[1,8,8]{2,1,0:T(8,128)}, u32[]{:S(2)}) copy-start(s32[1,8,8]{2,1,0:T(8,128)} %param.14) | copy-start | bytes 772
  3.4 63.3 %copy-start.2 = (bf16[1,192,4096]{2,1,0:T(8,128)(2,1)S(1)}, bf16[1,192,4096]{2,1,0:T(8,128)(2,1)}, u32[]{:S(2)}) copy-start(bf16[1,192,4096]{2,1,0:T(8,128)(2,1)} %param.17) | copy-start | bytes 4718596
  29.8 36.9 %copy-start.1 = (bf16[1,192,4096]{2,1,0:T(8,128)(2,1)S(1)}, bf16[1,192,4096]{2,1,0:T(8,128)(2,1)}, u32[]{:S(2)}) copy-start(bf16[1,192,4096]{2,1,0:T(8,128)(2,1)} %param.16) | copy-start | bytes 4718596
  48.8 18.0 %copy-start = (bf16[1,192,4096]{2,1,0:T(8,128)(2,1)S(1)}, bf16[1,192,4096]{2,1,0:T(8,128)(2,1)}, u32[]{:S(2)}) copy-start(bf16[1,192,4096]{2,1,0:T(8,128)(2,1)} %param.15) | copy-start | bytes 4718596
  48.8 10.6 %collective-permute-start.1 = (bf16[64,4224]{1,0:T(8,128)(2,1)S(1)}, bf16[64,4224]{1,0:T(8,128)(2,1)S(1)}, u32[]{:S(2)}, u32[]{:S(2)}) collective-permute-start(bf16[64,4224]{1,0:T(8,128)(2,1)S(1)} %bitcast.36), channel_id=1, source_target_pairs={{0,3},{1,0},{2,1},{3,2},{4,7},{5,4},{6,5},{7,6},{8,11},{9,8},{10,9... | collective-permute-start | bytes 1622024 | tf_op jit(solution)/shard_map/ppermute | solution.py:120
  49.6 9.9 %collective-permute-start = (bf16[64,4224]{1,0:T(8,128)(2,1)S(1)}, bf16[64,4224]{1,0:T(8,128)(2,1)S(1)}, u32[]{:S(2)}, u32[]{:S(2)}) collective-permute-start(bf16[64,4224]{1,0:T(8,128)(2,1)S(1)} %bitcast.37), channel_id=1, source_target_pairs={{0,1},{1,2},{2,3},{3,0},{4,5},{5,6},{6,7},{7,4},{8,9},{9,10},{10,1... | collective-permute-start | bytes 1622024 | tf_op jit(solution)/shard_map/ppermute | solution.py:120
  59.3 10.7 %collective-permute-start.5 = (bf16[32,4224]{1,0:T(8,128)(2,1)S(1)}, bf16[32,4224]{1,0:T(8,128)(2,1)S(1)}, u32[]{:S(2)}, u32[]{:S(2)}) collective-permute-start(bf16[32,4224]{1,0:T(8,128)(2,1)S(1)} %slice.9), channel_id=1, source_target_pairs={{0,3},{1,0},{2,1},{3,2},{4,7},{5,4},{6,5},{7,6},{8,11},{9,8},{10,9... | collective-permute-start | bytes 811016 | tf_op jit(solution)/shard_map/ppermute | solution.py:120
  59.5 10.5 %collective-permute-start.4 = (bf16[32,4224]{1,0:T(8,128)(2,1)S(1)}, bf16[32,4224]{1,0:T(8,128)(2,1)S(1)}, u32[]{:S(2)}, u32[]{:S(2)}) collective-permute-start(bf16[32,4224]{1,0:T(8,128)(2,1)S(1)} %slice.8), channel_id=1, source_target_pairs={{0,1},{1,2},{2,3},{3,0},{4,5},{5,6},{6,7},{7,4},{8,9},{9,10},{10,1... | collective-permute-start | bytes 811016 | tf_op jit(solution)/shard_map/ppermute | solution.py:120
  63.4 15.0 %collective-permute-start.2 = (bf16[112,4224]{1,0:T(8,128)(2,1)S(1)}, bf16[112,4224]{1,0:T(8,128)(2,1)S(1)}, u32[]{:S(2)}, u32[]{:S(2)}) collective-permute-start(bf16[112,4224]{1,0:T(8,128)(2,1)S(1)} %get-tuple-element.61), channel_id=1, source_target_pairs={{0,4},{1,5},{2,6},{3,7},{4,8},{5,9},{6,10},{7,11},{8,12},{9,13},{1... | collective-permute-start | bytes 2838536 | tf_op jit(solution)/shard_map/ppermute | solution.py:120
  66.6 13.7 %collective-permute-start.3 = (bf16[112,4224]{1,0:T(8,128)(2,1)S(1)}, bf16[112,4224]{1,0:T(8,128)(2,1)S(1)}, u32[]{:S(2)}, u32[]{:S(2)}) collective-permute-start(bf16[112,4224]{1,0:T(8,128)(2,1)S(1)} %get-tuple-element.62), channel_id=1, source_target_pairs={{0,12},{1,13},{2,14},{3,15},{4,0},{5,1},{6,2},{7,3},{8,4},{9,5},{1... | collective-permute-start | bytes 2838536 | tf_op jit(solution)/shard_map/ppermute | solution.py:120
  70.7 17.9 %collective-permute-start.6 = (bf16[112,4224]{1,0:T(8,128)(2,1)S(1)}, bf16[112,4224]{1,0:T(8,128)(2,1)S(1)}, u32[]{:S(2)}, u32[]{:S(2)}) collective-permute-start(bf16[112,4224]{1,0:T(8,128)(2,1)S(1)} %get-tuple-element.66), channel_id=1, source_target_pairs={{0,4},{1,5},{2,6},{3,7},{4,8},{5,9},{6,10},{7,11},{8,12},{9,13},{1... | collective-permute-start | bytes 2838536 | tf_op jit(solution)/shard_map/ppermute | solution.py:120
  73.5 16.9 %collective-permute-start.7 = (bf16[112,4224]{1,0:T(8,128)(2,1)S(1)}, bf16[112,4224]{1,0:T(8,128)(2,1)S(1)}, u32[]{:S(2)}, u32[]{:S(2)}) collective-permute-start(bf16[112,4224]{1,0:T(8,128)(2,1)S(1)} %get-tuple-element.67), channel_id=1, source_target_pairs={{0,12},{1,13},{2,14},{3,15},{4,0},{5,1},{6,2},{7,3},{8,4},{9,5},{1... | collective-permute-start | bytes 2838536 | tf_op jit(solution)/shard_map/ppermute | solution.py:120
  84.2 10.6 %collective-permute-start.9 = (bf16[48,4224]{1,0:T(8,128)(2,1)S(1)}, bf16[48,4224]{1,0:T(8,128)(2,1)S(1)}, u32[]{:S(2)}, u32[]{:S(2)}) collective-permute-start(bf16[48,4224]{1,0:T(8,128)(2,1)S(1)} %get-tuple-element.72), channel_id=1, source_target_pairs={{0,12},{1,13},{2,14},{3,15},{4,0},{5,1},{6,2},{7,3},{8,4},{9,5},{1... | collective-permute-start | bytes 1216520 | tf_op jit(solution)/shard_map/ppermute | solution.py:120
  85.8 9.1 %collective-permute-start.8 = (bf16[48,4224]{1,0:T(8,128)(2,1)S(1)}, bf16[48,4224]{1,0:T(8,128)(2,1)S(1)}, u32[]{:S(2)}, u32[]{:S(2)}) collective-permute-start(bf16[48,4224]{1,0:T(8,128)(2,1)S(1)} %get-tuple-element.65._), channel_id=1, source_target_pairs={{0,4},{1,5},{2,6},{3,7},{4,8},{5,9},{6,10},{7,11},{8,12},{9,13},{1... | collective-permute-start | bytes 1216520 | tf_op jit(solution)/shard_map/ppermute | solution.py:120
  91.1 9.2 %collective-permute-start.10 = (bf16[48,4224]{1,0:T(8,128)(2,1)S(1)}, bf16[48,4224]{1,0:T(8,128)(2,1)S(1)}, u32[]{:S(2)}, u32[]{:S(2)}) collective-permute-start(bf16[48,4224]{1,0:T(8,128)(2,1)S(1)} %get-tuple-element.74), channel_id=1, source_target_pairs={{0,4},{1,5},{2,6},{3,7},{4,8},{5,9},{6,10},{7,11},{8,12},{9,13},{1... | collective-permute-start | bytes 1216520 | tf_op jit(solution)/shard_map/ppermute | solution.py:120
  92.1 8.2 %collective-permute-start.11 = (bf16[48,4224]{1,0:T(8,128)(2,1)S(1)}, bf16[48,4224]{1,0:T(8,128)(2,1)S(1)}, u32[]{:S(2)}, u32[]{:S(2)}) collective-permute-start(bf16[48,4224]{1,0:T(8,128)(2,1)S(1)} %get-tuple-element.71._), channel_id=1, source_target_pairs={{0,12},{1,13},{2,14},{3,15},{4,0},{5,1},{6,2},{7,3},{8,4},{9,5},{1... | collective-permute-start | bytes 1216520 | tf_op jit(solution)/shard_map/ppermute | solution.py:120
  96.3 10.5 %collective-permute-start.13 = (bf16[48,4096]{1,0:T(8,128)(2,1)S(1)}, bf16[48,4096]{1,0:T(8,128)(2,1)S(1)}, u32[]{:S(2)}, u32[]{:S(2)}) collective-permute-start(bf16[48,4096]{1,0:T(8,128)(2,1)S(1)} %get-tuple-element.78), channel_id=1, source_target_pairs={{0,4},{1,5},{2,6},{3,7},{4,8},{5,9},{6,10},{7,11},{8,12},{9,13},{1... | collective-permute-start | bytes 1179656 | tf_op jit(solution)/shard_map/ppermute | solution.py:120
  97.3 9.5 %collective-permute-start.12 = (bf16[48,4096]{1,0:T(8,128)(2,1)S(1)}, bf16[48,4096]{1,0:T(8,128)(2,1)S(1)}, u32[]{:S(2)}, u32[]{:S(2)}) collective-permute-start(bf16[48,4096]{1,0:T(8,128)(2,1)S(1)} %get-tuple-element.73._), channel_id=1, source_target_pairs={{0,12},{1,13},{2,14},{3,15},{4,0},{5,1},{6,2},{7,3},{8,4},{9,5},{1... | collective-permute-start | bytes 1179656 | tf_op jit(solution)/shard_map/ppermute | solution.py:120
  101.7 9.1 %collective-permute-start.15 = (bf16[48,4096]{1,0:T(8,128)(2,1)S(1)}, bf16[48,4096]{1,0:T(8,128)(2,1)S(1)}, u32[]{:S(2)}, u32[]{:S(2)}) collective-permute-start(bf16[48,4096]{1,0:T(8,128)(2,1)S(1)} %get-tuple-element.79), channel_id=1, source_target_pairs={{0,4},{1,5},{2,6},{3,7},{4,8},{5,9},{6,10},{7,11},{8,12},{9,13},{1... | collective-permute-start | bytes 1179656 | tf_op jit(solution)/shard_map/ppermute | solution.py:120
  101.9 8.9 %collective-permute-start.14 = (bf16[48,4096]{1,0:T(8,128)(2,1)S(1)}, bf16[48,4096]{1,0:T(8,128)(2,1)S(1)}, u32[]{:S(2)}, u32[]{:S(2)}) collective-permute-start(bf16[48,4096]{1,0:T(8,128)(2,1)S(1)} %get-tuple-element.75._), channel_id=1, source_target_pairs={{0,12},{1,13},{2,14},{3,15},{4,0},{5,1},{6,2},{7,3},{8,4},{9,5},{1... | collective-permute-start | bytes 1179656 | tf_op jit(solution)/shard_map/ppermute | solution.py:120
  111.3 16.7 %collective-permute-start.19 = (bf16[112,4096]{1,0:T(8,128)(2,1)S(1)}, bf16[112,4096]{1,0:T(8,128)(2,1)S(1)}, u32[]{:S(2)}, u32[]{:S(2)}) collective-permute-start(bf16[112,4096]{1,0:T(8,128)(2,1)S(1)} %get-tuple-element.96), channel_id=1, source_target_pairs={{0,12},{1,13},{2,14},{3,15},{4,0},{5,1},{6,2},{7,3},{8,4},{9,5},{1... | collective-permute-start | bytes 2752520 | tf_op jit(solution)/shard_map/ppermute | solution.py:120
  114.7 17.4 %collective-permute-start.18 = (bf16[112,4096]{1,0:T(8,128)(2,1)S(1)}, bf16[112,4096]{1,0:T(8,128)(2,1)S(1)}, u32[]{:S(2)}, u32[]{:S(2)}) collective-permute-start(bf16[112,4096]{1,0:T(8,128)(2,1)S(1)} %get-tuple-element.84._), channel_id=1, source_target_pairs={{0,4},{1,5},{2,6},{3,7},{4,8},{5,9},{6,10},{7,11},{8,12},{9,13},{1... | collective-permute-start | bytes 2752520 | tf_op jit(solution)/shard_map/ppermute | solution.py:120
  115.1 32.4 %collective-permute-start.16 = (bf16[112,4096]{1,0:T(8,128)(2,1)S(1)}, bf16[112,4096]{1,0:T(8,128)(2,1)S(1)}, u32[]{:S(2)}, u32[]{:S(2)}) collective-permute-start(bf16[112,4096]{1,0:T(8,128)(2,1)S(1)} %get-tuple-element.91), channel_id=1, source_target_pairs={{0,4},{1,5},{2,6},{3,7},{4,8},{5,9},{6,10},{7,11},{8,12},{9,13},{1... | collective-permute-start | bytes 2752520 | tf_op jit(solution)/shard_map/ppermute | solution.py:120
  115.6 31.9 %collective-permute-start.17 = (bf16[112,4096]{1,0:T(8,128)(2,1)S(1)}, bf16[112,4096]{1,0:T(8,128)(2,1)S(1)}, u32[]{:S(2)}, u32[]{:S(2)}) collective-permute-start(bf16[112,4096]{1,0:T(8,128)(2,1)S(1)} %get-tuple-element.92), channel_id=1, source_target_pairs={{0,12},{1,13},{2,14},{3,15},{4,0},{5,1},{6,2},{7,3},{8,4},{9,5},{1... | collective-permute-start | bytes 2752520 | tf_op jit(solution)/shard_map/ppermute | solution.py:120
  132.6 15.5 %collective-permute-start.20 = (bf16[32,4096]{1,0:T(8,128)(2,1)S(1)}, bf16[32,4096]{1,0:T(8,128)(2,1)S(1)}, u32[]{:S(2)}, u32[]{:S(2)}) collective-permute-start(bf16[32,4096]{1,0:T(8,128)(2,1)S(1)} %get-tuple-element.101), channel_id=1, source_target_pairs={{0,1},{1,2},{2,3},{3,0},{4,5},{5,6},{6,7},{7,4},{8,9},{9,10},{10,1... | collective-permute-start | bytes 786440 | tf_op jit(solution)/shard_map/ppermute | solution.py:120
  133.2 14.9 %collective-permute-start.21 = (bf16[32,4096]{1,0:T(8,128)(2,1)S(1)}, bf16[32,4096]{1,0:T(8,128)(2,1)S(1)}, u32[]{:S(2)}, u32[]{:S(2)}) collective-permute-start(bf16[32,4096]{1,0:T(8,128)(2,1)S(1)} %get-tuple-element.102), channel_id=1, source_target_pairs={{0,3},{1,0},{2,1},{3,2},{4,7},{5,4},{6,5},{7,6},{8,11},{9,8},{10,9... | collective-permute-start | bytes 786440 | tf_op jit(solution)/shard_map/ppermute | solution.py:120
  148.2 9.3 %collective-permute-start.22 = (bf16[64,4096]{1,0:T(8,128)(2,1)S(1)}, bf16[64,4096]{1,0:T(8,128)(2,1)S(1)}, u32[]{:S(2)}, u32[]{:S(2)}) collective-permute-start(bf16[64,4096]{1,0:T(8,128)(2,1)S(1)} %get-tuple-element.103), channel_id=1, source_target_pairs={{0,1},{1,2},{2,3},{3,0},{4,5},{5,6},{6,7},{7,4},{8,9},{9,10},{10,1... | collective-permute-start | bytes 1572872 | tf_op jit(solution)/shard_map/ppermute | solution.py:120
  148.8 10.4 %collective-permute-start.23 = (bf16[64,4096]{1,0:T(8,128)(2,1)S(1)}, bf16[64,4096]{1,0:T(8,128)(2,1)S(1)}, u32[]{:S(2)}, u32[]{:S(2)}) collective-permute-start(bf16[64,4096]{1,0:T(8,128)(2,1)S(1)} %get-tuple-element.104), channel_id=1, source_target_pairs={{0,3},{1,0},{2,1},{3,2},{4,7},{5,4},{6,5},{7,6},{8,11},{9,8},{10,9... | collective-permute-start | bytes 1572872 | tf_op jit(solution)/shard_map/ppermute | solution.py:120

commit v13 on v11

--- a/solution.py
+++ b/solution.py
@@ -12,7 +12,7 @@
 SIDE = 4
 LANES = 128
 CHUNK = 1024
-STRIPE = 512
+STRIPE = 1024
 GRANT = 8 << 20
 STREAM = 62 << 20
 

time: 174 us -> 174 us (level)
  no operation moved by 1% of the time
where the time goes in v13:
time: 174 us; the launch traced here: 173 us
  waiting for transfers between devices  61.6 us (35%)
  blocking collectives  61.4 us (35%)
  starting transfers between devices  31.4 us (18%)
  Pallas kernels  17.7 us (10%)
    ppermute x24, waiting for transfers between devices, shift(): return lax.ppermute(value, ('dp', 'expert'), pairs)  61.6 us
    all_to_all x3, blocking collectives, swap_over_tensor(): lax.all_to_all(value, 'tensor', split_axis=0, concat_axis=0, tiled=True)  61.4 us
    ppermute x24, starting transfers between devices, shift(): return lax.ppermute(value, ('dp', 'expert'), pairs)  31.4 us
    pallas_call x6, Pallas kernels, run_expert(): pl.pallas_call(functools.partial(expert_kernel, count), out_shape=[jax.Sh...  9.4 us
  transfers between devices with their start and end apart: 24, of which 17 were waited for; matrix products, arithmetic and copies ran while one was open for 0% of the time, Pallas kernels for 7%

profile of v13, /device:TPU:24, one launch (start us, length us, event | category | flops | bytes accessed | tf_op | source)
XLA Modules:
  0.0 173.2 jit_solution(15410620599384290272)
XLA Ops:
  0.0 3.4 %shard_map.91 = bf16[64,4096]{1,0:T(8,128)(2,1)} custom-call(bf16[64,512]{1,0:T(8,128)(2,1)} %bitcast.46, bf16[512,4096]{1,0:T(8,128)(2,1)} %proj_hbm.1), custom_call_target="tpu_custom_call" | custom-call | flops 268435456 | bytes 4194304 | tf_op jit(solution)/shard_map/pallas_call | solution.py:47
  3.4 26.1 %all_to_all.31 = bf16[8,8,4096]{2,1,0:T(8,128)(2,1)S(1)} all-to-all(bf16[8,8,4096]{2,1,0:T(8,128)(2,1)} %bitcast.45), channel_id=1, replica_groups=mesh['dp'=2,'tensor'=8,'expert'=16] {'tensor'}, dimensions={0} | all-to-all | bytes 1048576 | tf_op jit(solution)/shard_map/all_to_all | solution.py:106
  29.8 18.9 %all_to_all.32 = bf16[8,8,4224]{2,1,0:T(8,128)(2,1)S(1)} all-to-all(bf16[8,8,4224]{2,1,0:T(8,128)(2,1)S(1)} %bitcast.40), channel_id=1, replica_groups=mesh['dp'=2,'tensor'=8,'expert'=16] {'tensor'}, dimensions={0} | all-to-all | bytes 1081344 | tf_op jit(solution)/shard_map/all_to_all | solution.py:106
  48.8 2.8 %collective-permute-start.1 = (bf16[64,4224]{1,0:T(8,128)(2,1)S(1)}, bf16[64,4224]{1,0:T(8,128)(2,1)S(1)}, u32[]{:S(2)}, u32[]{:S(2)}) collective-permute-start(bf16[64,4224]{1,0:T(8,128)(2,1)S(1)} %bitcast.36), channel_id=1, source_target_pairs={{0,3},{1,0},{2,1},{3,2},{4,7},{5,4},{6,5},{7,6},{8,11},{9,8},{10,9... | collective-permute-start | bytes 1622024 | tf_op jit(solution)/shard_map/ppermute | solution.py:120
  51.5 6.9 %collective-permute-done.1._.low_ref = bf16[64,4224]{1,0:T(8,128)(2,1)S(1)} collective-permute-done((bf16[64,4224]{1,0:T(8,128)(2,1)S(1)}, bf16[64,4224]{1,0:T(8,128)(2,1)S(1)}, u32[]{:S(2)}, u32[]{:S(2)}) %collective-permute-start.1) | collective-permute-done | bytes 540704 | tf_op jit(solution)/shard_map/ppermute | solution.py:120
  58.4 3.8 %collective-permute-start.5 = (bf16[32,4224]{1,0:T(8,128)(2,1)S(1)}, bf16[32,4224]{1,0:T(8,128)(2,1)S(1)}, u32[]{:S(2)}, u32[]{:S(2)}) collective-permute-start(bf16[32,4224]{1,0:T(8,128)(2,1)S(1)} %slice.9), channel_id=1, source_target_pairs={{0,3},{1,0},{2,1},{3,2},{4,7},{5,4},{6,5},{7,6},{8,11},{9,8},{10,9... | collective-permute-start | bytes 811016 | tf_op jit(solution)/shard_map/ppermute | solution.py:120
  62.3 0.6 shard_map.93
  63.2 1.8 %collective-permute-start.3 = (bf16[112,4224]{1,0:T(8,128)(2,1)S(1)}, bf16[112,4224]{1,0:T(8,128)(2,1)S(1)}, u32[]{:S(2)}, u32[]{:S(2)}) collective-permute-start(bf16[112,4224]{1,0:T(8,128)(2,1)S(1)} %get-tuple-element.62), channel_id=1, source_target_pairs={{0,12},{1,13},{2,14},{3,15},{4,0},{5,1},{6,2},{7,3},{8,4},{9,5},{1... | collective-permute-start | bytes 2838536 | tf_op jit(solution)/shard_map/ppermute | solution.py:120
  65.0 1.5 shard_map.94._.own_ref
  66.6 2.5 %collective-permute-done.5.refs_1_ = bf16[32,4224]{1,0:T(8,128)(2,1)S(1)} collective-permute-done((bf16[32,4224]{1,0:T(8,128)(2,1)S(1)}, bf16[32,4224]{1,0:T(8,128)(2,1)S(1)}, u32[]{:S(2)}, u32[]{:S(2)}) %collective-permute-start.5) | collective-permute-done | bytes 270368 | tf_op jit(solution)/shard_map/ppermute | solution.py:120
  69.1 3.8 %collective-permute-done.4.refs_0_ = bf16[32,4224]{1,0:T(8,128)(2,1)S(1)} collective-permute-done((bf16[32,4224]{1,0:T(8,128)(2,1)S(1)}, bf16[32,4224]{1,0:T(8,128)(2,1)S(1)}, u32[]{:S(2)}, u32[]{:S(2)}) %collective-permute-start.4) | collective-permute-done | bytes 270368 | tf_op jit(solution)/shard_map/ppermute | solution.py:120
  72.9 0.6 shard_map.96
  73.9 1.8 %collective-permute-start.7 = (bf16[112,4224]{1,0:T(8,128)(2,1)S(1)}, bf16[112,4224]{1,0:T(8,128)(2,1)S(1)}, u32[]{:S(2)}, u32[]{:S(2)}) collective-permute-start(bf16[112,4224]{1,0:T(8,128)(2,1)S(1)} %get-tuple-element.67), channel_id=1, source_target_pairs={{0,12},{1,13},{2,14},{3,15},{4,0},{5,1},{6,2},{7,3},{8,4},{9,5},{1... | collective-permute-start | bytes 2838536 | tf_op jit(solution)/shard_map/ppermute | solution.py:120
  75.7 1.1 collective-permute-done.2.refs_0_.back_ref
  76.7 1.4 collective-permute-done.3.refs_1_.front_ref
  78.1 1.7 shard_map.95
  79.9 1.5 shard_map.97._.own_ref
  81.4 0.6 shard_map.98
  82.0 0.9 collective-permute-start.9
  82.9 2.6 %collective-permute-start.8 = (bf16[48,4224]{1,0:T(8,128)(2,1)S(1)}, bf16[48,4224]{1,0:T(8,128)(2,1)S(1)}, u32[]{:S(2)}, u32[]{:S(2)}) collective-permute-start(bf16[48,4224]{1,0:T(8,128)(2,1)S(1)} %get-tuple-element.65._), channel_id=1, source_target_pairs={{0,4},{1,5},{2,6},{3,7},{4,8},{5,9},{6,10},{7,11},{8,12},{9,13},{1... | collective-permute-start | bytes 1216520 | tf_op jit(solution)/shard_map/ppermute | solution.py:120
  85.5 1.8 %collective-permute-done.6.back_ref.refs_0_ = bf16[112,4224]{1,0:T(8,128)(2,1)S(1)} collective-permute-done((bf16[112,4224]{1,0:T(8,128)(2,1)S(1)}, bf16[112,4224]{1,0:T(8,128)(2,1)S(1)}, u32[]{:S(2)}, u32[]{:S(2)}) %collective-permute-start.6) | collective-permute-done | bytes 946208 | tf_op jit(solution)/shard_map/ppermute | solution.py:120
  87.3 1.4 collective-permute-done.7.front_ref.refs_1_
  88.8 0.6 shard_map.99
  89.4 2.0 %collective-permute-start.10 = (bf16[48,4224]{1,0:T(8,128)(2,1)S(1)}, bf16[48,4224]{1,0:T(8,128)(2,1)S(1)}, u32[]{:S(2)}, u32[]{:S(2)}) collective-permute-start(bf16[48,4224]{1,0:T(8,128)(2,1)S(1)} %get-tuple-element.74), channel_id=1, source_target_pairs={{0,4},{1,5},{2,6},{3,7},{4,8},{5,9},{6,10},{7,11},{8,12},{9,13},{1... | collective-permute-start | bytes 1216520 | tf_op jit(solution)/shard_map/ppermute | solution.py:120
  91.5 1.6 collective-permute-done.9.refs_1_
  93.1 1.5 shard_map.100
  94.6 2.0 %collective-permute-start.13 = (bf16[48,4096]{1,0:T(8,128)(2,1)S(1)}, bf16[48,4096]{1,0:T(8,128)(2,1)S(1)}, u32[]{:S(2)}, u32[]{:S(2)}) collective-permute-start(bf16[48,4096]{1,0:T(8,128)(2,1)S(1)} %get-tuple-element.79), channel_id=1, source_target_pairs={{0,4},{1,5},{2,6},{3,7},{4,8},{5,9},{6,10},{7,11},{8,12},{9,13},{1... | collective-permute-start | bytes 1179656 | tf_op jit(solution)/shard_map/ppermute | solution.py:120
  96.7 0.7 collective-permute-done.10.refs_0_
  97.4 3.1 %collective-permute-done.11.refs_1_ = bf16[48,4224]{1,0:T(8,128)(2,1)S(1)} collective-permute-done((bf16[48,4224]{1,0:T(8,128)(2,1)S(1)}, bf16[48,4224]{1,0:T(8,128)(2,1)S(1)}, u32[]{:S(2)}, u32[]{:S(2)}) %collective-permute-start.11) | collective-permute-done | bytes 405536 | tf_op jit(solution)/shard_map/ppermute | solution.py:120
  100.5 1.5 shard_map.101
  102.0 2.0 %collective-permute-start.14 = (bf16[48,4096]{1,0:T(8,128)(2,1)S(1)}, bf16[48,4096]{1,0:T(8,128)(2,1)S(1)}, u32[]{:S(2)}, u32[]{:S(2)}) collective-permute-start(bf16[48,4096]{1,0:T(8,128)(2,1)S(1)} %get-tuple-element.75._), channel_id=1, source_target_pairs={{0,12},{1,13},{2,14},{3,15},{4,0},{5,1},{6,2},{7,3},{8,4},{9,5},{1... | collective-permute-start | bytes 1179656 | tf_op jit(solution)/shard_map/ppermute | solution.py:120
  104.1 1.7 shard_map.102
  105.8 4.0 %collective-permute-done.15.high_ref = bf16[48,4096]{1,0:T(8,128)(2,1)S(1)} collective-permute-done((bf16[48,4096]{1,0:T(8,128)(2,1)S(1)}, bf16[48,4096]{1,0:T(8,128)(2,1)S(1)}, u32[]{:S(2)}, u32[]{:S(2)}) %collective-permute-start.15) | collective-permute-done | bytes 393248 | tf_op jit(solution)/shard_map/ppermute | solution.py:120
  109.8 1.3 collective-permute-done.14.low_ref
  112.2 2.0 %collective-permute-start.19 = (bf16[112,4096]{1,0:T(8,128)(2,1)S(1)}, bf16[112,4096]{1,0:T(8,128)(2,1)S(1)}, u32[]{:S(2)}, u32[]{:S(2)}) collective-permute-start(bf16[112,4096]{1,0:T(8,128)(2,1)S(1)} %get-tuple-element.96), channel_id=1, source_target_pairs={{0,12},{1,13},{2,14},{3,15},{4,0},{5,1},{6,2},{7,3},{8,4},{9,5},{1... | collective-permute-start | bytes 2752520 | tf_op jit(solution)/shard_map/ppermute | solution.py:120
  114.2 1.3 collective-permute-start.16
  115.5 0.7 collective-permute-start.17
  116.2 12.0 %collective-permute-done.18.back_ref = bf16[112,4096]{1,0:T(8,128)(2,1)S(1)} collective-permute-done((bf16[112,4096]{1,0:T(8,128)(2,1)S(1)}, bf16[112,4096]{1,0:T(8,128)(2,1)S(1)}, u32[]{:S(2)}, u32[]{:S(2)}) %collective-permute-start.18) | collective-permute-done | bytes 917536 | tf_op jit(solution)/shard_map/ppermute | solution.py:120
  128.2 1.3 collective-permute-done.19.front_ref
  129.5 0.5 shard_map.106
  130.1 3.2 %collective-permute-start.21 = (bf16[32,4096]{1,0:T(8,128)(2,1)S(1)}, bf16[32,4096]{1,0:T(8,128)(2,1)S(1)}, u32[]{:S(2)}, u32[]{:S(2)}) collective-permute-start(bf16[32,4096]{1,0:T(8,128)(2,1)S(1)} %get-tuple-element.102), channel_id=1, source_target_pairs={{0,3},{1,0},{2,1},{3,2},{4,7},{5,4},{6,5},{7,6},{8,11},{9,8},{10,9... | collective-permute-start | bytes 786440 | tf_op jit(solution)/shard_map/ppermute | solution.py:120
  133.3 10.1 %collective-permute-done.16.back_ref = bf16[112,4096]{1,0:T(8,128)(2,1)S(1)} collective-permute-done((bf16[112,4096]{1,0:T(8,128)(2,1)S(1)}, bf16[112,4096]{1,0:T(8,128)(2,1)S(1)}, u32[]{:S(2)}, u32[]{:S(2)}) %collective-permute-start.16) | collective-permute-done | bytes 917536 | tf_op jit(solution)/shard_map/ppermute | solution.py:120
  143.5 1.3 collective-permute-done.17.front_ref
  144.8 0.5 shard_map.104
  145.6 3.2 %collective-permute-start.23 = (bf16[64,4096]{1,0:T(8,128)(2,1)S(1)}, bf16[64,4096]{1,0:T(8,128)(2,1)S(1)}, u32[]{:S(2)}, u32[]{:S(2)}) collective-permute-start(bf16[64,4096]{1,0:T(8,128)(2,1)S(1)} %get-tuple-element.104), channel_id=1, source_target_pairs={{0,3},{1,0},{2,1},{3,2},{4,7},{5,4},{6,5},{7,6},{8,11},{9,8},{10,9... | collective-permute-start | bytes 1572872 | tf_op jit(solution)/shard_map/ppermute | solution.py:120
  148.8 7.2 %collective-permute-done.22 = bf16[64,4096]{1,0:T(8,128)(2,1)S(1)} collective-permute-done((bf16[64,4096]{1,0:T(8,128)(2,1)S(1)}, bf16[64,4096]{1,0:T(8,128)(2,1)S(1)}, u32[]{:S(2)}, u32[]{:S(2)}) %collective-permute-start.22) | collective-permute-done | bytes 524320 | tf_op jit(solution)/shard_map/ppermute | solution.py:120
  156.1 16.3 %all_to_all.33 = bf16[8,8,4096]{2,1,0:T(8,128)(2,1)S(1)} all-to-all(bf16[8,8,4096]{2,1,0:T(8,128)(2,1)S(1)} %fusion), channel_id=1, replica_groups=mesh['dp'=2,'tensor'=8,'expert'=16] {'tensor'}, dimensions={0} | all-to-all | bytes 1048576 | tf_op jit(solution)/shard_map/all_to_all | solution.py:106
  172.5 0.7 fusion.1
  (39 shorter events, 2.9 us)
Async XLA Ops:
  0.0 29.5 %copy-start.3 = (bf16[1,8,4096]{2,1,0:T(8,128)(2,1)S(1)}, bf16[1,8,4096]{2,1,0:T(8,128)(2,1)}, u32[]{:S(2)}) copy-start(bf16[1,8,4096]{2,1,0:T(8,128)(2,1)} %param.11) | copy-start | bytes 196612
  0.0 29.5 %copy-start.4 = (f32[4096]{0:T(1024)S(1)}, f32[4096]{0:T(1024)}, u32[]{:S(2)}) copy-start(f32[4096]{0:T(1024)} %param.12) | copy-start | bytes 49156
  0.0 29.5 %copy-start.5 = (s32[1,8,8]{2,1,0:T(8,128)S(1)}, s32[1,8,8]{2,1,0:T(8,128)}, u32[]{:S(2)}) copy-start(s32[1,8,8]{2,1,0:T(8,128)} %param.13) | copy-start | bytes 772
  0.0 29.5 %copy-start.6 = (s32[1,8,8]{2,1,0:T(8,128)S(1)}, s32[1,8,8]{2,1,0:T(8,128)}, u32[]{:S(2)}) copy-start(s32[1,8,8]{2,1,0:T(8,128)} %param.14) | copy-start | bytes 772
  3.4 61.6 %copy-start.2 = (bf16[1,192,4096]{2,1,0:T(8,128)(2,1)S(1)}, bf16[1,192,4096]{2,1,0:T(8,128)(2,1)}, u32[]{:S(2)}) copy-start(bf16[1,192,4096]{2,1,0:T(8,128)(2,1)} %param.17) | copy-start | bytes 4718596
  29.8 35.2 %copy-start.1 = (bf16[1,192,4096]{2,1,0:T(8,128)(2,1)S(1)}, bf16[1,192,4096]{2,1,0:T(8,128)(2,1)}, u32[]{:S(2)}) copy-start(bf16[1,192,4096]{2,1,0:T(8,128)(2,1)} %param.16) | copy-start | bytes 4718596
  48.8 16.3 %copy-start = (bf16[1,192,4096]{2,1,0:T(8,128)(2,1)S(1)}, bf16[1,192,4096]{2,1,0:T(8,128)(2,1)}, u32[]{:S(2)}) copy-start(bf16[1,192,4096]{2,1,0:T(8,128)(2,1)} %param.15) | copy-start | bytes 4718596
  48.8 9.6 %collective-permute-start.1 = (bf16[64,4224]{1,0:T(8,128)(2,1)S(1)}, bf16[64,4224]{1,0:T(8,128)(2,1)S(1)}, u32[]{:S(2)}, u32[]{:S(2)}) collective-permute-start(bf16[64,4224]{1,0:T(8,128)(2,1)S(1)} %bitcast.36), channel_id=1, source_target_pairs={{0,3},{1,0},{2,1},{3,2},{4,7},{5,4},{6,5},{7,6},{8,11},{9,8},{10,9... | collective-permute-start | bytes 1622024 | tf_op jit(solution)/shard_map/ppermute | solution.py:120
  51.5 10.7 %collective-permute-start = (bf16[64,4224]{1,0:T(8,128)(2,1)S(1)}, bf16[64,4224]{1,0:T(8,128)(2,1)S(1)}, u32[]{:S(2)}, u32[]{:S(2)}) collective-permute-start(bf16[64,4224]{1,0:T(8,128)(2,1)S(1)} %bitcast.37), channel_id=1, source_target_pairs={{0,1},{1,2},{2,3},{3,0},{4,5},{5,6},{6,7},{7,4},{8,9},{9,10},{10,1... | collective-permute-start | bytes 1622024 | tf_op jit(solution)/shard_map/ppermute | solution.py:120
  58.4 10.7 %collective-permute-start.5 = (bf16[32,4224]{1,0:T(8,128)(2,1)S(1)}, bf16[32,4224]{1,0:T(8,128)(2,1)S(1)}, u32[]{:S(2)}, u32[]{:S(2)}) collective-permute-start(bf16[32,4224]{1,0:T(8,128)(2,1)S(1)} %slice.9), channel_id=1, source_target_pairs={{0,3},{1,0},{2,1},{3,2},{4,7},{5,4},{6,5},{7,6},{8,11},{9,8},{10,9... | collective-permute-start | bytes 811016 | tf_op jit(solution)/shard_map/ppermute | solution.py:120
  62.2 10.7 %collective-permute-start.4 = (bf16[32,4224]{1,0:T(8,128)(2,1)S(1)}, bf16[32,4224]{1,0:T(8,128)(2,1)S(1)}, u32[]{:S(2)}, u32[]{:S(2)}) collective-permute-start(bf16[32,4224]{1,0:T(8,128)(2,1)S(1)} %slice.8), channel_id=1, source_target_pairs={{0,1},{1,2},{2,3},{3,0},{4,5},{5,6},{6,7},{7,4},{8,9},{9,10},{10,1... | collective-permute-start | bytes 811016 | tf_op jit(solution)/shard_map/ppermute | solution.py:120
  62.9 13.8 %collective-permute-start.2 = (bf16[112,4224]{1,0:T(8,128)(2,1)S(1)}, bf16[112,4224]{1,0:T(8,128)(2,1)S(1)}, u32[]{:S(2)}, u32[]{:S(2)}) collective-permute-start(bf16[112,4224]{1,0:T(8,128)(2,1)S(1)} %get-tuple-element.61), channel_id=1, source_target_pairs={{0,4},{1,5},{2,6},{3,7},{4,8},{5,9},{6,10},{7,11},{8,12},{9,13},{1... | collective-permute-start | bytes 2838536 | tf_op jit(solution)/shard_map/ppermute | solution.py:120
  63.2 14.9 %collective-permute-start.3 = (bf16[112,4224]{1,0:T(8,128)(2,1)S(1)}, bf16[112,4224]{1,0:T(8,128)(2,1)S(1)}, u32[]{:S(2)}, u32[]{:S(2)}) collective-permute-start(bf16[112,4224]{1,0:T(8,128)(2,1)S(1)} %get-tuple-element.62), channel_id=1, source_target_pairs={{0,12},{1,13},{2,14},{3,15},{4,0},{5,1},{6,2},{7,3},{8,4},{9,5},{1... | collective-permute-start | bytes 2838536 | tf_op jit(solution)/shard_map/ppermute | solution.py:120
  73.6 13.8 %collective-permute-start.6 = (bf16[112,4224]{1,0:T(8,128)(2,1)S(1)}, bf16[112,4224]{1,0:T(8,128)(2,1)S(1)}, u32[]{:S(2)}, u32[]{:S(2)}) collective-permute-start(bf16[112,4224]{1,0:T(8,128)(2,1)S(1)} %get-tuple-element.66), channel_id=1, source_target_pairs={{0,4},{1,5},{2,6},{3,7},{4,8},{5,9},{6,10},{7,11},{8,12},{9,13},{1... | collective-permute-start | bytes 2838536 | tf_op jit(solution)/shard_map/ppermute | solution.py:120
  73.9 14.9 %collective-permute-start.7 = (bf16[112,4224]{1,0:T(8,128)(2,1)S(1)}, bf16[112,4224]{1,0:T(8,128)(2,1)S(1)}, u32[]{:S(2)}, u32[]{:S(2)}) collective-permute-start(bf16[112,4224]{1,0:T(8,128)(2,1)S(1)} %get-tuple-element.67), channel_id=1, source_target_pairs={{0,12},{1,13},{2,14},{3,15},{4,0},{5,1},{6,2},{7,3},{8,4},{9,5},{1... | collective-permute-start | bytes 2838536 | tf_op jit(solution)/shard_map/ppermute | solution.py:120
  82.0 11.1 %collective-permute-start.9 = (bf16[48,4224]{1,0:T(8,128)(2,1)S(1)}, bf16[48,4224]{1,0:T(8,128)(2,1)S(1)}, u32[]{:S(2)}, u32[]{:S(2)}) collective-permute-start(bf16[48,4224]{1,0:T(8,128)(2,1)S(1)} %get-tuple-element.72), channel_id=1, source_target_pairs={{0,12},{1,13},{2,14},{3,15},{4,0},{5,1},{6,2},{7,3},{8,4},{9,5},{1... | collective-permute-start | bytes 1216520 | tf_op jit(solution)/shard_map/ppermute | solution.py:120
  82.9 10.3 %collective-permute-start.8 = (bf16[48,4224]{1,0:T(8,128)(2,1)S(1)}, bf16[48,4224]{1,0:T(8,128)(2,1)S(1)}, u32[]{:S(2)}, u32[]{:S(2)}) collective-permute-start(bf16[48,4224]{1,0:T(8,128)(2,1)S(1)} %get-tuple-element.65._), channel_id=1, source_target_pairs={{0,4},{1,5},{2,6},{3,7},{4,8},{5,9},{6,10},{7,11},{8,12},{9,13},{1... | collective-permute-start | bytes 1216520 | tf_op jit(solution)/shard_map/ppermute | solution.py:120
  89.4 8.0 %collective-permute-start.10 = (bf16[48,4224]{1,0:T(8,128)(2,1)S(1)}, bf16[48,4224]{1,0:T(8,128)(2,1)S(1)}, u32[]{:S(2)}, u32[]{:S(2)}) collective-permute-start(bf16[48,4224]{1,0:T(8,128)(2,1)S(1)} %get-tuple-element.74), channel_id=1, source_target_pairs={{0,4},{1,5},{2,6},{3,7},{4,8},{5,9},{6,10},{7,11},{8,12},{9,13},{1... | collective-permute-start | bytes 1216520 | tf_op jit(solution)/shard_map/ppermute | solution.py:120
  91.4 9.1 %collective-permute-start.11 = (bf16[48,4224]{1,0:T(8,128)(2,1)S(1)}, bf16[48,4224]{1,0:T(8,128)(2,1)S(1)}, u32[]{:S(2)}, u32[]{:S(2)}) collective-permute-start(bf16[48,4224]{1,0:T(8,128)(2,1)S(1)} %get-tuple-element.71._), channel_id=1, source_target_pairs={{0,12},{1,13},{2,14},{3,15},{4,0},{5,1},{6,2},{7,3},{8,4},{9,5},{1... | collective-permute-start | bytes 1216520 | tf_op jit(solution)/shard_map/ppermute | solution.py:120
  94.6 11.2 %collective-permute-start.13 = (bf16[48,4096]{1,0:T(8,128)(2,1)S(1)}, bf16[48,4096]{1,0:T(8,128)(2,1)S(1)}, u32[]{:S(2)}, u32[]{:S(2)}) collective-permute-start(bf16[48,4096]{1,0:T(8,128)(2,1)S(1)} %get-tuple-element.79), channel_id=1, source_target_pairs={{0,4},{1,5},{2,6},{3,7},{4,8},{5,9},{6,10},{7,11},{8,12},{9,13},{1... | collective-permute-start | bytes 1179656 | tf_op jit(solution)/shard_map/ppermute | solution.py:120
  96.6 9.2 %collective-permute-start.12 = (bf16[48,4096]{1,0:T(8,128)(2,1)S(1)}, bf16[48,4096]{1,0:T(8,128)(2,1)S(1)}, u32[]{:S(2)}, u32[]{:S(2)}) collective-permute-start(bf16[48,4096]{1,0:T(8,128)(2,1)S(1)} %get-tuple-element.73._), channel_id=1, source_target_pairs={{0,12},{1,13},{2,14},{3,15},{4,0},{5,1},{6,2},{7,3},{8,4},{9,5},{1... | collective-permute-start | bytes 1179656 | tf_op jit(solution)/shard_map/ppermute | solution.py:120
  102.0 7.9 %collective-permute-start.15 = (bf16[48,4096]{1,0:T(8,128)(2,1)S(1)}, bf16[48,4096]{1,0:T(8,128)(2,1)S(1)}, u32[]{:S(2)}, u32[]{:S(2)}) collective-permute-start(bf16[48,4096]{1,0:T(8,128)(2,1)S(1)} %get-tuple-element.80), channel_id=1, source_target_pairs={{0,4},{1,5},{2,6},{3,7},{4,8},{5,9},{6,10},{7,11},{8,12},{9,13},{1... | collective-permute-start | bytes 1179656 | tf_op jit(solution)/shard_map/ppermute | solution.py:120
  102.0 9.1 %collective-permute-start.14 = (bf16[48,4096]{1,0:T(8,128)(2,1)S(1)}, bf16[48,4096]{1,0:T(8,128)(2,1)S(1)}, u32[]{:S(2)}, u32[]{:S(2)}) collective-permute-start(bf16[48,4096]{1,0:T(8,128)(2,1)S(1)} %get-tuple-element.75._), channel_id=1, source_target_pairs={{0,12},{1,13},{2,14},{3,15},{4,0},{5,1},{6,2},{7,3},{8,4},{9,5},{1... | collective-permute-start | bytes 1179656 | tf_op jit(solution)/shard_map/ppermute | solution.py:120
  112.1 16.1 %collective-permute-start.18 = (bf16[112,4096]{1,0:T(8,128)(2,1)S(1)}, bf16[112,4096]{1,0:T(8,128)(2,1)S(1)}, u32[]{:S(2)}, u32[]{:S(2)}) collective-permute-start(bf16[112,4096]{1,0:T(8,128)(2,1)S(1)} %get-tuple-element.95), channel_id=1, source_target_pairs={{0,4},{1,5},{2,6},{3,7},{4,8},{5,9},{6,10},{7,11},{8,12},{9,13},{1... | collective-permute-start | bytes 2752520 | tf_op jit(solution)/shard_map/ppermute | solution.py:120
  112.2 17.3 %collective-permute-start.19 = (bf16[112,4096]{1,0:T(8,128)(2,1)S(1)}, bf16[112,4096]{1,0:T(8,128)(2,1)S(1)}, u32[]{:S(2)}, u32[]{:S(2)}) collective-permute-start(bf16[112,4096]{1,0:T(8,128)(2,1)S(1)} %get-tuple-element.96), channel_id=1, source_target_pairs={{0,12},{1,13},{2,14},{3,15},{4,0},{5,1},{6,2},{7,3},{8,4},{9,5},{1... | collective-permute-start | bytes 2752520 | tf_op jit(solution)/shard_map/ppermute | solution.py:120
  114.2 29.3 %collective-permute-start.16 = (bf16[112,4096]{1,0:T(8,128)(2,1)S(1)}, bf16[112,4096]{1,0:T(8,128)(2,1)S(1)}, u32[]{:S(2)}, u32[]{:S(2)}) collective-permute-start(bf16[112,4096]{1,0:T(8,128)(2,1)S(1)} %get-tuple-element.85), channel_id=1, source_target_pairs={{0,4},{1,5},{2,6},{3,7},{4,8},{5,9},{6,10},{7,11},{8,12},{9,13},{1... | collective-permute-start | bytes 2752520 | tf_op jit(solution)/shard_map/ppermute | solution.py:120
  115.5 29.3 %collective-permute-start.17 = (bf16[112,4096]{1,0:T(8,128)(2,1)S(1)}, bf16[112,4096]{1,0:T(8,128)(2,1)S(1)}, u32[]{:S(2)}, u32[]{:S(2)}) collective-permute-start(bf16[112,4096]{1,0:T(8,128)(2,1)S(1)} %get-tuple-element.86._), channel_id=1, source_target_pairs={{0,12},{1,13},{2,14},{3,15},{4,0},{5,1},{6,2},{7,3},{8,4},{9,5},{1... | collective-permute-start | bytes 2752520 | tf_op jit(solution)/shard_map/ppermute | solution.py:120
  130.0 15.3 %collective-permute-start.20 = (bf16[32,4096]{1,0:T(8,128)(2,1)S(1)}, bf16[32,4096]{1,0:T(8,128)(2,1)S(1)}, u32[]{:S(2)}, u32[]{:S(2)}) collective-permute-start(bf16[32,4096]{1,0:T(8,128)(2,1)S(1)} %get-tuple-element.101), channel_id=1, source_target_pairs={{0,1},{1,2},{2,3},{3,0},{4,5},{5,6},{6,7},{7,4},{8,9},{9,10},{10,1... | collective-permute-start | bytes 786440 | tf_op jit(solution)/shard_map/ppermute | solution.py:120
  130.1 15.2 %collective-permute-start.21 = (bf16[32,4096]{1,0:T(8,128)(2,1)S(1)}, bf16[32,4096]{1,0:T(8,128)(2,1)S(1)}, u32[]{:S(2)}, u32[]{:S(2)}) collective-permute-start(bf16[32,4096]{1,0:T(8,128)(2,1)S(1)} %get-tuple-element.102), channel_id=1, source_target_pairs={{0,3},{1,0},{2,1},{3,2},{4,7},{5,4},{6,5},{7,6},{8,11},{9,8},{10,9... | collective-permute-start | bytes 786440 | tf_op jit(solution)/shard_map/ppermute | solution.py:120
  145.5 10.5 %collective-permute-start.22 = (bf16[64,4096]{1,0:T(8,128)(2,1)S(1)}, bf16[64,4096]{1,0:T(8,128)(2,1)S(1)}, u32[]{:S(2)}, u32[]{:S(2)}) collective-permute-start(bf16[64,4096]{1,0:T(8,128)(2,1)S(1)} %get-tuple-element.103), channel_id=1, source_target_pairs={{0,1},{1,2},{2,3},{3,0},{4,5},{5,6},{6,7},{7,4},{8,9},{9,10},{10,1... | collective-permute-start | bytes 1572872 | tf_op jit(solution)/shard_map/ppermute | solution.py:120
  145.6 10.4 %collective-permute-start.23 = (bf16[64,4096]{1,0:T(8,128)(2,1)S(1)}, bf16[64,4096]{1,0:T(8,128)(2,1)S(1)}, u32[]{:S(2)}, u32[]{:S(2)}) collective-permute-start(bf16[64,4096]{1,0:T(8,128)(2,1)S(1)} %get-tuple-element.104), channel_id=1, source_target_pairs={{0,3},{1,0},{2,1},{3,2},{4,7},{5,4},{6,5},{7,6},{8,11},{9,8},{10,9... | collective-permute-start | bytes 1572872 | tf_op jit(solution)/shard_map/ppermute | solution.py:120
